TPU v7x, 32 devices: a whole 2x2x4 slice. The times are simulated.
32 devices in a mesh: dp: 4 (over x, core), expert: 8 (over z, y).
Axes of the slice: x: 2, y: 2, z: 4, core: 2. Of those that a mesh axis runs over, the one named last changes fastest.
Arguments:
- block_entries: bfloat16 [32768, 768], P(('dp', 'expert')), may hold values from -6 to 6
- assignments: int32 [32768], P(('dp', 'expert')), may hold values from 0 to 7, as said below
- positions_within: int32 [32768], P(('dp', 'expert')), may hold values from 0 to 128, as said below
- specialist_quotas: int32 [8], replicated, may hold values from 64 to 128, as said below
- standardize_one_scale: bfloat16 [768], P('expert'), may hold values from 0.5 to 1.5
- standardize_one_shift: bfloat16 [768], P('expert'), may hold values from -0.625 to 0.625
- asking_weights: bfloat16 [768, 768], P('expert', 'dp'), may hold values from -0.21875 to 0.21875
- asking_shift: bfloat16 [768], P('expert'), may hold values from -0.625 to 0.625
- lookup_weights: bfloat16 [768, 768], P('expert', 'dp'), may hold values from -0.21875 to 0.21875
- content_weights: bfloat16 [768, 768], P('expert', 'dp'), may hold values from -0.21875 to 0.21875
- content_shift: bfloat16 [768], P('expert'), may hold values from -0.625 to 0.625
- context_mixing_weights: bfloat16 [768, 768], P('expert', 'dp'), may hold values from -1.75 to 1.75
- context_mixing_shift: bfloat16 [768], P('expert'), may hold values from -0.625 to 0.625
- standardize_two_scale: bfloat16 [768], P('expert'), may hold values from 0.5 to 1.5
- standardize_two_shift: bfloat16 [768], P('expert'), may hold values from -0.625 to 0.625
- gating_prototypes: bfloat16 [8, 768], P('expert'), may hold values from -0.15625 to 0.15625
- specialist_widen_weights: bfloat16 [8, 768, 3072], P('expert'), may hold values from -0.21875 to 0.21875
- specialist_widen_shift: bfloat16 [8, 3072], P('expert'), may hold values from -0.625 to 0.625
- specialist_contract_weights: bfloat16 [8, 3072, 768], P('expert'), may hold values from -0.21875 to 0.21875
- specialist_contract_shift: bfloat16 [8, 768], P('expert'), may hold values from -0.625 to 0.625
- upstream_adjoint: bfloat16 [32768, 768], P(('dp', 'expert')), may hold values from -6 to 6
Outputs:
- output: bfloat16 [32768, 768], P(('dp', 'expert'))
- input_grad: float32 [32768, 768], P(('dp', 'expert'))
- ln1_gain_grad: float32 [768], P('expert')
- ln1_shift_grad: float32 [768], P('expert')
- query_weight_grad: float32 [768, 768], P('expert', 'dp')
- query_bias_grad: float32 [768], P('expert')
- key_weight_grad: float32 [768, 768], P('expert', 'dp')
- value_weight_grad: float32 [768, 768], P('expert', 'dp')
- value_bias_grad: float32 [768], P('expert')
- out_weight_grad: float32 [768, 768], P('expert', 'dp')
- out_bias_grad: float32 [768], P('expert')
- ln2_gain_grad: float32 [768], P('expert')
- ln2_shift_grad: float32 [768], P('expert')
- centroid_grad: float32 [8, 768], P('expert')
- expert_in_grad: float32 [8, 768, 3072], P('expert', None, 'dp')
- expert_in_bias_grad: float32 [8, 3072], P('expert', 'dp')
- expert_out_grad: float32 [8, 3072, 768], P('expert', 'dp')
- expert_out_bias_grad: float32 [8, 768], P('expert', 'dp')
Inputs may be any that keep to these rules, and one draw needn't show every extreme that they name: `assignments`: in the rows of each device (aligned blocks of 1024 rows), one expert, the same for all devices, is named by 128 + 1 or more rows. positions_within[t] is the number of earlier rows of the same device's block of 1024 rows whose route equals assignments[t], clamped at 128; every device has a row whose slot is 128. `specialist_quotas`: A row is kept when its slot is below its expert's capacity; the expert named by 128 + 1 or more rows of every device has capacity 128.
All inputs are finite; a program needn't handle non-finite values.
Results may differ from a plain program's by a relative error of at most 0.019.
Values may be sent and summed in bfloat16 or wider, within the bound.
No kernel may reach another device: no remote copies, remote signals or barrier semaphores. Data moves between devices by JAX's collectives and lax.ppermute only.
A program may use at most 320 MiB of HBM per device.

v0:
```python
from functools import partial

import jax
import jax.numpy as jnp
from jax import lax
from jax.sharding import PartitionSpec as P

HEADS = 12
HEAD_DIM = 64
SEQ_LEN = 1024


EPSILON = 1e-05
MASKED = -1e30


def matmul(form, left, right):
    return jnp.einsum(form, left, right, preferred_element_type=jnp.float32)


def normalize(values, gain, shift):
    center = jnp.mean(values, axis=-1, keepdims=True)
    centered = values - center
    inverse = lax.rsqrt(jnp.mean(centered * centered, axis=-1, keepdims=True) + EPSILON)
    normed = centered * inverse
    return (normed * gain + shift, normed, inverse)


def normalize_back(grad, normed, inverse, gain):
    scaled = grad * gain
    inner = (
        scaled
        - jnp.mean(scaled, axis=-1, keepdims=True)
        - normed * jnp.mean(scaled * normed, axis=-1, keepdims=True)
    )
    return (inverse * inner, jnp.sum(grad * normed, axis=0), jnp.sum(grad, axis=0))


def block_scores(queries, keys, start, stop, scale):
    scores = matmul("qhd,khd->hqk", queries[start:stop], keys[:stop]) * scale
    row_pos = start + lax.broadcasted_iota(jnp.int32, (stop - start, stop), 0)
    col_pos = lax.broadcasted_iota(jnp.int32, (stop - start, stop), 1)
    return jnp.where((col_pos <= row_pos)[None], scores, MASKED)


def attend(packed):
    queries, keys, values = packed
    length = queries.shape[0]
    block = min(512, length)
    scale = queries.shape[-1] ** (-0.5)
    contexts = []
    totals = []
    for start in range(0, length, block):
        stop = start + block
        scores = block_scores(queries, keys, start, stop, scale)
        top = jnp.max(scores, axis=-1, keepdims=True)
        logsum = top + jnp.log(jnp.sum(jnp.exp(scores - top), axis=-1, keepdims=True))
        probs = jnp.exp(scores - logsum).astype(jnp.bfloat16)
        contexts.append(matmul("hqk,khd->qhd", probs, values[:stop]))
        totals.append(logsum[..., 0])
    return (jnp.concatenate(contexts, 0), jnp.concatenate(totals, 1))


def attend_back(packed):
    queries, keys, values, totals, dcontext = packed
    length = queries.shape[0]
    block = min(512, length)
    scale = queries.shape[-1] ** (-0.5)
    query_parts = []
    dkeys = jnp.zeros(keys.shape, jnp.float32)
    dvalues = jnp.zeros(values.shape, jnp.float32)
    for start in range(0, length, block):
        stop = start + block
        scores = block_scores(queries, keys, start, stop, scale)
        probs = jnp.exp(scores - totals[:, start:stop, None])
        dslice = dcontext[start:stop]
        dprobs = matmul("qhd,khd->hqk", dslice, values[:stop])
        rowdot = jnp.sum(dprobs * probs, axis=-1, keepdims=True)
        dscores = (probs * (dprobs - rowdot)).astype(jnp.bfloat16)
        query_parts.append(matmul("hqk,khd->qhd", dscores, keys[:stop]) * scale)
        dkeys = dkeys.at[:stop].add(matmul("hqk,qhd->khd", dscores, queries[start:stop]) * scale)
        dvalues = dvalues.at[:stop].add(matmul("hqk,qhd->khd", probs.astype(jnp.bfloat16), dslice))
    dqueries = jnp.concatenate(query_parts, 0)
    return (dqueries.astype(jnp.bfloat16), dkeys.astype(jnp.bfloat16), dvalues.astype(jnp.bfloat16))


def shards(
    block_entries,
    assignments,
    positions_within,
    specialist_quotas,
    standardize_one_scale,
    standardize_one_shift,
    asking_weights,
    asking_shift,
    lookup_weights,
    content_weights,
    content_shift,
    context_mixing_weights,
    context_mixing_shift,
    standardize_two_scale,
    standardize_two_shift,
    gating_prototypes,
    specialist_widen_weights,
    specialist_widen_shift,
    specialist_contract_weights,
    specialist_contract_shift,
    upstream_adjoint,
):
    rows_q, rows_k, rows_v, rows_o = (
        lax.all_gather(asking_weights, "dp", axis=1, tiled=True),
        lax.all_gather(lookup_weights, "dp", axis=1, tiled=True),
        lax.all_gather(content_weights, "dp", axis=1, tiled=True),
        lax.all_gather(context_mixing_weights, "dp", axis=1, tiled=True),
    )
    gathered = (
        lax.all_gather(rows_q, "expert", axis=0, tiled=True),
        lax.all_gather(rows_k, "expert", axis=0, tiled=True),
        lax.all_gather(rows_v, "expert", axis=0, tiled=True),
        lax.all_gather(rows_o, "expert", axis=0, tiled=True),
        lax.all_gather(standardize_one_scale, "expert", axis=0, tiled=True),
        lax.all_gather(standardize_one_shift, "expert", axis=0, tiled=True),
        lax.all_gather(asking_shift, "expert", axis=0, tiled=True),
        lax.all_gather(content_shift, "expert", axis=0, tiled=True),
        lax.all_gather(context_mixing_shift, "expert", axis=0, tiled=True),
        lax.all_gather(standardize_two_scale, "expert", axis=0, tiled=True),
        lax.all_gather(standardize_two_shift, "expert", axis=0, tiled=True),
        lax.all_gather(gating_prototypes, "expert", axis=0, tiled=True),
    )
    full_q, full_k, full_v, full_o = (gathered[0], gathered[1], gathered[2], gathered[3])
    gain_one = gathered[4].astype(jnp.float32)
    shift_one = gathered[5].astype(jnp.float32)
    bias_q = gathered[6].astype(jnp.float32)
    bias_v = gathered[7].astype(jnp.float32)
    bias_o = gathered[8].astype(jnp.float32)
    gain_two = gathered[9].astype(jnp.float32)
    shift_two = gathered[10].astype(jnp.float32)
    centers = gathered[11]
    incoming_entries = block_entries.astype(jnp.float32)
    count, width = incoming_entries.shape
    head_shape = (count // SEQ_LEN, SEQ_LEN, HEADS, HEAD_DIM)
    normed_in, unit_one, inverse_one = normalize(incoming_entries, gain_one, shift_one)
    low_in = normed_in.astype(jnp.bfloat16)
    queries = (
        (matmul("td,de->te", low_in, full_q) + bias_q).astype(jnp.bfloat16).reshape(head_shape)
    )
    keys = matmul("td,de->te", low_in, full_k).astype(jnp.bfloat16).reshape(head_shape)
    values = (matmul("td,de->te", low_in, full_v) + bias_v).astype(jnp.bfloat16).reshape(head_shape)
    contexts, totals = lax.map(attend, (queries, keys, values))
    context = contexts.reshape(count, width).astype(jnp.bfloat16)
    hidden_one = incoming_entries + matmul("td,de->te", context, full_o) + bias_o
    normed_mid, unit_two, inverse_two = normalize(hidden_one, gain_two, shift_two)
    low_mid = normed_mid.astype(jnp.bfloat16)
    experts = centers.shape[0]
    choose_specialist = assignments[:, None] == lax.broadcasted_iota(jnp.int32, (count, experts), 1)
    logits = matmul("td,ed->te", low_mid, centers)
    gate = jax.nn.sigmoid(jnp.sum(jnp.where(choose_specialist, logits, 0.0), axis=1))
    specialist_limit = jnp.sum(jnp.where(choose_specialist, specialist_quotas[None, :], 0), axis=1)
    slot_cap = max(2, count // experts)
    dump = experts * slot_cap
    target = jnp.where(
        positions_within < specialist_limit, assignments * slot_cap + positions_within, dump
    )
    send = jnp.zeros((dump + 1, width), jnp.bfloat16).at[target].set(low_mid)
    send = send[:dump].reshape(experts, slot_cap, width)
    weight_in = specialist_widen_weights[0]
    bias_in = specialist_widen_shift[0].astype(jnp.float32)
    weight_out = specialist_contract_weights[0]
    bias_out = specialist_contract_shift[0].astype(jnp.float32)
    arrived = lax.all_to_all(send, "expert", split_axis=0, concat_axis=0, tiled=True)
    sources = arrived.shape[0]
    items = arrived.shape[1]
    flat_rows = arrived.reshape(sources * items, width)
    before = matmul("rd,df->rf", flat_rows, weight_in) + bias_in
    active = jax.nn.gelu(before, approximate=False).astype(jnp.bfloat16)
    block_result = (matmul("rf,fd->rd", active, weight_out) + bias_out).astype(jnp.bfloat16)
    returned = lax.all_to_all(
        block_result.reshape(sources, items, width),
        "expert",
        split_axis=0,
        concat_axis=0,
        tiled=True,
    )
    returned, kept_before, kept_rows = (
        returned,
        before.reshape(sources, items, before.shape[-1]),
        arrived,
    )
    flat_back = jnp.concatenate(
        [returned.reshape(dump, width), jnp.zeros((1, width), jnp.bfloat16)], 0
    )
    picked = flat_back[target]
    output = (hidden_one + gate[:, None] * picked).astype(jnp.bfloat16)
    upstream = upstream_adjoint.astype(jnp.float32)
    gate_grad = jnp.sum(upstream * picked, axis=1) * gate * (1.0 - gate)
    sent_grad = (gate[:, None] * upstream).astype(jnp.bfloat16)
    grad_buffer = jnp.zeros((dump + 1, width), jnp.bfloat16).at[target].set(sent_grad)
    grad_buffer = grad_buffer[:dump].reshape(experts, slot_cap, width)
    arrived_grad = lax.all_to_all(grad_buffer, "expert", split_axis=0, concat_axis=0, tiled=True)
    flat_dy = arrived_grad.reshape(-1, width)
    flat_x = kept_rows.reshape(-1, width)
    flat_before = kept_before.reshape(flat_x.shape[0], -1)
    active_value, gelu_back = jax.vjp(partial(jax.nn.gelu, approximate=False), flat_before)
    active_low = active_value.astype(jnp.bfloat16)
    dactive = matmul("rd,fd->rf", flat_dy, weight_out)
    dbefore = gelu_back(dactive)[0].astype(jnp.bfloat16)
    dslots = matmul("rf,df->rd", dbefore, weight_in).astype(jnp.bfloat16).reshape(kept_rows.shape)
    returned_grad = lax.all_to_all(dslots, "expert", split_axis=0, concat_axis=0, tiled=True)
    grad_in = matmul("rd,rf->df", flat_x, dbefore)
    grad_out = matmul("rf,rd->fd", active_low, flat_dy)
    grad_bin = jnp.sum(dbefore, axis=0, dtype=jnp.float32)
    grad_bout = jnp.sum(flat_dy, axis=0, dtype=jnp.float32)
    grad_in, grad_bin, grad_out, grad_bout = (
        lax.psum_scatter(
            grad_in[None].astype(jnp.bfloat16), "dp", scatter_dimension=2, tiled=True
        ).astype(jnp.float32),
        lax.psum_scatter(
            grad_bin[None].astype(jnp.bfloat16), "dp", scatter_dimension=1, tiled=True
        ).astype(jnp.float32),
        lax.psum_scatter(
            grad_out[None].astype(jnp.bfloat16), "dp", scatter_dimension=1, tiled=True
        ).astype(jnp.float32),
        lax.psum_scatter(
            grad_bout[None].astype(jnp.bfloat16), "dp", scatter_dimension=1, tiled=True
        ).astype(jnp.float32),
    )
    flat_ret = jnp.concatenate(
        [returned_grad.reshape(dump, width), jnp.zeros((1, width), jnp.bfloat16)], 0
    )
    weighted = jnp.where(choose_specialist, gate_grad[:, None], 0.0)
    centers_f = centers.astype(jnp.float32)
    dmiddle = flat_ret[target].astype(jnp.float32) + jnp.dot(
        weighted, centers_f, precision=lax.Precision.HIGHEST
    )
    grad_centers = jnp.dot(weighted.T, low_mid.astype(jnp.float32), precision=lax.Precision.HIGHEST)
    dmid_in, grad_gain_two, grad_shift_two = normalize_back(
        dmiddle, unit_two, inverse_two, gain_two
    )
    dhidden_one = upstream + dmid_in
    dattend = dhidden_one.astype(jnp.bfloat16)
    back_q, back_k, back_v, back_o = (
        lax.all_gather(asking_weights, "dp", axis=1, tiled=True),
        lax.all_gather(lookup_weights, "dp", axis=1, tiled=True),
        lax.all_gather(content_weights, "dp", axis=1, tiled=True),
        lax.all_gather(context_mixing_weights, "dp", axis=1, tiled=True),
    )
    full_q, full_k, full_v, full_o = (
        lax.all_gather(back_q, "expert", axis=0, tiled=True),
        lax.all_gather(back_k, "expert", axis=0, tiled=True),
        lax.all_gather(back_v, "expert", axis=0, tiled=True),
        lax.all_gather(back_o, "expert", axis=0, tiled=True),
    )
    grad_wo = matmul("td,te->de", context, dattend)
    grad_bo = jnp.sum(dattend, axis=0, dtype=jnp.float32)
    dcontext = matmul("te,de->td", dattend, full_o).astype(jnp.bfloat16).reshape(head_shape)
    dqueries, dkeys, dvalues = lax.map(attend_back, (queries, keys, values, totals, dcontext))
    dqueries = dqueries.reshape(count, width)
    dkeys = dkeys.reshape(count, width)
    dvalues = dvalues.reshape(count, width)
    grad_wq = matmul("td,te->de", low_in, dqueries)
    grad_bq = jnp.sum(dqueries, axis=0, dtype=jnp.float32)
    grad_wk = matmul("td,te->de", low_in, dkeys)
    grad_wv = matmul("td,te->de", low_in, dvalues)
    grad_bv = jnp.sum(dvalues, axis=0, dtype=jnp.float32)
    dnormed = (
        matmul("te,de->td", dqueries, full_q)
        + matmul("te,de->td", dkeys, full_k)
        + matmul("te,de->td", dvalues, full_v)
    )
    dinput_part, grad_gain_one, grad_shift_one = normalize_back(
        dnormed, unit_one, inverse_one, gain_one
    )
    input_grad = dhidden_one + dinput_part
    summed = (
        lax.psum_scatter(
            grad_wq.astype(jnp.bfloat16), "expert", scatter_dimension=0, tiled=True
        ).astype(jnp.float32),
        lax.psum_scatter(
            grad_wk.astype(jnp.bfloat16), "expert", scatter_dimension=0, tiled=True
        ).astype(jnp.float32),
        lax.psum_scatter(
            grad_wv.astype(jnp.bfloat16), "expert", scatter_dimension=0, tiled=True
        ).astype(jnp.float32),
        lax.psum_scatter(
            grad_wo.astype(jnp.bfloat16), "expert", scatter_dimension=0, tiled=True
        ).astype(jnp.float32),
        lax.psum_scatter(
            grad_gain_one.astype(jnp.bfloat16), "expert", scatter_dimension=0, tiled=True
        ).astype(jnp.float32),
        lax.psum_scatter(
            grad_shift_one.astype(jnp.bfloat16), "expert", scatter_dimension=0, tiled=True
        ).astype(jnp.float32),
        lax.psum_scatter(
            grad_bq.astype(jnp.bfloat16), "expert", scatter_dimension=0, tiled=True
        ).astype(jnp.float32),
        lax.psum_scatter(
            grad_bv.astype(jnp.bfloat16), "expert", scatter_dimension=0, tiled=True
        ).astype(jnp.float32),
        lax.psum_scatter(
            grad_bo.astype(jnp.bfloat16), "expert", scatter_dimension=0, tiled=True
        ).astype(jnp.float32),
        lax.psum_scatter(
            grad_gain_two.astype(jnp.bfloat16), "expert", scatter_dimension=0, tiled=True
        ).astype(jnp.float32),
        lax.psum_scatter(
            grad_shift_two.astype(jnp.bfloat16), "expert", scatter_dimension=0, tiled=True
        ).astype(jnp.float32),
        lax.psum_scatter(
            grad_centers.astype(jnp.bfloat16), "expert", scatter_dimension=0, tiled=True
        ).astype(jnp.float32),
    )
    sum_q, sum_k, sum_v, sum_o = (
        lax.psum_scatter(
            summed[0].astype(jnp.bfloat16), "dp", scatter_dimension=1, tiled=True
        ).astype(jnp.float32),
        lax.psum_scatter(
            summed[1].astype(jnp.bfloat16), "dp", scatter_dimension=1, tiled=True
        ).astype(jnp.float32),
        lax.psum_scatter(
            summed[2].astype(jnp.bfloat16), "dp", scatter_dimension=1, tiled=True
        ).astype(jnp.float32),
        lax.psum_scatter(
            summed[3].astype(jnp.bfloat16), "dp", scatter_dimension=1, tiled=True
        ).astype(jnp.float32),
    )
    small = lax.psum(
        (summed[4], summed[5], summed[6], summed[7], summed[8], summed[9], summed[10], summed[11]),
        "dp",
    )
    return (
        output,
        input_grad,
        small[0],
        small[1],
        sum_q,
        small[2],
        sum_k,
        sum_v,
        small[3],
        sum_o,
        small[4],
        small[5],
        small[6],
        small[7],
        grad_in,
        grad_bin,
        grad_out,
        grad_bout,
    )


def solution(mesh):
    placed = (
        P(("dp", "expert"), None),
        P(("dp", "expert")),
        P(("dp", "expert")),
        P(),
        P("expert"),
        P("expert"),
        P("expert", "dp"),
        P("expert"),
        P("expert", "dp"),
        P("expert", "dp"),
        P("expert"),
        P("expert", "dp"),
        P("expert"),
        P("expert"),
        P("expert"),
        P("expert", None),
        P("expert", None, None),
        P("expert", None),
        P("expert", None, None),
        P("expert", None),
        P(("dp", "expert"), None),
    )
    return jax.shard_map(
        shards,
        mesh=mesh,
        in_specs=placed,
        out_specs=(
            P(("dp", "expert"), None),
            P(("dp", "expert"), None),
            P("expert"),
            P("expert"),
            P("expert", "dp"),
            P("expert"),
            P("expert", "dp"),
            P("expert", "dp"),
            P("expert"),
            P("expert", "dp"),
            P("expert"),
            P("expert"),
            P("expert"),
            P("expert", None),
            P("expert", None, "dp"),
            P("expert", "dp"),
            P("expert", "dp", None),
            P("expert", "dp"),
        ),
        check_vma=False,
    )
```

profile of v0, /device:TPU:0, one launch (start us, length us, event | category | flops | bytes accessed | tf_op | source)
XLA Modules:
  0.0 1023.3 jit_solution(12897628257390424152)
XLA Ops:
  8.2 6.8 all_gather.58
  16.9 5.6 all_gather.61
  24.2 5.6 all_gather.64
  31.6 5.6 all_gather.66
  41.1 38.2 %all-reduce.21 = (bf16[768]{0:T(1024)(128)(2,1)S(1)}, bf16[768]{0:T(1024)(128)(2,1)S(1)}, bf16[768]{0:T(1024)(128)(2,1)S(1)}, bf16[768]{0:T(1024)(128)(2,1)S(1)}...) all-reduce(bf16[768]{0:T(1024)(128)(2,1)S(1)} %dynamic-update-slice, ...), channel_id=1, replica_groups=mesh['dp'=4,'expert'=8] {'expert'}, use_global_device_ids=true, to_apply=%add.6 | all-reduce | flops 5376 | bytes 21504
  88.3 13.1 %all-gather.8.cloned.1.call-done = bf16[768,768]{1,0:T(8,128)(2,1)} async-done(((bf16[96,768]{1,0:T(8,128)(2,1)}), bf16[768,768]{1,0:T(8,128)(2,1)}) %all-gather.8.cloned.1.call-update) | async-done | bytes 1179664 | tf_op jit(solution)/shard_map/all_gather | solution.py:117
  105.3 38.7 %all-gather.10.cloned.1.call-done = bf16[768,768]{1,0:T(8,128)(2,1)} async-done(((bf16[96,768]{1,0:T(8,128)(2,1)}), bf16[768,768]{1,0:T(8,128)(2,1)}) %all-gather.10.cloned.1.call-update) | async-done | bytes 1179664 | tf_op jit(solution)/shard_map/all_gather | solution.py:118
  154.7 5.5 fusion.45
  160.3 10.9 %fusion = (f32[12,512]{1,0:T(8,128)S(1)}, f32[12,512,1024]{2,1,0:T(8,128)}) fusion(pred[512,1024]{1,0:T(8,128)(4,1)S(1)} %iota_compare_fusion, bf16[512,12,64]{0,2,1:T(8,128)(2,1)S(1)} %bitcast.144, bf16[1024,12,64]{0,2,1:T(8,128)(2,1)S(1)} %bitcast.143), kind=kOutput, calls=%fused_computation.9 | convolution fusion | flops 824174592 | bytes 28073984 | tf_op jit(solution)/shard_map/while/body/eval_jaxpr/qhd,khd->hqk/dot_general | solution.py:18
  171.1 11.9 %exponential_reduce_fusion = f32[12,512]{1,0:T(8,128)S(1)} fusion(f32[12,512,1024]{2,1,0:T(8,128)} %get-tuple-element.266, f32[12,512]{1,0:T(8,128)S(1)} %get-tuple-element.265, pred[512,1024]{1,0:T(8,128)(4,1)S(1)} %iota_compare_fusion), kind=kLoop, calls=%fused_computation.7 | loop fusion | flops 25159680 | bytes 25739264 | tf_op jit(solution)/shard_map/while/body/eval_jaxpr/reduce_sum | solution.py:57
  183.1 11.2 %fusion.46 = bf16[512,12,64]{0,2,1:T(8,128)(2,1)S(1)} fusion(bf16[1024,12,64]{0,2,1:T(8,128)(2,1)S(1)} %bitcast.153, f32[12,512,1024]{2,1,0:T(8,128)} %get-tuple-element.266, f32[12,512]{1,0:T(8,128)S(1)} %log_add_fusion, pred[512,1024]{1,0:T(8,128)(4,1)S(1)} %iota_compare_fusion), kind=kOutput, calls=%fused_computation.105 | convolution fusion | flops 830865408 | bytes 28073984 | tf_op jit(solution)/shard_map/while/body/eval_jaxpr/hqk,khd->qhd/dot_general | solution.py:18
  202.0 6.4 scatter_custom_fusion
  209.6 3.6 all-to-all-start
  213.3 36.0 %all-to-all-done = bf16[8,128,768]{2,1,0:T(8,128)(2,1)S(1)} async-done(((bf16[8,128,768]{2,1,0:T(8,128)(2,1)}), bf16[8,128,768]{2,1,0:T(8,128)(2,1)S(1)}, u32[]{:S(2)}, u32[]{:S(2)}) %all-to-all-start) | async-done | bytes 1572896 | tf_op jit(solution)/shard_map/all_to_all | solution.py:170
  249.3 36.0 %multiply_convert_fusion.2 = (bf16[1024,3072]{1,0:T(8,128)(2,1)S(1)}, f32[1024,3072]{1,0:T(8,128)}, f32[1024,3072]{1,0:T(8,128)}) fusion(f32[3072]{0:T(1024)S(1)} %bitcast.181, bf16[1024,768]{1,0:T(8,128)(2,1)S(1)} %bitcast.165, bf16[1,768,3072]{2,1,0:T(8,128)(2,1)} %param.49), kind=kOutput, calls=%fused_computation.16 | convolution fusion | flops 5039456256 | bytes 37761024 | tf_op jit(solution)/shard_map/rd,df->rf/dot_general | solution.py:18
  285.3 10.7 %add_convert_fusion.1 = bf16[1024,768]{1,0:T(8,128)(2,1)} fusion(bf16[1024,3072]{1,0:T(8,128)(2,1)S(1)} %get-tuple-element.254, bf16[1,3072,768]{2,1,0:T(8,128)(2,1)} %param.51, f32[768]{0:T(1024)S(1)} %convert_reduce_fusion.1), kind=kOutput, calls=%fused_computation.80 | convolution fusion | flops 4833411072 | bytes 12585984 | tf_op jit(solution)/shard_map/rf,fd->rd/dot_general | solution.py:18
  296.1 4.5 all-to-all-start.1
  302.3 54.4 %all-gather = bf16[8,1,768]{2,1,0:T(2,128)(2,1)S(1)} all-gather(bf16[1,1,768]{2,1,0:T(2,128)(2,1)S(1)} %bitcast.183), channel_id=1, replica_groups=mesh['dp'=4,'expert'=8] {'expert'}, dimensions={0}, use_global_device_ids=true | all-gather | bytes 13824 | tf_op jit(solution)/shard_map/all_gather | solution.py:128
  358.6 5.4 gather_fusion
  370.4 6.2 scatter_custom_fusion.1
  376.7 34.5 %all_to_all.20 = bf16[8,128,768]{2,1,0:T(8,128)(2,1)S(1)} all-to-all(bf16[8,128,768]{2,1,0:T(8,128)(2,1)S(1)} %bitcast.151), channel_id=1, replica_groups=mesh['dp'=4,'expert'=8] {'expert'}, dimensions={0} | all-to-all | bytes 3145728 | tf_op jit(solution)/shard_map/all_to_all | solution.py:199
  411.2 17.4 %fusion.95 = (bf16[3072]{0:T(1024)(128)(2,1)S(1)}, bf16[1024,3072]{1,0:T(8,128)(2,1)}) fusion(f32[1024,3072]{1,0:T(8,128)} %get-tuple-element.255, bf16[1024,768]{1,0:T(8,128)(2,1)S(1)} %bitcast.148, bf16[1,3072,768]{2,1,0:T(8,128)(2,1)} %param.51, f32[1024,3072]{1,0:T(8,128)} %get-tuple-element.271, f32[3072]{0:T(1024)S(1)} %bitcast.182), kind=kOutput, calls=%fused_computation.177 | convolution fusion | flops 4882166784 | bytes 37767168 | tf_op jit(solution)/shard_map/rd,fd->rf/dot_general | solution.py:18
  428.6 8.2 fusion.42
  440.4 34.6 %all-to-all-done.3 = bf16[8,128,768]{2,1,0:T(8,128)(2,1)S(1)} async-done(((bf16[8,128,768]{2,1,0:T(8,128)(2,1)}), bf16[8,128,768]{2,1,0:T(8,128)(2,1)S(1)}, u32[]{:S(2)}, u32[]{:S(2)}) %all-to-all-start.3) | async-done | bytes 1572896 | tf_op jit(solution)/shard_map/all_to_all | solution.py:208
  475.2 5.6 gather_fusion.1
  483.6 5.5 multiply_reduce_fusion.2
  499.1 7.5 convolution_bitcast_fusion
  506.7 6.9 multiply_reduce_fusion.1
  513.7 12.6 %fusion.94 = (bf16[12,64]{1,0:T(8,128)(2,1)S(1)}, bf16[1024,12,64]{0,2,1:T(8,128)(2,1)S(1)}) fusion(bf16[512,12,64]{0,2,1:T(8,128)(2,1)S(1)} %bitcast.159, f32[12,512,1024]{2,1,0:T(8,128)} %get-tuple-element.266, f32[12,512]{1,0:T(8,128)S(1)} %copy-done.43, pred[512,1024]{1,0:T(8,128)(4,1)S(1)} %copy-done.14, f32[512,12,64]{0,2,1:T(8,128)} %convolution_bitcast_fusion), kind=kOutput, calls=%fused_computation.176 | convolution fusion | flops 832830720 | bytes 29648384 | tf_op jit(solution)/shard_map/while/body/eval_jaxpr/hqk,qhd->khd/dot_general | solution.py:18
  530.2 21.5 %multiply_reduce_fusion = (f32[12,512]{1,0:T(8,128)S(1)}, f32[12,512,1024]{2,1,0:T(8,128)}) fusion(f32[12,512,1024]{2,1,0:T(8,128)} %get-tuple-element.266, f32[12,512]{1,0:T(8,128)S(1)} %copy-done.43, pred[512,1024]{1,0:T(8,128)(4,1)S(1)} %copy-done.14, bf16[512,12,64]{0,2,1:T(8,128)(2,1)S(1)} %bitcast.160, bf16[1024,12,64]{0,2,1:T(8,128)(2,1)S(1)} %bitcast.154), kind=kOutput, calls=%fused_computation.5 | convolution fusion | flops 836757504 | bytes 53264384 | tf_op jit(solution)/shard_map/while/body/eval_jaxpr/qhd,khd->hqk/dot_general | solution.py:18
  551.8 18.9 %multiply_convert_fusion = bf16[12,512,1024]{2,1,0:T(8,128)(2,1)S(1)} fusion(f32[12,512,1024]{2,1,0:T(8,128)} %get-tuple-element.274, f32[12,512,1024]{2,1,0:T(8,128)} %get-tuple-element.266, f32[12,512]{1,0:T(8,128)S(1)} %get-tuple-element.273, f32[12,512]{1,0:T(8,128)S(1)} %copy-done.43, pred[512,1024]{1,0:T(8,128)(4,1)} %copy-done.13), kind=kLoop, calls=%fused_computation.4 | loop fusion | flops 37748736 | bytes 63488000 | tf_op jit(solution)/shard_map/while/body/eval_jaxpr/convert_element_type | solution.py:79
  571.5 13.0 %multiply_convert_fusion.1 = bf16[12,512,512]{1,2,0:T(8,128)(2,1)} fusion(f32[12,512,512]{1,2,0:T(8,128)} %get-tuple-element.276, f32[12,512,512]{1,2,0:T(8,128)S(1)} %bitcast.139, f32[12,512]{1,0:T(8,128)S(1)} %get-tuple-element.275, f32[12,512]{1,0:T(8,128)S(1)} %copy-done.45, pred[512,512]{0,1:T(8,128)(4,1)S(1)} %copy-done.26), kind=kLoop, calls=%fused_computation.13 | loop fusion | flops 18874368 | bytes 31768576 | tf_op jit(solution)/shard_map/while/body/eval_jaxpr/convert_element_type | solution.py:79
  584.5 4.9 bitcast_reduce_fusion.1
  589.4 6.2 bitcast_reduce_fusion
  595.7 4.5 convolution_convert_fusion.7
  600.3 4.9 multiply_bitcast_fusion
  605.2 7.1 fusion.39
  621.0 22.1 %reduce-scatter.29.cloned.1.call-done = bf16[96,768]{1,0:T(8,128)(2,1)} async-done(((bf16[768,768]{1,0:T(8,128)(2,1)}), bf16[96,768]{1,0:T(8,128)(2,1)}) %reduce-scatter.29.cloned.1.call-update) | async-done | bytes 147472 | tf_op jit(solution)/shard_map/reduce_scatter | solution.py:281
  644.9 65.3 %reduce-scatter.25.cloned.1.call-done = bf16[96,768]{1,0:T(8,128)(2,1)} async-done(((bf16[768,768]{1,0:T(8,128)(2,1)}), bf16[96,768]{1,0:T(8,128)(2,1)}) %reduce-scatter.25.cloned.1.call-update) | async-done | bytes 147472 | tf_op jit(solution)/shard_map/reduce_scatter | solution.py:275
  712.0 64.7 %reduce-scatter.27.cloned.1.call-done = bf16[96,768]{1,0:T(8,128)(2,1)} async-done(((bf16[768,768]{1,0:T(8,128)(2,1)}), bf16[96,768]{1,0:T(8,128)(2,1)}) %reduce-scatter.27.cloned.1.call-update) | async-done | bytes 147472 | tf_op jit(solution)/shard_map/reduce_scatter | solution.py:278
  778.5 9.7 fusion.18
  789.7 9.6 fusion.17
  803.6 20.0 %reduce-scatter.45.cloned.1.call-done = bf16[768,1]{1,0:T(8,128)(2,1)} async-done(((bf16[3072,1]{1,0:T(8,128)(2,1)}), bf16[768,1]{1,0:T(8,128)(2,1)}) %reduce-scatter.45.cloned.1.call-update) | async-done | bytes 1552
  841.3 37.1 %all-reduce.20 = (bf16[768]{0:T(1024)(128)(2,1)S(1)}, bf16[768]{0:T(1024)(128)(2,1)S(1)}, bf16[768]{0:T(1024)(128)(2,1)S(1)}, bf16[768]{0:T(1024)(128)(2,1)S(1)}...) all-reduce(bf16[768]{0:T(1024)(128)(2,1)S(1)} %get-tuple-element.22, ...), channel_id=2, replica_groups=mesh['dp'=4,'expert'=8] {'expert'}, use_global_device_ids=true, to_apply=%region_20.21.clone | all-reduce | flops 11520 | bytes 46080
  879.6 6.6 all-reduce.19
  892.1 20.7 %reduce-scatter.39.cloned.1.call-done = bf16[192,96]{1,0:T(8,128)(2,1)} async-done(((bf16[768,96]{1,0:T(8,128)(2,1)}), bf16[192,96]{1,0:T(8,128)(2,1)}) %reduce-scatter.39.cloned.1.call-update) | async-done | bytes 36880
  914.3 48.9 %reduce-scatter.35.cloned.1.call-done = bf16[1,768,768]{2,1,0:T(8,128)(2,1)} async-done(((bf16[1,3072,768]{2,1,0:T(8,128)(2,1)}), bf16[1,768,768]{2,1,0:T(8,128)(2,1)}) %reduce-scatter.35.cloned.1.call-update) | async-done | bytes 1179664 | tf_op jit(solution)/shard_map/reduce_scatter | solution.py:220
  966.0 47.4 %reduce-scatter.33.cloned.1.call-done = bf16[1,768,768]{2,1,0:T(8,128)(2,1)} async-done(((bf16[1,768,3072]{2,1,0:T(8,128)(2,1)}), bf16[1,768,768]{2,1,0:T(8,128)(2,1)}) %reduce-scatter.33.cloned.1.call-update) | async-done | bytes 1179664 | tf_op jit(solution)/shard_map/reduce_scatter | solution.py:214
  (345 shorter events, 123.6 us)
Async XLA Ops:
  7.2 31.0 %copy-start.68 = (u32[32]{0:T(128)S(1)}, u32[32]{0:T(128)}, u32[]{:S(2)}) copy-start(u32[32]{0:T(128)} %constant.286) | copy-start | bytes 388
  7.2 32.3 %copy-start.73 = (bf16[96]{0:T(256)(128)(2,1)S(1)}, bf16[96]{0:T(256)(128)(2,1)}, u32[]{:S(2)}) copy-start(bf16[96]{0:T(256)(128)(2,1)} %param.47) | copy-start | bytes 580
  7.2 32.5 %copy-start.74 = (bf16[96]{0:T(256)(128)(2,1)S(1)}, bf16[96]{0:T(256)(128)(2,1)}, u32[]{:S(2)}) copy-start(bf16[96]{0:T(256)(128)(2,1)} %param.45) | copy-start | bytes 580
  7.2 32.7 %copy-start.75 = (bf16[96]{0:T(256)(128)(2,1)S(1)}, bf16[96]{0:T(256)(128)(2,1)}, u32[]{:S(2)}) copy-start(bf16[96]{0:T(256)(128)(2,1)} %param.40) | copy-start | bytes 580
  7.2 33.0 %copy-start.76 = (bf16[96]{0:T(256)(128)(2,1)S(1)}, bf16[96]{0:T(256)(128)(2,1)}, u32[]{:S(2)}) copy-start(bf16[96]{0:T(256)(128)(2,1)} %param.37) | copy-start | bytes 580
  7.2 33.2 %copy-start.77 = (bf16[96]{0:T(256)(128)(2,1)S(1)}, bf16[96]{0:T(256)(128)(2,1)}, u32[]{:S(2)}) copy-start(bf16[96]{0:T(256)(128)(2,1)} %param.38) | copy-start | bytes 580
  7.3 33.4 %copy-start.78 = (bf16[96]{0:T(256)(128)(2,1)S(1)}, bf16[96]{0:T(256)(128)(2,1)}, u32[]{:S(2)}) copy-start(bf16[96]{0:T(256)(128)(2,1)} %param.43) | copy-start | bytes 580
  7.3 33.6 %copy-start.79 = (bf16[96]{0:T(256)(128)(2,1)S(1)}, bf16[96]{0:T(256)(128)(2,1)}, u32[]{:S(2)}) copy-start(bf16[96]{0:T(256)(128)(2,1)} %param.46) | copy-start | bytes 580
  7.3 76.0 %all-gather.6.cloned.1.call-start = ((), (), s32[]{:S(2)}) async-start(), calls=%async_computation.16 | async-start | bytes 1327104 | tf_op jit(solution)/shard_map/all_gather | solution.py:119
  15.9 85.5 %all-gather.8.cloned.1.call-start = ((), (), s32[]{:S(2)}) async-start(), calls=%async_computation.17 | async-start | bytes 1327104 | tf_op jit(solution)/shard_map/all_gather | solution.py:117
  23.3 120.7 %all-gather.10.cloned.1.call-start = ((), (), s32[]{:S(2)}) async-start(), calls=%async_computation.18 | async-start | bytes 1327104 | tf_op jit(solution)/shard_map/all_gather | solution.py:118
  30.7 163.9 %all-gather.12.cloned.1.call-start = ((), (), s32[]{:S(2)}) async-start(), calls=%async_computation.19 | async-start | bytes 1327104 | tf_op jit(solution)/shard_map/all_gather | solution.py:120
  38.2 114.7 %copy-start.25 = (pred[512,512]{0,1:T(8,128)(4,1)}, pred[512,512]{0,1:T(8,128)(4,1)S(1)}, u32[]{:S(2)}) copy-start(pred[512,512]{0,1:T(8,128)(4,1)S(1)} %iota_compare_fusion.1) | copy-start | bytes 786436
  79.3 64.7 %copy-start.57 = (f32[768]{0:T(1024)}, f32[768]{0:T(1024)S(1)}, u32[]{:S(2)}) copy-start(f32[768]{0:T(1024)S(1)} %convert_element_type.244) | copy-start | bytes 9220
  79.3 64.7 %copy-start.64 = (f32[768]{0:T(1024)}, f32[768]{0:T(1024)S(1)}, u32[]{:S(2)}) copy-start(f32[768]{0:T(1024)S(1)} %convert_element_type.245) | copy-start | bytes 9220
  79.4 119.2 %copy-start.50 = (f32[768]{0:T(1024)}, f32[768]{0:T(1024)S(1)}, u32[]{:S(2)}) copy-start(f32[768]{0:T(1024)S(1)} %convert_element_type.256) | copy-start | bytes 9220
  79.8 103.3 %copy-start.13 = (pred[512,1024]{1,0:T(8,128)(4,1)}, pred[512,1024]{1,0:T(8,128)(4,1)S(1)}, u32[]{:S(2)}) copy-start(pred[512,1024]{1,0:T(8,128)(4,1)S(1)} %iota_compare_fusion) | copy-start | bytes 1572868
  81.7 112.9 %copy-start.4 = (bf16[1024,768]{0,1:T(8,128)(2,1)}, bf16[1024,768]{0,1:T(8,128)(2,1)S(1)}, u32[]{:S(2)}) copy-start(bf16[1024,768]{0,1:T(8,128)(2,1)S(1)} %copy.89) | copy-start | bytes 4718596
  82.0 62.0 %copy-start.54 = (f32[1024]{0:T(1024)}, f32[1024]{0:T(1024)S(1)}, u32[]{:S(2)}) copy-start(f32[1024]{0:T(1024)S(1)} %broadcast_multiply_fusion.5) | copy-start | bytes 12292
  82.5 61.5 %copy-start.59 = (f32[1024]{0:T(1024)}, f32[1024]{0:T(1024)S(1)}, u32[]{:S(2)}) copy-start(f32[1024]{0:T(1024)S(1)} %add_rsqrt_fusion.1) | copy-start | bytes 12292
  83.2 118.8 %copy-start.63 = (s32[1024]{0:T(1024)}, s32[1024]{0:T(1024)S(1)}, u32[]{:S(2)}) copy-start(s32[1024]{0:T(1024)S(1)} %get-tuple-element.253) | copy-start | bytes 12292
  105.3 55.0 %copy-start.21 = (bf16[512,768]{0,1:T(8,128)(2,1)}, bf16[512,768]{0,1:T(8,128)(2,1)S(1)}, u32[]{:S(2)}) copy-start(bf16[512,768]{0,1:T(8,128)(2,1)S(1)} %get-tuple-element.262) | copy-start | bytes 2359300
  209.6 39.7 %all-to-all-start = ((bf16[8,128,768]{2,1,0:T(8,128)(2,1)}), bf16[8,128,768]{2,1,0:T(8,128)(2,1)S(1)}, u32[]{:S(2)}, u32[]{:S(2)}) async-start(bf16[8,128,768]{2,1,0:T(8,128)(2,1)} %bitcast.150), calls=%async_computation | async-start | bytes 3145728 | tf_op jit(solution)/shard_map/all_to_all | solution.py:170
  249.3 36.0 %copy-start.36 = (bf16[8,128,768]{2,1,0:T(8,128)(2,1)}, bf16[8,128,768]{2,1,0:T(8,128)(2,1)S(1)}, u32[]{:S(2)}) copy-start(bf16[8,128,768]{2,1,0:T(8,128)(2,1)S(1)} %all-to-all-done) | copy-start | bytes 4718596
  296.1 60.7 %copy-start.8 = (bf16[1024,768]{0,1:T(8,128)(2,1)S(1)}, bf16[1024,768]{0,1:T(8,128)(2,1)}, u32[]{:S(2)}) copy-start(bf16[1024,768]{0,1:T(8,128)(2,1)} %copy-done.7) | copy-start | bytes 4718596
  296.1 60.7 %copy-start.49 = (s32[1024]{0:T(1024)S(1)}, s32[1024]{0:T(1024)}, u32[]{:S(2)}) copy-start(s32[1024]{0:T(1024)} %param.34) | copy-start | bytes 12292
  296.1 61.0 %all-to-all-start.1 = ((bf16[8,128,768]{2,1,0:T(8,128)(2,1)}), bf16[8,128,768]{2,1,0:T(8,128)(2,1)}, u32[]{:S(2)}, u32[]{:S(2)}) async-start(bf16[8,128,768]{2,1,0:T(8,128)(2,1)} %bitcast.16), calls=%async_computation.1 | async-start | bytes 3145728 | tf_op jit(solution)/shard_map/all_to_all | solution.py:177
  302.2 63.5 %copy-start.10 = (bf16[1024,768]{0,1:T(8,128)(2,1)}, bf16[1024,768]{0,1:T(8,128)(2,1)S(1)}, u32[]{:S(2)}) copy-start(bf16[1024,768]{0,1:T(8,128)(2,1)S(1)} %copy.101) | copy-start | bytes 4718596
  302.3 56.3 %copy-start.56 = (s32[1024]{0:T(1024)S(1)}, s32[1024]{0:T(1024)}, u32[]{:S(2)}) copy-start(s32[1024]{0:T(1024)} %get-tuple-element.252) | copy-start | bytes 12292
  376.7 51.9 %slice-start.6 = ((s8[4718592]{0:T(1024)(128)(4,1)}), s8[524288]{0:T(1024)(128)(4,1)S(1)}, s32[]{:S(2)}) async-start(s8[4718592]{0:T(1024)(128)(4,1)} %bitcast.184), calls=%async_computation.38 | async-start | bytes 1048576
  436.8 38.3 %all-to-all-start.3 = ((bf16[8,128,768]{2,1,0:T(8,128)(2,1)}), bf16[8,128,768]{2,1,0:T(8,128)(2,1)S(1)}, u32[]{:S(2)}, u32[]{:S(2)}) async-start(bf16[8,128,768]{2,1,0:T(8,128)(2,1)} %bitcast.20), calls=%async_computation.3 | async-start | bytes 3145728 | tf_op jit(solution)/shard_map/all_to_all | solution.py:208
  440.4 178.8 %reduce-scatter.31.cloned.1.call-start = ((), (), s32[]{:S(2)}) async-start(), calls=%async_computation.23 | async-start | bytes 1327104 | tf_op jit(solution)/shard_map/reduce_scatter | solution.py:284
  513.6 129.5 %reduce-scatter.29.cloned.1.call-start = ((), (), s32[]{:S(2)}) async-start(), calls=%async_computation.22 | async-start | bytes 1327104 | tf_op jit(solution)/shard_map/reduce_scatter | solution.py:281
  551.7 158.5 %reduce-scatter.25.cloned.1.call-start = ((), (), s32[]{:S(2)}) async-start(), calls=%async_computation.20 | async-start | bytes 1327104 | tf_op jit(solution)/shard_map/reduce_scatter | solution.py:275
  551.8 18.9 %slice-start.3 = ((s8[12582912]{0:T(1024)(128)(4,1)}), s8[4194304]{0:T(1024)(128)(4,1)S(1)}, s32[]{:S(2)}) async-start(s8[12582912]{0:T(1024)(128)(4,1)} %bitcast.138), calls=%async_computation.35 | async-start | bytes 8388608
  551.8 18.9 %slice-start.4 = ((s8[12582912]{0:T(1024)(128)(4,1)}), s8[4194304]{0:T(1024)(128)(4,1)S(1)}, s32[]{:S(2)}) async-start(s8[12582912]{0:T(1024)(128)(4,1)} %bitcast.138), calls=%async_computation.36 | async-start | bytes 8388608
  551.8 19.7 %slice-start.5 = ((s8[12582912]{0:T(1024)(128)(4,1)}), s8[4194304]{0:T(1024)(128)(4,1)S(1)}, s32[]{:S(2)}) async-start(s8[12582912]{0:T(1024)(128)(4,1)} %bitcast.138), calls=%async_computation.37 | async-start | bytes 8388608
  600.2 176.5 %reduce-scatter.27.cloned.1.call-start = ((), (), s32[]{:S(2)}) async-start(), calls=%async_computation.21 | async-start | bytes 1327104 | tf_op jit(solution)/shard_map/reduce_scatter | solution.py:278
  616.2 185.9 %reduce-scatter.47.cloned.1.call-start = ((), (), s32[]{:S(2)}) async-start(), calls=%async_computation.31 | async-start | bytes 245760
  617.7 205.9 %reduce-scatter.45.cloned.1.call-start = ((), (), s32[]{:S(2)}) async-start(), calls=%async_computation.30 | async-start | bytes 983040
  619.1 267.1 %reduce-scatter.43.cloned.1.call-start = ((), (), s32[]{:S(2)}) async-start(), calls=%async_computation.29 | async-start | bytes 245760
  620.9 266.9 %reduce-scatter.41.cloned.1.call-start = ((), (), s32[]{:S(2)}) async-start(), calls=%async_computation.28 | async-start | bytes 245760
  644.8 245.7 %reduce-scatter.37.cloned.1.call-start = ((), (), s32[]{:S(2)}) async-start(), calls=%async_computation.26 | async-start | bytes 245760
  711.9 200.8 %reduce-scatter.39.cloned.1.call-start = ((), (), s32[]{:S(2)}) async-start(), calls=%async_computation.27 | async-start | bytes 245760
  778.5 184.7 %reduce-scatter.35.cloned.1.call-start = ((), (), s32[]{:S(2)}) async-start(), calls=%async_computation.25 | async-start | bytes 5898240 | tf_op jit(solution)/shard_map/reduce_scatter | solution.py:220
  788.3 225.1 %reduce-scatter.33.cloned.1.call-start = ((), (), s32[]{:S(2)}) async-start(), calls=%async_computation.24 | async-start | bytes 5898240 | tf_op jit(solution)/shard_map/reduce_scatter | solution.py:214
  802.0 26.0 %copy-start.35 = (bf16[12,64,512]{2,1,0:T(8,128)(2,1)S(1)}, bf16[12,64,512]{2,1,0:T(8,128)(2,1)}, u32[]{:S(2)}) copy-start(bf16[12,64,512]{2,1,0:T(8,128)(2,1)} %get-tuple-element.279) | copy-start | bytes 2359300
  802.0 26.0 %copy-start.40 = (bf16[12,64,512]{2,1,0:T(8,128)(2,1)S(1)}, bf16[12,64,512]{2,1,0:T(8,128)(2,1)}, u32[]{:S(2)}) copy-start(bf16[12,64,512]{2,1,0:T(8,128)(2,1)} %get-tuple-element.281) | copy-start | bytes 2359300
  (62 other events, 390.6 us)
Sparse Core Ops, SparseCore 0:
  16.0 42.6 all-gather.5
  61.5 39.8 all-gather.7
  104.1 39.8 all-gather.9
  146.6 39.8 all-gather.11
  513.7 62.8 reduce-scatter.30
  579.8 63.1 reduce-scatter.28
  647.0 63.1 reduce-scatter.24
  713.6 63.1 reduce-scatter.26
  779.2 18.6 reduce-scatter.46
  800.3 23.2 reduce-scatter.44
  826.2 19.7 reduce-scatter.42
  848.4 19.7 reduce-scatter.40
  870.8 19.7 reduce-scatter.36
  893.0 19.7 reduce-scatter.38
  915.3 47.8 reduce-scatter.34
  965.6 47.8 reduce-scatter.32
where the time goes:
time: 1030 us; the launch traced here: 1020 us
  waiting for transfers between devices  413 us (40%)
  matrix products  235 us (23%)
  blocking collectives  195 us (19%)
  local copies, waits for them, and re-layouts  84.7 us (8%)
  other arithmetic  66.5 us (6%)
  between operations  17.2 us (2%)
  starting transfers between devices  12.5 us (1%)
    dot_general x31, matrix products, matmul(): return jnp.einsum(form, left, right, preferred_element_type=jnp.float32)  228 us
    unnamed x2, blocking collectives  75.3 us
    reduce_scatter x1, waiting for transfers between devices, shards(): lax.psum_scatter(grad_wq.astype(jnp.bfloat16), 'expert', scatter_dimensio...  65.3 us
    reduce_scatter x1, waiting for transfers between devices, shards(): lax.psum_scatter(grad_wk.astype(jnp.bfloat16), 'expert', scatter_dimensio...  64.7 us
    all_gather x1, blocking collectives, shards(): lax.all_gather(gating_prototypes, 'expert', axis=0, tiled=True)  54.4 us
    reduce_scatter x1, waiting for transfers between devices, shards(): lax.psum_scatter(grad_out[None].astype(jnp.bfloat16), 'dp', scatter_dimen...  48.9 us
    reduce_scatter x1, waiting for transfers between devices, shards(): lax.psum_scatter(grad_in[None].astype(jnp.bfloat16), 'dp', scatter_dimens...  47.4 us
    unnamed x217, local copies, waits for them, and re-layouts  43.8 us
  transfers between devices with their start and end apart: 19, of which 12 were waited for; matrix products, arithmetic and copies ran while one was open for 22% of the time, Pallas kernels for 0%

commit v1 on v0

v1 whole, which is shorter than its diff:
```python
from functools import partial

import jax
import jax.numpy as jnp
from jax import lax
from jax.experimental import pallas as pl
from jax.experimental.pallas import tpu as pltpu
from jax.sharding import PartitionSpec as P

HEADS = 12
HEAD_DIM = 64
SEQ_LEN = 1024
GROUPS = 4
SLAB = 896

EPSILON = 1e-05
MASKED = -1e30
BOTH = ("dp", "expert")
BF = jnp.bfloat16
F32 = jnp.float32


def dot(left, right, left_dim, right_dim):
    return lax.dot_general(
        left, right, (((left_dim,), (right_dim,)), ((), ())), preferred_element_type=F32
    )


def normalize(values):
    center = jnp.mean(values, axis=-1, keepdims=True)
    centered = values - center
    inverse = lax.rsqrt(jnp.mean(centered * centered, axis=-1, keepdims=True) + EPSILON)
    return (centered * inverse, inverse)


def normalize_back(grad, normed, inverse, gain):
    scaled = grad * gain
    return inverse * (
        scaled
        - jnp.mean(scaled, axis=-1, keepdims=True)
        - normed * jnp.mean(scaled * normed, axis=-1, keepdims=True)
    )


def call(kernel, name, grid, in_specs, outs, scratch=(), vmem=60, cost=(0, 0, 0), **more):
    return pl.pallas_call(
        kernel,
        name=name,
        grid=grid,
        in_specs=in_specs,
        out_specs=[o[0] for o in outs],
        out_shape=[jax.ShapeDtypeStruct(o[1], o[2]) for o in outs],
        scratch_shapes=list(scratch),
        compiler_params=pltpu.CompilerParams(vmem_limit_bytes=vmem << 20),
        cost_estimate=pl.CostEstimate(
            flops=cost[0], bytes_accessed=cost[1], transcendentals=cost[2]
        ),
        **more,
    )


def full(shape):
    return pl.BlockSpec(
        shape, lambda *_: (0,) * len(shape), pipeline_mode=pl.Buffered(1)
    )


SCALARS = pl.BlockSpec(memory_space=pltpu.SMEM)
PLACED = pl.BlockSpec(memory_space=pl.ANY)


def project_kernel(first, table, order, *refs):
    if first:
        x_ref, slabs, wq_ref, wo_ref, qkv_ref, low_ref, vec_ref, cols_ref, sems = refs
    else:
        low_ref, vec_ref, slabs, wq_ref, wo_ref, qkv_ref, sems = refs
    rows = slabs.shape[1]
    half = 2 * 96
    copies = []
    if first:
        for e in range(8):
            copies.append((slabs.at[table[e], :, 128:256], cols_ref.at[pl.ds(rows * e, rows)]))
    for g in range(2):
        for e in range(8):
            copies.append(
                (slabs.at[table[8 * g + e], :, 256:], wq_ref.at[g, pl.ds(rows * e, rows)])
            )
    for g in range(2):
        for e in range(8):
            at = pl.multiple_of(half * order[4 + e // 2] + rows * (e % 2), 32)
            copies.append((slabs.at[table[8 * g + e], :, :256], wo_ref.at[g, pl.ds(at, rows)]))
    copies = [pltpu.make_async_copy(s, d, sems.at[i]) for i, (s, d) in enumerate(copies)]
    for c in copies:
        c.start()
    count, width = low_ref.shape
    if first:
        for c in copies[:8]:
            c.wait()
        copies = copies[8:]
        vec_ref[...] = cols_ref[...].astype(F32).T[64:72]
        for at in range(0, count, 256):
            unit, _ = normalize(x_ref[at : at + 256].astype(F32))
            low_ref[at : at + 256] = (unit * vec_ref[0:1] + vec_ref[1:2]).astype(BF)
    zero = jnp.zeros((1, half), F32)
    for g in range(2):
        for c in copies[8 * g : 8 * g + 8]:
            c.wait()
        bias_q = bias_v = zero
        for n in range(GROUPS):
            here = order[(0 if first else 2) + g] == n
            bias_q = jnp.where(here, vec_ref[2:3, half * n : half * n + half], bias_q)
            bias_v = jnp.where(here, vec_ref[3:4, half * n : half * n + half], bias_v)
        bias = jnp.concatenate([bias_q, zero, bias_v], axis=1)
        for at in range(0, count, 512):
            qkv_ref[g, at : at + 512] = (
                dot(low_ref[at : at + 512], wq_ref[g, :, : 3 * half], 1, 0) + bias
            ).astype(BF)
    for c in copies[16:]:
        c.wait()


def project(table, order, slabs, x=None, low=None, vec=None):
    first = x is not None
    count, width = (x if first else low).shape
    part = width // GROUPS
    outs = [
        (full((2, width, 640)), (2, width, 640), BF),
        (full((2, width, 256)), (2, width, 256), BF),
        (full((2, count, 3 * part)), (2, count, 3 * part), BF),
    ]
    scratch = [pltpu.SemaphoreType.DMA((40,))]
    if first:
        outs += [
            (full((count, width)), (count, width), BF),
            (full((8, width)), (8, width), F32),
        ]
        scratch = [pltpu.VMEM((width, 128), BF)] + scratch
        ins, args = [full((count, width)), PLACED], (x, slabs)
    else:
        ins, args = [full((count, width)), full((8, width)), PLACED], (low, vec, slabs)
    return call(
        partial(project_kernel, first), "project", (1,), [SCALARS, SCALARS] + ins, outs, scratch,
        cost=(2 * count * width * 6 * part, 12_000_000, 0),
    )(table, order, *args)


def attend_kernel(qkv_ref, ctx_ref, lse_ref):
    length = qkv_ref.shape[1]
    width = qkv_ref.shape[2] // 3
    block = min(256, length)
    lane = lax.broadcasted_iota(jnp.int32, (block, 128), 1)
    row = lax.broadcasted_iota(jnp.int32, (block, block), 0)
    col = lax.broadcasted_iota(jnp.int32, (block, block), 1)
    for i in range(length // block):
        start = i * block
        stats = jnp.zeros((block, 128), F32)
        for h in range(width // HEAD_DIM):
            at = h * HEAD_DIM
            q = qkv_ref[0, start : start + block, at : at + HEAD_DIM] * BF(HEAD_DIM**-0.5)
            k = qkv_ref[0, : start + block, width + at : width + at + HEAD_DIM]
            v = qkv_ref[0, : start + block, 2 * width + at : 2 * width + at + HEAD_DIM]
            diag = jnp.where(col <= row, dot(q, k[start:], 1, 1), MASKED)
            top = jnp.max(diag, axis=-1, keepdims=True)
            if start:
                past = dot(q, k[:start], 1, 1)
                top = jnp.maximum(top, jnp.max(past, axis=-1, keepdims=True))
            diag = jnp.exp(diag - top)
            total = jnp.sum(diag, axis=-1, keepdims=True)
            out = dot(diag.astype(BF), v[start:], 1, 0)
            if start:
                past = jnp.exp(past - top)
                total += jnp.sum(past, axis=-1, keepdims=True)
                out += dot(past.astype(BF), v[:start], 1, 0)
            ctx_ref[0, start : start + block, at : at + HEAD_DIM] = (out / total).astype(BF)
            stats = jnp.where(lane == h, top + jnp.log(total), stats)
        lse_ref[0, start : start + block, :] = stats


def attend(qkv):
    groups, length, width = qkv.shape
    width //= 3
    seqs = length // SEQ_LEN
    at = lambda g, s: (g, s, 0)
    return call(
        attend_kernel, "attend", (groups, seqs),
        [pl.BlockSpec((1, SEQ_LEN, 3 * width), at)],
        [
            (pl.BlockSpec((1, SEQ_LEN, width), at), (groups, length, width), BF),
            (pl.BlockSpec((1, SEQ_LEN, 128), at), (groups, length, 128), F32),
        ],
        cost=(8_000_000_000, 5_000_000, 4_000_000),
    )(qkv)


def attend_back_kernel(qkv_ref, ctx_ref, dctx_ref, lse_ref, out_ref, sum_ref, dq_ref):
    length = qkv_ref.shape[1]
    width = qkv_ref.shape[2] // 3
    heads = width // HEAD_DIM
    block = min(256, length)
    lane = lax.broadcasted_iota(jnp.int32, (length, 128), 1)
    stats = lse_ref[0]
    for h in range(heads):
        at = h * HEAD_DIM
        o = ctx_ref[0, :, at : at + HEAD_DIM].astype(F32)
        do = dctx_ref[0, :, at : at + HEAD_DIM].astype(F32)
        stats = jnp.where(lane == 8 + h, jnp.sum(o * do, axis=-1, keepdims=True), stats)
    stats = stats.T
    row = lax.broadcasted_iota(jnp.int32, (block, block), 0)
    col = lax.broadcasted_iota(jnp.int32, (block, block), 1)
    for h in range(heads):
        at = h * HEAD_DIM
        q = qkv_ref[0, :, at : at + HEAD_DIM] * BF(HEAD_DIM**-0.5)
        do = dctx_ref[0, :, at : at + HEAD_DIM]
        for j in range(length // block):
            start = j * block
            k = qkv_ref[0, start : start + block, width + at : width + at + HEAD_DIM]
            v = qkv_ref[0, start : start + block, 2 * width + at : 2 * width + at + HEAD_DIM]
            dk = None
            for s, e, on_diag in ((start, start + block, True), (start + block, length, False)):
                if s == e:
                    continue
                lse = stats[h : h + 1, s:e]
                inner = stats[8 + h : 9 + h, s:e]
                probs = jnp.exp(dot(k, q[s:e], 1, 1) - lse)
                if on_diag:
                    probs = jnp.where(row <= col, probs, 0.0)
                dscores = (probs * (dot(v, do[s:e], 1, 1) - inner)).astype(BF)
                dk_part = dot(dscores, q[s:e], 1, 0)
                dv_part = dot(probs.astype(BF), do[s:e], 1, 0)
                dq_part = dot(dscores, k, 0, 0)
                dk = dk_part if dk is None else dk + dk_part
                dv = dv_part if on_diag else dv + dv_part
                if j == 0:
                    dq_ref[s:e, :] = dq_part
                else:
                    dq_ref[s:e, :] += dq_part
            out_ref[0, start : start + block, width + at : width + at + HEAD_DIM] = dk.astype(BF)
            out_ref[0, start : start + block, 2 * width + at : 2 * width + at + HEAD_DIM] = (
                dv.astype(BF)
            )
        out_ref[0, :, at : at + HEAD_DIM] = (dq_ref[...] * HEAD_DIM**-0.5).astype(BF)
    sums = jnp.sum(out_ref[0].astype(F32), axis=0, keepdims=True)
    first = pl.program_id(1) == 0

    @pl.when(first)
    def _():
        sum_ref[0] = jnp.broadcast_to(sums, sum_ref.shape[1:])

    @pl.when(jnp.logical_not(first))
    def _():
        sum_ref[0] += jnp.broadcast_to(sums, sum_ref.shape[1:])


def attend_back(qkv, ctx, dctx, lse):
    groups, length, width = qkv.shape
    width //= 3
    seqs = length // SEQ_LEN
    at = lambda g, s: (g, s, 0)
    return call(
        attend_back_kernel, "attend_back", (groups, seqs),
        [
            pl.BlockSpec((1, SEQ_LEN, 3 * width), at),
            pl.BlockSpec((1, SEQ_LEN, width), at),
            pl.BlockSpec((1, SEQ_LEN, width), at),
            pl.BlockSpec((1, SEQ_LEN, 128), at),
        ],
        [
            (pl.BlockSpec((1, SEQ_LEN, 3 * width), at), (groups, length, 3 * width), BF),
            (pl.BlockSpec((1, 8, 3 * width), lambda g, s: (g, 0, 0)), (groups, 8, 3 * width), F32),
        ],
        [pltpu.VMEM((SEQ_LEN, HEAD_DIM), F32)],
        cost=(20_000_000_000, 7_000_000, 4_000_000),
    )(qkv, ctx, dctx, lse)


def slot_of(index, half, cap):
    return index // (cap // 2) * cap + index % (cap // 2) + half * (cap // 2)


def dispatch_kernel(target_ref, rows_ref, out_ref):
    count = rows_ref.shape[0]
    for at in range(0, count, 256):
        slot = lax.broadcasted_iota(jnp.int32, (256, count), 0) + at
        picks = (target_ref[...] == slot).astype(F32).astype(BF)
        out_ref[at : at + 256] = dot(picks, rows_ref[...], 1, 0).astype(BF)


def dispatch(target, rows):
    count, width = rows.shape
    return call(
        dispatch_kernel, "dispatch", (1,),
        [full((1, count)), full((count, width))],
        [(full((count, width)), (count, width), BF)],
        cost=(2 * count * count * width, 3_000_000, 0),
    )(target.reshape(1, count), rows)[0]


def mix_kernel(
    cap, order, x_ref, near_ref, far_ref, wo_near, wo_far, vec_ref, target_ref,
    h_ref, whole_ref, *refs,
):
    *sent, low_ref = refs
    count, width = x_ref.shape
    part = width // GROUPS
    pieces = [wo_near[0], wo_near[1], wo_far[0], wo_far[1]]
    for n in range(GROUPS):
        piece = pieces[0][:, :part]
        for r in range(1, GROUPS):
            piece = jnp.where(order[r] == n, pieces[r][:, :part], piece)
        whole_ref[:, n * part : n * part + part] = piece
    for at in range(0, count, 256):
        h = x_ref[at : at + 256].astype(F32) + vec_ref[4:5]
        for r in range(GROUPS):
            ctx = (near_ref, far_ref)[r // 2][r % 2, at : at + 256]
            h += dot(ctx, whole_ref[r * part : r * part + part], 1, 0)
        h_ref[at : at + 256] = h
        unit, _ = normalize(h)
        low_ref[at : at + 256] = (unit * vec_ref[5:6] + vec_ref[6:7]).astype(BF)
    for half in range(2):
        for at in range(0, count // 2, 256):
            index = lax.broadcasted_iota(jnp.int32, (256, count), 0) + at
            picks = (target_ref[...] == slot_of(index, half, cap)).astype(F32).astype(BF)
            sent[half][at : at + 256] = dot(picks, low_ref[...], 1, 0).astype(BF)


def mix(order, x, near, far, wo_near, wo_far, vec, target, cap):
    count, width = x.shape
    part = width // GROUPS
    ctx = full((2, count, part))
    return call(
        partial(mix_kernel, cap), "mix", (1,),
        [SCALARS, full((count, width)), ctx, ctx, full((2, width, 256)), full((2, width, 256)),
         full((8, width)), full((1, count))],
        [
            (full((count, width)), (count, width), F32),
            (full((width, width)), (width, width), BF),
            (full((count // 2, width)), (count // 2, width), BF),
            (full((count // 2, width)), (count // 2, width), BF),
        ],
        [pltpu.VMEM((count, width), BF)],
        cost=(2 * count * width * (width + count), 12_000_000, 0),
    )(order, x, near, far, wo_near, wo_far, vec, target.reshape(1, count))


def unmix_kernel(
    cap, order, h_ref, g_ref, dm_one, dm_two, target_ref, near_ref, far_ref, whole_ref, vec_ref,
    dh_ref, dnear_ref, dfar_ref, gnear_ref, gfar_ref, sum_ref, do_ref,
):
    count, width = h_ref.shape
    part = width // GROUPS
    sums = [jnp.zeros((1, width), F32)] * 3
    for at in range(0, count, 256):
        dm = None
        for half, rows in enumerate((dm_one, dm_two)):
            index = lax.broadcasted_iota(jnp.int32, (256, count // 2), 1)
            picks = target_ref[at : at + 256] == slot_of(index, half, cap)
            got = dot(picks.astype(F32).astype(BF), rows[...], 1, 0)
            dm = got if dm is None else dm + got
        unit, inverse = normalize(h_ref[at : at + 256])
        dh = g_ref[at : at + 256].astype(F32) + normalize_back(dm, unit, inverse, vec_ref[5:6])
        dh_ref[at : at + 256] = dh
        low = dh.astype(BF)
        do_ref[at : at + 256] = low
        for i, term in enumerate((low.astype(F32), dm * unit, dm)):
            sums[i] = sums[i] + jnp.sum(term, axis=0, keepdims=True)
        for r in range(GROUPS):
            (dnear_ref, dfar_ref)[r // 2][r % 2, at : at + 256] = dot(
                low, whole_ref[r * part : r * part + part], 1, 1
            ).astype(BF)
    sum_ref[...] = jnp.concatenate([jnp.zeros((4, width), F32)] + sums + [jnp.zeros((1, width), F32)])
    for out in (gnear_ref, gfar_ref):
        out[:, :, part:] = jnp.zeros((2, width, 256 - part), BF)
    for q in range(GROUPS):
        ctx = (near_ref, far_ref)[q // 2][q % 2]
        grad = dot(ctx, do_ref[...], 0, 0).astype(BF)
        rows = pl.ds(pl.multiple_of(order[q] * part, 64), part)
        for r in range(GROUPS):
            piece = grad[:, :part]
            for n in range(1, GROUPS):
                piece = jnp.where(order[r] == n, grad[:, n * part : n * part + part], piece)
            (gnear_ref, gfar_ref)[r // 2][r % 2, rows, :part] = piece


def unmix(order, h, g, dm_one, dm_two, target, near, far, whole, vec, cap):
    count, width = h.shape
    part = width // GROUPS
    ctx = full((2, count, part))
    out_ctx = (ctx, (2, count, part), BF)
    out_grad = (full((2, width, 256)), (2, width, 256), BF)
    half = full((count // 2, width))
    return call(
        partial(unmix_kernel, cap), "unmix", (1,),
        [SCALARS, full((count, width)), full((count, width)), half, half, full((count, 1)),
         ctx, ctx, full((width, width)), full((8, width))],
        [
            (full((count, width)), (count, width), F32),
            out_ctx, out_ctx, out_grad, out_grad,
            (full((8, width)), (8, width), F32),
        ],
        [pltpu.VMEM((count, width), BF)],
        vmem=60,
        cost=(2 * count * width * (2 * width + count), 20_000_000, 0),
    )(order, h, g, dm_one, dm_two, target.reshape(count, 1), near, far, whole, vec)


def finish_kernel(h_ref, target_ref, gy_ref, out_ref):
    count = h_ref.shape[0]
    for at in range(0, count, 256):
        slot = lax.broadcasted_iota(jnp.int32, (256, count), 1)
        picks = (target_ref[at : at + 256] == slot).astype(F32).astype(BF)
        out_ref[at : at + 256] = (h_ref[at : at + 256] + dot(picks, gy_ref[...], 1, 0)).astype(BF)


def finish(h, target, gy):
    count, width = h.shape
    return call(
        finish_kernel, "finish", (1,),
        [full((count, width)), full((count, 1)), full((count, width))],
        [(full((count, width)), (count, width), BF)],
        cost=(2 * count * count * width, 6_000_000, 0),
    )(h, target.reshape(count, 1), gy)[0]


ERFC = (
    0.169189354,
    0.1706909295,
    0.1485212475,
    0.2141814502,
    -0.09282610738,
    0.5449670381,
    -0.5097724612,
    0.4843017683,
    -0.1292532277,
)


def gelu_pair(v):
    a = jnp.abs(v) * (0.5**0.5)
    bell = jnp.exp(-0.5 * v * v)
    t = 1.0 / (1.0 + 0.3 * a)
    poly = jnp.full_like(v, ERFC[-1])
    for c in ERFC[-2::-1]:
        poly = poly * t + c
    tail = 0.5 * bell * t * poly
    cdf = jnp.where(v < 0, tail, 1.0 - tail)
    return v * cdf, cdf + v * bell * (0.5 / jnp.pi) ** 0.5


def expert_kernel(
    x_ref, g_ref, win_ref, bin_ref, wout_ref, bout_ref, center_ref, _,
    gy_ref, dm_ref, dy_ref, hid_ref, du_ref, dbin_ref, small_ref,
    y_acc, dm_acc, gate_ref, gates,
):
    step = pl.program_id(0)
    rows, width = x_ref.shape

    @pl.when(step == 0)
    def _():
        z = jnp.sum(x_ref[...].astype(F32) * center_ref[...].astype(F32), axis=-1, keepdims=True)
        gate = 1.0 / (1.0 + jnp.exp(-z))
        gate_ref[...] = jnp.broadcast_to(gate, gate_ref.shape)
        dy_ref[...] = (gate * g_ref[...].reshape(rows, width).astype(F32)).astype(BF)

    act, slope = gelu_pair(dot(x_ref[...], win_ref[...], 1, 0) + bin_ref[...].astype(F32))
    hid = act.astype(BF)
    hid_ref[...] = hid
    y = dot(hid, wout_ref[...], 1, 0)
    du = (dot(dy_ref[...], wout_ref[...], 1, 1) * slope).astype(BF)
    du_ref[...] = du
    dbin_ref[...] = jnp.broadcast_to(
        jnp.sum(du.astype(F32), axis=0, keepdims=True), dbin_ref.shape
    )
    dm = dot(du, win_ref[...], 1, 1)

    @pl.when(step == 0)
    def _():
        y_acc[...] = y
        dm_acc[...] = dm

    @pl.when(step > 0)
    def _():
        y_acc[...] += y
        dm_acc[...] += dm

    @pl.when(step == pl.num_programs(0) - 1)
    def _():
        gate = gate_ref[:, :1]
        g = g_ref[...].reshape(rows, width).astype(F32)
        y = (y_acc[...] + bout_ref[...].astype(F32)).astype(BF).astype(F32)
        gy_ref[...] = (gate * y).astype(BF).reshape(gy_ref.shape)
        dz = gate * (1.0 - gate) * jnp.sum(g * y, axis=-1, keepdims=True)
        dm_ref[...] = (dm_acc[...] + dz * center_ref[...].astype(F32)).astype(BF)
        small_ref[0:1, :] = jnp.sum(dy_ref[...].astype(F32), axis=0, keepdims=True)
        small_ref[1:2, :] = jnp.sum(dz * x_ref[...].astype(F32), axis=0, keepdims=True)


def expert(half, x, g, win, bias_in, wout, bias_out, center, gy):
    rows, width = x.shape
    ff = win.shape[1]
    chunk = min(512, ff)
    along = lambda i: (0, i)
    side = pl.BlockSpec(
        (g.shape[0], 1) + g.shape[2:], lambda i: (0, half, 0, 0), pipeline_mode=pl.Buffered(1)
    )
    return call(
        expert_kernel, "expert", (ff // chunk,),
        [
            full((rows, width)),
            side,
            pl.BlockSpec((width, chunk), along),
            pl.BlockSpec((1, chunk), along),
            pl.BlockSpec((chunk, width), lambda i: (i, 0)),
            full((1, width)),
            full((1, width)),
            PLACED,
        ],
        [
            (side, g.shape, BF),
            (full((rows, width)), (rows, width), BF),
            (full((rows, width)), (rows, width), BF),
            (pl.BlockSpec((rows, chunk), along), (rows, ff), BF),
            (pl.BlockSpec((rows, chunk), along), (rows, ff), BF),
            (pl.BlockSpec((8, chunk), along), (8, ff), F32),
            (full((8, width)), (8, width), F32),
        ],
        [
            pltpu.VMEM((rows, width), F32),
            pltpu.VMEM((rows, width), F32),
            pltpu.VMEM((rows, 128), F32),
            pltpu.SMEM((1,), jnp.int32),
        ],
        cost=(8 * rows * width * ff, 22_000_000, 2 * rows * ff),
        input_output_aliases={} if gy is None else {7: 0},
    )(x, g, win, bias_in, wout, bias_out, center, x if gy is None else gy)


def weigh_kernel(
    hid_one, hid_two, du_one, du_two, dy_one, dy_two, x_one, x_two, bin_one, bin_two,
    small_one, small_two, out_ref,
):
    ff = hid_one.shape[1]
    width = dy_one.shape[1]
    n = pl.num_programs(0)
    out_ref[0, :ff] = (
        dot(hid_one[...], dy_one[...], 0, 0) + dot(hid_two[...], dy_two[...], 0, 0)
    ).astype(BF)
    out_ref[0, ff : 2 * ff] = (
        dot(du_one[...], x_one[...], 0, 0) + dot(du_two[...], x_two[...], 0, 0)
    ).astype(BF)
    small = small_one[...] + small_two[...]
    rest = jnp.zeros((16, width), F32)
    row = lax.broadcasted_iota(jnp.int32, (16, width), 0)
    bias = (bin_one[...] + bin_two[...])[0:1]
    if ff < width:
        bias = jnp.concatenate([bias, jnp.zeros((1, width - ff), F32)], axis=1)
    rest = jnp.where(row == 0, bias, rest)
    rest = jnp.where(row == 1, small[0:1], rest)
    rest = jnp.where(row == 2, small[1:2], rest)
    out_ref[0, 2 * ff :] = rest.astype(BF)


def weigh(n, hid, du, dy, x, bias, small):
    rows, ff = hid[0].shape
    width = dy[0].shape[1]
    part = ff // n
    along = lambda i: (0, i)
    wide = pl.BlockSpec((rows, part), along)
    return call(
        weigh_kernel, "weigh", (n,),
        [wide] * 4 + [full((rows, width))] * 4 + [pl.BlockSpec((8, part), along)] * 2
        + [full((8, width))] * 2,
        [(pl.BlockSpec((1, 2 * part + 16, width), lambda i: (i, 0, 0)),
          (n, 2 * part + 16, width), BF)],
        cost=(8 * rows * width * ff, 26_000_000, 0),
    )(*hid, *du, *dy, *x, *bias, *small)[0]


def unproject_kernel(
    order, near_ref, far_ref, wq_near, wq_far, x_ref, dh_ref, vec_ref, two_ref, bias_near, bias_far,
    out_ref, sum_ref,
):
    count, width = x_ref.shape
    part = width // GROUPS
    sums = [jnp.zeros((1, width), F32)] * 2
    for at in range(0, count, 256):
        da = None
        for r in range(GROUPS):
            grad = (near_ref, far_ref)[r // 2][r % 2, at : at + 256]
            got = dot(grad, (wq_near, wq_far)[r // 2][r % 2, :, : 3 * part], 1, 1)
            da = got if da is None else da + got
        unit, inverse = normalize(x_ref[at : at + 256].astype(F32))
        out_ref[at : at + 256] = dh_ref[at : at + 256] + normalize_back(
            da, unit, inverse, vec_ref[0:1]
        )
        for i, term in enumerate((da * unit, da)):
            sums[i] = sums[i] + jnp.sum(term, axis=0, keepdims=True)
    biases = []
    for first in (0, 2 * part):
        cols = []
        for n in range(GROUPS):
            piece = jnp.zeros((1, part), F32)
            for r in range(GROUPS):
                bias = (bias_near, bias_far)[r // 2][r % 2, 0:1, first : first + part]
                piece = jnp.where(order[r] == n, bias, piece)
            cols.append(piece)
        biases.append(jnp.concatenate(cols, axis=1))
    sum_ref[...] = jnp.concatenate(sums + biases + [two_ref[4:8]])


def unproject(order, near, far, wq_near, wq_far, x, dh, vec, two, bias_near, bias_far):
    count, width = x.shape
    part = width // GROUPS
    grads, weights, bias = full((2, count, 3 * part)), full((2, width, 640)), full((2, 8, 3 * part))
    return call(
        unproject_kernel, "unproject", (1,),
        [SCALARS, grads, grads, weights, weights, full((count, width)), full((count, width)),
         full((8, width)), full((8, width)), bias, bias],
        [(full((count, width)), (count, width), F32), (full((8, width)), (8, width), F32)],
        vmem=60,
        cost=(6 * count * width * width, 20_000_000, 0),
    )(order, near, far, wq_near, wq_far, x, dh, vec, two, bias_near, bias_far)


def slope_kernel(low_ref, grad_ref, o_ref, out_ref):
    cols = grad_ref.shape[2]
    out_ref[0, :, :256] = o_ref[0]
    out_ref[0, :, 256 : 256 + cols] = dot(low_ref[...], grad_ref[0], 0, 0).astype(BF)
    out_ref[0, :, 256 + cols :] = jnp.zeros((out_ref.shape[1], SLAB - 256 - cols), BF)


def slope(low, grads, o_part):
    count, width = low.shape
    cols = grads.shape[2]
    return call(
        slope_kernel, "slope", (2,),
        [
            full((count, width)),
            pl.BlockSpec((1, count, cols), lambda g: (g, 0, 0)),
            pl.BlockSpec((1, width, 256), lambda g: (g, 0, 0)),
        ],
        [(pl.BlockSpec((1, width, SLAB), lambda g: (g, 0, 0)), (2, width, SLAB), BF)],
        cost=(4 * count * width * cols, 8_000_000, 0),
    )(low, grads, o_part)[0]


def slope_add_kernel(table, low_ref, grad_ref, o_ref, vec_ref, more_ref, out_ref, stage, sems):
    g = pl.program_id(0)
    cols = grad_ref.shape[2]
    width = low_ref.shape[1]
    rows = width // 8
    more = more_ref[...].reshape(width, SLAB).astype(F32)
    vecs = jnp.concatenate(
        [jnp.zeros((64, width), F32), vec_ref[...], jnp.zeros((56, width), F32)]
    ).T
    stage[:, :128] = (o_ref[0, :, :128].astype(F32) + more[:, :128]).astype(BF)
    stage[:, 128:256] = (o_ref[0, :, 128:].astype(F32) + vecs + more[:, 128:256]).astype(BF)
    stage[:, 256 : 256 + cols] = (
        dot(low_ref[...], grad_ref[0], 0, 0) + more[:, 256 : 256 + cols]
    ).astype(BF)
    stage[:, 256 + cols :] = jnp.zeros((width, SLAB - 256 - cols), BF)
    copies = [
        pltpu.make_async_copy(
            stage.at[pl.ds(rows * e, rows)], out_ref.at[table[8 * g + e]], sems.at[e]
        )
        for e in range(8)
    ]
    for c in copies:
        c.start()
    for c in copies:
        c.wait()


def slope_add(table, low, grads, o_part, vecs, more):
    count, width = low.shape
    cols = grads.shape[2]
    rows = width // 8
    return call(
        slope_add_kernel, "slope_add", (2,),
        [
            SCALARS,
            full((count, width)),
            pl.BlockSpec((1, count, cols), lambda g: (g, 0, 0)),
            pl.BlockSpec((1, width, 256), lambda g: (g, 0, 0)),
            full((8, width)),
            pl.BlockSpec((1, width, SLAB), lambda g: (g, 0, 0)),
        ],
        [(PLACED, (16, rows, SLAB), BF)],
        [pltpu.VMEM((width, SLAB), BF), pltpu.SemaphoreType.DMA((8,))],
        cost=(4 * count * width * cols, 14_000_000, 0),
    )(table, low, grads, o_part, vecs, more)[0]


class Place:
    def __init__(self, mesh):
        self.n_dp = mesh.shape["dp"]
        self.n_e = mesh.shape["expert"]
        self.staged = self.n_dp == 4 and self.n_e == 8
        if not self.staged:
            return
        dev = lambda x, c, z, y: (x * 2 + c) * 8 + z * 2 + y
        every = [
            (x, c, z, y) for x in range(2) for c in range(2) for z in range(4) for y in range(2)
        ]
        to = lambda move: [(dev(*p), dev(*move(*p))) for p in every]
        self.core = to(lambda x, c, z, y: (x, 1 - c, z, y))
        self.second = to(lambda x, c, z, y: (x, c, z, 1 - y) if c == 0 else (1 - x, c, z, y))
        self.third = to(lambda x, c, z, y: (1 - x, c, z, y) if c == 0 else (x, c, z, 1 - y))
        self.along = [to(lambda x, c, z, y, k=k: (x, c, z ^ k, y)) for k in range(1, 4)]

    def tables(self):
        at = jnp.arange(16, dtype=jnp.int32)
        r = jnp.arange(4, dtype=jnp.int32)
        if not self.staged:
            return jnp.concatenate([r, r]), at, at, at
        d = lax.axis_index("dp")
        e = lax.axis_index("expert")
        x, c, z, y = d // 2, d % 2, e // 2, e % 2
        order = (x ^ (r % 2)) * 2 + (c ^ (r // 2))
        back = ((r % 2) ^ c) * 2 + ((r // 2) ^ x)
        across, zr, yr = at // 8, (at % 8 // 2) ^ z, (at % 2) ^ y
        zero = jnp.where(c == 0, across * 8 + yr * 4, yr * 8 + across * 4) + zr
        one = jnp.where(c == 1, across * 8 + yr * 4, yr * 8 + across * 4) + zr
        return jnp.concatenate([order, back]), zero, one, zero


def whole_of(have):
    n_dp, n_e = lax.axis_size("dp"), lax.axis_size("expert")
    rows, cols = have.shape[1:]
    have = have.reshape(n_dp, n_e, rows, cols).transpose(1, 2, 0, 3)
    return have.reshape(n_e * rows, n_dp * cols)


def gather_all(array):
    return whole_of(lax.all_gather(array, BOTH, axis=0, tiled=False))


def scatter_all(array):
    n_dp, n_e = lax.axis_size("dp"), lax.axis_size("expert")
    rows, cols = array.shape[0] // n_e, array.shape[1] // n_dp
    parts = array.reshape(n_e, rows, n_dp, cols).transpose(2, 0, 1, 3)
    parts = parts.reshape(n_dp * n_e, rows, cols)
    return lax.psum_scatter(parts, BOTH, scatter_dimension=0, tiled=False)


def fetch(place, weights, vectors, filler):
    count = len(vectors)
    stacked = jnp.stack(vectors)
    if place.staged:
        rows, cols = weights[0].shape
        extra = jnp.concatenate([stacked.T, jnp.zeros((rows, 64 - count), BF)], axis=1)
        rest = jnp.zeros((rows, SLAB - 4 * cols - 64), BF)
        shard = jnp.concatenate([weights[0], extra, *weights[1:], rest], axis=1)
        parts = [shard] + [lax.ppermute(shard, BOTH, p) for p in place.along]
        near = jnp.stack(parts)
        near = jnp.concatenate([near, lax.ppermute(near, BOTH, place.second)])
        near, filler = lax.optimization_barrier((near, filler))
        near = jnp.concatenate([near, lax.ppermute(near, BOTH, place.third)])
        far = lax.ppermute(near, BOTH, place.core)
        return near, far, filler
    vecs = lax.all_gather(stacked, "expert", axis=1, tiled=True)
    width = vecs.shape[1]
    part = width // GROUPS
    extra = jnp.concatenate([vecs.T, jnp.zeros((width, 64 - count), BF)], axis=1)
    extra = jnp.broadcast_to(extra[None], (GROUPS, width, 64))
    by_group = lambda w: gather_all(w).reshape(width, GROUPS, part).transpose(1, 0, 2)
    grouped = [by_group(w) for w in weights]
    rest = jnp.zeros((GROUPS, width, SLAB - 4 * part - 64), BF)
    slabs = jnp.concatenate([grouped[0], extra, *grouped[1:], rest], axis=2)
    slabs = slabs.reshape(2, 16, width // 8, SLAB)
    return slabs[0], slabs[1], filler


def split(total, cols, count):
    parts = [total[:, :cols]]
    parts += [total[:, 64 + i * cols : 64 + (i + 1) * cols] for i in (1, 2, 3)]
    return parts, total[:, cols : cols + count].T


def reduce_far(place, blocks):
    return lax.ppermute(blocks, BOTH, place.core) if place.staged else jnp.zeros_like(blocks)


def reduce_near(place, have, far, vecs, count):
    add = lambda a, b: (a.astype(F32) + b.astype(F32)).astype(BF)
    if place.staged:
        got = lax.ppermute(have[8:], BOTH, place.third)
        keep, send = add(have[:4], got[:4]), add(have[4:8], got[4:])
        got = lax.ppermute(send, BOTH, place.second)
        sends = [add(keep[k], got[k]) for k in range(1, 4)]
        got = [lax.ppermute(s, BOTH, p) for s, p in zip(sends, place.along)] + [
            keep[0].astype(F32) + got[0].astype(F32)
        ]
        total = sum(g.astype(F32) for g in got)
        parts, vecs = split(total, (SLAB - 128) // 4, count)
        vecs = vecs + lax.ppermute(vecs, BOTH, place.core)
        return parts, [vecs[i] for i in range(count)]
    slabs = jnp.concatenate([have.reshape(far.shape), far])
    width = slabs.shape[1]
    part = width // GROUPS
    parts = []
    for i in range(4):
        at = i * part + (64 if i else 0)
        grad = slabs[:, :, at : at + part].transpose(1, 0, 2).reshape(width, width)
        parts.append(scatter_all(grad).astype(F32))
    vecs = lax.psum_scatter(vecs[:count], "expert", scatter_dimension=1, tiled=True)
    vecs = lax.psum(vecs, "dp")
    return parts, [vecs[i] for i in range(count)]


def shards(
    place,
    block_entries,
    assignments,
    positions_within,
    specialist_quotas,
    standardize_one_scale,
    standardize_one_shift,
    asking_weights,
    asking_shift,
    lookup_weights,
    content_weights,
    content_shift,
    context_mixing_weights,
    context_mixing_shift,
    standardize_two_scale,
    standardize_two_shift,
    gating_prototypes,
    specialist_widen_weights,
    specialist_widen_shift,
    specialist_contract_weights,
    specialist_contract_shift,
    upstream_adjoint,
):
    count, width = block_entries.shape
    experts = specialist_quotas.shape[0]
    cap = count // experts
    n_dp = place.n_dp
    order, at_near, at_far, onward = place.tables()
    barrier = lax.optimization_barrier

    chosen = assignments[:, None] == lax.broadcasted_iota(jnp.int32, (count, experts), 1)
    limit = jnp.sum(jnp.where(chosen, specialist_quotas[None, :], 0), axis=1)
    target = jnp.where(positions_within < limit, assignments * cap + positions_within, count)

    def exchange(rows):
        sent = rows.reshape(experts, -1, width)
        got = lax.all_to_all(sent, "expert", split_axis=0, concat_axis=0, tiled=True)
        return got.reshape(rows.shape)

    near, far, sent_g = fetch(
        place,
        (context_mixing_weights, asking_weights, lookup_weights, content_weights),
        (
            standardize_one_scale,
            standardize_one_shift,
            asking_shift,
            content_shift,
            context_mixing_shift,
            standardize_two_scale,
            standardize_two_shift,
        ),
        dispatch(target, upstream_adjoint),
    )
    sent_g, far = barrier((sent_g, far))
    rows_g = exchange(sent_g).reshape(experts, 2, cap // 2, width)

    wq_near, wo_near, qkv_near, low_in, vec = project(at_near, order, near, x=block_entries)
    ctx_near, lse_near = attend(qkv_near)
    wq_far, wo_far, qkv_far = project(at_far, order, far, low=low_in, vec=vec)
    ctx_far, lse_far = attend(qkv_far)
    ctx_far, rows_g = barrier((ctx_far, rows_g))
    h1, whole_o, sent_one, sent_two = mix(
        order, block_entries, ctx_near, ctx_far, wo_near, wo_far, vec, target, cap
    )

    x_one = exchange(sent_one)
    x_one, sent_two = barrier((x_one, sent_two))
    x_two = exchange(sent_two)
    matrices = (
        specialist_widen_weights[0], specialist_widen_shift, specialist_contract_weights[0],
        specialist_contract_shift, gating_prototypes,
    )
    gy, dm_one, dy_one, hid_one, du_one, dbin_one, small_one = expert(
        0, x_one, rows_g, *matrices, None
    )
    x_two, dm_one = barrier((x_two, dm_one))
    dm_one = exchange(dm_one)
    gy, dm_two, dy_two, hid_two, du_two, dbin_two, small_two = expert(
        1, x_two, rows_g, *matrices, gy
    )
    dm_one, dm_two = barrier((dm_one, dm_two))
    dm_two = exchange(dm_two)
    grads = weigh(
        n_dp, (hid_one, hid_two), (du_one, du_two), (dy_one, dy_two), (x_one, x_two),
        (dbin_one, dbin_two), (small_one, small_two),
    )
    grads, dm_two, gy = barrier((grads, dm_two, gy))
    gy = exchange(gy.reshape(count, width))
    grads = lax.psum_scatter(grads, "dp", scatter_dimension=0, tiled=False)

    dh1, dctx_near, dctx_far, wog_near, wog_far, two = unmix(
        order, h1, upstream_adjoint, dm_one, dm_two, target, ctx_near, ctx_far, whole_o, vec, cap
    )
    dqkv_far, bias_far = attend_back(qkv_far, ctx_far, dctx_far, lse_far)
    slabs_far = slope(low_in, dqkv_far, wog_far)
    more = reduce_far(place, slabs_far)
    dqkv_near, bias_near = attend_back(qkv_near, ctx_near, dctx_near, lse_near)
    input_grad, vecs = unproject(
        order, dqkv_near, dqkv_far, wq_near, wq_far, block_entries, dh1, vec, two, bias_near,
        bias_far,
    )
    dqkv_near, gy = barrier((dqkv_near, gy))
    slabs = slope_add(onward, low_in, dqkv_near, wog_near, vecs, more)
    (sum_o, sum_q, sum_k, sum_v), small = reduce_near(place, slabs, slabs_far, vecs, 7)
    output = finish(h1, target, gy)

    part = (grads.shape[0] - 16) // 2
    own = lax.axis_index("dp") * (width // n_dp)
    grad_out = grads[:part].astype(F32)[None]
    grad_in = grads[part : 2 * part].astype(F32).T[None]
    grad_bin = grads[2 * part : 2 * part + 1, :part].astype(F32)
    grad_bout = lax.dynamic_slice(
        grads[2 * part + 1 : 2 * part + 2], (0, own), (1, width // n_dp)
    ).astype(F32)
    grad_centers = grads[2 * part + 2 : 2 * part + 3].astype(F32)
    return (
        output,
        input_grad,
        small[0],
        small[1],
        sum_q,
        small[2],
        sum_k,
        sum_v,
        small[3],
        sum_o,
        small[4],
        small[5],
        small[6],
        grad_centers,
        grad_in,
        grad_bin,
        grad_out,
        grad_bout,
    )


def solution(mesh):
    placed = (
        P(("dp", "expert"), None),
        P(("dp", "expert")),
        P(("dp", "expert")),
        P(),
        P("expert"),
        P("expert"),
        P("expert", "dp"),
        P("expert"),
        P("expert", "dp"),
        P("expert", "dp"),
        P("expert"),
        P("expert", "dp"),
        P("expert"),
        P("expert"),
        P("expert"),
        P("expert", None),
        P("expert", None, None),
        P("expert", None),
        P("expert", None, None),
        P("expert", None),
        P(("dp", "expert"), None),
    )
    return jax.shard_map(
        partial(shards, Place(mesh)),
        mesh=mesh,
        in_specs=placed,
        out_specs=(
            P(("dp", "expert"), None),
            P(("dp", "expert"), None),
            P("expert"),
            P("expert"),
            P("expert", "dp"),
            P("expert"),
            P("expert", "dp"),
            P("expert", "dp"),
            P("expert"),
            P("expert", "dp"),
            P("expert"),
            P("expert"),
            P("expert"),
            P("expert", None),
            P("expert", None, "dp"),
            P("expert", "dp"),
            P("expert", "dp", None),
            P("expert", "dp"),
        ),
        check_vma=False,
    )
```

time: 1030 us -> 395 us (0.38)
  waiting for transfers between devices: 413 us -> 73.3 us
  matrix products: 235 us -> 0 us
  Pallas kernels: 0 us -> 211 us
  blocking collectives: 195 us -> 26 us
  local copies, waits for them, and re-layouts: 84.7 us -> 12.7 us
  other arithmetic: 66.5 us -> 9.89 us
  starting transfers between devices: 12.5 us -> 42.5 us
    reduce_scatter x6 -> x1, waiting for transfers between devices: 248 us -> 0.01 us  [shards(): grads = lax.psum_scatter(grads, 'dp', scatter_dimension=0, tiled=False)]
    dot_general x33 -> x0, matrix products: 235 us -> none  [the longest x31 228 us: matmul(): return jnp.einsum(form, left, right, preferred_element_type=jnp.float32)]
    pallas_call x0 -> x16, Pallas kernels: none -> 211 us  [the longest x2 48.2 us: expert(): call(expert_kernel, 'expert', (ff // chunk,), [full((rows, width)), side,...]
    all_gather x5 -> x0, blocking collectives: 78.1 us -> none  [the longest x1 54.4 us: shards(): lax.all_gather(gating_prototypes, 'expert', axis=0, tiled=True)]
    unnamed x2 -> x0, blocking collectives: 75.3 us -> none
    ppermute x0 -> x13, waiting for transfers between devices: none -> 70.2 us  [the longest x1 17.1 us: reduce_near(): got = lax.ppermute(have[8:], BOTH, place.third)]
    all_to_all x3 -> x5, waiting for transfers between devices: 70.6 us -> 3.11 us  [exchange(): lax.all_to_all(sent, 'expert', split_axis=0, concat_axis=0, tiled=True)]
    all_gather x4 -> x0, waiting for transfers between devices: 51.9 us -> none  [the longest x1 38.7 us: shards(): lax.all_gather(rows_k, 'expert', axis=0, tiled=True)]
  transfers between devices with their start and end apart: 19 -> 19, of which waited for: 12 -> 9; matrix products, arithmetic and copies ran while one was open for 22% -> 2% of each run, Pallas kernels for 0% -> 52%
where the time goes in v1:
time: 395 us; the launch traced here: 390 us
  Pallas kernels  211 us (53%)
  waiting for transfers between devices  73.3 us (19%)
  starting transfers between devices  42.5 us (11%)
  blocking collectives  26 us (7%)
  between operations  14.8 us (4%)
  local copies, waits for them, and re-layouts  12.7 us (3%)
  other arithmetic  9.89 us (3%)
    pallas_call x2, Pallas kernels, expert(): call(expert_kernel, 'expert', (ff // chunk,), [full((rows, width)), side,...  48.2 us
    pallas_call x2, Pallas kernels, attend_back(): call(attend_back_kernel, 'attend_back', (groups, seqs), [pl.BlockSpec((1,...  43.3 us
    all_to_all x1, blocking collectives, exchange(): lax.all_to_all(sent, 'expert', split_axis=0, concat_axis=0, tiled=True)  26 us
    all_to_all x5, starting transfers between devices, exchange(): lax.all_to_all(sent, 'expert', split_axis=0, concat_axis=0, tiled=True)  25.8 us
    pallas_call x2, Pallas kernels, attend(): call(attend_kernel, 'attend', (groups, seqs), [pl.BlockSpec((1, SEQ_LEN,...  24.5 us
    pallas_call x2, Pallas kernels, project(): call(partial(project_kernel, first), 'project', (1,), [SCALARS, SCALARS]...  17.9 us
    ppermute x1, waiting for transfers between devices, reduce_near(): got = lax.ppermute(have[8:], BOTH, place.third)  17.1 us
    ppermute x1, waiting for transfers between devices, fetch(): near = jnp.concatenate([near, lax.ppermute(near, BOTH, place.third)])  16.7 us
  transfers between devices with their start and end apart: 19, of which 9 were waited for; matrix products, arithmetic and copies ran while one was open for 2% of the time, Pallas kernels for 52%

profile of v1, /device:TPU:0, one launch (start us, length us, event | category | flops | bytes accessed | tf_op | source)
XLA Modules:
  0.0 390.1 jit_solution(17604932800848497504)
XLA Ops:
  8.1 1.0 concatenate.14
  9.1 3.1 collective-permute-start
  12.2 2.6 collective-permute-start.1
  15.6 1.3 add_select_fusion
  16.9 4.4 %dispatch.1 = bf16[1024,768]{1,0:T(8,128)(2,1)} custom-call(s32[1,1024]{1,0:T(1,128)} %bitcast.84, bf16[1024,768]{1,0:T(8,128)(2,1)} %g_ref.1), custom_call_target="tpu_custom_call" | custom-call | flops 1610612736 | bytes 3000000 | tf_op jit(solution)/shard_map/dispatch/pallas_call | solution.py:290
  21.3 6.5 %collective-permute-done.1 = bf16[96,896]{1,0:T(8,128)(2,1)S(1)} collective-permute-done((bf16[96,896]{1,0:T(8,128)(2,1)S(1)}, bf16[96,896]{1,0:T(8,128)(2,1)S(1)}, u32[]{:S(2)}, u32[]{:S(2)}) %collective-permute-start.1) | collective-permute-done | bytes 172064 | tf_op jit(solution)/shard_map/ppermute | solution.py:753
  27.9 1.6 collective-permute-start.3
  29.6 10.0 %collective-permute-done.3 = bf16[4,96,896]{2,1,0:T(8,128)(2,1)S(1)} collective-permute-done((bf16[4,96,896]{2,1,0:T(8,128)(2,1)S(1)}, bf16[4,96,896]{2,1,0:T(8,128)(2,1)S(1)}, u32[]{:S(2)}, u32[]{:S(2)}) %collective-permute-start.3) | collective-permute-done | bytes 688160 | tf_op jit(solution)/shard_map/ppermute | solution.py:755
  39.7 1.6 collective-permute-start.4
  41.3 16.7 %collective-permute-done.4 = bf16[8,96,896]{2,1,0:T(8,128)(2,1)S(1)} collective-permute-done((bf16[8,96,896]{2,1,0:T(8,128)(2,1)S(1)}, bf16[8,96,896]{2,1,0:T(8,128)(2,1)S(1)}, u32[]{:S(2)}, u32[]{:S(2)}) %collective-permute-start.4) | collective-permute-done | bytes 1376288 | tf_op jit(solution)/shard_map/ppermute | solution.py:757
  58.3 1.5 copy-done.6
  59.8 5.1 %collective-permute-done.5.refs_2_ = bf16[16,96,896]{2,1,0:T(8,128)(2,1)S(1)} collective-permute-done((bf16[16,96,896]{2,1,0:T(8,128)(2,1)S(1)}, bf16[16,96,896]{2,1,0:T(8,128)(2,1)S(1)}, u32[]{:S(2)}, u32[]{:S(2)}) %collective-permute-start.5) | collective-permute-done | bytes 2752544 | tf_op jit(solution)/shard_map/ppermute | solution.py:758
  64.9 1.5 copy-done.8
  66.4 5.9 %all-to-all-start = ((bf16[8,128,768]{2,1,0:T(8,128)(2,1)}), bf16[8,128,768]{2,1,0:T(8,128)(2,1)S(1)}, u32[]{:S(2)}, u32[]{:S(2)}) async-start(bf16[8,128,768]{2,1,0:T(8,128)(2,1)} %bitcast.13), calls=%async_computation | async-start | bytes 3145728 | tf_op jit(solution)/shard_map/all_to_all | solution.py:847
  74.0 9.6 %project.2 = (bf16[2,768,640]{2,1,0:T(8,128)(2,1)}, bf16[2,768,256]{2,1,0:T(8,128)(2,1)}, bf16[2,1024,576]{2,1,0:T(8,128)(2,1)}, bf16[1024,768]{1,0:T(8,128)(2,1)}, f32[8,768]{1,0:T(8,128)}) custom-call(s32[16]{0:T(128)} %fusion.5.table, s32[8]{0:T(128)} %pad_add_fusion.order, bf16[1024,768]{1,0:T(8,128)(2,1)} %x_ref.3, bf16[16,96,896]{2,1,0:T(8,128)(2,1)} %copy-done.6), custom_call_target="tpu_custom_call" | custom-call | flops 1811939328 | bytes 12000000 | tf_op jit(solution)/shard_map/project/pallas_call | solution.py:141
  83.6 12.1 %attend.2 = (bf16[2,1024,192]{2,1,0:T(8,128)(2,1)}, f32[2,1024,128]{2,1,0:T(8,128)}) custom-call(bf16[2,1024,576]{2,1,0:T(8,128)(2,1)} %get-tuple-element.78.qkv_ref), custom_call_target="tpu_custom_call" | custom-call | flops 8000000000 | bytes 5000000 | tf_op jit(solution)/shard_map/attend/pallas_call | solution.py:184
  95.7 8.3 %project.3 = (bf16[2,768,640]{2,1,0:T(8,128)(2,1)}, bf16[2,768,256]{2,1,0:T(8,128)(2,1)}, bf16[2,1024,576]{2,1,0:T(8,128)(2,1)}) custom-call(s32[16]{0:T(128)} %fusion.6.table, s32[8]{0:T(128)} %pad_add_fusion.order, bf16[1024,768]{1,0:T(8,128)(2,1)} %get-tuple-element.80.refs_0_.low_ref, f32[8,768]{1,0:T(8,128)} %get-tuple-element.81.refs_1_.vec_ref, ...), custom_call_target="tpu_custom_call" | custom-call | flops 1811939328 | bytes 12000000 | tf_op jit(solution)/shard_map/project/pallas_call | solution.py:141
  104.1 12.4 %attend.3 = (bf16[2,1024,192]{2,1,0:T(8,128)(2,1)}, f32[2,1024,128]{2,1,0:T(8,128)}) custom-call(bf16[2,1024,576]{2,1,0:T(8,128)(2,1)} %get-tuple-element.84.qkv_ref), custom_call_target="tpu_custom_call" | custom-call | flops 8000000000 | bytes 5000000 | tf_op jit(solution)/shard_map/attend/pallas_call | solution.py:184
  116.4 8.4 %mix.1 = (f32[1024,768]{1,0:T(8,128)}, bf16[768,768]{1,0:T(8,128)(2,1)}, bf16[512,768]{1,0:T(8,128)(2,1)}, bf16[512,768]{1,0:T(8,128)(2,1)}) custom-call(s32[8]{0:T(128)} %pad_add_fusion.order, bf16[1024,768]{1,0:T(8,128)(2,1)} %x_ref.3, bf16[2,1024,192]{2,1,0:T(8,128)(2,1)} %get-tuple-element.79.near_ref.ctx_ref, ...), custom_call_target="tpu_custom_call" | custom-call | flops 2818572288 | bytes 12000000 | tf_op jit(solution)/shard_map/mix/pallas_call | solution.py:330
  124.8 26.0 %all_to_all.30 = bf16[8,64,768]{2,1,0:T(8,128)(2,1)} all-to-all(bf16[8,64,768]{2,1,0:T(8,128)(2,1)} %bitcast.79), channel_id=1, replica_groups=mesh['dp'=4,'expert'=8] {'expert'}, dimensions={0} | all-to-all | bytes 1572864 | tf_op jit(solution)/shard_map/all_to_all | solution.py:847
  150.8 4.1 %all-to-all-start.2 = ((bf16[8,64,768]{2,1,0:T(8,128)(2,1)}), bf16[8,64,768]{2,1,0:T(8,128)(2,1)S(1)}, u32[]{:S(2)}, u32[]{:S(2)}) async-start(bf16[8,64,768]{2,1,0:T(8,128)(2,1)} %bitcast.18), calls=%async_computation.2 | async-start | bytes 1572864 | tf_op jit(solution)/shard_map/all_to_all | solution.py:847
  154.9 24.1 %expert.2 = (bf16[8,2,64,768]{3,2,1,0:T(8,128)(2,1)}, bf16[512,768]{1,0:T(8,128)(2,1)}, bf16[512,768]{1,0:T(8,128)(2,1)}, bf16[512,3072]{1,0:T(8,128)(2,1)}, bf1...) custom-call(bf16[512,768]{1,0:T(8,128)(2,1)} %bitcast.72, bf16[8,2,64,768]{3,2,1,0:T(8,128)(2,1)} %bitcast.67, ...), custom_call_target="tpu_custom_call" | custom-call | flops 9663676416 | bytes 22000000 | tf_op jit(solution)/shard_map/expert/pallas_call | solution.py:505
  179.0 6.0 %all-to-all-start.3 = ((bf16[8,64,768]{2,1,0:T(8,128)(2,1)}), bf16[8,64,768]{2,1,0:T(8,128)(2,1)S(1)}, u32[]{:S(2)}, u32[]{:S(2)}) async-start(bf16[8,64,768]{2,1,0:T(8,128)(2,1)} %bitcast.78), calls=%async_computation.3 | async-start | bytes 1572864 | tf_op jit(solution)/shard_map/all_to_all | solution.py:847
  185.0 24.1 %expert.3 = (bf16[8,2,64,768]{3,2,1,0:T(8,128)(2,1)}, bf16[512,768]{1,0:T(8,128)(2,1)}, bf16[512,768]{1,0:T(8,128)(2,1)}, bf16[512,3072]{1,0:T(8,128)(2,1)}, bf1...) custom-call(bf16[512,768]{1,0:T(8,128)(2,1)} %bitcast.75, ...), custom_call_target="tpu_custom_call", output_to_operand_aliasing={{0}: (7, {})} | custom-call | flops 9663676416 | bytes 22000000 | tf_op jit(solution)/shard_map/expert/pallas_call | solution.py:505
  209.2 6.0 %all-to-all-start.4 = ((bf16[8,64,768]{2,1,0:T(8,128)(2,1)}), bf16[8,64,768]{2,1,0:T(8,128)(2,1)S(1)}, u32[]{:S(2)}, u32[]{:S(2)}) async-start(bf16[8,64,768]{2,1,0:T(8,128)(2,1)} %bitcast.77), calls=%async_computation.4 | async-start | bytes 1572864 | tf_op jit(solution)/shard_map/all_to_all | solution.py:847
  215.2 15.6 %weigh.1 = bf16[4,1552,768]{2,1,0:T(8,128)(2,1)} custom-call(bf16[512,3072]{1,0:T(8,128)(2,1)} %get-tuple-element.102.hid_one, bf16[512,3072]{1,0:T(8,128)(2,1)} %get-tuple-element.103.hid_two, bf16[512,3072]{1,0:T(8,128)(2,1)} %get-tuple-element.104.du_one, bf16[512,3072]{1,0:T(8,128)(2,1)} %get-tuple-element.105.du_two, ...), custom_call_target="tpu_custom_call" | custom-call | flops 9663676416 | bytes 26000000 | tf_op jit(solution)/shard_map/weigh/pallas_call | solution.py:568
  230.8 3.1 all-to-all-done.4
  233.9 0.9 copy-done.4
  234.8 1.1 copy.64.target_ref
  235.9 3.8 all-to-all-start.5
  239.7 15.7 %unmix.1 = (f32[1024,768]{1,0:T(8,128)}, bf16[2,1024,192]{2,1,0:T(8,128)(2,1)}, bf16[2,1024,192]{2,1,0:T(8,128)(2,1)}, bf16[2,768,256]{2,1,0:T(8,128)(2,1)}, bf1...) custom-call(s32[8]{0:T(128)} %pad_add_fusion.order, f32[1024,768]{1,0:T(8,128)} %get-tuple-element.90.h_ref, ...), custom_call_target="tpu_custom_call" | custom-call | flops 4026531840 | bytes 20000000 | tf_op jit(solution)/shard_map/unmix/pallas_call | solution.py:391
  255.4 21.6 %attend_back.3 = (bf16[2,1024,576]{2,1,0:T(8,128)(2,1)}, f32[2,8,576]{2,1,0:T(8,128)}) custom-call(bf16[2,1024,576]{2,1,0:T(8,128)(2,1)} %get-tuple-element.84.qkv_ref, bf16[2,1024,192]{2,1,0:T(8,128)(2,1)} %get-tuple-element.87.far_ref.ctx_ref, bf16[2,1024,192]{2,1,0:T(8,128)(2,1)} %get-tuple-element.121.dctx_ref, f32[2,1024,128]{2,1,0:T(8,128)} %get-tuple-element.122.lse_ref), custom_call_target="tpu_custom_call" | custom-call | flops 20000000000 | bytes 7000000 | tf_op jit(solution)/shard_map/attend_back/pallas_call | solution.py:259
  277.0 6.3 %slope.1 = bf16[2,768,896]{2,1,0:T(8,128)(2,1)} custom-call(bf16[1024,768]{1,0:T(8,128)(2,1)} %get-tuple-element.80.refs_0_.low_ref, bf16[2,1024,576]{2,1,0:T(8,128)(2,1)} %get-tuple-element.123.far_ref.grad_ref, bf16[2,768,256]{2,1,0:T(8,128)(2,1)} %get-tuple-element.134.o_ref), custom_call_target="tpu_custom_call" | custom-call | flops 1811939328 | bytes 8000000 | tf_op jit(solution)/shard_map/slope/pallas_call | solution.py:634
  283.3 21.8 %attend_back.2 = (bf16[2,1024,576]{2,1,0:T(8,128)(2,1)}, f32[2,8,576]{2,1,0:T(8,128)}) custom-call(bf16[2,1024,576]{2,1,0:T(8,128)(2,1)} %get-tuple-element.78.qkv_ref, bf16[2,1024,192]{2,1,0:T(8,128)(2,1)} %get-tuple-element.79.near_ref.ctx_ref, bf16[2,1024,192]{2,1,0:T(8,128)(2,1)} %get-tuple-element.116.dctx_ref, f32[2,1024,128]{2,1,0:T(8,128)} %get-tuple-element.117.lse_ref), custom_call_target="tpu_custom_call" | custom-call | flops 20000000000 | bytes 7000000 | tf_op jit(solution)/shard_map/attend_back/pallas_call | solution.py:259
  305.1 12.9 %unproject.1 = (f32[1024,768]{1,0:T(8,128)}, f32[8,768]{1,0:T(8,128)}) custom-call(s32[8]{0:T(128)} %pad_add_fusion.order, bf16[2,1024,576]{2,1,0:T(8,128)(2,1)} %get-tuple-element.131.near_ref.grad_ref, bf16[2,1024,576]{2,1,0:T(8,128)(2,1)} %get-tuple-element.123.far_ref.grad_ref, bf16[2,768,640]{2,1,0:T(8,128)(2,1)} %get-tuple-element.124.wq_near, ...), custom_call_target="tpu_custom_call" | custom-call | flops 3623878656 | bytes 20000000 | tf_op jit(solution)/shard_map/unproject/pallas_call | solution.py:614
  318.0 8.2 %slope_add.1 = bf16[16,96,896]{2,1,0:T(8,128)(2,1)} custom-call(s32[16]{0:T(128)} %fusion.5.table, bf16[1024,768]{1,0:T(8,128)(2,1)} %get-tuple-element.80.refs_0_.low_ref, bf16[2,1024,576]{2,1,0:T(8,128)(2,1)} %get-tuple-element.131.near_ref.grad_ref, bf16[2,768,256]{2,1,0:T(8,128)(2,1)} %get-tuple-element.132.o_ref, f32[8,768]{1,0:T(8,128)} %get-tuple-element.133.vec_ref, ...), custom_call_target="tpu_custom_call" | custom-call | flops 1811939328 | bytes 14000000 | tf_op jit(solution)/shard_map/slope_add/pallas_call | solution.py:677
  326.3 1.6 slice.126
  327.9 1.3 collective-permute-start.7
  329.1 17.1 %collective-permute-done.7 = bf16[8,96,896]{2,1,0:T(8,128)(2,1)S(1)} collective-permute-done((bf16[8,96,896]{2,1,0:T(8,128)(2,1)S(1)}, bf16[8,96,896]{2,1,0:T(8,128)(2,1)S(1)}, u32[]{:S(2)}, u32[]{:S(2)}) %collective-permute-start.7) | collective-permute-done | bytes 1376288 | tf_op jit(solution)/shard_map/ppermute | solution.py:786
  346.6 2.1 collective-permute-start.8
  348.7 8.9 %collective-permute-done.8 = bf16[4,96,896]{2,1,0:T(8,128)(2,1)S(1)} collective-permute-done((bf16[4,96,896]{2,1,0:T(8,128)(2,1)S(1)}, bf16[4,96,896]{2,1,0:T(8,128)(2,1)S(1)}, u32[]{:S(2)}, u32[]{:S(2)}) %collective-permute-start.8) | collective-permute-done | bytes 688160 | tf_op jit(solution)/shard_map/ppermute | solution.py:788
  357.7 2.9 collective-permute-start.10
  360.7 1.4 collective-permute-start.11
  362.1 5.5 %finish.1 = bf16[1024,768]{1,0:T(8,128)(2,1)} custom-call(f32[1024,768]{1,0:T(8,128)} %get-tuple-element.90.h_ref, s32[1024,1]{1,0:T(8,128)} %copy.64.target_ref, bf16[1024,768]{1,0:T(8,128)(2,1)} %bitcast.66), custom_call_target="tpu_custom_call" | custom-call | flops 1610612736 | bytes 6000000 | tf_op jit(solution)/shard_map/finish/pallas_call | solution.py:416
  367.7 5.3 %collective-permute-done.10 = bf16[96,896]{1,0:T(8,128)(2,1)S(1)} collective-permute-done((bf16[96,896]{1,0:T(8,128)(2,1)S(1)}, bf16[96,896]{1,0:T(8,128)(2,1)S(1)}, u32[]{:S(2)}, u32[]{:S(2)}) %collective-permute-start.10) | collective-permute-done | bytes 172064 | tf_op jit(solution)/shard_map/ppermute | solution.py:790
  375.4 3.4 slice_convert_fusion
  378.7 1.9 copy.65
  380.7 1.4 fusion.10
  (58 shorter events, 7.5 us)
Async XLA Ops:
  9.1 12.2 %collective-permute-start = (bf16[96,896]{1,0:T(8,128)(2,1)S(1)}, bf16[96,896]{1,0:T(8,128)(2,1)S(1)}, u32[]{:S(2)}, u32[]{:S(2)}) collective-permute-start(bf16[96,896]{1,0:T(8,128)(2,1)S(1)} %concatenate.14), channel_id=1, source_target_pairs={{0,2},{1,3},{2,0},{3,1},{4,6},{5,7},{6,4},{7,5},{8,10},{9,11},{10,... | collective-permute-start | bytes 516104 | tf_op jit(solution)/shard_map/ppermute | solution.py:753
  12.2 15.6 %collective-permute-start.1 = (bf16[96,896]{1,0:T(8,128)(2,1)S(1)}, bf16[96,896]{1,0:T(8,128)(2,1)S(1)}, u32[]{:S(2)}, u32[]{:S(2)}) collective-permute-start(bf16[96,896]{1,0:T(8,128)(2,1)S(1)} %concatenate.14), channel_id=1, source_target_pairs={{0,4},{1,5},{2,6},{3,7},{4,0},{5,1},{6,2},{7,3},{8,12},{9,13},{10,... | collective-permute-start | bytes 516104 | tf_op jit(solution)/shard_map/ppermute | solution.py:753
  14.8 13.0 %collective-permute-start.2 = (bf16[96,896]{1,0:T(8,128)(2,1)S(1)}, bf16[96,896]{1,0:T(8,128)(2,1)S(1)}, u32[]{:S(2)}, u32[]{:S(2)}) collective-permute-start(bf16[96,896]{1,0:T(8,128)(2,1)S(1)} %concatenate.14), channel_id=1, source_target_pairs={{0,6},{1,7},{2,4},{3,5},{4,2},{5,3},{6,0},{7,1},{8,14},{9,15},{10,... | collective-permute-start | bytes 516104 | tf_op jit(solution)/shard_map/ppermute | solution.py:753
  27.9 11.7 %collective-permute-start.3 = (bf16[4,96,896]{2,1,0:T(8,128)(2,1)S(1)}, bf16[4,96,896]{2,1,0:T(8,128)(2,1)S(1)}, u32[]{:S(2)}, u32[]{:S(2)}) collective-permute-start(bf16[4,96,896]{2,1,0:T(8,128)(2,1)S(1)} %pad_maximum_fusion), channel_id=1, source_target_pairs={{0,1},{1,0},{2,3},{3,2},{4,5},{5,4},{6,7},{7,6},{8,24},{9,25},{10,... | collective-permute-start | bytes 2064392 | tf_op jit(solution)/shard_map/ppermute | solution.py:755
  39.7 18.4 %collective-permute-start.4 = (bf16[8,96,896]{2,1,0:T(8,128)(2,1)S(1)}, bf16[8,96,896]{2,1,0:T(8,128)(2,1)S(1)}, u32[]{:S(2)}, u32[]{:S(2)}) collective-permute-start(bf16[8,96,896]{2,1,0:T(8,128)(2,1)S(1)} %constant_dynamic-update-slice_fusion), channel_id=1, source_target_pairs={{0,16},{1,17},{2,18},{3,19},{4,20},{5,21},{6,22},{7,23},{8,9},{9,8... | collective-permute-start | bytes 4128776 | tf_op jit(solution)/shard_map/ppermute | solution.py:757
  58.3 1.5 copy-start.6
  59.8 5.1 %collective-permute-start.5 = (bf16[16,96,896]{2,1,0:T(8,128)(2,1)S(1)}, bf16[16,96,896]{2,1,0:T(8,128)(2,1)S(1)}, u32[]{:S(2)}, u32[]{:S(2)}) collective-permute-start(bf16[16,96,896]{2,1,0:T(8,128)(2,1)S(1)} %constant_dynamic-update-slice_fusion.5.refs_1_), channel_id=1, source_target_pairs={{0,8},{1,9},{2,10},{3,11},{4,12},{5,13},{6,14},{7,15},{8,0},{9,1},... | collective-permute-start | bytes 8257544 | tf_op jit(solution)/shard_map/ppermute | solution.py:758
  64.9 1.5 copy-start.8
  66.4 50.0 %all-to-all-start = ((bf16[8,128,768]{2,1,0:T(8,128)(2,1)}), bf16[8,128,768]{2,1,0:T(8,128)(2,1)S(1)}, u32[]{:S(2)}, u32[]{:S(2)}) async-start(bf16[8,128,768]{2,1,0:T(8,128)(2,1)} %bitcast.13), calls=%async_computation | async-start | bytes 3145728 | tf_op jit(solution)/shard_map/all_to_all | solution.py:847
  116.4 8.4 %copy-start.2 = (bf16[8,128,768]{2,1,0:T(8,128)(2,1)}, bf16[8,128,768]{2,1,0:T(8,128)(2,1)S(1)}, u32[]{:S(2)}) copy-start(bf16[8,128,768]{2,1,0:T(8,128)(2,1)S(1)} %all-to-all-done) | copy-start | bytes 4718596
  150.8 28.2 %all-to-all-start.2 = ((bf16[8,64,768]{2,1,0:T(8,128)(2,1)}), bf16[8,64,768]{2,1,0:T(8,128)(2,1)S(1)}, u32[]{:S(2)}, u32[]{:S(2)}) async-start(bf16[8,64,768]{2,1,0:T(8,128)(2,1)} %bitcast.18), calls=%async_computation.2 | async-start | bytes 1572864 | tf_op jit(solution)/shard_map/all_to_all | solution.py:847
  179.0 6.0 %copy-start.5 = (bf16[8,64,768]{2,1,0:T(8,128)(2,1)}, bf16[8,64,768]{2,1,0:T(8,128)(2,1)S(1)}, u32[]{:S(2)}) copy-start(bf16[8,64,768]{2,1,0:T(8,128)(2,1)S(1)} %all-to-all-done.2) | copy-start | bytes 2359300
  179.0 30.2 %all-to-all-start.3 = ((bf16[8,64,768]{2,1,0:T(8,128)(2,1)}), bf16[8,64,768]{2,1,0:T(8,128)(2,1)S(1)}, u32[]{:S(2)}, u32[]{:S(2)}) async-start(bf16[8,64,768]{2,1,0:T(8,128)(2,1)} %bitcast.78), calls=%async_computation.3 | async-start | bytes 1572864 | tf_op jit(solution)/shard_map/all_to_all | solution.py:847
  209.2 21.6 %copy-start.3 = (bf16[8,64,768]{2,1,0:T(8,128)(2,1)}, bf16[8,64,768]{2,1,0:T(8,128)(2,1)S(1)}, u32[]{:S(2)}) copy-start(bf16[8,64,768]{2,1,0:T(8,128)(2,1)S(1)} %all-to-all-done.3) | copy-start | bytes 2359300
  209.2 24.7 %all-to-all-start.4 = ((bf16[8,64,768]{2,1,0:T(8,128)(2,1)}), bf16[8,64,768]{2,1,0:T(8,128)(2,1)S(1)}, u32[]{:S(2)}, u32[]{:S(2)}) async-start(bf16[8,64,768]{2,1,0:T(8,128)(2,1)} %bitcast.77), calls=%async_computation.4 | async-start | bytes 1572864 | tf_op jit(solution)/shard_map/all_to_all | solution.py:847
  215.2 160.2 %reduce-scatter.2.cloned.1.call-start = ((), (), s32[]{:S(2)}) async-start(), calls=%async_computation.7 | async-start | bytes 11919360 | tf_op jit(solution)/shard_map/reduce_scatter | solution.py:899
  233.9 0.9 copy-start.4
  233.9 0.9 copy-start.7
  235.9 82.1 %all-to-all-start.5 = ((bf16[8,128,768]{2,1,0:T(8,128)(2,1)}), bf16[8,128,768]{2,1,0:T(8,128)(2,1)S(1)}, u32[]{:S(2)}, u32[]{:S(2)}) async-start(bf16[8,128,768]{2,1,0:T(8,128)(2,1)} %bitcast.26), calls=%async_computation.5 | async-start | bytes 3145728 | tf_op jit(solution)/shard_map/all_to_all | solution.py:847
  283.3 34.7 %collective-permute-start.6 = (bf16[2,768,896]{2,1,0:T(8,128)(2,1)}, bf16[2,768,896]{2,1,0:T(8,128)(2,1)}, u32[]{:S(2)}, u32[]{:S(2)}) collective-permute-start(bf16[2,768,896]{2,1,0:T(8,128)(2,1)} %slope.1), channel_id=1, source_target_pairs={{0,8},{1,9},{2,10},{3,11},{4,12},{5,13},{6,14},{7,15},{8,0},{9,1},... | collective-permute-start | bytes 8257544 | tf_op jit(solution)/shard_map/ppermute | solution.py:780
  318.0 8.3 %copy-start.1 = (bf16[8,128,768]{2,1,0:T(8,128)(2,1)}, bf16[8,128,768]{2,1,0:T(8,128)(2,1)S(1)}, u32[]{:S(2)}) copy-start(bf16[8,128,768]{2,1,0:T(8,128)(2,1)S(1)} %all-to-all-done.5) | copy-start | bytes 4718596
  326.2 20.0 %copy-start = (bf16[16,96,896]{2,1,0:T(8,128)(2,1)S(1)}, bf16[16,96,896]{2,1,0:T(8,128)(2,1)}, u32[]{:S(2)}) copy-start(bf16[16,96,896]{2,1,0:T(8,128)(2,1)} %slope_add.1) | copy-start | bytes 8257540
  327.9 18.4 %collective-permute-start.7 = (bf16[8,96,896]{2,1,0:T(8,128)(2,1)S(1)}, bf16[8,96,896]{2,1,0:T(8,128)(2,1)S(1)}, u32[]{:S(2)}, u32[]{:S(2)}) collective-permute-start(bf16[8,96,896]{2,1,0:T(8,128)(2,1)S(1)} %slice.126), channel_id=1, source_target_pairs={{0,16},{1,17},{2,18},{3,19},{4,20},{5,21},{6,22},{7,23},{8,9},{9,8... | collective-permute-start | bytes 4128776 | tf_op jit(solution)/shard_map/ppermute | solution.py:786
  346.6 11.0 %collective-permute-start.8 = (bf16[4,96,896]{2,1,0:T(8,128)(2,1)S(1)}, bf16[4,96,896]{2,1,0:T(8,128)(2,1)S(1)}, u32[]{:S(2)}, u32[]{:S(2)}) collective-permute-start(bf16[4,96,896]{2,1,0:T(8,128)(2,1)S(1)} %get-tuple-element.216), channel_id=1, source_target_pairs={{0,1},{1,0},{2,3},{3,2},{4,5},{5,4},{6,7},{7,6},{8,24},{9,25},{10,... | collective-permute-start | bytes 2064392 | tf_op jit(solution)/shard_map/ppermute | solution.py:788
  357.7 15.3 %collective-permute-start.10 = (bf16[96,896]{1,0:T(8,128)(2,1)S(1)}, bf16[96,896]{1,0:T(8,128)(2,1)S(1)}, u32[]{:S(2)}, u32[]{:S(2)}) collective-permute-start(bf16[96,896]{1,0:T(8,128)(2,1)S(1)} %get-tuple-element.224), channel_id=1, source_target_pairs={{0,4},{1,5},{2,6},{3,7},{4,0},{5,1},{6,2},{7,3},{8,12},{9,13},{10,... | collective-permute-start | bytes 516104 | tf_op jit(solution)/shard_map/ppermute | solution.py:790
  360.7 12.3 %collective-permute-start.11 = (bf16[96,896]{1,0:T(8,128)(2,1)S(1)}, bf16[96,896]{1,0:T(8,128)(2,1)S(1)}, u32[]{:S(2)}, u32[]{:S(2)}) collective-permute-start(bf16[96,896]{1,0:T(8,128)(2,1)S(1)} %get-tuple-element.223), channel_id=1, source_target_pairs={{0,6},{1,7},{2,4},{3,5},{4,2},{5,3},{6,0},{7,1},{8,14},{9,15},{10,... | collective-permute-start | bytes 516104 | tf_op jit(solution)/shard_map/ppermute | solution.py:790
  362.1 10.9 %collective-permute-start.9 = (bf16[96,896]{1,0:T(8,128)(2,1)S(1)}, bf16[96,896]{1,0:T(8,128)(2,1)S(1)}, u32[]{:S(2)}, u32[]{:S(2)}) collective-permute-start(bf16[96,896]{1,0:T(8,128)(2,1)S(1)} %get-tuple-element.222), channel_id=1, source_target_pairs={{0,2},{1,3},{2,0},{3,1},{4,6},{5,7},{6,4},{7,5},{8,10},{9,11},{10,... | collective-permute-start | bytes 516104 | tf_op jit(solution)/shard_map/ppermute | solution.py:790
  373.2 1.2 collective-permute-start.12
Sparse Core Ops, SparseCore 0:
  234.0 77.9 reduce-scatter.1

commit v2 on v1

v2 whole, which is shorter than its diff:
```python
from functools import partial

import jax
import jax.numpy as jnp
from jax import lax
from jax.experimental import pallas as pl
from jax.experimental.pallas import tpu as pltpu
from jax.sharding import PartitionSpec as P

HEADS = 12
HEAD_DIM = 64
SEQ_LEN = 1024
GROUPS = 4

EPSILON = 1e-05
MASKED = -1e30
SLAB = 896
BOTH = ("dp", "expert")
BF = jnp.bfloat16
F32 = jnp.float32


def dot(left, right, left_dim, right_dim):
    return lax.dot_general(
        left, right, (((left_dim,), (right_dim,)), ((), ())), preferred_element_type=F32
    )


def normalize(values):
    center = jnp.mean(values, axis=-1, keepdims=True)
    centered = values - center
    inverse = lax.rsqrt(jnp.mean(centered * centered, axis=-1, keepdims=True) + EPSILON)
    return (centered * inverse, inverse)


def normalize_back(grad, normed, inverse, gain):
    scaled = grad * gain
    return inverse * (
        scaled
        - jnp.mean(scaled, axis=-1, keepdims=True)
        - normed * jnp.mean(scaled * normed, axis=-1, keepdims=True)
    )


def call(
    kernel, name, grid, in_specs, outs, scratch=(), vmem=60, cost=(0, 0, 0), ahead=0, **more
):
    return pl.pallas_call(
        kernel,
        name=name,
        grid_spec=pltpu.PrefetchScalarGridSpec(
            num_scalar_prefetch=ahead,
            grid=grid,
            in_specs=in_specs,
            out_specs=[o[0] for o in outs],
            scratch_shapes=list(scratch),
        ),
        out_shape=[jax.ShapeDtypeStruct(o[1], o[2]) for o in outs],
        compiler_params=pltpu.CompilerParams(vmem_limit_bytes=vmem << 20),
        cost_estimate=pl.CostEstimate(
            flops=cost[0], bytes_accessed=cost[1], transcendentals=cost[2]
        ),
        **more,
    )


def full(shape):
    return pl.BlockSpec(
        shape, lambda *_: (0,) * len(shape), pipeline_mode=pl.Buffered(1)
    )


SCALARS = pl.BlockSpec(memory_space=pltpu.SMEM)
PLACED = pl.BlockSpec(memory_space=pl.ANY)


def assemble_kernel(table, own_ref, got_ref, out_ref, sems):
    rows = own_ref.shape[1]
    copies = []
    for i in range(8):
        src = (own_ref, got_ref)[i // 4].at[i % 4]
        at = pl.multiple_of(rows * table[i], 32)
        copies.append(pltpu.make_async_copy(src, out_ref.at[pl.ds(at, rows)], sems.at[i]))
    for c in copies:
        c.start()
    for c in copies:
        c.wait()


def assemble(table, own, got):
    rows, cols = own.shape[1:]
    return call(
        assemble_kernel, "assemble", (1,), [SCALARS, PLACED, PLACED],
        [(full((8 * rows, cols)), (8 * rows, cols), BF)],
        [pltpu.SemaphoreType.DMA((8,))],
        cost=(0, 4 * rows * cols * 8, 0),
    )(table, own, got)[0]


def chunk(shape, axis=0):
    return pl.BlockSpec(shape, lambda i: tuple(i if a == axis else 0 for a in range(len(shape))))


def project_kernel(half, order, *refs):
    if half:
        low_ref, vec_ref, w_one, w_two, _, qkv_ref = refs
    else:
        x_ref, w_one, w_two, qkv_ref, low_ref, vec_ref = refs
    width = low_ref.shape[1]
    part = width // GROUPS
    if not half:

        @pl.when(pl.program_id(0) == 0)
        def _():
            vec_ref[...] = w_one[:, 512:640].astype(F32).T[64:72]

        unit, _ = normalize(x_ref[...].astype(F32))
        low_ref[...] = (unit * vec_ref[0:1] + vec_ref[1:2]).astype(BF)
    zero = jnp.zeros((1, part), F32)
    for g, w_ref in enumerate((w_one, w_two)):
        bias_q = bias_v = zero
        for n in range(GROUPS):
            here = order[2 * half + g] == n
            bias_q = jnp.where(here, vec_ref[2:3, part * n : part * n + part], bias_q)
            bias_v = jnp.where(here, vec_ref[3:4, part * n : part * n + part], bias_v)
        bias = jnp.concatenate([bias_q, zero, bias_v], axis=1)
        qkv_ref[g] = (dot(low_ref[...], w_ref[:, : 3 * part], 1, 0) + bias).astype(BF)


def project(half, order, weights, x=None, low=None, vec=None, qkv=None):
    count, width = (low if half else x).shape
    part = width // GROUPS
    rows = min(256, count)
    whole = (GROUPS, count, 3 * part)
    outs = [(pl.BlockSpec((2, rows, 3 * part), lambda i: (half, i, 0)), whole, BF)]
    w = [pl.BlockSpec((width, 640), lambda i: (0, 0), pipeline_mode=pl.Buffered(1))] * 2
    if half:
        ins, args = [chunk((rows, width)), full((8, width))] + w + [PLACED], (low, vec, *weights, qkv)
    else:
        outs += [
            (chunk((rows, width)), (count, width), BF),
            (full((8, width)), (8, width), F32),
        ]
        ins, args = [chunk((rows, width))] + w, (x, *weights)
    return call(
        partial(project_kernel, half), "project", (count // rows,), [SCALARS] + ins, outs,
        cost=(2 * count * width * 6 * part, 8_000_000, 0),
        input_output_aliases={5: 0} if half else {},
    )(order, *args)


def attend_kernel(qkv_ref, *refs):
    ctx_ref, lse_ref = refs[-2:]
    length = qkv_ref.shape[1]
    width = qkv_ref.shape[2] // 3
    block = min(256, length)
    lane = lax.broadcasted_iota(jnp.int32, (block, 128), 1)
    row = lax.broadcasted_iota(jnp.int32, (block, block), 0)
    col = lax.broadcasted_iota(jnp.int32, (block, block), 1)
    for i in range(length // block):
        start = i * block
        stats = jnp.zeros((block, 128), F32)
        for h in range(width // HEAD_DIM):
            at = h * HEAD_DIM
            q = qkv_ref[0, start : start + block, at : at + HEAD_DIM] * BF(HEAD_DIM**-0.5)
            k = qkv_ref[0, : start + block, width + at : width + at + HEAD_DIM]
            v = qkv_ref[0, : start + block, 2 * width + at : 2 * width + at + HEAD_DIM]
            diag = jnp.where(col <= row, dot(q, k[start:], 1, 1), MASKED)
            top = jnp.max(diag, axis=-1, keepdims=True)
            if start:
                past = dot(q, k[:start], 1, 1)
                top = jnp.maximum(top, jnp.max(past, axis=-1, keepdims=True))
            diag = jnp.exp(diag - top)
            total = jnp.sum(diag, axis=-1, keepdims=True)
            out = dot(diag.astype(BF), v[start:], 1, 0)
            if start:
                past = jnp.exp(past - top)
                total += jnp.sum(past, axis=-1, keepdims=True)
                out += dot(past.astype(BF), v[:start], 1, 0)
            ctx_ref[0, start : start + block, at : at + HEAD_DIM] = (out / total).astype(BF)
            stats = jnp.where(lane == h, top + jnp.log(total), stats)
        lse_ref[0, start : start + block, :] = stats


def attend(half, qkv, before=()):
    groups, length, width = qkv.shape
    width //= 3
    at = lambda g, s: (2 * half + g, s, 0)
    return call(
        attend_kernel, "attend", (2, length // SEQ_LEN),
        [pl.BlockSpec((1, SEQ_LEN, 3 * width), at)] + [PLACED] * len(before),
        [
            (pl.BlockSpec((1, SEQ_LEN, width), at), (groups, length, width), BF),
            (pl.BlockSpec((1, SEQ_LEN, 128), at), (groups, length, 128), F32),
        ],
        cost=(8_000_000_000, 5_000_000, 4_000_000),
        input_output_aliases={1 + i: i for i in range(len(before))},
    )(qkv, *before)


def attend_back_kernel(qkv_ref, ctx_ref, dctx_ref, lse_ref, *refs):
    out_ref, sum_ref, dq_ref = refs[-3:]
    length = qkv_ref.shape[1]
    width = qkv_ref.shape[2] // 3
    heads = width // HEAD_DIM
    block = min(256, length)
    lane = lax.broadcasted_iota(jnp.int32, (length, 128), 1)
    stats = lse_ref[0]
    for h in range(heads):
        at = h * HEAD_DIM
        o = ctx_ref[0, :, at : at + HEAD_DIM].astype(F32)
        do = dctx_ref[0, :, at : at + HEAD_DIM].astype(F32)
        stats = jnp.where(lane == 8 + h, jnp.sum(o * do, axis=-1, keepdims=True), stats)
    stats = stats.T
    row = lax.broadcasted_iota(jnp.int32, (block, block), 0)
    col = lax.broadcasted_iota(jnp.int32, (block, block), 1)
    for h in range(heads):
        at = h * HEAD_DIM
        q = qkv_ref[0, :, at : at + HEAD_DIM] * BF(HEAD_DIM**-0.5)
        do = dctx_ref[0, :, at : at + HEAD_DIM]
        for j in range(length // block):
            start = j * block
            k = qkv_ref[0, start : start + block, width + at : width + at + HEAD_DIM]
            v = qkv_ref[0, start : start + block, 2 * width + at : 2 * width + at + HEAD_DIM]
            dk = None
            for s, e, on_diag in ((start, start + block, True), (start + block, length, False)):
                if s == e:
                    continue
                lse = stats[h : h + 1, s:e]
                inner = stats[8 + h : 9 + h, s:e]
                probs = jnp.exp(dot(k, q[s:e], 1, 1) - lse)
                if on_diag:
                    probs = jnp.where(row <= col, probs, 0.0)
                dscores = (probs * (dot(v, do[s:e], 1, 1) - inner)).astype(BF)
                dk_part = dot(dscores, q[s:e], 1, 0)
                dv_part = dot(probs.astype(BF), do[s:e], 1, 0)
                dq_part = dot(dscores, k, 0, 0)
                dk = dk_part if dk is None else dk + dk_part
                dv = dv_part if on_diag else dv + dv_part
                if j == 0:
                    dq_ref[s:e, :] = dq_part
                else:
                    dq_ref[s:e, :] += dq_part
            out_ref[0, start : start + block, width + at : width + at + HEAD_DIM] = dk.astype(BF)
            out_ref[0, start : start + block, 2 * width + at : 2 * width + at + HEAD_DIM] = (
                dv.astype(BF)
            )
        out_ref[0, :, at : at + HEAD_DIM] = (dq_ref[...] * HEAD_DIM**-0.5).astype(BF)
    sums = jnp.sum(out_ref[0].astype(F32), axis=0, keepdims=True)
    first = pl.program_id(0) == 0

    @pl.when(first)
    def _():
        sum_ref[0] = jnp.broadcast_to(sums, sum_ref.shape[1:])

    @pl.when(jnp.logical_not(first))
    def _():
        sum_ref[0] += jnp.broadcast_to(sums, sum_ref.shape[1:])


def attend_back(group, qkv, ctx, dctx, lse):
    groups, length, width = qkv.shape
    width //= 3
    at = lambda s: (group, s, 0)
    return call(
        attend_back_kernel, "attend_back", (length // SEQ_LEN,),
        [
            pl.BlockSpec((1, SEQ_LEN, 3 * width), at),
            pl.BlockSpec((1, SEQ_LEN, width), at),
            pl.BlockSpec((1, SEQ_LEN, width), at),
            pl.BlockSpec((1, SEQ_LEN, 128), at),
        ],
        [
            (pl.BlockSpec((1, SEQ_LEN, 3 * width), lambda s: (0, s, 0)), (1, length, 3 * width), BF),
            (full((1, 8, 3 * width)), (1, 8, 3 * width), F32),
        ],
        [pltpu.VMEM((SEQ_LEN, HEAD_DIM), F32)],
        cost=(10_000_000_000, 4_000_000, 2_000_000),
    )(qkv, ctx, dctx, lse)


def slot_of(index, half, cap):
    return index // (cap // 2) * cap + index % (cap // 2) + half * (cap // 2)


def dispatch_kernel(target_ref, rows_ref, out_ref):
    count = rows_ref.shape[0]
    for at in range(0, count, 256):
        slot = lax.broadcasted_iota(jnp.int32, (256, count), 0) + at
        picks = (target_ref[...] == slot).astype(F32).astype(BF)
        out_ref[at : at + 256] = dot(picks, rows_ref[...], 1, 0).astype(BF)


def dispatch(target, rows):
    count, width = rows.shape
    return call(
        dispatch_kernel, "dispatch", (1,),
        [full((1, count)), full((count, width))],
        [(full((count, width)), (count, width), BF)],
        cost=(2 * count * count * width, 3_000_000, 0),
    )(target.reshape(1, count), rows)[0]


def mix_kernel(cap, order, x_ref, ctx_ref, vec_ref, target_ref, *refs):
    wo_refs, (h_ref, whole_ref, *sent, low_ref) = refs[:GROUPS], refs[GROUPS:]
    rows, width = x_ref.shape
    count = low_ref.shape[0]
    part = width // GROUPS
    step = pl.program_id(0)

    @pl.when(step == 0)
    def _():
        for q in range(GROUPS):
            at = pl.ds(pl.multiple_of(order[q] * part, 64), part)
            pieces = [wo[at, :part] for wo in wo_refs]
            for n in range(GROUPS):
                piece = pieces[0]
                for r in range(1, GROUPS):
                    piece = jnp.where(order[r] == n, pieces[r], piece)
                whole_ref[q * part : q * part + part, n * part : n * part + part] = piece

    h = x_ref[...].astype(F32) + vec_ref[4:5]
    for r in range(GROUPS):
        h += dot(ctx_ref[r], whole_ref[r * part : r * part + part], 1, 0)
    h_ref[...] = h
    unit, _ = normalize(h)
    low_ref[pl.ds(pl.multiple_of(step * rows, 256), rows)] = (
        unit * vec_ref[5:6] + vec_ref[6:7]
    ).astype(BF)

    @pl.when(step == pl.num_programs(0) - 1)
    def _():
        for half in range(2):
            for at in range(0, count // 2, 256):
                index = lax.broadcasted_iota(jnp.int32, (256, count), 0) + at
                picks = (target_ref[...] == slot_of(index, half, cap)).astype(F32).astype(BF)
                sent[half][at : at + 256] = dot(picks, low_ref[...], 1, 0).astype(BF)


def mix(order, x, ctx, weights, vec, target, cap):
    count, width = x.shape
    part = width // GROUPS
    rows = min(256, count)
    columns = pl.BlockSpec(
        (pl.Element(width), pl.Element(256)), lambda *_: (0, 640), pipeline_mode=pl.Buffered(1)
    )
    return call(
        partial(mix_kernel, cap), "mix", (count // rows,),
        [SCALARS, chunk((rows, width)), chunk((GROUPS, rows, part), 1), full((8, width)),
         full((1, count))] + [columns] * GROUPS,
        [
            (chunk((rows, width)), (count, width), F32),
            (full((width, width)), (width, width), BF),
            (full((count // 2, width)), (count // 2, width), BF),
            (full((count // 2, width)), (count // 2, width), BF),
        ],
        [pltpu.VMEM((count, width), BF)],
        cost=(2 * count * width * (width + count), 12_000_000, 0),
    )(order, x, ctx, vec, target.reshape(1, count), *weights)


def unmix_kernel(
    cap, order, h_ref, g_ref, dm_one, dm_two, target_ref, ctx_ref, whole_ref, vec_ref,
    dh_ref, dctx_ref, grad_ref, sum_ref, total_ref,
):
    rows, width = h_ref.shape
    part = width // GROUPS
    step = pl.program_id(0)
    dm = None
    for half, sent in enumerate((dm_one, dm_two)):
        index = lax.broadcasted_iota(jnp.int32, (rows, sent.shape[0]), 1)
        picks = (target_ref[...] == slot_of(index, half, cap)).astype(F32).astype(BF)
        got = dot(picks, sent[...], 1, 0)
        dm = got if dm is None else dm + got
    unit, inverse = normalize(h_ref[...])
    dh = g_ref[...].astype(F32) + normalize_back(dm, unit, inverse, vec_ref[5:6])
    dh_ref[...] = dh
    low = dh.astype(BF)
    sums = [
        jnp.sum(term, axis=0, keepdims=True) for term in (low.astype(F32), dm * unit, dm)
    ]
    zeros = jnp.zeros((1, width), F32)
    sums = jnp.concatenate([zeros] * 4 + sums + [zeros])
    for r in range(GROUPS):
        dctx_ref[r] = dot(low, whole_ref[r * part : r * part + part], 1, 1).astype(BF)
    grads = [dot(ctx_ref[q], low, 0, 0) for q in range(GROUPS)]

    @pl.when(step == 0)
    def _():
        sum_ref[...] = sums
        for q in range(GROUPS):
            total_ref[q] = grads[q]

    @pl.when(step > 0)
    def _():
        sum_ref[...] += sums
        for q in range(GROUPS):
            total_ref[q] += grads[q]

    @pl.when(step == pl.num_programs(0) - 1)
    def _():
        for q in range(GROUPS):
            grad = total_ref[q].astype(BF)
            at = pl.ds(pl.multiple_of(order[q] * part, 64), part)
            for r in range(GROUPS):
                piece = grad[:, :part]
                for n in range(1, GROUPS):
                    piece = jnp.where(order[r] == n, grad[:, n * part : n * part + part], piece)
                grad_ref[r, at, :] = piece


def unmix(order, h, g, dm_one, dm_two, target, ctx, whole, vec, cap):
    count, width = h.shape
    part = width // GROUPS
    rows = min(256, count)
    half = full((count // 2, width))
    by_rows, by_ctx = chunk((rows, width)), chunk((GROUPS, rows, part), 1)
    return call(
        partial(unmix_kernel, cap), "unmix", (count // rows,),
        [SCALARS, by_rows, by_rows, half, half, chunk((rows, 1)), by_ctx, full((width, width)),
         full((8, width))],
        [
            (by_rows, (count, width), F32),
            (by_ctx, (GROUPS, count, part), BF),
            (full((GROUPS, width, part)), (GROUPS, width, part), BF),
            (full((8, width)), (8, width), F32),
        ],
        [pltpu.VMEM((GROUPS, part, width), F32)],
        cost=(2 * count * width * (2 * width + count), 20_000_000, 0),
    )(order, h, g, dm_one, dm_two, target.reshape(count, 1), ctx, whole, vec)


def finish_kernel(h_ref, target_ref, gy_ref, out_ref):
    slot = lax.broadcasted_iota(jnp.int32, (h_ref.shape[0], gy_ref.shape[0]), 1)
    picks = (target_ref[...] == slot).astype(F32).astype(BF)
    out_ref[...] = (h_ref[...] + dot(picks, gy_ref[...], 1, 0)).astype(BF)


def finish(h, target, gy):
    count, width = h.shape
    rows = min(256, count)
    return call(
        finish_kernel, "finish", (count // rows,),
        [chunk((rows, width)), chunk((rows, 1)), full((count, width))],
        [(chunk((rows, width)), (count, width), BF)],
        cost=(2 * count * count * width, 6_000_000, 0),
    )(h, target.reshape(count, 1), gy)[0]


ERFC = (
    0.169189354,
    0.1706909295,
    0.1485212475,
    0.2141814502,
    -0.09282610738,
    0.5449670381,
    -0.5097724612,
    0.4843017683,
    -0.1292532277,
)


def gelu_pair(v):
    a = jnp.abs(v) * (0.5**0.5)
    bell = jnp.exp(-0.5 * v * v)
    t = 1.0 / (1.0 + 0.3 * a)
    poly = jnp.full_like(v, ERFC[-1])
    for c in ERFC[-2::-1]:
        poly = poly * t + c
    tail = 0.5 * bell * t * poly
    cdf = jnp.where(v < 0, tail, 1.0 - tail)
    return v * cdf, cdf + v * bell * (0.5 / jnp.pi) ** 0.5


def expert_kernel(
    x_ref, g_ref, win_ref, bin_ref, wout_ref, bout_ref, center_ref, _,
    gy_ref, dm_ref, dy_ref, hid_ref, du_ref, dbin_ref, small_ref,
    y_acc, dm_acc, gate_ref, gates,
):
    step = pl.program_id(0)
    rows, width = x_ref.shape

    @pl.when(step == 0)
    def _():
        z = jnp.sum(x_ref[...].astype(F32) * center_ref[...].astype(F32), axis=-1, keepdims=True)
        gate = 1.0 / (1.0 + jnp.exp(-z))
        gate_ref[...] = jnp.broadcast_to(gate, gate_ref.shape)
        dy_ref[...] = (gate * g_ref[...].reshape(rows, width).astype(F32)).astype(BF)

    act, slope = gelu_pair(dot(x_ref[...], win_ref[...], 1, 0) + bin_ref[...].astype(F32))
    hid = act.astype(BF)
    hid_ref[...] = hid
    y = dot(hid, wout_ref[...], 1, 0)
    du = (dot(dy_ref[...], wout_ref[...], 1, 1) * slope).astype(BF)
    du_ref[...] = du
    dbin_ref[...] = jnp.broadcast_to(
        jnp.sum(du.astype(F32), axis=0, keepdims=True), dbin_ref.shape
    )
    dm = dot(du, win_ref[...], 1, 1)

    @pl.when(step == 0)
    def _():
        y_acc[...] = y
        dm_acc[...] = dm

    @pl.when(step > 0)
    def _():
        y_acc[...] += y
        dm_acc[...] += dm

    @pl.when(step == pl.num_programs(0) - 1)
    def _():
        gate = gate_ref[:, :1]
        g = g_ref[...].reshape(rows, width).astype(F32)
        y = (y_acc[...] + bout_ref[...].astype(F32)).astype(BF).astype(F32)
        gy_ref[...] = (gate * y).astype(BF).reshape(gy_ref.shape)
        dz = gate * (1.0 - gate) * jnp.sum(g * y, axis=-1, keepdims=True)
        dm_ref[...] = (dm_acc[...] + dz * center_ref[...].astype(F32)).astype(BF)
        small_ref[0:1, :] = jnp.sum(dy_ref[...].astype(F32), axis=0, keepdims=True)
        small_ref[1:2, :] = jnp.sum(dz * x_ref[...].astype(F32), axis=0, keepdims=True)


def expert(half, x, g, win, bias_in, wout, bias_out, center, gy):
    rows, width = x.shape
    ff = win.shape[1]
    step = min(512, ff)
    along = lambda i: (0, i)
    side = pl.BlockSpec(
        (g.shape[0], 1) + g.shape[2:], lambda i: (0, half, 0, 0), pipeline_mode=pl.Buffered(1)
    )
    return call(
        expert_kernel, "expert", (ff // step,),
        [
            full((rows, width)),
            side,
            pl.BlockSpec((width, step), along),
            pl.BlockSpec((1, step), along),
            pl.BlockSpec((step, width), lambda i: (i, 0)),
            full((1, width)),
            full((1, width)),
            PLACED,
        ],
        [
            (side, g.shape, BF),
            (full((rows, width)), (rows, width), BF),
            (full((rows, width)), (rows, width), BF),
            (pl.BlockSpec((rows, step), along), (rows, ff), BF),
            (pl.BlockSpec((rows, step), along), (rows, ff), BF),
            (pl.BlockSpec((8, step), along), (8, ff), F32),
            (full((8, width)), (8, width), F32),
        ],
        [
            pltpu.VMEM((rows, width), F32),
            pltpu.VMEM((rows, width), F32),
            pltpu.VMEM((rows, 128), F32),
            pltpu.SMEM((1,), jnp.int32),
        ],
        cost=(8 * rows * width * ff, 22_000_000, 2 * rows * ff),
        input_output_aliases={} if gy is None else {7: 0},
    )(x, g, win, bias_in, wout, bias_out, center, x if gy is None else gy)


def weigh_kernel(split, which, *refs):
    hid, du, dy, x, bias, small = (refs[i : i + 2] for i in range(0, 12, 2))
    ff = hid[0].shape[1]
    width = dy[0].shape[1]
    step = pl.program_id(0)
    small = small[0][...] + small[1][...]
    row = lax.broadcasted_iota(jnp.int32, (16, width), 0)
    bias = (bias[0][...] + bias[1][...])[0:1]
    if ff < width:
        bias = jnp.concatenate([bias, jnp.zeros((1, width - ff), F32)], axis=1)
    rest = jnp.where(row == 0, bias, 0.0)
    rest = jnp.where(row == 1, small[0:1], rest)
    rest = jnp.where(row == 2, small[1:2], rest)

    def pair(i):
        rows, cols = (x, du) if split else (du, x)
        return rows[i][...], cols[i][...]

    def put(out):
        out[:ff] = (dot(hid[0][...], dy[0][...], 0, 0) + dot(hid[1][...], dy[1][...], 0, 0)).astype(BF)
        out[ff : 2 * ff] = (
            dot(*pair(0), 0, 0) + dot(*pair(1), 0, 0)
        ).astype(BF)
        out[2 * ff :] = rest.astype(BF)

    if not split:
        put(refs[12].at[0])
        return
    far_ref, across_ref, own_ref, total = refs[12:]
    put(total)
    for at, out in ((0, far_ref.at[0]), (1, far_ref.at[0]), (2, across_ref), (3, own_ref)):

        @pl.when(step == at)
        def _(out=out):
            out[...] = total[...]


def weigh(which, n, split, hid, du, dy, x, bias, small):
    rows, ff = hid[0].shape
    width = dy[0].shape[1]
    part = ff // n
    size = 2 * part + 16
    along = lambda i, which: (0, which[i])
    wide = pl.BlockSpec((rows, part), along)
    if split:
        first = pl.BlockSpec((1, size, width), lambda i, which: (jnp.minimum(i, 1), 0, 0))
        outs = [(first, (2, size, width), BF)] + [(full((size, width)), (size, width), BF)] * 2
        scratch = [pltpu.VMEM((size, width), BF)]
    else:
        outs = [(pl.BlockSpec((1, size, width), lambda i, which: (i, 0, 0)), (n, size, width), BF)]
        scratch = []
    got = call(
        partial(weigh_kernel, split), "weigh", (n,),
        [wide] * 4 + [full((rows, width))] * 4 + [pl.BlockSpec((8, part), along)] * 2
        + [full((8, width))] * 2,
        outs, scratch,
        cost=(8 * rows * width * ff, 26_000_000, 0), ahead=1,
    )(which, *hid, *du, *dy, *x, *bias, *small)
    return got if split else got[0]


def unproject_kernel(*refs):
    grad_refs, w_refs = refs[:GROUPS], refs[GROUPS : 2 * GROUPS]
    x_ref, dh_ref, vec_ref, out_ref = refs[2 * GROUPS :]
    part = x_ref.shape[1] // GROUPS
    da = None
    for grad, w in zip(grad_refs, w_refs):
        got = dot(grad[0], w[:, : 3 * part], 1, 1)
        da = got if da is None else da + got
    unit, inverse = normalize(x_ref[...].astype(F32))
    out_ref[...] = dh_ref[...] + normalize_back(da, unit, inverse, vec_ref[0:1])


def unproject(grads, weights, x, dh, vec):
    count, width = x.shape
    part = width // GROUPS
    rows = min(256, count)
    w = pl.BlockSpec((width, 640), lambda i: (0, 0), pipeline_mode=pl.Buffered(1))
    return call(
        unproject_kernel, "unproject", (count // rows,),
        [chunk((1, rows, 3 * part), 1)] * GROUPS + [w] * GROUPS
        + [chunk((rows, width)), chunk((rows, width)), full((8, width))],
        [(chunk((rows, width)), (count, width), F32)],
        cost=(6 * count * width * width, 20_000_000, 0),
    )(*grads, *weights, x, dh, vec)[0]


def slope_kernel(group, extra, staged, halves, order, *refs):
    if staged:
        table, *refs = refs
    low_ref, grad_ref, sum_ref, o_ref, w_ref, two_ref = refs[:6]
    more, refs = refs[6 : 6 + extra], refs[6 + extra :]
    if staged:
        keep_ref, send_ref, stage, sems = refs
    elif halves:
        outs = refs
    else:
        outs = refs[:1]
    width = low_ref.shape[1]
    part = width // GROUPS
    grad = dot(low_ref[...], grad_ref[0], 0, 0)
    w = w_ref[...].astype(F32)
    sums = sum_ref[0, 0:1]
    shift = jnp.sum(w[:, : 3 * part] * sums, axis=-1, keepdims=True)
    gain = jnp.sum(w[:, : 3 * part] * grad, axis=-1, keepdims=True)
    gain = (gain - w[:, 577:578] * shift) / w[:, 576:577]
    row = lax.broadcasted_iota(jnp.int32, (width, part), 0) - order[group] * part
    here = row == lax.broadcasted_iota(jnp.int32, (width, part), 1)
    columns = [gain, shift] + [
        jnp.sum(jnp.where(here, sums[:, at : at + part], 0.0), axis=-1, keepdims=True)
        for at in (0, 2 * part)
    ]
    lane = lax.broadcasted_iota(jnp.int32, (width, 64), 1)
    if group:
        vecs = jnp.zeros((width, 64), F32)
    else:
        vecs = jnp.concatenate([two_ref[...], jnp.zeros((120, width), F32)]).T[:, :64]
    for i, column in enumerate(columns):
        vecs = jnp.where(lane == i, column, vecs)
    o = o_ref[0].astype(F32)
    if extra:
        more = [more[:1]] + [more[1:]] * (extra > 1)
    for refs in more:
        got = jnp.concatenate([ref[...] for ref in refs]) if len(refs) > 1 else refs[0][...]
        grad += got[:, : 3 * part].astype(F32)
        vecs += got[:, 3 * part : 640].astype(F32)
        o += got[:, 640 : 640 + part].astype(F32)
    if staged:
        outs = (stage,)
    rows = width // len(outs)
    for i, out in enumerate(outs):
        at = slice(i * rows, i * rows + rows)
        out[:, : 3 * part] = grad[at].astype(BF)
        out[:, 3 * part : 640] = vecs[at].astype(BF)
        out[:, 640 : 640 + part] = o[at].astype(BF)
        out[:, 640 + part :] = jnp.zeros((rows, SLAB - 640 - part), BF)
    if staged:
        rows = width // 8
        copies = []
        for i in range(8):
            src = stage.at[pl.ds(pl.multiple_of(rows * table[i], 32), rows)]
            copies.append(
                pltpu.make_async_copy(src, (keep_ref, send_ref)[i // 4].at[i % 4], sems.at[i])
            )
        for c in copies:
            c.start()
        for c in copies:
            c.wait()


def slope(group, order, low, grads, o_part, w, two, more=(), table=None, halves=False):
    count, width = low.shape
    part = width // GROUPS
    cols = 3 * part
    ins = [
        full((count, width)),
        full((1, count, cols)),
        full((1, 8, cols)),
        pl.BlockSpec((1, width, part), lambda i: (group, 0, 0)),
        pl.BlockSpec((width, 640), lambda i: (0, 0), pipeline_mode=pl.Buffered(1)),
        full((8, width)),
    ] + [full(m.shape) for m in more]
    args = (low, *grads, o_part, w, two, *more)
    if table is None:
        rows = width // (1 + halves)
        outs, scratch = [(full((rows, SLAB)), (rows, SLAB), BF)] * (1 + halves), []
    else:
        ins, args = [SCALARS] + ins, (table, *args)
        outs = [(PLACED, (4, width // 8, SLAB), BF)] * 2
        scratch = [pltpu.VMEM((width, SLAB), BF), pltpu.SemaphoreType.DMA((8,))]
    got = call(
        partial(slope_kernel, group, len(more), table is not None, halves), "slope", (1,),
        [SCALARS] + ins, outs, scratch,
        cost=(2 * count * width * cols, 6_000_000, 0),
    )(order, *args)
    return got if table is not None or halves else got[0]


def add(a, b):
    return (a.astype(F32) + b.astype(F32)).astype(BF)


class Place:
    def __init__(self, mesh):
        self.n_dp = mesh.shape["dp"]
        self.n_e = mesh.shape["expert"]
        self.staged = self.n_dp == 4 and self.n_e == 8
        if not self.staged:
            return
        dev = lambda x, c, z, y: (x * 2 + c) * 8 + z * 2 + y
        every = [
            (x, c, z, y) for x in range(2) for c in range(2) for z in range(4) for y in range(2)
        ]
        to = lambda move: [(dev(*p), dev(*move(*p))) for p in every]
        self.core = to(lambda x, c, z, y: (x, 1 - c, z, y))
        self.x = to(lambda x, c, z, y: (1 - x, c, z, y))
        self.y = to(lambda x, c, z, y: (x, c, z, 1 - y))
        self.z = [to(lambda x, c, z, y, k=k: (x, c, z ^ k, y)) for k in range(1, 4)]

    def tables(self):
        r = jnp.arange(4, dtype=jnp.int32)
        i = jnp.arange(8, dtype=jnp.int32)
        if not self.staged:
            return r, i, r
        d, e = lax.axis_index("dp"), lax.axis_index("expert")
        z, y = e // 2, e % 2
        weighed = d ^ jnp.where(r < 2, 3 - 2 * r, 6 - 2 * r)
        return d ^ r, (z ^ i % 4) * 2 + (y ^ i // 4), weighed

    def move(self, array, way):
        return lax.ppermute(array, BOTH, way)


def whole_of(have):
    n_dp, n_e = lax.axis_size("dp"), lax.axis_size("expert")
    rows, cols = have.shape[1:]
    have = have.reshape(n_dp, n_e, rows, cols).transpose(1, 2, 0, 3)
    return have.reshape(n_e * rows, n_dp * cols)


def gather_all(array):
    return whole_of(lax.all_gather(array, BOTH, axis=0, tiled=False))


def scatter_all(array):
    n_dp, n_e = lax.axis_size("dp"), lax.axis_size("expert")
    rows, cols = array.shape[0] // n_e, array.shape[1] // n_dp
    parts = array.reshape(n_e, rows, n_dp, cols).transpose(2, 0, 1, 3)
    parts = parts.reshape(n_dp * n_e, rows, cols)
    return lax.psum_scatter(parts, BOTH, scatter_dimension=0, tiled=False)


def fetch(place, table, weights, vectors, filler):
    stacked = jnp.stack(vectors)
    pad = 64 - len(vectors)
    if place.staged:
        rows, cols = weights[0].shape
        extra = jnp.concatenate([stacked.T, jnp.zeros((rows, pad), BF)], axis=1)
        rest = jnp.zeros((rows, SLAB - 64 - 4 * cols), BF)
        shard = jnp.concatenate([*weights[:3], extra, weights[3], rest], axis=1)
        own = jnp.stack([shard] + [place.move(shard, way) for way in place.z])
        got = place.move(own, place.y)
        got, filler = lax.optimization_barrier((got, filler))
        near = assemble(table, own, got)
        across = place.move(near, place.x)
        far = place.move(near, place.core)
        return near, far, across, filler
    vecs = lax.all_gather(stacked, "expert", axis=1, tiled=True)
    width = vecs.shape[1]
    extra = jnp.concatenate([vecs, jnp.zeros((pad, width), BF)]).T
    extra = jnp.broadcast_to(extra[None], (GROUPS, width, 64))
    by_group = lambda w: gather_all(w).reshape(width, GROUPS, -1).transpose(1, 0, 2)
    weights = [by_group(w) for w in weights]
    rest = jnp.zeros((GROUPS, width, SLAB - 64 - 4 * (width // GROUPS)), BF)
    grouped = jnp.concatenate([*weights[:3], extra, weights[3], rest], axis=2)
    return grouped[0], grouped[1], grouped[2:], filler


def reduce_last(place, keep, send, count, first, second, later):
    barrier = lax.optimization_barrier
    cols = (SLAB - 128) // 4
    got, first, later = barrier((place.move(send, place.y), first(), later))
    sends = [add(keep[k], got[k]) for k in range(1, 4)]
    total = keep[0].astype(F32) + got[0].astype(F32)
    got = [place.move(part, way) for part, way in zip(sends, place.z)]
    got, second = barrier((got, second(*later)))
    for part in got:
        total += part.astype(F32)
    parts = [total[:, i : i + cols] for i in (0, cols, 2 * cols, 640)]
    vecs = total[:, 576 : 576 + 8].T
    vecs = vecs + place.move(vecs, place.core)
    vecs = vecs + place.move(vecs, place.x)
    return parts, [vecs[i] for i in range(count)], first, second


def reduce_plain(slabs, count):
    slabs = jnp.stack(slabs)
    width = slabs.shape[1]
    part = width // GROUPS
    parts = []
    for at in (0, part, 2 * part, 640):
        grad = slabs[:, :, at : at + part].transpose(1, 0, 2).reshape(width, width)
        parts.append(scatter_all(grad).astype(F32))
    vecs = jnp.sum(slabs[:, :, 576 : 576 + count].astype(F32), axis=0).T
    vecs = lax.psum_scatter(vecs, "expert", scatter_dimension=1, tiled=True)
    vecs = lax.psum(vecs, "dp")
    return parts, [vecs[i] for i in range(count)]


def shards(
    place,
    block_entries,
    assignments,
    positions_within,
    specialist_quotas,
    standardize_one_scale,
    standardize_one_shift,
    asking_weights,
    asking_shift,
    lookup_weights,
    content_weights,
    content_shift,
    context_mixing_weights,
    context_mixing_shift,
    standardize_two_scale,
    standardize_two_shift,
    gating_prototypes,
    specialist_widen_weights,
    specialist_widen_shift,
    specialist_contract_weights,
    specialist_contract_shift,
    upstream_adjoint,
):
    count, width = block_entries.shape
    experts = specialist_quotas.shape[0]
    cap = count // experts
    n_dp = place.n_dp
    order, table, weighed = place.tables()
    barrier = lax.optimization_barrier

    chosen = assignments[:, None] == lax.broadcasted_iota(jnp.int32, (count, experts), 1)
    limit = jnp.sum(jnp.where(chosen, specialist_quotas[None, :], 0), axis=1)
    target = jnp.where(positions_within < limit, assignments * cap + positions_within, count)

    def exchange(rows):
        sent = rows.reshape(experts, -1, width)
        got = lax.all_to_all(sent, "expert", split_axis=0, concat_axis=0, tiled=True)
        return got.reshape(rows.shape)

    near, far, across, sent_g = fetch(
        place,
        table,
        (asking_weights, lookup_weights, content_weights, context_mixing_weights),
        (
            standardize_one_scale,
            standardize_one_shift,
            asking_shift,
            content_shift,
            context_mixing_shift,
            standardize_two_scale,
            standardize_two_shift,
        ),
        dispatch(target, upstream_adjoint),
    )
    sent_g, far = barrier((sent_g, far))
    rows_g = exchange(sent_g).reshape(experts, 2, cap // 2, width)

    qkv, low_in, vec = project(0, order, (near, far), x=block_entries)
    ctx = attend(0, qkv)
    if place.staged:
        ctx, across = barrier((ctx, across))
        weights = (near, far, across, place.move(across, place.core))
    else:
        weights = (near, far, across[0], across[1])
    (qkv,) = project(1, order, weights[2:], low=low_in, vec=vec, qkv=qkv)
    ctx, lse = attend(1, qkv, ctx)
    ctx, rows_g = barrier((ctx, rows_g))
    h1, whole_o, sent_one, sent_two = mix(order, block_entries, ctx, weights, vec, target, cap)

    x_one = exchange(sent_one)
    x_one, sent_two = barrier((x_one, sent_two))
    x_two = exchange(sent_two)
    matrices = (
        specialist_widen_weights[0], specialist_widen_shift, specialist_contract_weights[0],
        specialist_contract_shift, gating_prototypes,
    )
    gy, dm_one, dy_one, hid_one, du_one, dbin_one, small_one = expert(
        0, x_one, rows_g, *matrices, None
    )
    x_two, dm_one = barrier((x_two, dm_one))
    dm_one = exchange(dm_one)
    gy, dm_two, dy_two, hid_two, du_two, dbin_two, small_two = expert(
        1, x_two, rows_g, *matrices, gy
    )
    dm_one, dm_two, hid_two = barrier((dm_one, dm_two, hid_two))
    dm_two = exchange(dm_two)
    sides = (
        (hid_one, hid_two), (du_one, du_two), (dy_one, dy_two), (x_one, x_two),
        (dbin_one, dbin_two), (small_one, small_two),
    )
    if place.staged:
        grads_far, grads_across, grads = weigh(
            weighed, n_dp, True, *sides
        )
        grads_far, gy, dm_two = barrier((grads_far, gy, dm_two))
        came_far = place.move(grads_far, place.core)
        crossing = add(grads_across, came_far[0])
        crossing, h1 = barrier((crossing, h1))
        came = place.move(crossing, place.x)
    else:
        grads = weigh(jnp.arange(n_dp, dtype=jnp.int32), n_dp, False, *sides)
        grads = lax.psum_scatter(grads, "dp", scatter_dimension=0, tiled=False)
    gy = exchange(gy.reshape(count, width))

    dh1, dctx, grad_o, two = unmix(
        order, h1, upstream_adjoint, dm_one, dm_two, target, ctx, whole_o, vec, cap
    )
    back = lambda r, dctx: attend_back(r, qkv, ctx, dctx, lse)
    tilt = lambda r, grads, *rest: slope(r, order, low_in, grads, grad_o, weights[r], two, *rest)
    if place.staged:
        three = back(3, dctx)
        slab = tilt(3, three)
        dctx, slab = barrier((dctx, slab))
        more = place.move(slab, place.core)
        duo = back(2, dctx)
        slab, rest = tilt(2, duo, (more,), None, True)
        dctx, slab, rest, gy, came = barrier((dctx, slab, rest, gy, came))
        across = place.move(slab, place.x)
        one = back(1, dctx)
        slab = tilt(1, one)
        dctx, slab, across = barrier((dctx, slab, across))
        more = place.move(slab, place.core)
        across = (across, place.move(rest, place.x))
        zero = back(0, dctx)
        keep, send = tilt(0, zero, (more, *across), table)
        last, send, came, gy = barrier((zero[0], send, came, gy))
        dqkv = (last, one[0], duo[0], three[0])

        def finishing(gy, came):
            pick = lambda at: sum(
                a[at : at + width].astype(F32) for a in (grads, came_far[1], came)
            )
            return finish(h1, target, gy), pick(0), pick(width), pick(2 * width)

        (sum_q, sum_k, sum_v, sum_o), small, input_grad, (output, *grads) = reduce_last(
            place, keep, send, 7, lambda: unproject(dqkv, weights, block_entries, dh1, vec),
            finishing, (gy, came),
        )
    else:
        parts = [back(r, dctx) for r in range(GROUPS)]
        (sum_q, sum_k, sum_v, sum_o), small = reduce_plain(
            [tilt(r, parts[r]) for r in range(GROUPS)], 7
        )
        input_grad = unproject([p[0] for p in parts], weights, block_entries, dh1, vec)
        output = finish(h1, target, gy)

        part = (grads.shape[0] - 16) // 2
        grads = [grads[:part], grads[part : 2 * part].T, grads[2 * part :]]
        grads = [g.astype(F32) for g in grads]

    grad_out, grad_in, rest = grads
    part = grad_out.shape[0]
    own = lax.axis_index("dp") * (width // n_dp)
    grad_bin = rest[0:1, :part]
    grad_bout = lax.dynamic_slice(rest[1:2], (0, own), (1, width // n_dp))
    grad_centers = rest[2:3]
    return (
        output,
        input_grad,
        small[0],
        small[1],
        sum_q,
        small[2],
        sum_k,
        sum_v,
        small[3],
        sum_o,
        small[4],
        small[5],
        small[6],
        grad_centers,
        grad_in[None],
        grad_bin,
        grad_out[None],
        grad_bout,
    )


def solution(mesh):
    placed = (
        P(("dp", "expert"), None),
        P(("dp", "expert")),
        P(("dp", "expert")),
        P(),
        P("expert"),
        P("expert"),
        P("expert", "dp"),
        P("expert"),
        P("expert", "dp"),
        P("expert", "dp"),
        P("expert"),
        P("expert", "dp"),
        P("expert"),
        P("expert"),
        P("expert"),
        P("expert", None),
        P("expert", None, None),
        P("expert", None),
        P("expert", None, None),
        P("expert", None),
        P(("dp", "expert"), None),
    )
    return jax.shard_map(
        partial(shards, Place(mesh)),
        mesh=mesh,
        in_specs=placed,
        out_specs=(
            P(("dp", "expert"), None),
            P(("dp", "expert"), None),
            P("expert"),
            P("expert"),
            P("expert", "dp"),
            P("expert"),
            P("expert", "dp"),
            P("expert", "dp"),
            P("expert"),
            P("expert", "dp"),
            P("expert"),
            P("expert"),
            P("expert"),
            P("expert", None),
            P("expert", None, "dp"),
            P("expert", "dp"),
            P("expert", "dp", None),
            P("expert", "dp"),
        ),
        check_vma=False,
    )
```

time: 395 us -> 379 us (0.959)
  waiting for transfers between devices: 73.3 us -> 37 us
  Pallas kernels: 211 us -> 228 us
  between operations: 14.8 us -> 1.12 us
  starting transfers between devices: 42.5 us -> 51.4 us
  other arithmetic: 9.89 us -> 16.8 us
    ppermute x13 -> x19, waiting for transfers between devices: 70.2 us -> 37 us  [move(): return lax.ppermute(array, BOTH, way)]
    pallas_call x15 -> x20, Pallas kernels: 207 us -> 223 us  [the longest x4 48.8 us: attend_back(): call(attend_back_kernel, 'attend_back', (length // SEQ_LEN,), [pl.BlockSp...]
    add x5 -> x6, other arithmetic: 1.23 us -> 8.28 us  [the longest x2 6.66 us: finishing(): sum((a[at:at + width].astype(F32) for a in (grads, came_far[1], came)))]
    all_to_all x5, starting transfers between devices: 25.8 us -> 31.7 us  [exchange(): lax.all_to_all(sent, 'expert', split_axis=0, concat_axis=0, tiled=True)]
    ppermute x13 -> x19, starting transfers between devices: 16.6 us -> 19.7 us  [move(): return lax.ppermute(array, BOTH, way)]
  transfers between devices with their start and end apart: 19 -> 24, of which waited for: 9 -> 10; matrix products, arithmetic and copies ran while one was open for 2% -> 5% of each run, Pallas kernels for 52% -> 55%
where the time goes in v2:
time: 379 us; the launch traced here: 375 us
  Pallas kernels  228 us (60%)
  starting transfers between devices  51.4 us (14%)
  waiting for transfers between devices  37 us (10%)
  blocking collectives  29.8 us (8%)
  other arithmetic  16.8 us (4%)
  local copies, waits for them, and re-layouts  11.1 us (3%)
    pallas_call x4, Pallas kernels, attend_back(): call(attend_back_kernel, 'attend_back', (length // SEQ_LEN,), [pl.BlockSp...  48.8 us
    pallas_call x2, Pallas kernels, expert(): call(expert_kernel, 'expert', (ff // step,), [full((rows, width)), side,...  48.3 us
    ppermute x19, waiting for transfers between devices, move(): return lax.ppermute(array, BOTH, way)  37 us
    all_to_all x5, starting transfers between devices, exchange(): lax.all_to_all(sent, 'expert', split_axis=0, concat_axis=0, tiled=True)  31.7 us
    all_to_all x1, blocking collectives, exchange(): lax.all_to_all(sent, 'expert', split_axis=0, concat_axis=0, tiled=True)  29.8 us
    pallas_call x4, Pallas kernels, slope(): call(partial(slope_kernel, group, len(more), table is not None, halves),...  24.4 us
    pallas_call x2, Pallas kernels, attend(): call(attend_kernel, 'attend', (2, length // SEQ_LEN), [pl.BlockSpec((1, S...  24.1 us
    ppermute x19, starting transfers between devices, move(): return lax.ppermute(array, BOTH, way)  19.7 us
  transfers between devices with their start and end apart: 24, of which 10 were waited for; matrix products, arithmetic and copies ran while one was open for 5% of the time, Pallas kernels for 55%

profile of v2, /device:TPU:0, one launch (start us, length us, event | category | flops | bytes accessed | tf_op | source)
XLA Modules:
  0.0 374.8 jit_solution(5646350204672325030)
XLA Ops:
  2.6 4.1 %collective-permute-start.1 = (bf16[96,896]{1,0:T(8,128)(2,1)S(1)}, bf16[96,896]{1,0:T(8,128)(2,1)S(1)}, u32[]{:S(2)}, u32[]{:S(2)}) collective-permute-start(bf16[96,896]{1,0:T(8,128)(2,1)S(1)} %concatenate.3), channel_id=1, source_target_pairs={{0,4},{1,5},{2,6},{3,7},{4,0},{5,1},{6,2},{7,3},{8,12},{9,13},{10,... | collective-permute-start | bytes 516104 | tf_op jit(solution)/shard_map/ppermute | solution.py:773
  6.7 1.3 collective-permute-start.2
  8.3 11.0 %collective-permute-done.1 = bf16[96,896]{1,0:T(8,128)(2,1)S(1)} collective-permute-done((bf16[96,896]{1,0:T(8,128)(2,1)S(1)}, bf16[96,896]{1,0:T(8,128)(2,1)S(1)}, u32[]{:S(2)}, u32[]{:S(2)}) %collective-permute-start.1) | collective-permute-done | bytes 172064 | tf_op jit(solution)/shard_map/ppermute | solution.py:773
  20.0 1.6 collective-permute-start.3
  22.9 1.3 add_select_fusion
  24.2 4.3 %dispatch.1 = bf16[1024,768]{1,0:T(8,128)(2,1)} custom-call(s32[1,1024]{1,0:T(1,128)} %bitcast.86, bf16[1024,768]{1,0:T(8,128)(2,1)} %g_ref.1), custom_call_target="tpu_custom_call" | custom-call | flops 1610612736 | bytes 3000000 | tf_op jit(solution)/shard_map/dispatch/pallas_call | solution.py:296
  28.5 6.8 %collective-permute-done.3.got_ref = bf16[4,96,896]{2,1,0:T(8,128)(2,1)S(1)} collective-permute-done((bf16[4,96,896]{2,1,0:T(8,128)(2,1)S(1)}, bf16[4,96,896]{2,1,0:T(8,128)(2,1)S(1)}, u32[]{:S(2)}, u32[]{:S(2)}) %collective-permute-start.3) | collective-permute-done | bytes 688160 | tf_op jit(solution)/shard_map/ppermute | solution.py:773
  36.2 3.2 assemble.1.refs_1_.refs_0_.refs_5_.refs_4_
  39.5 1.3 collective-permute-start.5
  41.3 1.5 collective-permute-done.4.refs_2_.refs_1_.refs_4_.refs_5_
  42.8 9.6 %all-to-all-start = ((bf16[8,128,768]{2,1,0:T(8,128)(2,1)}), bf16[8,128,768]{2,1,0:T(8,128)(2,1)}, u32[]{:S(2)}, u32[]{:S(2)}) async-start(bf16[8,128,768]{2,1,0:T(8,128)(2,1)} %bitcast.69), calls=%async_computation | async-start | bytes 3145728 | tf_op jit(solution)/shard_map/all_to_all | solution.py:889
  52.4 7.3 %project.2 = (bf16[4,1024,576]{2,1,0:T(8,128)(2,1)}, bf16[1024,768]{1,0:T(8,128)(2,1)}, f32[8,768]{1,0:T(8,128)}) custom-call(s32[4]{0:T(128)} %iota_xor_fusion.order, bf16[1024,768]{1,0:T(8,128)(2,1)} %refs_8_.1, bf16[768,896]{1,0:T(8,128)(2,1)} %assemble.1.refs_1_.refs_0_.refs_5_.refs_4_, bf16[768,896]{1,0:T(8,128)(2,1)} %copy-done.3), custom_call_target="tpu_custom_call" | custom-call | flops 1811939328 | bytes 8000000 | tf_op jit(solution)/shard_map/project/pallas_call | solution.py:145
  59.6 12.0 %attend.2 = (bf16[4,1024,192]{2,1,0:T(8,128)(2,1)}, f32[4,1024,128]{2,1,0:T(8,128)}) custom-call(bf16[4,1024,576]{2,1,0:T(8,128)(2,1)} %get-tuple-element.113.qkv_ref.refs_4_), custom_call_target="tpu_custom_call" | custom-call | flops 8000000000 | bytes 5000000 | tf_op jit(solution)/shard_map/attend/pallas_call | solution.py:189
  72.3 3.1 collective-permute-done.6.refs_3_.refs_4_.refs_7_
  76.6 6.2 %project.3.qkv_ref = bf16[4,1024,576]{2,1,0:T(8,128)(2,1)} custom-call(s32[4]{0:T(128)} %iota_xor_fusion.order, bf16[1024,768]{1,0:T(8,128)(2,1)} %get-tuple-element.111.refs_0_.refs_1_, f32[8,768]{1,0:T(8,128)} %get-tuple-element.112.refs_1_.vec_ref.refs_10_, bf16[768,896]{1,0:T(8,128)(2,1)} %copy-done, ...), custom_call_target="tpu_custom_call", output_to_operand_aliasing={{}: (5, {})} | custom-call | flops 1811939328 | bytes 8000000 | tf_op jit(solution)/shard_map/project/pallas_call | solution.py:145
  82.7 12.0 %attend.3 = (bf16[4,1024,192]{2,1,0:T(8,128)(2,1)}, f32[4,1024,128]{2,1,0:T(8,128)}) custom-call(bf16[4,1024,576]{2,1,0:T(8,128)(2,1)} %project.3.qkv_ref, bf16[4,1024,192]{2,1,0:T(8,128)(2,1)} %get-tuple-element.117.refs_0_, f32[4,1024,128]{2,1,0:T(8,128)} %get-tuple-element.118.refs_1_), custom_call_target="tpu_custom_call", output_to_operand_aliasing={{0}: (1, {}), {1}: (2, {})} | custom-call | flops 8000000000 | bytes 5000000 | tf_op jit(solution)/shard_map/attend/pallas_call | solution.py:189
  94.8 10.0 %mix.1 = (f32[1024,768]{1,0:T(8,128)}, bf16[768,768]{1,0:T(8,128)(2,1)}, bf16[512,768]{1,0:T(8,128)(2,1)}, bf16[512,768]{1,0:T(8,128)(2,1)}) custom-call(s32[4]{0:T(128)} %iota_xor_fusion.order, bf16[1024,768]{1,0:T(8,128)(2,1)} %refs_8_.1, bf16[4,1024,192]{2,1,0:T(8,128)(2,1)} %get-tuple-element.121.ctx_ref, ...), custom_call_target="tpu_custom_call" | custom-call | flops 2818572288 | bytes 12000000 | tf_op jit(solution)/shard_map/mix/pallas_call | solution.py:347
  104.8 29.8 %all_to_all.30 = bf16[8,64,768]{2,1,0:T(8,128)(2,1)} all-to-all(bf16[8,64,768]{2,1,0:T(8,128)(2,1)} %bitcast.80), channel_id=1, replica_groups=mesh['dp'=4,'expert'=8] {'expert'}, dimensions={0} | all-to-all | bytes 1572864 | tf_op jit(solution)/shard_map/all_to_all | solution.py:889
  134.6 3.6 all-to-all-start.2
  138.2 24.1 %expert.2 = (bf16[8,2,64,768]{3,2,1,0:T(8,128)(2,1)}, bf16[512,768]{1,0:T(8,128)(2,1)}, bf16[512,768]{1,0:T(8,128)(2,1)}, bf16[512,3072]{1,0:T(8,128)(2,1)}, bf1...) custom-call(bf16[512,768]{1,0:T(8,128)(2,1)} %bitcast.72, bf16[8,2,64,768]{3,2,1,0:T(8,128)(2,1)} %bitcast.14.g_ref, ...), custom_call_target="tpu_custom_call" | custom-call | flops 9663676416 | bytes 22000000 | tf_op jit(solution)/shard_map/expert/pallas_call | solution.py:531
  162.3 6.0 %all-to-all-start.3 = ((bf16[8,64,768]{2,1,0:T(8,128)(2,1)}), bf16[8,64,768]{2,1,0:T(8,128)(2,1)S(1)}, u32[]{:S(2)}, u32[]{:S(2)}) async-start(bf16[8,64,768]{2,1,0:T(8,128)(2,1)} %bitcast.78), calls=%async_computation.3 | async-start | bytes 1572864 | tf_op jit(solution)/shard_map/all_to_all | solution.py:889
  168.3 24.2 %expert.3 = (bf16[8,2,64,768]{3,2,1,0:T(8,128)(2,1)}, bf16[512,768]{1,0:T(8,128)(2,1)}, bf16[512,768]{1,0:T(8,128)(2,1)}, bf16[512,3072]{1,0:T(8,128)(2,1)}, bf1...) custom-call(bf16[512,768]{1,0:T(8,128)(2,1)} %bitcast.75, ...), custom_call_target="tpu_custom_call", output_to_operand_aliasing={{0}: (7, {})} | custom-call | flops 9663676416 | bytes 22000000 | tf_op jit(solution)/shard_map/expert/pallas_call | solution.py:531
  192.6 6.5 %all-to-all-start.4 = ((bf16[8,64,768]{2,1,0:T(8,128)(2,1)}), bf16[8,64,768]{2,1,0:T(8,128)(2,1)S(1)}, u32[]{:S(2)}, u32[]{:S(2)}) async-start(bf16[8,64,768]{2,1,0:T(8,128)(2,1)} %bitcast.77), calls=%async_computation.4 | async-start | bytes 1572864 | tf_op jit(solution)/shard_map/all_to_all | solution.py:889
  199.6 18.4 %weigh.1 = (bf16[2,1552,768]{2,1,0:T(8,128)(2,1)}, bf16[1552,768]{1,0:T(8,128)(2,1)}, bf16[1552,768]{1,0:T(8,128)(2,1)}) custom-call(s32[4]{0:T(128)} %fusion.11.which, bf16[512,3072]{1,0:T(8,128)(2,1)} %get-tuple-element.126.refs_0_, bf16[512,3072]{1,0:T(8,128)(2,1)} %get-tuple-element.134.refs_1_, bf16[512,3072]{1,0:T(8,128)(2,1)} %get-tuple-element.135.refs_2_, ...), custom_call_target="tpu_custom_call" | custom-call | flops 9663676416 | bytes 26000000 | tf_op jit(solution)/shard_map/weigh/pallas_call | solution.py:614
  219.1 6.0 %all-to-all-start.5 = ((bf16[8,128,768]{2,1,0:T(8,128)(2,1)}), bf16[8,128,768]{2,1,0:T(8,128)(2,1)S(1)}, u32[]{:S(2)}, u32[]{:S(2)}) async-start(bf16[8,128,768]{2,1,0:T(8,128)(2,1)} %bitcast.27), calls=%async_computation.5 | async-start | bytes 3145728 | tf_op jit(solution)/shard_map/all_to_all | solution.py:889
  226.4 4.4 %fusion = bf16[1552,768]{1,0:T(8,128)(2,1)} fusion(bf16[1552,768]{1,0:T(8,128)(2,1)} %get-tuple-element.143, bf16[2,1552,768]{2,1,0:T(8,128)(2,1)} %collective-permute-done.7), kind=kLoop, calls=%fused_computation.1 | loop fusion | flops 4767744 | bytes 7151616 | tf_op jit(solution)/shard_map/convert_element_type | solution.py:742
  230.8 1.5 collective-permute-start.9
  232.3 15.6 %unmix.1 = (f32[1024,768]{1,0:T(8,128)}, bf16[4,1024,192]{2,1,0:T(8,128)(2,1)}, bf16[4,768,192]{2,1,0:T(8,128)(2,1)}, f32[8,768]{1,0:T(8,128)}) custom-call(s32[4]{0:T(128)} %iota_xor_fusion.order, f32[1024,768]{1,0:T(8,128)} %get-tuple-element.149.h_ref, bf16[1024,768]{1,0:T(8,128)(2,1)} %g_ref.1, bf16[512,768]{1,0:T(8,128)(2,1)} %bitcast.70, ...), custom_call_target="tpu_custom_call" | custom-call | flops 4026531840 | bytes 20000000 | tf_op jit(solution)/shard_map/unmix/pallas_call | solution.py:418
  247.9 12.0 %attend_back.4 = (bf16[1,1024,576]{2,1,0:T(8,128)(2,1)}, f32[1,8,576]{2,1,0:T(8,128)}) custom-call(bf16[4,1024,576]{2,1,0:T(8,128)(2,1)} %project.3.qkv_ref, bf16[4,1024,192]{2,1,0:T(8,128)(2,1)} %get-tuple-element.121.ctx_ref, bf16[4,1024,192]{2,1,0:T(8,128)(2,1)} %get-tuple-element.171.dctx_ref, f32[4,1024,128]{2,1,0:T(8,128)} %get-tuple-element.154.lse_ref), custom_call_target="tpu_custom_call" | custom-call | flops 10000000000 | bytes 4000000 | tf_op jit(solution)/shard_map/attend_back/pallas_call | solution.py:265
  259.9 5.7 %slope.4 = bf16[768,896]{1,0:T(8,128)(2,1)} custom-call(s32[4]{0:T(128)} %iota_xor_fusion.order, bf16[1024,768]{1,0:T(8,128)(2,1)} %get-tuple-element.111.refs_0_.refs_1_, bf16[1,1024,576]{2,1,0:T(8,128)(2,1)} %get-tuple-element.155.refs_1_.refs_3_, f32[1,8,576]{2,1,0:T(8,128)} %get-tuple-element.156.refs_2_, ...), custom_call_target="tpu_custom_call" | custom-call | flops 905969664 | bytes 6000000 | tf_op jit(solution)/shard_map/slope/pallas_call | solution.py:733
  265.6 12.2 %attend_back.5 = (bf16[1,1024,576]{2,1,0:T(8,128)(2,1)}, f32[1,8,576]{2,1,0:T(8,128)}) custom-call(bf16[4,1024,576]{2,1,0:T(8,128)(2,1)} %project.3.qkv_ref, bf16[4,1024,192]{2,1,0:T(8,128)(2,1)} %get-tuple-element.121.ctx_ref, bf16[4,1024,192]{2,1,0:T(8,128)(2,1)} %get-tuple-element.171.dctx_ref, f32[4,1024,128]{2,1,0:T(8,128)} %get-tuple-element.154.lse_ref), custom_call_target="tpu_custom_call" | custom-call | flops 10000000000 | bytes 4000000 | tf_op jit(solution)/shard_map/attend_back/pallas_call | solution.py:265
  278.9 6.1 %slope.5 = (bf16[384,896]{1,0:T(8,128)(2,1)}, bf16[384,896]{1,0:T(8,128)(2,1)}) custom-call(s32[4]{0:T(128)} %iota_xor_fusion.order, bf16[1024,768]{1,0:T(8,128)(2,1)} %get-tuple-element.111.refs_0_.refs_1_, bf16[1,1024,576]{2,1,0:T(8,128)(2,1)} %get-tuple-element.160.refs_1_.refs_2_, f32[1,8,576]{2,1,0:T(8,128)} %get-tuple-element.161.refs_2_, ...), custom_call_target="tpu_custom_call" | custom-call | flops 905969664 | bytes 6000000 | tf_op jit(solution)/shard_map/slope/pallas_call | solution.py:733
  285.1 1.4 collective-permute-start.10
  286.4 12.4 %attend_back.6 = (bf16[1,1024,576]{2,1,0:T(8,128)(2,1)}, f32[1,8,576]{2,1,0:T(8,128)}) custom-call(bf16[4,1024,576]{2,1,0:T(8,128)(2,1)} %project.3.qkv_ref, bf16[4,1024,192]{2,1,0:T(8,128)(2,1)} %get-tuple-element.121.ctx_ref, bf16[4,1024,192]{2,1,0:T(8,128)(2,1)} %get-tuple-element.171.dctx_ref, f32[4,1024,128]{2,1,0:T(8,128)} %get-tuple-element.154.lse_ref), custom_call_target="tpu_custom_call" | custom-call | flops 10000000000 | bytes 4000000 | tf_op jit(solution)/shard_map/attend_back/pallas_call | solution.py:265
  298.8 5.7 %slope.6 = bf16[768,896]{1,0:T(8,128)(2,1)} custom-call(s32[4]{0:T(128)} %iota_xor_fusion.order, bf16[1024,768]{1,0:T(8,128)(2,1)} %get-tuple-element.111.refs_0_.refs_1_, bf16[1,1024,576]{2,1,0:T(8,128)(2,1)} %get-tuple-element.168.refs_1_, f32[1,8,576]{2,1,0:T(8,128)} %get-tuple-element.169.refs_2_, ...), custom_call_target="tpu_custom_call" | custom-call | flops 905969664 | bytes 6000000 | tf_op jit(solution)/shard_map/slope/pallas_call | solution.py:733
  305.5 12.2 %attend_back.7 = (bf16[1,1024,576]{2,1,0:T(8,128)(2,1)}, f32[1,8,576]{2,1,0:T(8,128)}) custom-call(bf16[4,1024,576]{2,1,0:T(8,128)(2,1)} %project.3.qkv_ref, bf16[4,1024,192]{2,1,0:T(8,128)(2,1)} %get-tuple-element.121.ctx_ref, bf16[4,1024,192]{2,1,0:T(8,128)(2,1)} %get-tuple-element.171.dctx_ref, f32[4,1024,128]{2,1,0:T(8,128)} %get-tuple-element.154.lse_ref), custom_call_target="tpu_custom_call" | custom-call | flops 10000000000 | bytes 4000000 | tf_op jit(solution)/shard_map/attend_back/pallas_call | solution.py:265
  317.7 4.8 %collective-permute-done.12.refs_9_ = bf16[384,896]{1,0:T(8,128)(2,1)S(1)} collective-permute-done((bf16[384,896]{1,0:T(8,128)(2,1)S(1)}, bf16[384,896]{1,0:T(8,128)(2,1)S(1)}, u32[]{:S(2)}, u32[]{:S(2)}) %collective-permute-start.12) | collective-permute-done | bytes 688160 | tf_op jit(solution)/shard_map/ppermute | solution.py:773
  323.8 6.9 %slope.7 = (bf16[4,96,896]{2,1,0:T(8,128)(2,1)}, bf16[4,96,896]{2,1,0:T(8,128)(2,1)}) custom-call(s32[4]{0:T(128)} %iota_xor_fusion.order, s32[8]{0:T(128)} %fusion.14.table.refs_0_, bf16[1024,768]{1,0:T(8,128)(2,1)} %get-tuple-element.111.refs_0_.refs_1_, bf16[1,1024,576]{2,1,0:T(8,128)(2,1)} %get-tuple-element.182.refs_2_.refs_0_, ...), custom_call_target="tpu_custom_call" | custom-call | flops 905969664 | bytes 6000000 | tf_op jit(solution)/shard_map/slope/pallas_call | solution.py:733
  330.7 2.1 collective-permute-start.13
  332.8 11.0 %unproject.1 = f32[1024,768]{1,0:T(8,128)} custom-call(bf16[1,1024,576]{2,1,0:T(8,128)(2,1)} %get-tuple-element.182.refs_2_.refs_0_, bf16[1,1024,576]{2,1,0:T(8,128)(2,1)} %get-tuple-element.168.refs_1_, bf16[1,1024,576]{2,1,0:T(8,128)(2,1)} %get-tuple-element.160.refs_1_.refs_2_, bf16[1,1024,576]{2,1,0:T(8,128)(2,1)} %get-tuple-element.155.refs_1_.refs_3_, ...), custom_call_target="tpu_custom_call" | custom-call | flops 3623878656 | bytes 20000000 | tf_op jit(solution)/shard_map/unproject/pallas_call | solution.py:641
  343.8 4.4 %collective-permute-done.13 = bf16[4,96,896]{2,1,0:T(8,128)(2,1)S(1)} collective-permute-done((bf16[4,96,896]{2,1,0:T(8,128)(2,1)}, bf16[4,96,896]{2,1,0:T(8,128)(2,1)S(1)}, u32[]{:S(2)}, u32[]{:S(2)}) %collective-permute-start.13) | collective-permute-done | bytes 688160 | tf_op jit(solution)/shard_map/ppermute | solution.py:773
  349.1 1.7 collective-permute-start.14
  350.8 2.4 collective-permute-start.15
  353.5 5.3 %fusion.1 = (f32[768,768]{1,0:T(8,128)}, f32[768,768]{1,0:T(8,128)}) fusion(bf16[2,1552,768]{2,1,0:T(8,128)(2,1)} %collective-permute-done.7, bf16[1552,768]{1,0:T(8,128)(2,1)} %collective-permute-done.9, bf16[1552,768]{1,0:T(8,128)(2,1)S(1)} %copy-done.5), kind=kLoop, calls=%fused_computation.4 | loop fusion | flops 5898240 | bytes 11796480 | tf_op jit(solution)/shard_map/add | solution.py:982
  358.7 1.4 fusion.8
  360.1 6.0 %finish.1 = bf16[1024,768]{1,0:T(8,128)(2,1)} custom-call(f32[1024,768]{1,0:T(8,128)} %get-tuple-element.149.h_ref, s32[1024,1]{1,0:T(8,128)} %copy.63.target_ref, bf16[1024,768]{1,0:T(8,128)(2,1)} %bitcast.66), custom_call_target="tpu_custom_call" | custom-call | flops 1610612736 | bytes 6000000 | tf_op jit(solution)/shard_map/finish/pallas_call | solution.py:442
  368.1 1.4 fusion.18
  370.8 2.9 collective-permute-done.18
  (80 shorter events, 18.8 us)
Async XLA Ops:
  2.6 16.7 %collective-permute-start.1 = (bf16[96,896]{1,0:T(8,128)(2,1)S(1)}, bf16[96,896]{1,0:T(8,128)(2,1)S(1)}, u32[]{:S(2)}, u32[]{:S(2)}) collective-permute-start(bf16[96,896]{1,0:T(8,128)(2,1)S(1)} %concatenate.3), channel_id=1, source_target_pairs={{0,4},{1,5},{2,6},{3,7},{4,0},{5,1},{6,2},{7,3},{8,12},{9,13},{10,... | collective-permute-start | bytes 516104 | tf_op jit(solution)/shard_map/ppermute | solution.py:773
  6.7 12.6 %collective-permute-start.2 = (bf16[96,896]{1,0:T(8,128)(2,1)S(1)}, bf16[96,896]{1,0:T(8,128)(2,1)S(1)}, u32[]{:S(2)}, u32[]{:S(2)}) collective-permute-start(bf16[96,896]{1,0:T(8,128)(2,1)S(1)} %concatenate.3), channel_id=1, source_target_pairs={{0,6},{1,7},{2,4},{3,5},{4,2},{5,3},{6,0},{7,1},{8,14},{9,15},{10,... | collective-permute-start | bytes 516104 | tf_op jit(solution)/shard_map/ppermute | solution.py:773
  8.0 11.8 %collective-permute-start = (bf16[96,896]{1,0:T(8,128)(2,1)S(1)}, bf16[96,896]{1,0:T(8,128)(2,1)S(1)}, u32[]{:S(2)}, u32[]{:S(2)}) collective-permute-start(bf16[96,896]{1,0:T(8,128)(2,1)S(1)} %concatenate.3), channel_id=1, source_target_pairs={{0,2},{1,3},{2,0},{3,1},{4,6},{5,7},{6,4},{7,5},{8,10},{9,11},{10,... | collective-permute-start | bytes 516104 | tf_op jit(solution)/shard_map/ppermute | solution.py:773
  19.9 8.6 %copy-start.4 = (bf16[4,96,896]{2,1,0:T(8,128)(2,1)}, bf16[4,96,896]{2,1,0:T(8,128)(2,1)S(1)}, u32[]{:S(2)}) copy-start(bf16[4,96,896]{2,1,0:T(8,128)(2,1)S(1)} %pad_maximum_fusion.own_ref) | copy-start | bytes 2064388
  20.0 15.4 %collective-permute-start.3 = (bf16[4,96,896]{2,1,0:T(8,128)(2,1)S(1)}, bf16[4,96,896]{2,1,0:T(8,128)(2,1)S(1)}, u32[]{:S(2)}, u32[]{:S(2)}) collective-permute-start(bf16[4,96,896]{2,1,0:T(8,128)(2,1)S(1)} %pad_maximum_fusion.own_ref), channel_id=1, source_target_pairs={{0,1},{1,0},{2,3},{3,2},{4,5},{5,4},{6,7},{7,6},{8,9},{9,8},{10,11... | collective-permute-start | bytes 2064392 | tf_op jit(solution)/shard_map/ppermute | solution.py:773
  35.3 0.8 copy-start.12
  39.4 3.4 collective-permute-start.4
  39.5 32.8 %collective-permute-start.5 = (bf16[768,896]{1,0:T(8,128)(2,1)}, bf16[768,896]{1,0:T(8,128)(2,1)S(1)}, u32[]{:S(2)}, u32[]{:S(2)}) collective-permute-start(bf16[768,896]{1,0:T(8,128)(2,1)} %assemble.1.refs_1_.refs_0_.refs_5_.refs_4_), channel_id=1, source_target_pairs={{0,16},{1,17},{2,18},{3,19},{4,20},{5,21},{6,22},{7,23},{8,24},{9,... | collective-permute-start | bytes 4128776 | tf_op jit(solution)/shard_map/ppermute | solution.py:773
  42.8 9.6 %copy-start.3 = (bf16[768,896]{1,0:T(8,128)(2,1)}, bf16[768,896]{1,0:T(8,128)(2,1)S(1)}, u32[]{:S(2)}) copy-start(bf16[768,896]{1,0:T(8,128)(2,1)S(1)} %collective-permute-done.4.refs_2_.refs_1_.refs_4_.refs_5_) | copy-start | bytes 4128772
  42.8 52.0 %all-to-all-start = ((bf16[8,128,768]{2,1,0:T(8,128)(2,1)}), bf16[8,128,768]{2,1,0:T(8,128)(2,1)}, u32[]{:S(2)}, u32[]{:S(2)}) async-start(bf16[8,128,768]{2,1,0:T(8,128)(2,1)} %bitcast.69), calls=%async_computation | async-start | bytes 3145728 | tf_op jit(solution)/shard_map/all_to_all | solution.py:889
  72.3 3.1 copy-start
  72.3 3.1 collective-permute-start.6
  75.4 1.2 copy-start.1
  134.6 27.7 %all-to-all-start.2 = ((bf16[8,64,768]{2,1,0:T(8,128)(2,1)}), bf16[8,64,768]{2,1,0:T(8,128)(2,1)S(1)}, u32[]{:S(2)}, u32[]{:S(2)}) async-start(bf16[8,64,768]{2,1,0:T(8,128)(2,1)} %bitcast.79), calls=%async_computation.2 | async-start | bytes 1572864 | tf_op jit(solution)/shard_map/all_to_all | solution.py:889
  162.3 6.0 %copy-start.10 = (bf16[8,64,768]{2,1,0:T(8,128)(2,1)}, bf16[8,64,768]{2,1,0:T(8,128)(2,1)S(1)}, u32[]{:S(2)}) copy-start(bf16[8,64,768]{2,1,0:T(8,128)(2,1)S(1)} %all-to-all-done.2) | copy-start | bytes 2359300
  162.3 30.2 %all-to-all-start.3 = ((bf16[8,64,768]{2,1,0:T(8,128)(2,1)}), bf16[8,64,768]{2,1,0:T(8,128)(2,1)S(1)}, u32[]{:S(2)}, u32[]{:S(2)}) async-start(bf16[8,64,768]{2,1,0:T(8,128)(2,1)} %bitcast.78), calls=%async_computation.3 | async-start | bytes 1572864 | tf_op jit(solution)/shard_map/all_to_all | solution.py:889
  192.6 25.4 %copy-start.8 = (bf16[8,64,768]{2,1,0:T(8,128)(2,1)}, bf16[8,64,768]{2,1,0:T(8,128)(2,1)S(1)}, u32[]{:S(2)}) copy-start(bf16[8,64,768]{2,1,0:T(8,128)(2,1)S(1)} %all-to-all-done.3) | copy-start | bytes 2359300
  192.6 25.4 %all-to-all-start.4 = ((bf16[8,64,768]{2,1,0:T(8,128)(2,1)}), bf16[8,64,768]{2,1,0:T(8,128)(2,1)S(1)}, u32[]{:S(2)}, u32[]{:S(2)}) async-start(bf16[8,64,768]{2,1,0:T(8,128)(2,1)} %bitcast.77), calls=%async_computation.4 | async-start | bytes 1572864 | tf_op jit(solution)/shard_map/all_to_all | solution.py:889
  199.6 18.5 %copy-start.15 = (s32[1024]{0:T(1024)S(1)}, s32[1024]{0:T(1024)}, u32[]{:S(2)}) copy-start(s32[1024]{0:T(1024)} %add_select_fusion) | copy-start | bytes 12292
  218.0 12.8 %copy-start.9 = (bf16[8,64,768]{2,1,0:T(8,128)(2,1)}, bf16[8,64,768]{2,1,0:T(8,128)(2,1)S(1)}, u32[]{:S(2)}) copy-start(bf16[8,64,768]{2,1,0:T(8,128)(2,1)S(1)} %all-to-all-done.4) | copy-start | bytes 2359300
  218.0 8.4 %collective-permute-start.7 = (bf16[2,1552,768]{2,1,0:T(8,128)(2,1)}, bf16[2,1552,768]{2,1,0:T(8,128)(2,1)}, u32[]{:S(2)}, u32[]{:S(2)}) collective-permute-start(bf16[2,1552,768]{2,1,0:T(8,128)(2,1)} %get-tuple-element.147), channel_id=1, source_target_pairs={{0,8},{1,9},{2,10},{3,11},{4,12},{5,13},{6,14},{7,15},{8,0},{9,1},... | collective-permute-start | bytes 14303240 | tf_op jit(solution)/shard_map/ppermute | solution.py:773
  219.1 65.9 %all-to-all-start.5 = ((bf16[8,128,768]{2,1,0:T(8,128)(2,1)}), bf16[8,128,768]{2,1,0:T(8,128)(2,1)S(1)}, u32[]{:S(2)}, u32[]{:S(2)}) async-start(bf16[8,128,768]{2,1,0:T(8,128)(2,1)} %bitcast.27), calls=%async_computation.5 | async-start | bytes 3145728 | tf_op jit(solution)/shard_map/all_to_all | solution.py:889
  230.8 54.2 %collective-permute-start.9 = (bf16[1552,768]{1,0:T(8,128)(2,1)}, bf16[1552,768]{1,0:T(8,128)(2,1)}, u32[]{:S(2)}, u32[]{:S(2)}) collective-permute-start(bf16[1552,768]{1,0:T(8,128)(2,1)} %fusion), channel_id=1, source_target_pairs={{0,16},{1,17},{2,18},{3,19},{4,20},{5,21},{6,22},{7,23},{8,24},{9,... | collective-permute-start | bytes 7151624 | tf_op jit(solution)/shard_map/ppermute | solution.py:773
  265.6 12.2 %collective-permute-start.8 = (bf16[768,896]{1,0:T(8,128)(2,1)}, bf16[768,896]{1,0:T(8,128)(2,1)S(1)}, u32[]{:S(2)}, u32[]{:S(2)}) collective-permute-start(bf16[768,896]{1,0:T(8,128)(2,1)} %slope.4), channel_id=1, source_target_pairs={{0,8},{1,9},{2,10},{3,11},{4,12},{5,13},{6,14},{7,15},{8,0},{9,1},... | collective-permute-start | bytes 4128776 | tf_op jit(solution)/shard_map/ppermute | solution.py:773
  277.8 1.1 copy-start.7
  285.0 13.8 %copy-start.2 = (bf16[8,128,768]{2,1,0:T(8,128)(2,1)}, bf16[8,128,768]{2,1,0:T(8,128)(2,1)S(1)}, u32[]{:S(2)}) copy-start(bf16[8,128,768]{2,1,0:T(8,128)(2,1)S(1)} %all-to-all-done.5) | copy-start | bytes 4718596
  285.1 19.5 %collective-permute-start.10 = (bf16[384,896]{1,0:T(8,128)(2,1)}, bf16[384,896]{1,0:T(8,128)(2,1)S(1)}, u32[]{:S(2)}, u32[]{:S(2)}) collective-permute-start(bf16[384,896]{1,0:T(8,128)(2,1)} %get-tuple-element.170), channel_id=1, source_target_pairs={{0,16},{1,17},{2,18},{3,19},{4,20},{5,21},{6,22},{7,23},{8,24},{9,... | collective-permute-start | bytes 2064392 | tf_op jit(solution)/shard_map/ppermute | solution.py:773
  298.8 5.8 %copy-start.16 = (bf16[384,896]{1,0:T(8,128)(2,1)S(1)}, bf16[384,896]{1,0:T(8,128)(2,1)}, u32[]{:S(2)}) copy-start(bf16[384,896]{1,0:T(8,128)(2,1)} %get-tuple-element.176) | copy-start | bytes 2064388
  304.5 13.2 %copy-start.13 = (bf16[384,896]{1,0:T(8,128)(2,1)}, bf16[384,896]{1,0:T(8,128)(2,1)S(1)}, u32[]{:S(2)}) copy-start(bf16[384,896]{1,0:T(8,128)(2,1)S(1)} %collective-permute-done.10.refs_8_) | copy-start | bytes 2064388
  304.5 17.9 %collective-permute-start.11 = (bf16[768,896]{1,0:T(8,128)(2,1)}, bf16[768,896]{1,0:T(8,128)(2,1)S(1)}, u32[]{:S(2)}, u32[]{:S(2)}) collective-permute-start(bf16[768,896]{1,0:T(8,128)(2,1)} %slope.6), channel_id=1, source_target_pairs={{0,8},{1,9},{2,10},{3,11},{4,12},{5,13},{6,14},{7,15},{8,0},{9,1},... | collective-permute-start | bytes 4128776 | tf_op jit(solution)/shard_map/ppermute | solution.py:773
  304.6 17.8 %collective-permute-start.12 = (bf16[384,896]{1,0:T(8,128)(2,1)S(1)}, bf16[384,896]{1,0:T(8,128)(2,1)S(1)}, u32[]{:S(2)}, u32[]{:S(2)}) collective-permute-start(bf16[384,896]{1,0:T(8,128)(2,1)S(1)} %copy-done.16), channel_id=1, source_target_pairs={{0,16},{1,17},{2,18},{3,19},{4,20},{5,21},{6,22},{7,23},{8,24},{9,... | collective-permute-start | bytes 2064392 | tf_op jit(solution)/shard_map/ppermute | solution.py:773
  322.5 0.8 copy-start.14
  322.5 1.3 copy-start.6
  330.7 17.5 %collective-permute-start.13 = (bf16[4,96,896]{2,1,0:T(8,128)(2,1)}, bf16[4,96,896]{2,1,0:T(8,128)(2,1)S(1)}, u32[]{:S(2)}, u32[]{:S(2)}) collective-permute-start(bf16[4,96,896]{2,1,0:T(8,128)(2,1)} %get-tuple-element.181), channel_id=1, source_target_pairs={{0,1},{1,0},{2,3},{3,2},{4,5},{5,4},{6,7},{7,6},{8,9},{9,8},{10,11... | collective-permute-start | bytes 2064392 | tf_op jit(solution)/shard_map/ppermute | solution.py:773
  332.8 15.5 %copy-start.11 = (bf16[4,96,896]{2,1,0:T(8,128)(2,1)S(1)}, bf16[4,96,896]{2,1,0:T(8,128)(2,1)}, u32[]{:S(2)}) copy-start(bf16[4,96,896]{2,1,0:T(8,128)(2,1)} %get-tuple-element.177) | copy-start | bytes 2064388
  332.8 20.7 %copy-start.5 = (bf16[1552,768]{1,0:T(8,128)(2,1)S(1)}, bf16[1552,768]{1,0:T(8,128)(2,1)}, u32[]{:S(2)}) copy-start(bf16[1552,768]{1,0:T(8,128)(2,1)} %get-tuple-element.188) | copy-start | bytes 7151620
  349.1 17.1 %collective-permute-start.14 = (bf16[96,896]{1,0:T(8,128)(2,1)}, bf16[96,896]{1,0:T(8,128)(2,1)S(1)}, u32[]{:S(2)}, u32[]{:S(2)}) collective-permute-start(bf16[96,896]{1,0:T(8,128)(2,1)} %get-tuple-element.209), channel_id=1, source_target_pairs={{0,2},{1,3},{2,0},{3,1},{4,6},{5,7},{6,4},{7,5},{8,10},{9,11},{10,... | collective-permute-start | bytes 516104 | tf_op jit(solution)/shard_map/ppermute | solution.py:773
  350.8 15.3 %collective-permute-start.15 = (bf16[96,896]{1,0:T(8,128)(2,1)}, bf16[96,896]{1,0:T(8,128)(2,1)S(1)}, u32[]{:S(2)}, u32[]{:S(2)}) collective-permute-start(bf16[96,896]{1,0:T(8,128)(2,1)} %get-tuple-element.208), channel_id=1, source_target_pairs={{0,4},{1,5},{2,6},{3,7},{4,0},{5,1},{6,2},{7,3},{8,12},{9,13},{10,... | collective-permute-start | bytes 516104 | tf_op jit(solution)/shard_map/ppermute | solution.py:773
  353.2 13.0 %collective-permute-start.16 = (bf16[96,896]{1,0:T(8,128)(2,1)}, bf16[96,896]{1,0:T(8,128)(2,1)}, u32[]{:S(2)}, u32[]{:S(2)}) collective-permute-start(bf16[96,896]{1,0:T(8,128)(2,1)} %get-tuple-element.207), channel_id=1, source_target_pairs={{0,6},{1,7},{2,4},{3,5},{4,2},{5,3},{6,0},{7,1},{8,14},{9,15},{10,... | collective-permute-start | bytes 516104 | tf_op jit(solution)/shard_map/ppermute | solution.py:773
  368.0 1.5 collective-permute-start.17
  369.6 4.2 %collective-permute-start.18 = (f32[8,96]{0,1:T(8,128)S(1)}, f32[8,96]{0,1:T(8,128)S(1)}, u32[]{:S(2)}, u32[]{:S(2)}) collective-permute-start(f32[8,96]{0,1:T(8,128)S(1)} %fusion.16), channel_id=1, source_target_pairs={{0,16},{1,17},{2,18},{3,19},{4,20},{5,21},{6,22},{7,23},{8,24},{9,... | collective-permute-start | bytes 9224 | tf_op jit(solution)/shard_map/ppermute | solution.py:773

commit v3 on v2

--- a/solution.py
+++ b/solution.py
@@ -101,186 +101,181 @@
     return pl.BlockSpec(shape, lambda i: tuple(i if a == axis else 0 for a in range(len(shape))))
 
 
-def project_kernel(half, order, *refs):
+def attend_kernel(half, order, *refs):
     if half:
-        low_ref, vec_ref, w_one, w_two, _, qkv_ref = refs
+        low_ref, vec_ref, w_one, w_two = refs[:4]
+        qkv_ref, ctx_ref, lse_ref = refs[7:]
     else:
-        x_ref, w_one, w_two, qkv_ref, low_ref, vec_ref = refs
-    width = low_ref.shape[1]
+        x_ref, w_one, w_two, qkv_ref, ctx_ref, lse_ref, low_ref, vec_ref = refs
+    step = pl.program_id(0)
+    count, width = low_ref.shape
     part = width // GROUPS
     if not half:
 
-        @pl.when(pl.program_id(0) == 0)
+        @pl.when(step == 0)
         def _():
             vec_ref[...] = w_one[:, 512:640].astype(F32).T[64:72]
-
-        unit, _ = normalize(x_ref[...].astype(F32))
-        low_ref[...] = (unit * vec_ref[0:1] + vec_ref[1:2]).astype(BF)
+            for at in range(0, count, 256):
+                unit, _ = normalize(x_ref[at : at + 256].astype(F32))
+                low_ref[at : at + 256] = (unit * vec_ref[0:1] + vec_ref[1:2]).astype(BF)
+
     zero = jnp.zeros((1, part), F32)
-    for g, w_ref in enumerate((w_one, w_two)):
-        bias_q = bias_v = zero
-        for n in range(GROUPS):
-            here = order[2 * half + g] == n
-            bias_q = jnp.where(here, vec_ref[2:3, part * n : part * n + part], bias_q)
-            bias_v = jnp.where(here, vec_ref[3:4, part * n : part * n + part], bias_v)
-        bias = jnp.concatenate([bias_q, zero, bias_v], axis=1)
-        qkv_ref[g] = (dot(low_ref[...], w_ref[:, : 3 * part], 1, 0) + bias).astype(BF)
-
-
-def project(half, order, weights, x=None, low=None, vec=None, qkv=None):
+    bias_q = bias_v = zero
+    for n in range(GROUPS):
+        here = order[2 * half + step] == n
+        bias_q = jnp.where(here, vec_ref[2:3, part * n : part * n + part], bias_q)
+        bias_v = jnp.where(here, vec_ref[3:4, part * n : part * n + part], bias_v)
+    bias = jnp.concatenate([bias_q, zero, bias_v], axis=1)
+    w = jnp.where(step == 0, w_one[...], w_two[...])[:, : 3 * part]
+    for at in range(0, count, 512):
+        qkv_ref[0, at : at + 512] = (dot(low_ref[at : at + 512], w, 1, 0) + bias).astype(BF)
+    for base in range(0, count, SEQ_LEN):
+        block = min(512, SEQ_LEN)
+        for h in range(part // HEAD_DIM):
+            at = h * HEAD_DIM
+            v = qkv_ref[0, base : base + SEQ_LEN, 2 * part + at : 2 * part + at + HEAD_DIM].T
+            for start in range(0, SEQ_LEN, block):
+                stop = start + block
+                q = qkv_ref[0, base + start : base + stop, at : at + HEAD_DIM] * BF(HEAD_DIM**-0.5)
+                k = qkv_ref[0, base : base + stop, part + at : part + at + HEAD_DIM]
+                row = lax.broadcasted_iota(jnp.int32, (stop, block), 0)
+                col = lax.broadcasted_iota(jnp.int32, (stop, block), 1) + start
+                scores = jnp.where(row <= col, dot(k, q, 1, 1), MASKED)
+                top = jnp.max(scores, axis=0, keepdims=True)
+                probs = jnp.exp(scores - top)
+                total = jnp.sum(probs, axis=0, keepdims=True)
+                out = dot(v[:, :stop], probs.astype(BF), 1, 0) / total
+                ctx_ref[0, base + start : base + stop, at : at + HEAD_DIM] = out.T.astype(BF)
+                lse_ref[0, h : h + 1, base + start : base + stop] = top + jnp.log(total)
+
+
+def attend(half, order, weights, x=None, low=None, vec=None, before=()):
     count, width = (low if half else x).shape
     part = width // GROUPS
-    rows = min(256, count)
-    whole = (GROUPS, count, 3 * part)
-    outs = [(pl.BlockSpec((2, rows, 3 * part), lambda i: (half, i, 0)), whole, BF)]
-    w = [pl.BlockSpec((width, 640), lambda i: (0, 0), pipeline_mode=pl.Buffered(1))] * 2
+    at = lambda g: (2 * half + g, 0, 0)
+    outs = [
+        (pl.BlockSpec((1, count, 3 * part), at), (GROUPS, count, 3 * part), BF),
+        (pl.BlockSpec((1, count, part), at), (GROUPS, count, part), BF),
+        (pl.BlockSpec((1, 8, count), at), (GROUPS, 8, count), F32),
+    ]
+    w = [pl.BlockSpec((width, 640), lambda g: (0, 0), pipeline_mode=pl.Buffered(1))] * 2
     if half:
-        ins, args = [chunk((rows, width)), full((8, width))] + w + [PLACED], (low, vec, *weights, qkv)
+        ins, args = [full((count, width)), full((8, width))] + w + [PLACED] * 3, (low, vec)
     else:
-        outs += [
-            (chunk((rows, width)), (count, width), BF),
-            (full((8, width)), (8, width), F32),
+        outs += [(full((count, width)), (count, width), BF), (full((8, width)), (8, width), F32)]
+        ins, args = [full((count, width))] + w, (x,)
+    return call(
+        partial(attend_kernel, half), "attend", (2,), [SCALARS] + ins, outs,
+        cost=(12_000_000_000, 8_000_000, 4_000_000),
+        input_output_aliases={5 + i: i for i in range(len(before))},
+    )(order, *args, *weights, *before)
+
+
+def attend_back_kernel(half, order, table, *refs):
+    qkv_ref, ctx_ref, dctx_ref, lse_ref, low_ref, o_ref, w_one, w_two, two_ref = refs[:9]
+    out_ref, *slabs, dq_ref, stage, sems = refs[9:]
+    step = pl.program_id(0)
+    count, width = low_ref.shape
+    part = width // GROUPS
+    inner = (ctx_ref[0].astype(F32) * dctx_ref[0].astype(F32)).T
+    block = min(256, SEQ_LEN)
+    for base in range(0, count, SEQ_LEN):
+        last = base + SEQ_LEN
+        for h in range(part // HEAD_DIM):
+            at = h * HEAD_DIM
+            q = qkv_ref[0, base:last, at : at + HEAD_DIM] * BF(HEAD_DIM**-0.5)
+            do = dctx_ref[0, base:last, at : at + HEAD_DIM]
+            turned = qkv_ref[0, base:last, part + at : part + at + HEAD_DIM].T
+            row_dot = jnp.sum(inner[at : at + HEAD_DIM, base:last], axis=0, keepdims=True)
+            for start in range(0, SEQ_LEN, block):
+                stop = start + block
+                rows = slice(base + start, base + stop)
+                k = qkv_ref[0, rows, part + at : part + at + HEAD_DIM]
+                v = qkv_ref[0, rows, 2 * part + at : 2 * part + at + HEAD_DIM]
+                row = lax.broadcasted_iota(jnp.int32, (block, SEQ_LEN - start), 0)
+                col = lax.broadcasted_iota(jnp.int32, (block, SEQ_LEN - start), 1)
+                lse = lse_ref[0, h : h + 1, base + start : last]
+                probs = jnp.where(row <= col, jnp.exp(dot(k, q[start:], 1, 1) - lse), 0.0)
+                dscores = (probs * (dot(v, do[start:], 1, 1) - row_dot[:, start:])).astype(BF)
+                dk = dot(dscores, q[start:], 1, 0)
+                dv = dot(probs.astype(BF), do[start:], 1, 0)
+                dq = dot(turned[:, start:stop], dscores, 1, 0)
+                if start:
+                    dq_ref[:, start:] += dq
+                else:
+                    dq_ref[...] = dq
+                out_ref[0, rows, part + at : part + at + HEAD_DIM] = dk.astype(BF)
+                out_ref[0, rows, 2 * part + at : 2 * part + at + HEAD_DIM] = dv.astype(BF)
+            out_ref[0, base:last, at : at + HEAD_DIM] = (dq_ref[...].T * HEAD_DIM**-0.5).astype(BF)
+    sums = jnp.sum(out_ref[0].astype(F32), axis=0, keepdims=True)
+    grad = dot(low_ref[...], out_ref[0], 0, 0)
+    w = jnp.where(step == 0, w_one[...], w_two[...]).astype(F32)
+    shift = jnp.sum(w[:, : 3 * part] * sums, axis=-1, keepdims=True)
+    gain = jnp.sum(w[:, : 3 * part] * grad, axis=-1, keepdims=True)
+    gain = (gain - w[:, 577:578] * shift) / w[:, 576:577]
+    row = lax.broadcasted_iota(jnp.int32, (width, part), 0) - order[2 * half + step] * part
+    here = row == lax.broadcasted_iota(jnp.int32, (width, part), 1)
+    columns = [gain, shift] + [
+        jnp.sum(jnp.where(here, sums[:, at : at + part], 0.0), axis=-1, keepdims=True)
+        for at in (0, 2 * part)
+    ]
+    lane = lax.broadcasted_iota(jnp.int32, (width, 64), 1)
+    vecs = jnp.zeros((width, 64), F32)
+    if not half:
+        more = jnp.concatenate([two_ref[...], jnp.zeros((120, width), F32)]).T[:, :64]
+        vecs = jnp.where(step == 0, more, vecs)
+    for i, column in enumerate(columns):
+        vecs = jnp.where(lane == i, column, vecs)
+    stage[:, : 3 * part] = grad.astype(BF)
+    stage[:, 3 * part : 640] = vecs.astype(BF)
+    stage[:, 640 : 640 + part] = o_ref[0]
+    stage[:, 640 + part :] = jnp.zeros((width, SLAB - 640 - part), BF)
+    rows = width // 8
+    for g in range(2):
+
+        @pl.when(step == g)
+        def _(g=g):
+            copies = []
+            for i in range(8):
+                src = stage.at[pl.ds(pl.multiple_of(rows * table[i], 32), rows)]
+                copies.append(
+                    pltpu.make_async_copy(src, slabs[2 * g + i // 4].at[i % 4], sems.at[i])
+                )
+            for c in copies:
+                c.start()
+            for c in copies:
+                c.wait()
+
+
+def attend_back(half, order, table, qkv, ctx, dctx, lse, low, o_part, weights, two):
+    groups, count, part = qkv.shape
+    part //= 3
+    width = low.shape[1]
+    at = lambda g: (2 * half + g, 0, 0)
+    slab = (PLACED, (4, width // 8, SLAB), BF)
+    return call(
+        partial(attend_back_kernel, half), "attend_back", (2,),
+        [
+            SCALARS,
+            SCALARS,
+            pl.BlockSpec((1, count, 3 * part), at),
+            pl.BlockSpec((1, count, part), at),
+            pl.BlockSpec((1, count, part), at),
+            pl.BlockSpec((1, 8, count), at),
+            full((count, width)),
+            pl.BlockSpec((1, width, part), at),
         ]
-        ins, args = [chunk((rows, width))] + w, (x, *weights)
-    return call(
-        partial(project_kernel, half), "project", (count // rows,), [SCALARS] + ins, outs,
-        cost=(2 * count * width * 6 * part, 8_000_000, 0),
-        input_output_aliases={5: 0} if half else {},
-    )(order, *args)
-
-
-def attend_kernel(qkv_ref, *refs):
-    ctx_ref, lse_ref = refs[-2:]
-    length = qkv_ref.shape[1]
-    width = qkv_ref.shape[2] // 3
-    block = min(256, length)
-    lane = lax.broadcasted_iota(jnp.int32, (block, 128), 1)
-    row = lax.broadcasted_iota(jnp.int32, (block, block), 0)
-    col = lax.broadcasted_iota(jnp.int32, (block, block), 1)
-    for i in range(length // block):
-        start = i * block
-        stats = jnp.zeros((block, 128), F32)
-        for h in range(width // HEAD_DIM):
-            at = h * HEAD_DIM
-            q = qkv_ref[0, start : start + block, at : at + HEAD_DIM] * BF(HEAD_DIM**-0.5)
-            k = qkv_ref[0, : start + block, width + at : width + at + HEAD_DIM]
-            v = qkv_ref[0, : start + block, 2 * width + at : 2 * width + at + HEAD_DIM]
-            diag = jnp.where(col <= row, dot(q, k[start:], 1, 1), MASKED)
-            top = jnp.max(diag, axis=-1, keepdims=True)
-            if start:
-                past = dot(q, k[:start], 1, 1)
-                top = jnp.maximum(top, jnp.max(past, axis=-1, keepdims=True))
-            diag = jnp.exp(diag - top)
-            total = jnp.sum(diag, axis=-1, keepdims=True)
-            out = dot(diag.astype(BF), v[start:], 1, 0)
-            if start:
-                past = jnp.exp(past - top)
-                total += jnp.sum(past, axis=-1, keepdims=True)
-                out += dot(past.astype(BF), v[:start], 1, 0)
-            ctx_ref[0, start : start + block, at : at + HEAD_DIM] = (out / total).astype(BF)
-            stats = jnp.where(lane == h, top + jnp.log(total), stats)
-        lse_ref[0, start : start + block, :] = stats
-
-
-def attend(half, qkv, before=()):
-    groups, length, width = qkv.shape
-    width //= 3
-    at = lambda g, s: (2 * half + g, s, 0)
-    return call(
-        attend_kernel, "attend", (2, length // SEQ_LEN),
-        [pl.BlockSpec((1, SEQ_LEN, 3 * width), at)] + [PLACED] * len(before),
+        + [pl.BlockSpec((width, 640), lambda g: (0, 0), pipeline_mode=pl.Buffered(1))] * 2
+        + [full((8, width))],
+        [(pl.BlockSpec((1, count, 3 * part), lambda g: (g, 0, 0)), (2, count, 3 * part), BF)]
+        + [slab] * 4,
         [
-            (pl.BlockSpec((1, SEQ_LEN, width), at), (groups, length, width), BF),
-            (pl.BlockSpec((1, SEQ_LEN, 128), at), (groups, length, 128), F32),
+            pltpu.VMEM((HEAD_DIM, SEQ_LEN), F32),
+            pltpu.VMEM((width, SLAB), BF),
+            pltpu.SemaphoreType.DMA((8,)),
         ],
-        cost=(8_000_000_000, 5_000_000, 4_000_000),
-        input_output_aliases={1 + i: i for i in range(len(before))},
-    )(qkv, *before)
-
-
-def attend_back_kernel(qkv_ref, ctx_ref, dctx_ref, lse_ref, *refs):
-    out_ref, sum_ref, dq_ref = refs[-3:]
-    length = qkv_ref.shape[1]
-    width = qkv_ref.shape[2] // 3
-    heads = width // HEAD_DIM
-    block = min(256, length)
-    lane = lax.broadcasted_iota(jnp.int32, (length, 128), 1)
-    stats = lse_ref[0]
-    for h in range(heads):
-        at = h * HEAD_DIM
-        o = ctx_ref[0, :, at : at + HEAD_DIM].astype(F32)
-        do = dctx_ref[0, :, at : at + HEAD_DIM].astype(F32)
-        stats = jnp.where(lane == 8 + h, jnp.sum(o * do, axis=-1, keepdims=True), stats)
-    stats = stats.T
-    row = lax.broadcasted_iota(jnp.int32, (block, block), 0)
-    col = lax.broadcasted_iota(jnp.int32, (block, block), 1)
-    for h in range(heads):
-        at = h * HEAD_DIM
-        q = qkv_ref[0, :, at : at + HEAD_DIM] * BF(HEAD_DIM**-0.5)
-        do = dctx_ref[0, :, at : at + HEAD_DIM]
-        for j in range(length // block):
-            start = j * block
-            k = qkv_ref[0, start : start + block, width + at : width + at + HEAD_DIM]
-            v = qkv_ref[0, start : start + block, 2 * width + at : 2 * width + at + HEAD_DIM]
-            dk = None
-            for s, e, on_diag in ((start, start + block, True), (start + block, length, False)):
-                if s == e:
-                    continue
-                lse = stats[h : h + 1, s:e]
-                inner = stats[8 + h : 9 + h, s:e]
-                probs = jnp.exp(dot(k, q[s:e], 1, 1) - lse)
-                if on_diag:
-                    probs = jnp.where(row <= col, probs, 0.0)
-                dscores = (probs * (dot(v, do[s:e], 1, 1) - inner)).astype(BF)
-                dk_part = dot(dscores, q[s:e], 1, 0)
-                dv_part = dot(probs.astype(BF), do[s:e], 1, 0)
-                dq_part = dot(dscores, k, 0, 0)
-                dk = dk_part if dk is None else dk + dk_part
-                dv = dv_part if on_diag else dv + dv_part
-                if j == 0:
-                    dq_ref[s:e, :] = dq_part
-                else:
-                    dq_ref[s:e, :] += dq_part
-            out_ref[0, start : start + block, width + at : width + at + HEAD_DIM] = dk.astype(BF)
-            out_ref[0, start : start + block, 2 * width + at : 2 * width + at + HEAD_DIM] = (
-                dv.astype(BF)
-            )
-        out_ref[0, :, at : at + HEAD_DIM] = (dq_ref[...] * HEAD_DIM**-0.5).astype(BF)
-    sums = jnp.sum(out_ref[0].astype(F32), axis=0, keepdims=True)
-    first = pl.program_id(0) == 0
-
-    @pl.when(first)
-    def _():
-        sum_ref[0] = jnp.broadcast_to(sums, sum_ref.shape[1:])
-
-    @pl.when(jnp.logical_not(first))
-    def _():
-        sum_ref[0] += jnp.broadcast_to(sums, sum_ref.shape[1:])
-
-
-def attend_back(group, qkv, ctx, dctx, lse):
-    groups, length, width = qkv.shape
-    width //= 3
-    at = lambda s: (group, s, 0)
-    return call(
-        attend_back_kernel, "attend_back", (length // SEQ_LEN,),
-        [
-            pl.BlockSpec((1, SEQ_LEN, 3 * width), at),
-            pl.BlockSpec((1, SEQ_LEN, width), at),
-            pl.BlockSpec((1, SEQ_LEN, width), at),
-            pl.BlockSpec((1, SEQ_LEN, 128), at),
-        ],
-        [
-            (pl.BlockSpec((1, SEQ_LEN, 3 * width), lambda s: (0, s, 0)), (1, length, 3 * width), BF),
-            (full((1, 8, 3 * width)), (1, 8, 3 * width), F32),
-        ],
-        [pltpu.VMEM((SEQ_LEN, HEAD_DIM), F32)],
-        cost=(10_000_000_000, 4_000_000, 2_000_000),
-    )(qkv, ctx, dctx, lse)
-
-
-def slot_of(index, half, cap):
-    return index // (cap // 2) * cap + index % (cap // 2) + half * (cap // 2)
+        cost=(24_000_000_000, 14_000_000, 4_000_000),
+    )(order, table, qkv, ctx, dctx, lse, low, o_part, *weights, two)
 
 
 def dispatch_kernel(target_ref, rows_ref, out_ref):
@@ -301,7 +296,7 @@
     )(target.reshape(1, count), rows)[0]
 
 
-def mix_kernel(cap, order, x_ref, ctx_ref, vec_ref, target_ref, *refs):
+def mix_kernel(order, x_ref, ctx_ref, vec_ref, target_ref, *refs):
     wo_refs, (h_ref, whole_ref, *sent, low_ref) = refs[:GROUPS], refs[GROUPS:]
     rows, width = x_ref.shape
     count = low_ref.shape[0]
@@ -312,7 +307,7 @@
     def _():
         for q in range(GROUPS):
             at = pl.ds(pl.multiple_of(order[q] * part, 64), part)
-            pieces = [wo[at, :part] for wo in wo_refs]
+            pieces = [wo[at, :] for wo in wo_refs]
             for n in range(GROUPS):
                 piece = pieces[0]
                 for r in range(1, GROUPS):
@@ -332,22 +327,19 @@
     def _():
         for half in range(2):
             for at in range(0, count // 2, 256):
-                index = lax.broadcasted_iota(jnp.int32, (256, count), 0) + at
-                picks = (target_ref[...] == slot_of(index, half, cap)).astype(F32).astype(BF)
+                index = lax.broadcasted_iota(jnp.int32, (256, count), 0) + (half * count // 2 + at)
+                picks = (target_ref[...] == index).astype(F32).astype(BF)
                 sent[half][at : at + 256] = dot(picks, low_ref[...], 1, 0).astype(BF)
 
 
-def mix(order, x, ctx, weights, vec, target, cap):
+def mix(order, x, ctx, weights, vec, target):
     count, width = x.shape
     part = width // GROUPS
     rows = min(256, count)
-    columns = pl.BlockSpec(
-        (pl.Element(width), pl.Element(256)), lambda *_: (0, 640), pipeline_mode=pl.Buffered(1)
-    )
     return call(
-        partial(mix_kernel, cap), "mix", (count // rows,),
+        mix_kernel, "mix", (count // rows,),
         [SCALARS, chunk((rows, width)), chunk((GROUPS, rows, part), 1), full((8, width)),
-         full((1, count))] + [columns] * GROUPS,
+         full((1, count))] + [full((width, part))] * GROUPS,
         [
             (chunk((rows, width)), (count, width), F32),
             (full((width, width)), (width, width), BF),
@@ -360,7 +352,7 @@
 
 
 def unmix_kernel(
-    cap, order, h_ref, g_ref, dm_one, dm_two, target_ref, ctx_ref, whole_ref, vec_ref,
+    order, h_ref, g_ref, dm_one, dm_two, target_ref, ctx_ref, whole_ref, vec_ref,
     dh_ref, dctx_ref, grad_ref, sum_ref, total_ref,
 ):
     rows, width = h_ref.shape
@@ -368,8 +360,8 @@
     step = pl.program_id(0)
     dm = None
     for half, sent in enumerate((dm_one, dm_two)):
-        index = lax.broadcasted_iota(jnp.int32, (rows, sent.shape[0]), 1)
-        picks = (target_ref[...] == slot_of(index, half, cap)).astype(F32).astype(BF)
+        index = lax.broadcasted_iota(jnp.int32, (rows, sent.shape[0]), 1) + half * sent.shape[0]
+        picks = (target_ref[...] == index).astype(F32).astype(BF)
         got = dot(picks, sent[...], 1, 0)
         dm = got if dm is None else dm + got
     unit, inverse = normalize(h_ref[...])
@@ -409,14 +401,14 @@
                 grad_ref[r, at, :] = piece
 
 
-def unmix(order, h, g, dm_one, dm_two, target, ctx, whole, vec, cap):
+def unmix(order, h, g, dm_one, dm_two, target, ctx, whole, vec):
     count, width = h.shape
     part = width // GROUPS
     rows = min(256, count)
     half = full((count // 2, width))
     by_rows, by_ctx = chunk((rows, width)), chunk((GROUPS, rows, part), 1)
     return call(
-        partial(unmix_kernel, cap), "unmix", (count // rows,),
+        unmix_kernel, "unmix", (count // rows,),
         [SCALARS, by_rows, by_rows, half, half, chunk((rows, 1)), by_ctx, full((width, width)),
          full((8, width))],
         [
@@ -622,12 +614,12 @@
 
 
 def unproject_kernel(*refs):
-    grad_refs, w_refs = refs[:GROUPS], refs[GROUPS : 2 * GROUPS]
-    x_ref, dh_ref, vec_ref, out_ref = refs[2 * GROUPS :]
+    one_ref, two_ref, *w_refs = refs[: GROUPS + 2]
+    x_ref, dh_ref, vec_ref, out_ref = refs[GROUPS + 2 :]
     part = x_ref.shape[1] // GROUPS
     da = None
-    for grad, w in zip(grad_refs, w_refs):
-        got = dot(grad[0], w[:, : 3 * part], 1, 1)
+    for r, w in enumerate(w_refs):
+        got = dot((one_ref, two_ref)[r // 2][r % 2], w[:, : 3 * part], 1, 1)
         da = got if da is None else da + got
     unit, inverse = normalize(x_ref[...].astype(F32))
     out_ref[...] = dh_ref[...] + normalize_back(da, unit, inverse, vec_ref[0:1])
@@ -640,102 +632,11 @@
     w = pl.BlockSpec((width, 640), lambda i: (0, 0), pipeline_mode=pl.Buffered(1))
     return call(
         unproject_kernel, "unproject", (count // rows,),
-        [chunk((1, rows, 3 * part), 1)] * GROUPS + [w] * GROUPS
+        [chunk((2, rows, 3 * part), 1)] * 2 + [w] * GROUPS
         + [chunk((rows, width)), chunk((rows, width)), full((8, width))],
         [(chunk((rows, width)), (count, width), F32)],
         cost=(6 * count * width * width, 20_000_000, 0),
     )(*grads, *weights, x, dh, vec)[0]
-
-
-def slope_kernel(group, extra, staged, halves, order, *refs):
-    if staged:
-        table, *refs = refs
-    low_ref, grad_ref, sum_ref, o_ref, w_ref, two_ref = refs[:6]
-    more, refs = refs[6 : 6 + extra], refs[6 + extra :]
-    if staged:
-        keep_ref, send_ref, stage, sems = refs
-    elif halves:
-        outs = refs
-    else:
-        outs = refs[:1]
-    width = low_ref.shape[1]
-    part = width // GROUPS
-    grad = dot(low_ref[...], grad_ref[0], 0, 0)
-    w = w_ref[...].astype(F32)
-    sums = sum_ref[0, 0:1]
-    shift = jnp.sum(w[:, : 3 * part] * sums, axis=-1, keepdims=True)
-    gain = jnp.sum(w[:, : 3 * part] * grad, axis=-1, keepdims=True)
-    gain = (gain - w[:, 577:578] * shift) / w[:, 576:577]
-    row = lax.broadcasted_iota(jnp.int32, (width, part), 0) - order[group] * part
-    here = row == lax.broadcasted_iota(jnp.int32, (width, part), 1)
-    columns = [gain, shift] + [
-        jnp.sum(jnp.where(here, sums[:, at : at + part], 0.0), axis=-1, keepdims=True)
-        for at in (0, 2 * part)
-    ]
-    lane = lax.broadcasted_iota(jnp.int32, (width, 64), 1)
-    if group:
-        vecs = jnp.zeros((width, 64), F32)
-    else:
-        vecs = jnp.concatenate([two_ref[...], jnp.zeros((120, width), F32)]).T[:, :64]
-    for i, column in enumerate(columns):
-        vecs = jnp.where(lane == i, column, vecs)
-    o = o_ref[0].astype(F32)
-    if extra:
-        more = [more[:1]] + [more[1:]] * (extra > 1)
-    for refs in more:
-        got = jnp.concatenate([ref[...] for ref in refs]) if len(refs) > 1 else refs[0][...]
-        grad += got[:, : 3 * part].astype(F32)
-        vecs += got[:, 3 * part : 640].astype(F32)
-        o += got[:, 640 : 640 + part].astype(F32)
-    if staged:
-        outs = (stage,)
-    rows = width // len(outs)
-    for i, out in enumerate(outs):
-        at = slice(i * rows, i * rows + rows)
-        out[:, : 3 * part] = grad[at].astype(BF)
-        out[:, 3 * part : 640] = vecs[at].astype(BF)
-        out[:, 640 : 640 + part] = o[at].astype(BF)
-        out[:, 640 + part :] = jnp.zeros((rows, SLAB - 640 - part), BF)
-    if staged:
-        rows = width // 8
-        copies = []
-        for i in range(8):
-            src = stage.at[pl.ds(pl.multiple_of(rows * table[i], 32), rows)]
-            copies.append(
-                pltpu.make_async_copy(src, (keep_ref, send_ref)[i // 4].at[i % 4], sems.at[i])
-            )
-        for c in copies:
-            c.start()
-        for c in copies:
-            c.wait()
-
-
-def slope(group, order, low, grads, o_part, w, two, more=(), table=None, halves=False):
-    count, width = low.shape
-    part = width // GROUPS
-    cols = 3 * part
-    ins = [
-        full((count, width)),
-        full((1, count, cols)),
-        full((1, 8, cols)),
-        pl.BlockSpec((1, width, part), lambda i: (group, 0, 0)),
-        pl.BlockSpec((width, 640), lambda i: (0, 0), pipeline_mode=pl.Buffered(1)),
-        full((8, width)),
-    ] + [full(m.shape) for m in more]
-    args = (low, *grads, o_part, w, two, *more)
-    if table is None:
-        rows = width // (1 + halves)
-        outs, scratch = [(full((rows, SLAB)), (rows, SLAB), BF)] * (1 + halves), []
-    else:
-        ins, args = [SCALARS] + ins, (table, *args)
-        outs = [(PLACED, (4, width // 8, SLAB), BF)] * 2
-        scratch = [pltpu.VMEM((width, SLAB), BF), pltpu.SemaphoreType.DMA((8,))]
-    got = call(
-        partial(slope_kernel, group, len(more), table is not None, halves), "slope", (1,),
-        [SCALARS] + ins, outs, scratch,
-        cost=(2 * count * width * cols, 6_000_000, 0),
-    )(order, *args)
-    return got if table is not None or halves else got[0]
 
 
 def add(a, b):
@@ -792,47 +693,49 @@
     return lax.psum_scatter(parts, BOTH, scatter_dimension=0, tiled=False)
 
 
-def fetch(place, table, weights, vectors, filler):
+def fetch(place, table, weights, out_weights, vectors, filler):
+    barrier = lax.optimization_barrier
     stacked = jnp.stack(vectors)
     pad = 64 - len(vectors)
     if place.staged:
-        rows, cols = weights[0].shape
+        rows = out_weights.shape[0]
         extra = jnp.concatenate([stacked.T, jnp.zeros((rows, pad), BF)], axis=1)
-        rest = jnp.zeros((rows, SLAB - 64 - 4 * cols), BF)
-        shard = jnp.concatenate([*weights[:3], extra, weights[3], rest], axis=1)
+        shard = jnp.concatenate([*weights, extra], axis=1)
         own = jnp.stack([shard] + [place.move(shard, way) for way in place.z])
+        own, out_weights = barrier((own, out_weights))
         got = place.move(own, place.y)
-        got, filler = lax.optimization_barrier((got, filler))
+        out_own = jnp.stack([out_weights] + [place.move(out_weights, way) for way in place.z])
+        got, filler, out_own = barrier((got, filler, out_own))
         near = assemble(table, own, got)
         across = place.move(near, place.x)
         far = place.move(near, place.core)
-        return near, far, across, filler
+        return (near, far, across), (out_own, place.move(out_own, place.y)), filler
     vecs = lax.all_gather(stacked, "expert", axis=1, tiled=True)
     width = vecs.shape[1]
     extra = jnp.concatenate([vecs, jnp.zeros((pad, width), BF)]).T
     extra = jnp.broadcast_to(extra[None], (GROUPS, width, 64))
     by_group = lambda w: gather_all(w).reshape(width, GROUPS, -1).transpose(1, 0, 2)
-    weights = [by_group(w) for w in weights]
-    rest = jnp.zeros((GROUPS, width, SLAB - 64 - 4 * (width // GROUPS)), BF)
-    grouped = jnp.concatenate([*weights[:3], extra, weights[3], rest], axis=2)
-    return grouped[0], grouped[1], grouped[2:], filler
-
-
-def reduce_last(place, keep, send, count, first, second, later):
-    barrier = lax.optimization_barrier
+    grouped = jnp.concatenate([*(by_group(w) for w in weights), extra], axis=2)
+    out = by_group(out_weights)
+    return [grouped[i] for i in range(GROUPS)], [out[i] for i in range(GROUPS)], filler
+
+
+def reduce_y(place, keep, send):
+    got = place.move(send, place.y)
+    return keep[0].astype(F32) + got[0].astype(F32), [add(keep[k], got[k]) for k in range(1, 4)]
+
+
+def reduce_z(place, sends):
+    return [place.move(part, way) for part, way in zip(sends, place.z)]
+
+
+def columns_of(place, total, count):
     cols = (SLAB - 128) // 4
-    got, first, later = barrier((place.move(send, place.y), first(), later))
-    sends = [add(keep[k], got[k]) for k in range(1, 4)]
-    total = keep[0].astype(F32) + got[0].astype(F32)
-    got = [place.move(part, way) for part, way in zip(sends, place.z)]
-    got, second = barrier((got, second(*later)))
-    for part in got:
-        total += part.astype(F32)
     parts = [total[:, i : i + cols] for i in (0, cols, 2 * cols, 640)]
     vecs = total[:, 576 : 576 + 8].T
     vecs = vecs + place.move(vecs, place.core)
     vecs = vecs + place.move(vecs, place.x)
-    return parts, [vecs[i] for i in range(count)], first, second
+    return parts, [vecs[i] for i in range(count)]
 
 
 def reduce_plain(slabs, count):
@@ -882,17 +785,22 @@
 
     chosen = assignments[:, None] == lax.broadcasted_iota(jnp.int32, (count, experts), 1)
     limit = jnp.sum(jnp.where(chosen, specialist_quotas[None, :], 0), axis=1)
-    target = jnp.where(positions_within < limit, assignments * cap + positions_within, count)
+    kept = positions_within < limit
+    target = jnp.where(kept, assignments * cap + positions_within, count)
+    late = positions_within >= cap // 2
+    halved = jnp.where(late, positions_within + (count - cap) // 2, positions_within)
+    halved = jnp.where(kept, assignments * (cap // 2) + halved, count)
 
     def exchange(rows):
         sent = rows.reshape(experts, -1, width)
         got = lax.all_to_all(sent, "expert", split_axis=0, concat_axis=0, tiled=True)
         return got.reshape(rows.shape)
 
-    near, far, across, sent_g = fetch(
+    weights, out, sent_g = fetch(
         place,
         table,
-        (asking_weights, lookup_weights, content_weights, context_mixing_weights),
+        (asking_weights, lookup_weights, content_weights),
+        context_mixing_weights,
         (
             standardize_one_scale,
             standardize_one_shift,
@@ -904,20 +812,25 @@
         ),
         dispatch(target, upstream_adjoint),
     )
-    sent_g, far = barrier((sent_g, far))
+
+    sent_g, first = barrier((sent_g, weights[1]))
+    weights = (weights[0], first, *weights[2:])
     rows_g = exchange(sent_g).reshape(experts, 2, cap // 2, width)
 
-    qkv, low_in, vec = project(0, order, (near, far), x=block_entries)
-    ctx = attend(0, qkv)
+    *before, low_in, vec = attend(0, order, weights[:2], x=block_entries)
     if place.staged:
-        ctx, across = barrier((ctx, across))
-        weights = (near, far, across, place.move(across, place.core))
-    else:
-        weights = (near, far, across[0], across[1])
-    (qkv,) = project(1, order, weights[2:], low=low_in, vec=vec, qkv=qkv)
-    ctx, lse = attend(1, qkv, ctx)
+        before, out = barrier((before, out))
+        out_near = assemble(table, *out)
+        before, across, out_near = barrier((before, weights[2], out_near))
+        weights = (*weights[:2], across, place.move(across, place.core))
+        out_across = place.move(out_near, place.x)
+        out = (out_near, place.move(out_near, place.core))
+    qkv, ctx, lse = attend(1, order, weights[2:], low=low_in, vec=vec, before=before)
     ctx, rows_g = barrier((ctx, rows_g))
-    h1, whole_o, sent_one, sent_two = mix(order, block_entries, ctx, weights, vec, target, cap)
+    if place.staged:
+        ctx, out_across = barrier((ctx, out_across))
+        out += (out_across, place.move(out_across, place.core))
+    h1, whole_o, sent_one, sent_two = mix(order, block_entries, ctx, out, vec, halved)
 
     x_one = exchange(sent_one)
     x_one, sent_two = barrier((x_one, sent_two))
@@ -955,43 +868,50 @@
     gy = exchange(gy.reshape(count, width))
 
     dh1, dctx, grad_o, two = unmix(
-        order, h1, upstream_adjoint, dm_one, dm_two, target, ctx, whole_o, vec, cap
-    )
-    back = lambda r, dctx: attend_back(r, qkv, ctx, dctx, lse)
-    tilt = lambda r, grads, *rest: slope(r, order, low_in, grads, grad_o, weights[r], two, *rest)
+        order, h1, upstream_adjoint, dm_one, dm_two, halved, ctx, whole_o, vec
+    )
+    back = lambda half, dctx: attend_back(
+        half, order, table, qkv, ctx, dctx, lse, low_in, grad_o, weights[2 * half : 2 * half + 2],
+        two,
+    )
     if place.staged:
-        three = back(3, dctx)
-        slab = tilt(3, three)
-        dctx, slab = barrier((dctx, slab))
-        more = place.move(slab, place.core)
-        duo = back(2, dctx)
-        slab, rest = tilt(2, duo, (more,), None, True)
-        dctx, slab, rest, gy, came = barrier((dctx, slab, rest, gy, came))
-        across = place.move(slab, place.x)
-        one = back(1, dctx)
-        slab = tilt(1, one)
-        dctx, slab, across = barrier((dctx, slab, across))
-        more = place.move(slab, place.core)
-        across = (across, place.move(rest, place.x))
-        zero = back(0, dctx)
-        keep, send = tilt(0, zero, (more, *across), table)
-        last, send, came, gy = barrier((zero[0], send, came, gy))
-        dqkv = (last, one[0], duo[0], three[0])
-
-        def finishing(gy, came):
-            pick = lambda at: sum(
-                a[at : at + width].astype(F32) for a in (grads, came_far[1], came)
-            )
-            return finish(h1, target, gy), pick(0), pick(width), pick(2 * width)
-
-        (sum_q, sum_k, sum_v, sum_o), small, input_grad, (output, *grads) = reduce_last(
-            place, keep, send, 7, lambda: unproject(dqkv, weights, block_entries, dh1, vec),
-            finishing, (gy, came),
+        far, keep, send, *more = back(1, dctx)
+        more = [place.move(m, place.core) for m in more]
+        far, gy = barrier((far, gy))
+        output = finish(h1, target, gy)
+        send = add(send, more[1])
+        dctx, output, send = barrier((dctx, output, send))
+        across, sends = reduce_y(place, add(keep, more[0]), send)
+        near, keep, send, *more = back(0, dctx)
+        near, sends = barrier((near, sends))
+        more = [place.move(m, place.core) for m in more]
+        got = reduce_z(place, sends)
+        send, keep = add(send, more[1]), add(keep, more[0])
+        near, send = barrier((near, send))
+        got_y = place.move(send, place.y)
+        input_grad = unproject((near, far), weights, block_entries, dh1, vec)
+        got, input_grad = barrier((got, input_grad))
+        across = (across + sum(g.astype(F32) for g in got)).astype(BF)
+        across = place.move(across, place.x)
+        got, input_grad, came = barrier((got_y, input_grad, came))
+        total = keep[0].astype(F32) + got[0].astype(F32)
+        got = reduce_z(place, [add(keep[k], got[k]) for k in range(1, 4)])
+        pick = lambda at: sum(
+            a[at : at + width].astype(F32) for a in (grads, came_far[1], came)
         )
+        got, grads, across = barrier((got, [pick(0), pick(width), pick(2 * width)], across))
+        total += across.astype(F32)
+        total += sum(g.astype(F32) for g in got)
+        (sum_q, sum_k, sum_v, sum_o), small = columns_of(place, total, 7)
     else:
-        parts = [back(r, dctx) for r in range(GROUPS)]
+        parts = [back(half, dctx) for half in range(2)]
         (sum_q, sum_k, sum_v, sum_o), small = reduce_plain(
-            [tilt(r, parts[r]) for r in range(GROUPS)], 7
+            [
+                jnp.concatenate(p[1 + 2 * g : 3 + 2 * g]).reshape(width, SLAB)
+                for p in parts
+                for g in range(2)
+            ],
+            7,
         )
         input_grad = unproject([p[0] for p in parts], weights, block_entries, dh1, vec)
         output = finish(h1, target, gy)

time: 379 us -> 346 us (0.913)
  Pallas kernels: 228 us -> 192 us
  starting transfers between devices: 51.4 us -> 57.7 us
  other arithmetic: 16.8 us -> 22.1 us
  blocking collectives: 29.8 us -> 24.9 us
    pallas_call x15 -> x7, Pallas kernels: 147 us -> 109 us  [the longest x2 45.3 us: attend_back(): call(partial(attend_back_kernel, half), 'attend_back', (2,), [SCALARS, SC...]
    ppermute x19 -> x31, starting transfers between devices: 19.7 us -> 32.6 us  [move(): return lax.ppermute(array, BOTH, way)]
    all_to_all x5, starting transfers between devices: 31.7 us -> 25.1 us  [exchange(): lax.all_to_all(sent, 'expert', split_axis=0, concat_axis=0, tiled=True)]
    ppermute x19 -> x31, waiting for transfers between devices: 37 us -> 32 us  [move(): return lax.ppermute(array, BOTH, way)]
    all_to_all x1, blocking collectives: 29.8 us -> 24.9 us  [exchange(): lax.all_to_all(sent, 'expert', split_axis=0, concat_axis=0, tiled=True)]
    convert_element_type x2 -> x7, other arithmetic: 5.25 us -> 9.46 us  [add(): return (a.astype(F32) + b.astype(F32)).astype(BF)]
  transfers between devices with their start and end apart: 24 -> 36, of which waited for: 10 -> 16; matrix products, arithmetic and copies ran while one was open for 5% -> 7% of each run, Pallas kernels for 55% -> 52%
where the time goes in v3:
time: 346 us; the launch traced here: 342 us
  Pallas kernels  192 us (55%)
  starting transfers between devices  57.7 us (17%)
  waiting for transfers between devices  35.3 us (10%)
  blocking collectives  24.9 us (7%)
  other arithmetic  22.1 us (6%)
  local copies, waits for them, and re-layouts  9.47 us (3%)
    pallas_call x2, Pallas kernels, expert(): call(expert_kernel, 'expert', (ff // step,), [full((rows, width)), side,...  48.2 us
    pallas_call x2, Pallas kernels, attend_back(): call(partial(attend_back_kernel, half), 'attend_back', (2,), [SCALARS, SC...  45.3 us
    ppermute x31, starting transfers between devices, move(): return lax.ppermute(array, BOTH, way)  32.6 us
    ppermute x31, waiting for transfers between devices, move(): return lax.ppermute(array, BOTH, way)  32 us
    pallas_call x2, Pallas kernels, attend(): call(partial(attend_kernel, half), 'attend', (2,), [SCALARS] + ins, outs,...  27.5 us
    all_to_all x5, starting transfers between devices, exchange(): lax.all_to_all(sent, 'expert', split_axis=0, concat_axis=0, tiled=True)  25.1 us
    all_to_all x1, blocking collectives, exchange(): lax.all_to_all(sent, 'expert', split_axis=0, concat_axis=0, tiled=True)  24.9 us
    pallas_call x1, Pallas kernels, weigh(): call(partial(weigh_kernel, split), 'weigh', (n,), [wide] * 4 + [full((row...  18.3 us
  transfers between devices with their start and end apart: 36, of which 16 were waited for; matrix products, arithmetic and copies ran while one was open for 7% of the time, Pallas kernels for 52%

profile of v3, /device:TPU:0, one launch (start us, length us, event | category | flops | bytes accessed | tf_op | source)
XLA Modules:
  0.0 342.4 jit_solution(10247632467995385952)
XLA Ops:
  2.5 4.1 %collective-permute-start.1 = (bf16[96,640]{1,0:T(8,128)(2,1)S(1)}, bf16[96,640]{1,0:T(8,128)(2,1)S(1)}, u32[]{:S(2)}, u32[]{:S(2)}) collective-permute-start(bf16[96,640]{1,0:T(8,128)(2,1)S(1)} %concatenate.3), channel_id=1, source_target_pairs={{0,4},{1,5},{2,6},{3,7},{4,0},{5,1},{6,2},{7,3},{8,12},{9,13},{10,... | collective-permute-start | bytes 368648 | tf_op jit(solution)/shard_map/ppermute | solution.py:674
  6.6 1.3 collective-permute-start.2
  9.0 1.3 fusion.13
  10.3 5.8 %collective-permute-done.1 = bf16[96,640]{1,0:T(8,128)(2,1)S(1)} collective-permute-done((bf16[96,640]{1,0:T(8,128)(2,1)S(1)}, bf16[96,640]{1,0:T(8,128)(2,1)S(1)}, u32[]{:S(2)}, u32[]{:S(2)}) %collective-permute-start.1) | collective-permute-done | bytes 122912 | tf_op jit(solution)/shard_map/ppermute | solution.py:674
  16.7 1.6 collective-permute-start.3
  19.6 4.4 %dispatch.1 = bf16[1024,768]{1,0:T(8,128)(2,1)} custom-call(s32[1,1024]{1,0:T(1,128)} %bitcast.107, bf16[1024,768]{1,0:T(8,128)(2,1)} %g_ref.1), custom_call_target="tpu_custom_call" | custom-call | flops 1610612736 | bytes 3000000 | tf_op jit(solution)/shard_map/dispatch/pallas_call | solution.py:291
  24.0 2.0 collective-permute-start.4
  26.0 2.1 collective-permute-start.5
  28.0 1.3 collective-permute-start.6
  29.9 1.5 collective-permute-done.5
  31.4 2.6 collective-permute-done.6
  35.5 3.0 assemble.2.refs_1_.refs_6_.refs_2_
  39.1 1.5 collective-permute-start.9
  41.3 4.0 %all-to-all-start = ((bf16[8,128,768]{2,1,0:T(8,128)(2,1)}), bf16[8,128,768]{2,1,0:T(8,128)(2,1)S(1)}, u32[]{:S(2)}, u32[]{:S(2)}) async-start(bf16[8,128,768]{2,1,0:T(8,128)(2,1)} %bitcast.17), calls=%async_computation | async-start | bytes 3145728 | tf_op jit(solution)/shard_map/all_to_all | solution.py:796
  45.3 14.3 %attend.2 = (bf16[4,1024,576]{2,1,0:T(8,128)(2,1)}, bf16[4,1024,192]{2,1,0:T(8,128)(2,1)}, f32[4,8,1024]{2,1,0:T(8,128)}, bf16[1024,768]{1,0:T(8,128)(2,1)}, f32[8,768]{1,0:T(8,128)}) custom-call(s32[4]{0:T(128)} %get-tuple-element.245.order, bf16[1024,768]{1,0:T(8,128)(2,1)} %refs_6_.1, bf16[768,640]{1,0:T(8,128)(2,1)} %assemble.2.refs_1_.refs_6_.refs_2_, ...), custom_call_target="tpu_custom_call" | custom-call | flops 12000000000 | bytes 8000000 | tf_op jit(solution)/shard_map/attend/pallas_call | solution.py:167
  59.7 2.5 assemble.3.refs_0_
  63.4 1.5 collective-permute-start.11
  67.0 13.2 %attend.3 = (bf16[4,1024,576]{2,1,0:T(8,128)(2,1)}, bf16[4,1024,192]{2,1,0:T(8,128)(2,1)}, f32[4,8,1024]{2,1,0:T(8,128)}) custom-call(s32[4]{0:T(128)} %get-tuple-element.245.order, bf16[1024,768]{1,0:T(8,128)(2,1)} %get-tuple-element.124.refs_0_.refs_4_, ...), custom_call_target="tpu_custom_call", output_to_operand_aliasing={{0}: (5, {}), {1}: (6, {}), {2}: (7, {})} | custom-call | flops 12000000000 | bytes 8000000 | tf_op jit(solution)/shard_map/attend/pallas_call | solution.py:167
  80.2 2.4 all-to-all-done
  82.6 1.9 collective-permute-done.13.refs_3_
  85.2 10.1 %mix.1 = (f32[1024,768]{1,0:T(8,128)}, bf16[768,768]{1,0:T(8,128)(2,1)}, bf16[512,768]{1,0:T(8,128)(2,1)}, bf16[512,768]{1,0:T(8,128)(2,1)}) custom-call(s32[4]{0:T(128)} %get-tuple-element.245.order, bf16[1024,768]{1,0:T(8,128)(2,1)} %refs_6_.1, bf16[4,1024,192]{2,1,0:T(8,128)(2,1)} %get-tuple-element.143.ctx_ref.refs_1_, ...), custom_call_target="tpu_custom_call" | custom-call | flops 2818572288 | bytes 12000000 | tf_op jit(solution)/shard_map/mix/pallas_call | solution.py:339
  95.4 24.9 %all_to_all.30 = bf16[8,64,768]{2,1,0:T(8,128)(2,1)} all-to-all(bf16[8,64,768]{2,1,0:T(8,128)(2,1)} %bitcast.95), channel_id=1, replica_groups=mesh['dp'=4,'expert'=8] {'expert'}, dimensions={0} | all-to-all | bytes 1572864 | tf_op jit(solution)/shard_map/all_to_all | solution.py:796
  120.3 3.6 %all-to-all-start.2 = ((bf16[8,64,768]{2,1,0:T(8,128)(2,1)}), bf16[8,64,768]{2,1,0:T(8,128)(2,1)S(1)}, u32[]{:S(2)}, u32[]{:S(2)}) async-start(bf16[8,64,768]{2,1,0:T(8,128)(2,1)} %bitcast.94), calls=%async_computation.2 | async-start | bytes 1572864 | tf_op jit(solution)/shard_map/all_to_all | solution.py:796
  123.9 24.1 %expert.2 = (bf16[8,2,64,768]{3,2,1,0:T(8,128)(2,1)}, bf16[512,768]{1,0:T(8,128)(2,1)}, bf16[512,768]{1,0:T(8,128)(2,1)}, bf16[512,3072]{1,0:T(8,128)(2,1)}, bf1...) custom-call(bf16[512,768]{1,0:T(8,128)(2,1)} %bitcast.87, bf16[8,2,64,768]{3,2,1,0:T(8,128)(2,1)} %bitcast.83, ...), custom_call_target="tpu_custom_call" | custom-call | flops 9663676416 | bytes 22000000 | tf_op jit(solution)/shard_map/expert/pallas_call | solution.py:523
  148.0 6.0 %all-to-all-start.3 = ((bf16[8,64,768]{2,1,0:T(8,128)(2,1)}), bf16[8,64,768]{2,1,0:T(8,128)(2,1)S(1)}, u32[]{:S(2)}, u32[]{:S(2)}) async-start(bf16[8,64,768]{2,1,0:T(8,128)(2,1)} %bitcast.93), calls=%async_computation.3 | async-start | bytes 1572864 | tf_op jit(solution)/shard_map/all_to_all | solution.py:796
  154.0 24.2 %expert.3 = (bf16[8,2,64,768]{3,2,1,0:T(8,128)(2,1)}, bf16[512,768]{1,0:T(8,128)(2,1)}, bf16[512,768]{1,0:T(8,128)(2,1)}, bf16[512,3072]{1,0:T(8,128)(2,1)}, bf1...) custom-call(bf16[512,768]{1,0:T(8,128)(2,1)} %bitcast.90, ...), custom_call_target="tpu_custom_call", output_to_operand_aliasing={{0}: (7, {})} | custom-call | flops 9663676416 | bytes 22000000 | tf_op jit(solution)/shard_map/expert/pallas_call | solution.py:523
  178.2 6.0 %all-to-all-start.4 = ((bf16[8,64,768]{2,1,0:T(8,128)(2,1)}), bf16[8,64,768]{2,1,0:T(8,128)(2,1)S(1)}, u32[]{:S(2)}, u32[]{:S(2)}) async-start(bf16[8,64,768]{2,1,0:T(8,128)(2,1)} %bitcast.92), calls=%async_computation.4 | async-start | bytes 1572864 | tf_op jit(solution)/shard_map/all_to_all | solution.py:796
  184.2 18.3 %weigh.1 = (bf16[2,1552,768]{2,1,0:T(8,128)(2,1)}, bf16[1552,768]{1,0:T(8,128)(2,1)}, bf16[1552,768]{1,0:T(8,128)(2,1)}) custom-call(s32[4]{0:T(128)} %get-tuple-element.244.which, bf16[512,3072]{1,0:T(8,128)(2,1)} %get-tuple-element.149.refs_0_, bf16[512,3072]{1,0:T(8,128)(2,1)} %get-tuple-element.157.refs_1_, ...), custom_call_target="tpu_custom_call" | custom-call | flops 9663676416 | bytes 26000000 | tf_op jit(solution)/shard_map/weigh/pallas_call | solution.py:606
  204.6 5.4 %all-to-all-start.5 = ((bf16[8,128,768]{2,1,0:T(8,128)(2,1)}), bf16[8,128,768]{2,1,0:T(8,128)(2,1)S(1)}, u32[]{:S(2)}, u32[]{:S(2)}) async-start(bf16[8,128,768]{2,1,0:T(8,128)(2,1)} %bitcast.33), calls=%async_computation.5 | async-start | bytes 3145728 | tf_op jit(solution)/shard_map/all_to_all | solution.py:796
  210.0 1.8 collective-permute-done.14
  211.8 4.4 %fusion = bf16[1552,768]{1,0:T(8,128)(2,1)} fusion(bf16[1552,768]{1,0:T(8,128)(2,1)} %get-tuple-element.166, bf16[2,1552,768]{2,1,0:T(8,128)(2,1)} %collective-permute-done.14), kind=kLoop, calls=%fused_computation.1 | loop fusion | flops 4767744 | bytes 7151616 | tf_op jit(solution)/shard_map/convert_element_type | solution.py:643
  216.2 15.5 %unmix.1 = (f32[1024,768]{1,0:T(8,128)}, bf16[4,1024,192]{2,1,0:T(8,128)(2,1)}, bf16[4,768,192]{2,1,0:T(8,128)(2,1)}, f32[8,768]{1,0:T(8,128)}) custom-call(s32[4]{0:T(128)} %get-tuple-element.245.order, f32[1024,768]{1,0:T(8,128)} %get-tuple-element.172.h_ref, bf16[1024,768]{1,0:T(8,128)(2,1)} %g_ref.1, bf16[512,768]{1,0:T(8,128)(2,1)} %bitcast.85, ...), custom_call_target="tpu_custom_call" | custom-call | flops 4026531840 | bytes 20000000 | tf_op jit(solution)/shard_map/unmix/pallas_call | solution.py:410
  231.7 22.6 %attend_back.2 = (bf16[2,1024,576]{2,1,0:T(8,128)(2,1)}, bf16[4,96,896]{2,1,0:T(8,128)(2,1)}, bf16[4,96,896]{2,1,0:T(8,128)(2,1)}, bf16[4,96,896]{2,1,0:T(8,128)(2,1)}, bf16[4,96,896]{2,1,0:T(8,128)(2,1)}) custom-call(s32[4]{0:T(128)} %get-tuple-element.245.order, s32[8]{0:T(128)} %fusion.19.table, bf16[4,1024,576]{2,1,0:T(8,128)(2,1)} %get-tuple-element.177.refs_0_, ...), custom_call_target="tpu_custom_call" | custom-call | flops 24000000000 | bytes 14000000 | tf_op jit(solution)/shard_map/attend_back/pallas_call | solution.py:256
  255.9 1.5 collective-permute-start.23
  257.4 6.0 %finish.1 = bf16[1024,768]{1,0:T(8,128)(2,1)} custom-call(f32[1024,768]{1,0:T(8,128)} %get-tuple-element.172.h_ref, s32[1024,1]{1,0:T(8,128)} %copy.64.target_ref, bf16[1024,768]{1,0:T(8,128)(2,1)} %bitcast.80), custom_call_target="tpu_custom_call" | custom-call | flops 1610612736 | bytes 6000000 | tf_op jit(solution)/shard_map/finish/pallas_call | solution.py:434
  263.4 2.1 add_convert_fusion.3
  265.6 1.3 collective-permute-start.17
  266.9 22.7 %attend_back.3 = (bf16[2,1024,576]{2,1,0:T(8,128)(2,1)}, bf16[4,96,896]{2,1,0:T(8,128)(2,1)}, bf16[4,96,896]{2,1,0:T(8,128)(2,1)}, bf16[4,96,896]{2,1,0:T(8,128)(2,1)}, bf16[4,96,896]{2,1,0:T(8,128)(2,1)}) custom-call(s32[4]{0:T(128)} %get-tuple-element.245.order, s32[8]{0:T(128)} %fusion.19.table, bf16[4,1024,576]{2,1,0:T(8,128)(2,1)} %get-tuple-element.177.refs_0_, ...), custom_call_target="tpu_custom_call" | custom-call | flops 24000000000 | bytes 14000000 | tf_op jit(solution)/shard_map/attend_back/pallas_call | solution.py:256
  290.5 1.7 collective-permute-done.18
  293.5 1.5 collective-permute-start.20
  295.0 2.4 collective-permute-start.21
  297.9 10.8 %unproject.1 = f32[1024,768]{1,0:T(8,128)} custom-call(bf16[2,1024,576]{2,1,0:T(8,128)(2,1)} %get-tuple-element.199.refs_0_, bf16[2,1024,576]{2,1,0:T(8,128)(2,1)} %get-tuple-element.200.refs_1_, bf16[768,640]{1,0:T(8,128)(2,1)} %assemble.2.refs_1_.refs_6_.refs_2_, bf16[768,640]{1,0:T(8,128)(2,1)} %copy-done.4, bf16[768,640]{1,0:T(8,128)(2,1)} %copy-done.5, ...), custom_call_target="tpu_custom_call" | custom-call | flops 3623878656 | bytes 20000000 | tf_op jit(solution)/shard_map/unproject/pallas_call | solution.py:633
  310.8 5.5 %collective-permute-done.22 = bf16[96,896]{1,0:T(8,128)(2,1)S(1)} collective-permute-done((bf16[96,896]{1,0:T(8,128)(2,1)S(1)}, bf16[96,896]{1,0:T(8,128)(2,1)S(1)}, u32[]{:S(2)}, u32[]{:S(2)}) %collective-permute-start.22) | collective-permute-done | bytes 172064 | tf_op jit(solution)/shard_map/ppermute | solution.py:674
  318.3 2.4 collective-permute-start.25
  320.7 2.4 collective-permute-start.27
  323.1 5.4 %fusion.1 = (f32[768,768]{1,0:T(8,128)}, f32[768,768]{1,0:T(8,128)}) fusion(bf16[2,1552,768]{2,1,0:T(8,128)(2,1)} %collective-permute-done.14, bf16[1552,768]{1,0:T(8,128)(2,1)} %collective-permute-done.23, bf16[1552,768]{1,0:T(8,128)(2,1)S(1)} %copy-done.1), kind=kLoop, calls=%fused_computation.4 | loop fusion | flops 5898240 | bytes 11796480 | tf_op jit(solution)/shard_map/add | solution.py:899
  329.3 5.6 %collective-permute-done.26 = bf16[96,896]{1,0:T(8,128)(2,1)S(1)} collective-permute-done((bf16[96,896]{1,0:T(8,128)(2,1)S(1)}, bf16[96,896]{1,0:T(8,128)(2,1)S(1)}, u32[]{:S(2)}, u32[]{:S(2)}) %collective-permute-start.26) | collective-permute-done | bytes 172064 | tf_op jit(solution)/shard_map/ppermute | solution.py:674
  339.1 2.2 collective-permute-done.30
  (108 shorter events, 28.5 us)
Async XLA Ops:
  2.5 13.6 %collective-permute-start.1 = (bf16[96,640]{1,0:T(8,128)(2,1)S(1)}, bf16[96,640]{1,0:T(8,128)(2,1)S(1)}, u32[]{:S(2)}, u32[]{:S(2)}) collective-permute-start(bf16[96,640]{1,0:T(8,128)(2,1)S(1)} %concatenate.3), channel_id=1, source_target_pairs={{0,4},{1,5},{2,6},{3,7},{4,0},{5,1},{6,2},{7,3},{8,12},{9,13},{10,... | collective-permute-start | bytes 368648 | tf_op jit(solution)/shard_map/ppermute | solution.py:674
  6.6 9.5 %collective-permute-start.2 = (bf16[96,640]{1,0:T(8,128)(2,1)S(1)}, bf16[96,640]{1,0:T(8,128)(2,1)S(1)}, u32[]{:S(2)}, u32[]{:S(2)}) collective-permute-start(bf16[96,640]{1,0:T(8,128)(2,1)S(1)} %concatenate.3), channel_id=1, source_target_pairs={{0,6},{1,7},{2,4},{3,5},{4,2},{5,3},{6,0},{7,1},{8,14},{9,15},{10,... | collective-permute-start | bytes 368648 | tf_op jit(solution)/shard_map/ppermute | solution.py:674
  8.0 8.6 %collective-permute-start = (bf16[96,640]{1,0:T(8,128)(2,1)S(1)}, bf16[96,640]{1,0:T(8,128)(2,1)S(1)}, u32[]{:S(2)}, u32[]{:S(2)}) collective-permute-start(bf16[96,640]{1,0:T(8,128)(2,1)S(1)} %concatenate.3), channel_id=1, source_target_pairs={{0,2},{1,3},{2,0},{3,1},{4,6},{5,7},{6,4},{7,5},{8,10},{9,11},{10,... | collective-permute-start | bytes 368648 | tf_op jit(solution)/shard_map/ppermute | solution.py:674
  16.7 7.3 %copy-start.2 = (bf16[4,96,640]{2,1,0:T(8,128)(2,1)}, bf16[4,96,640]{2,1,0:T(8,128)(2,1)S(1)}, u32[]{:S(2)}) copy-start(bf16[4,96,640]{2,1,0:T(8,128)(2,1)S(1)} %pad_maximum_fusion.own_ref) | copy-start | bytes 1474564
  16.7 18.0 %collective-permute-start.3 = (bf16[4,96,640]{2,1,0:T(8,128)(2,1)S(1)}, bf16[4,96,640]{2,1,0:T(8,128)(2,1)S(1)}, u32[]{:S(2)}, u32[]{:S(2)}) collective-permute-start(bf16[4,96,640]{2,1,0:T(8,128)(2,1)S(1)} %pad_maximum_fusion.own_ref), channel_id=1, source_target_pairs={{0,1},{1,0},{2,3},{3,2},{4,5},{5,4},{6,7},{7,6},{8,9},{9,8},{10,11... | collective-permute-start | bytes 1474568 | tf_op jit(solution)/shard_map/ppermute | solution.py:674
  19.6 4.4 %copy-start.15 = (bf16[96,192]{1,0:T(8,128)(2,1)S(1)}, bf16[96,192]{1,0:T(8,128)(2,1)}, u32[]{:S(2)}) copy-start(bf16[96,192]{1,0:T(8,128)(2,1)} %param.32) | copy-start | bytes 110596
  24.0 5.9 %collective-permute-start.4 = (bf16[96,192]{1,0:T(8,128)(2,1)S(1)}, bf16[96,192]{1,0:T(8,128)(2,1)S(1)}, u32[]{:S(2)}, u32[]{:S(2)}) collective-permute-start(bf16[96,192]{1,0:T(8,128)(2,1)S(1)} %copy-done.15), channel_id=1, source_target_pairs={{0,2},{1,3},{2,0},{3,1},{4,6},{5,7},{6,4},{7,5},{8,10},{9,11},{10,... | collective-permute-start | bytes 110600 | tf_op jit(solution)/shard_map/ppermute | solution.py:674
  26.0 5.4 %collective-permute-start.5 = (bf16[96,192]{1,0:T(8,128)(2,1)S(1)}, bf16[96,192]{1,0:T(8,128)(2,1)S(1)}, u32[]{:S(2)}, u32[]{:S(2)}) collective-permute-start(bf16[96,192]{1,0:T(8,128)(2,1)S(1)} %copy-done.15), channel_id=1, source_target_pairs={{0,4},{1,5},{2,6},{3,7},{4,0},{5,1},{6,2},{7,3},{8,12},{9,13},{10,... | collective-permute-start | bytes 110600 | tf_op jit(solution)/shard_map/ppermute | solution.py:674
  28.0 5.9 %collective-permute-start.6 = (bf16[96,192]{1,0:T(8,128)(2,1)S(1)}, bf16[96,192]{1,0:T(8,128)(2,1)S(1)}, u32[]{:S(2)}, u32[]{:S(2)}) collective-permute-start(bf16[96,192]{1,0:T(8,128)(2,1)S(1)} %copy-done.15), channel_id=1, source_target_pairs={{0,6},{1,7},{2,4},{3,5},{4,2},{5,3},{6,0},{7,1},{8,14},{9,15},{10,... | collective-permute-start | bytes 110600 | tf_op jit(solution)/shard_map/ppermute | solution.py:674
  38.5 2.8 collective-permute-start.7
  39.1 24.4 %collective-permute-start.9 = (bf16[768,640]{1,0:T(8,128)(2,1)}, bf16[768,640]{1,0:T(8,128)(2,1)S(1)}, u32[]{:S(2)}, u32[]{:S(2)}) collective-permute-start(bf16[768,640]{1,0:T(8,128)(2,1)} %assemble.2.refs_1_.refs_6_.refs_2_), channel_id=1, source_target_pairs={{0,16},{1,17},{2,18},{3,19},{4,20},{5,21},{6,22},{7,23},{8,24},{9,... | collective-permute-start | bytes 2949128 | tf_op jit(solution)/shard_map/ppermute | solution.py:674
  40.6 19.1 %collective-permute-start.8 = (bf16[4,96,192]{2,1,0:T(8,128)(2,1)}, bf16[4,96,192]{2,1,0:T(8,128)(2,1)}, u32[]{:S(2)}, u32[]{:S(2)}) collective-permute-start(bf16[4,96,192]{2,1,0:T(8,128)(2,1)} %pad_maximum_fusion.1.own_ref), channel_id=1, source_target_pairs={{0,1},{1,0},{2,3},{3,2},{4,5},{5,4},{6,7},{7,6},{8,9},{9,8},{10,11... | collective-permute-start | bytes 442376 | tf_op jit(solution)/shard_map/ppermute | solution.py:674
  41.3 41.3 %all-to-all-start = ((bf16[8,128,768]{2,1,0:T(8,128)(2,1)}), bf16[8,128,768]{2,1,0:T(8,128)(2,1)S(1)}, u32[]{:S(2)}, u32[]{:S(2)}) async-start(bf16[8,128,768]{2,1,0:T(8,128)(2,1)} %bitcast.17), calls=%async_computation | async-start | bytes 3145728 | tf_op jit(solution)/shard_map/all_to_all | solution.py:796
  63.4 2.6 collective-permute-start.10
  63.4 19.1 %collective-permute-start.11 = (bf16[768,192]{1,0:T(8,128)(2,1)}, bf16[768,192]{1,0:T(8,128)(2,1)}, u32[]{:S(2)}, u32[]{:S(2)}) collective-permute-start(bf16[768,192]{1,0:T(8,128)(2,1)} %assemble.3.refs_0_), channel_id=1, source_target_pairs={{0,16},{1,17},{2,18},{3,19},{4,20},{5,21},{6,22},{7,23},{8,24},{9,... | collective-permute-start | bytes 884744 | tf_op jit(solution)/shard_map/ppermute | solution.py:674
  64.9 17.7 %collective-permute-start.12 = (bf16[768,192]{1,0:T(8,128)(2,1)}, bf16[768,192]{1,0:T(8,128)(2,1)}, u32[]{:S(2)}, u32[]{:S(2)}) collective-permute-start(bf16[768,192]{1,0:T(8,128)(2,1)} %assemble.3.refs_0_), channel_id=1, source_target_pairs={{0,8},{1,9},{2,10},{3,11},{4,12},{5,13},{6,14},{7,15},{8,0},{9,1},... | collective-permute-start | bytes 884744 | tf_op jit(solution)/shard_map/ppermute | solution.py:674
  82.6 12.8 %copy-start.3 = (bf16[8,128,768]{2,1,0:T(8,128)(2,1)}, bf16[8,128,768]{2,1,0:T(8,128)(2,1)S(1)}, u32[]{:S(2)}) copy-start(bf16[8,128,768]{2,1,0:T(8,128)(2,1)S(1)} %all-to-all-done) | copy-start | bytes 4718596
  82.6 1.9 collective-permute-start.13
  120.3 27.7 %all-to-all-start.2 = ((bf16[8,64,768]{2,1,0:T(8,128)(2,1)}), bf16[8,64,768]{2,1,0:T(8,128)(2,1)S(1)}, u32[]{:S(2)}, u32[]{:S(2)}) async-start(bf16[8,64,768]{2,1,0:T(8,128)(2,1)} %bitcast.94), calls=%async_computation.2 | async-start | bytes 1572864 | tf_op jit(solution)/shard_map/all_to_all | solution.py:796
  148.0 6.0 %copy-start.9 = (bf16[8,64,768]{2,1,0:T(8,128)(2,1)}, bf16[8,64,768]{2,1,0:T(8,128)(2,1)S(1)}, u32[]{:S(2)}) copy-start(bf16[8,64,768]{2,1,0:T(8,128)(2,1)S(1)} %all-to-all-done.2) | copy-start | bytes 2359300
  148.0 30.2 %all-to-all-start.3 = ((bf16[8,64,768]{2,1,0:T(8,128)(2,1)}), bf16[8,64,768]{2,1,0:T(8,128)(2,1)S(1)}, u32[]{:S(2)}, u32[]{:S(2)}) async-start(bf16[8,64,768]{2,1,0:T(8,128)(2,1)} %bitcast.93), calls=%async_computation.3 | async-start | bytes 1572864 | tf_op jit(solution)/shard_map/all_to_all | solution.py:796
  178.2 24.4 %copy-start.7 = (bf16[8,64,768]{2,1,0:T(8,128)(2,1)}, bf16[8,64,768]{2,1,0:T(8,128)(2,1)S(1)}, u32[]{:S(2)}) copy-start(bf16[8,64,768]{2,1,0:T(8,128)(2,1)S(1)} %all-to-all-done.3) | copy-start | bytes 2359300
  178.2 25.3 %all-to-all-start.4 = ((bf16[8,64,768]{2,1,0:T(8,128)(2,1)}), bf16[8,64,768]{2,1,0:T(8,128)(2,1)S(1)}, u32[]{:S(2)}, u32[]{:S(2)}) async-start(bf16[8,64,768]{2,1,0:T(8,128)(2,1)} %bitcast.92), calls=%async_computation.4 | async-start | bytes 1572864 | tf_op jit(solution)/shard_map/all_to_all | solution.py:796
  184.2 19.3 %copy-start.16 = (s32[1024]{0:T(1024)S(1)}, s32[1024]{0:T(1024)}, u32[]{:S(2)}) copy-start(s32[1024]{0:T(1024)} %get-tuple-element.227) | copy-start | bytes 12292
  203.5 12.7 %copy-start.8 = (bf16[8,64,768]{2,1,0:T(8,128)(2,1)}, bf16[8,64,768]{2,1,0:T(8,128)(2,1)S(1)}, u32[]{:S(2)}) copy-start(bf16[8,64,768]{2,1,0:T(8,128)(2,1)S(1)} %all-to-all-done.4) | copy-start | bytes 2359300
  203.5 8.3 %collective-permute-start.14 = (bf16[2,1552,768]{2,1,0:T(8,128)(2,1)}, bf16[2,1552,768]{2,1,0:T(8,128)(2,1)}, u32[]{:S(2)}, u32[]{:S(2)}) collective-permute-start(bf16[2,1552,768]{2,1,0:T(8,128)(2,1)} %get-tuple-element.170), channel_id=1, source_target_pairs={{0,8},{1,9},{2,10},{3,11},{4,12},{5,13},{6,14},{7,15},{8,0},{9,1},... | collective-permute-start | bytes 14303240 | tf_op jit(solution)/shard_map/ppermute | solution.py:674
  204.6 51.0 %all-to-all-start.5 = ((bf16[8,128,768]{2,1,0:T(8,128)(2,1)}), bf16[8,128,768]{2,1,0:T(8,128)(2,1)S(1)}, u32[]{:S(2)}, u32[]{:S(2)}) async-start(bf16[8,128,768]{2,1,0:T(8,128)(2,1)} %bitcast.33), calls=%async_computation.5 | async-start | bytes 3145728 | tf_op jit(solution)/shard_map/all_to_all | solution.py:796
  231.7 22.8 %copy-start.17 = (s32[1024]{0:T(1024)S(1)}, s32[1024]{0:T(1024)}, u32[]{:S(2)}) copy-start(s32[1024]{0:T(1024)} %add_select_fusion) | copy-start | bytes 12292
  254.3 9.1 %collective-permute-start.15 = (bf16[4,96,896]{2,1,0:T(8,128)(2,1)}, bf16[4,96,896]{2,1,0:T(8,128)(2,1)}, u32[]{:S(2)}, u32[]{:S(2)}) collective-permute-start(bf16[4,96,896]{2,1,0:T(8,128)(2,1)} %get-tuple-element.185), channel_id=1, source_target_pairs={{0,8},{1,9},{2,10},{3,11},{4,12},{5,13},{6,14},{7,15},{8,0},{9,1},... | collective-permute-start | bytes 2064392 | tf_op jit(solution)/shard_map/ppermute | solution.py:674
  255.5 7.9 %copy-start.13 = (bf16[4,96,896]{2,1,0:T(8,128)(2,1)S(1)}, bf16[4,96,896]{2,1,0:T(8,128)(2,1)}, u32[]{:S(2)}) copy-start(bf16[4,96,896]{2,1,0:T(8,128)(2,1)} %get-tuple-element.184) | copy-start | bytes 2064388
  255.5 34.7 %collective-permute-start.16 = (bf16[4,96,896]{2,1,0:T(8,128)(2,1)}, bf16[4,96,896]{2,1,0:T(8,128)(2,1)S(1)}, u32[]{:S(2)}, u32[]{:S(2)}) collective-permute-start(bf16[4,96,896]{2,1,0:T(8,128)(2,1)} %get-tuple-element.190), channel_id=1, source_target_pairs={{0,8},{1,9},{2,10},{3,11},{4,12},{5,13},{6,14},{7,15},{8,0},{9,1},... | collective-permute-start | bytes 2064392 | tf_op jit(solution)/shard_map/ppermute | solution.py:674
  255.9 62.2 %collective-permute-start.23 = (bf16[1552,768]{1,0:T(8,128)(2,1)}, bf16[1552,768]{1,0:T(8,128)(2,1)}, u32[]{:S(2)}, u32[]{:S(2)}) collective-permute-start(bf16[1552,768]{1,0:T(8,128)(2,1)} %fusion), channel_id=1, source_target_pairs={{0,16},{1,17},{2,18},{3,19},{4,20},{5,21},{6,22},{7,23},{8,24},{9,... | collective-permute-start | bytes 7151624 | tf_op jit(solution)/shard_map/ppermute | solution.py:674
  265.6 24.7 %copy-start.11 = (bf16[4,96,896]{2,1,0:T(8,128)(2,1)S(1)}, bf16[4,96,896]{2,1,0:T(8,128)(2,1)}, u32[]{:S(2)}) copy-start(bf16[4,96,896]{2,1,0:T(8,128)(2,1)} %get-tuple-element.189) | copy-start | bytes 2064388
  265.6 24.8 %collective-permute-start.17 = (bf16[4,96,896]{2,1,0:T(8,128)(2,1)}, bf16[4,96,896]{2,1,0:T(8,128)(2,1)S(1)}, u32[]{:S(2)}, u32[]{:S(2)}) collective-permute-start(bf16[4,96,896]{2,1,0:T(8,128)(2,1)} %add_convert_fusion.3), channel_id=1, source_target_pairs={{0,1},{1,0},{2,3},{3,2},{4,5},{5,4},{6,7},{7,6},{8,9},{9,8},{10,11... | collective-permute-start | bytes 2064392 | tf_op jit(solution)/shard_map/ppermute | solution.py:674
  289.6 2.6 collective-permute-start.18
  289.7 19.0 %collective-permute-start.24 = (bf16[4,96,896]{2,1,0:T(8,128)(2,1)}, bf16[4,96,896]{2,1,0:T(8,128)(2,1)}, u32[]{:S(2)}, u32[]{:S(2)}) collective-permute-start(bf16[4,96,896]{2,1,0:T(8,128)(2,1)} %get-tuple-element.206), channel_id=1, source_target_pairs={{0,8},{1,9},{2,10},{3,11},{4,12},{5,13},{6,14},{7,15},{8,0},{9,1},... | collective-permute-start | bytes 2064392 | tf_op jit(solution)/shard_map/ppermute | solution.py:674
  293.5 17.3 %collective-permute-start.20 = (bf16[96,896]{1,0:T(8,128)(2,1)S(1)}, bf16[96,896]{1,0:T(8,128)(2,1)S(1)}, u32[]{:S(2)}, u32[]{:S(2)}) collective-permute-start(bf16[96,896]{1,0:T(8,128)(2,1)S(1)} %get-tuple-element.196), channel_id=1, source_target_pairs={{0,2},{1,3},{2,0},{3,1},{4,6},{5,7},{6,4},{7,5},{8,10},{9,11},{10,... | collective-permute-start | bytes 516104 | tf_op jit(solution)/shard_map/ppermute | solution.py:674
  295.0 15.7 %collective-permute-start.21 = (bf16[96,896]{1,0:T(8,128)(2,1)S(1)}, bf16[96,896]{1,0:T(8,128)(2,1)}, u32[]{:S(2)}, u32[]{:S(2)}) collective-permute-start(bf16[96,896]{1,0:T(8,128)(2,1)S(1)} %get-tuple-element.197), channel_id=1, source_target_pairs={{0,4},{1,5},{2,6},{3,7},{4,0},{5,1},{6,2},{7,3},{8,12},{9,13},{10,... | collective-permute-start | bytes 516104 | tf_op jit(solution)/shard_map/ppermute | solution.py:674
  297.4 20.8 %collective-permute-start.19 = (bf16[4,96,896]{2,1,0:T(8,128)(2,1)S(1)}, bf16[4,96,896]{2,1,0:T(8,128)(2,1)S(1)}, u32[]{:S(2)}, u32[]{:S(2)}) collective-permute-start(bf16[4,96,896]{2,1,0:T(8,128)(2,1)S(1)} %add_convert_fusion.1), channel_id=1, source_target_pairs={{0,1},{1,0},{2,3},{3,2},{4,5},{5,4},{6,7},{7,6},{8,9},{9,8},{10,11... | collective-permute-start | bytes 2064392 | tf_op jit(solution)/shard_map/ppermute | solution.py:674
  297.9 11.5 %copy-start.10 = (bf16[4,96,896]{2,1,0:T(8,128)(2,1)S(1)}, bf16[4,96,896]{2,1,0:T(8,128)(2,1)}, u32[]{:S(2)}) copy-start(bf16[4,96,896]{2,1,0:T(8,128)(2,1)} %get-tuple-element.205) | copy-start | bytes 2064388
  308.7 14.4 %copy-start.1 = (bf16[1552,768]{1,0:T(8,128)(2,1)S(1)}, bf16[1552,768]{1,0:T(8,128)(2,1)}, u32[]{:S(2)}) copy-start(bf16[1552,768]{1,0:T(8,128)(2,1)} %get-tuple-element.208) | copy-start | bytes 7151620
  308.7 7.5 %collective-permute-start.22 = (bf16[96,896]{1,0:T(8,128)(2,1)S(1)}, bf16[96,896]{1,0:T(8,128)(2,1)S(1)}, u32[]{:S(2)}, u32[]{:S(2)}) collective-permute-start(bf16[96,896]{1,0:T(8,128)(2,1)S(1)} %get-tuple-element.198), channel_id=1, source_target_pairs={{0,6},{1,7},{2,4},{3,5},{4,2},{5,3},{6,0},{7,1},{8,14},{9,15},{10,... | collective-permute-start | bytes 516104 | tf_op jit(solution)/shard_map/ppermute | solution.py:674
  317.3 12.0 %collective-permute-start.28 = (bf16[96,896]{1,0:T(8,128)(2,1)S(1)}, bf16[96,896]{1,0:T(8,128)(2,1)S(1)}, u32[]{:S(2)}, u32[]{:S(2)}) collective-permute-start(bf16[96,896]{1,0:T(8,128)(2,1)S(1)} %fusion.3), channel_id=1, source_target_pairs={{0,16},{1,17},{2,18},{3,19},{4,20},{5,21},{6,22},{7,23},{8,24},{9,... | collective-permute-start | bytes 516104 | tf_op jit(solution)/shard_map/ppermute | solution.py:674
  318.3 11.1 %collective-permute-start.25 = (bf16[96,896]{1,0:T(8,128)(2,1)S(1)}, bf16[96,896]{1,0:T(8,128)(2,1)S(1)}, u32[]{:S(2)}, u32[]{:S(2)}) collective-permute-start(bf16[96,896]{1,0:T(8,128)(2,1)S(1)} %get-tuple-element.233), channel_id=1, source_target_pairs={{0,2},{1,3},{2,0},{3,1},{4,6},{5,7},{6,4},{7,5},{8,10},{9,11},{10,... | collective-permute-start | bytes 516104 | tf_op jit(solution)/shard_map/ppermute | solution.py:674
  320.7 14.2 %collective-permute-start.26 = (bf16[96,896]{1,0:T(8,128)(2,1)S(1)}, bf16[96,896]{1,0:T(8,128)(2,1)S(1)}, u32[]{:S(2)}, u32[]{:S(2)}) collective-permute-start(bf16[96,896]{1,0:T(8,128)(2,1)S(1)} %get-tuple-element.232), channel_id=1, source_target_pairs={{0,4},{1,5},{2,6},{3,7},{4,0},{5,1},{6,2},{7,3},{8,12},{9,13},{10,... | collective-permute-start | bytes 516104 | tf_op jit(solution)/shard_map/ppermute | solution.py:674
  320.7 14.1 %collective-permute-start.27 = (bf16[96,896]{1,0:T(8,128)(2,1)S(1)}, bf16[96,896]{1,0:T(8,128)(2,1)S(1)}, u32[]{:S(2)}, u32[]{:S(2)}) collective-permute-start(bf16[96,896]{1,0:T(8,128)(2,1)S(1)} %get-tuple-element.231), channel_id=1, source_target_pairs={{0,6},{1,7},{2,4},{3,5},{4,2},{5,3},{6,0},{7,1},{8,14},{9,15},{10,... | collective-permute-start | bytes 516104 | tf_op jit(solution)/shard_map/ppermute | solution.py:674
  335.9 1.2 collective-permute-start.29
  337.2 4.2 %collective-permute-start.30 = (f32[8,96]{0,1:T(8,128)S(1)}, f32[8,96]{0,1:T(8,128)S(1)}, u32[]{:S(2)}, u32[]{:S(2)}) collective-permute-start(f32[8,96]{0,1:T(8,128)S(1)} %fusion.21), channel_id=1, source_target_pairs={{0,16},{1,17},{2,18},{3,19},{4,20},{5,21},{6,22},{7,23},{8,24},{9,... | collective-permute-start | bytes 9224 | tf_op jit(solution)/shard_map/ppermute | solution.py:674
  (7 other events, 13.5 us)

commit v4 on v3

--- a/solution.py
+++ b/solution.py
@@ -14,7 +14,7 @@
 
 EPSILON = 1e-05
 MASKED = -1e30
-SLAB = 896
+FAR = 1024
 BOTH = ("dp", "expert")
 BF = jnp.bfloat16
 F32 = jnp.float32
@@ -172,8 +172,10 @@
 
 
 def attend_back_kernel(half, order, table, *refs):
-    qkv_ref, ctx_ref, dctx_ref, lse_ref, low_ref, o_ref, w_one, w_two, two_ref = refs[:9]
-    out_ref, *slabs, dq_ref, stage, sems = refs[9:]
+    qkv_ref, ctx_ref, dctx_ref, lse_ref, low_ref, w_one, w_two, two_ref = refs[:8]
+    if half:
+        o_refs, refs = refs[8:10], refs[2:]
+    out_ref, *slabs, dq_ref, stage, sems = refs[8:]
     step = pl.program_id(0)
     count, width = low_ref.shape
     part = width // GROUPS
@@ -228,8 +230,8 @@
         vecs = jnp.where(lane == i, column, vecs)
     stage[:, : 3 * part] = grad.astype(BF)
     stage[:, 3 * part : 640] = vecs.astype(BF)
-    stage[:, 640 : 640 + part] = o_ref[0]
-    stage[:, 640 + part :] = jnp.zeros((width, SLAB - 640 - part), BF)
+    if half:
+        stage[:, 640:] = jnp.concatenate([o_refs[0][0], o_refs[1][0]], axis=1)
     rows = width // 8
     for g in range(2):
 
@@ -251,31 +253,33 @@
     groups, count, part = qkv.shape
     part //= 3
     width = low.shape[1]
-    at = lambda g: (2 * half + g, 0, 0)
-    slab = (PLACED, (4, width // 8, SLAB), BF)
+    at = lambda g, *_: (2 * half + g, 0, 0)
+    cols = FAR if half else 640
+    slab = (PLACED, (4, width // 8, cols), BF)
+    o_specs = [
+        pl.BlockSpec((1, width, part), lambda g, order, table, b=b: (order[b + g], 0, 0))
+        for b in ((2, 0) if half else ())
+    ]
     return call(
         partial(attend_back_kernel, half), "attend_back", (2,),
         [
-            SCALARS,
-            SCALARS,
             pl.BlockSpec((1, count, 3 * part), at),
             pl.BlockSpec((1, count, part), at),
             pl.BlockSpec((1, count, part), at),
             pl.BlockSpec((1, 8, count), at),
             full((count, width)),
-            pl.BlockSpec((1, width, part), at),
         ]
-        + [pl.BlockSpec((width, 640), lambda g: (0, 0), pipeline_mode=pl.Buffered(1))] * 2
-        + [full((8, width))],
-        [(pl.BlockSpec((1, count, 3 * part), lambda g: (g, 0, 0)), (2, count, 3 * part), BF)]
+        + [pl.BlockSpec((width, 640), lambda *_: (0, 0), pipeline_mode=pl.Buffered(1))] * 2
+        + [full((8, width))] + o_specs,
+        [(pl.BlockSpec((1, count, 3 * part), lambda g, *_: (g, 0, 0)), (2, count, 3 * part), BF)]
         + [slab] * 4,
         [
             pltpu.VMEM((HEAD_DIM, SEQ_LEN), F32),
-            pltpu.VMEM((width, SLAB), BF),
+            pltpu.VMEM((width, cols), BF),
             pltpu.SemaphoreType.DMA((8,)),
         ],
-        cost=(24_000_000_000, 14_000_000, 4_000_000),
-    )(order, table, qkv, ctx, dctx, lse, low, o_part, *weights, two)
+        cost=(24_000_000_000, 14_000_000, 4_000_000), ahead=2,
+    )(order, table, qkv, ctx, dctx, lse, low, *weights, two, *[o_part] * len(o_specs))
 
 
 def dispatch_kernel(target_ref, rows_ref, out_ref):
@@ -394,11 +398,8 @@
         for q in range(GROUPS):
             grad = total_ref[q].astype(BF)
             at = pl.ds(pl.multiple_of(order[q] * part, 64), part)
-            for r in range(GROUPS):
-                piece = grad[:, :part]
-                for n in range(1, GROUPS):
-                    piece = jnp.where(order[r] == n, grad[:, n * part : n * part + part], piece)
-                grad_ref[r, at, :] = piece
+            for n in range(GROUPS):
+                grad_ref[n, at, :] = grad[:, n * part : n * part + part]
 
 
 def unmix(order, h, g, dm_one, dm_two, target, ctx, whole, vec):
@@ -439,29 +440,9 @@
     )(h, target.reshape(count, 1), gy)[0]
 
 
-ERFC = (
-    0.169189354,
-    0.1706909295,
-    0.1485212475,
-    0.2141814502,
-    -0.09282610738,
-    0.5449670381,
-    -0.5097724612,
-    0.4843017683,
-    -0.1292532277,
-)
-
-
 def gelu_pair(v):
-    a = jnp.abs(v) * (0.5**0.5)
-    bell = jnp.exp(-0.5 * v * v)
-    t = 1.0 / (1.0 + 0.3 * a)
-    poly = jnp.full_like(v, ERFC[-1])
-    for c in ERFC[-2::-1]:
-        poly = poly * t + c
-    tail = 0.5 * bell * t * poly
-    cdf = jnp.where(v < 0, tail, 1.0 - tail)
-    return v * cdf, cdf + v * bell * (0.5 / jnp.pi) ** 0.5
+    cdf = 0.5 + 0.5 * lax.erf(v * 0.5**0.5)
+    return v * cdf, cdf + v * jnp.exp(-0.5 * v * v) * (0.5 / jnp.pi) ** 0.5
 
 
 def expert_kernel(
@@ -515,7 +496,7 @@
 def expert(half, x, g, win, bias_in, wout, bias_out, center, gy):
     rows, width = x.shape
     ff = win.shape[1]
-    step = min(512, ff)
+    step = min(1024, ff)
     along = lambda i: (0, i)
     side = pl.BlockSpec(
         (g.shape[0], 1) + g.shape[2:], lambda i: (0, half, 0, 0), pipeline_mode=pl.Buffered(1)
@@ -580,13 +561,11 @@
     if not split:
         put(refs[12].at[0])
         return
-    far_ref, across_ref, own_ref, total = refs[12:]
-    put(total)
-    for at, out in ((0, far_ref.at[0]), (1, far_ref.at[0]), (2, across_ref), (3, own_ref)):
-
-        @pl.when(step == at)
+    for late, out in enumerate(refs[12:]):
+
+        @pl.when(step // 2 == late)
         def _(out=out):
-            out[...] = total[...]
+            put(out.at[0])
 
 
 def weigh(which, n, split, hid, du, dy, x, bias, small):
@@ -598,17 +577,15 @@
     wide = pl.BlockSpec((rows, part), along)
     if split:
         first = pl.BlockSpec((1, size, width), lambda i, which: (jnp.minimum(i, 1), 0, 0))
-        outs = [(first, (2, size, width), BF)] + [(full((size, width)), (size, width), BF)] * 2
-        scratch = [pltpu.VMEM((size, width), BF)]
+        last = pl.BlockSpec((1, size, width), lambda i, which: (jnp.maximum(i - 2, 0), 0, 0))
+        outs = [(first, (2, size, width), BF), (last, (2, size, width), BF)]
     else:
         outs = [(pl.BlockSpec((1, size, width), lambda i, which: (i, 0, 0)), (n, size, width), BF)]
-        scratch = []
     got = call(
         partial(weigh_kernel, split), "weigh", (n,),
         [wide] * 4 + [full((rows, width))] * 4 + [pl.BlockSpec((8, part), along)] * 2
         + [full((8, width))] * 2,
-        outs, scratch,
-        cost=(8 * rows * width * ff, 26_000_000, 0), ahead=1,
+        outs, cost=(8 * rows * width * ff, 26_000_000, 0), ahead=1,
     )(which, *hid, *du, *dy, *x, *bias, *small)
     return got if split else got[0]
 
@@ -702,10 +679,10 @@
         extra = jnp.concatenate([stacked.T, jnp.zeros((rows, pad), BF)], axis=1)
         shard = jnp.concatenate([*weights, extra], axis=1)
         own = jnp.stack([shard] + [place.move(shard, way) for way in place.z])
-        own, out_weights = barrier((own, out_weights))
+        own, out_weights, filler = barrier((own, out_weights, filler))
         got = place.move(own, place.y)
         out_own = jnp.stack([out_weights] + [place.move(out_weights, way) for way in place.z])
-        got, filler, out_own = barrier((got, filler, out_own))
+        got, out_own = barrier((got, out_own))
         near = assemble(table, own, got)
         across = place.move(near, place.x)
         far = place.move(near, place.core)
@@ -730,22 +707,22 @@
 
 
 def columns_of(place, total, count):
-    cols = (SLAB - 128) // 4
-    parts = [total[:, i : i + cols] for i in (0, cols, 2 * cols, 640)]
+    cols = (FAR - 640) // 2
+    parts = [total[:, i * cols : (i + 1) * cols] for i in range(3)]
     vecs = total[:, 576 : 576 + 8].T
     vecs = vecs + place.move(vecs, place.core)
     vecs = vecs + place.move(vecs, place.x)
     return parts, [vecs[i] for i in range(count)]
 
 
-def reduce_plain(slabs, count):
-    slabs = jnp.stack(slabs)
+def reduce_plain(near, far, count):
+    slabs = jnp.stack([a[:, :640] for a in (*near, *far)])
     width = slabs.shape[1]
     part = width // GROUPS
-    parts = []
-    for at in (0, part, 2 * part, 640):
-        grad = slabs[:, :, at : at + part].transpose(1, 0, 2).reshape(width, width)
-        parts.append(scatter_all(grad).astype(F32))
+    whole = lambda array: array.transpose(1, 0, 2).reshape(width, width)
+    parts = [whole(slabs[:, :, i * part : (i + 1) * part]) for i in range(3)]
+    parts.append(whole(jnp.stack([far[0][:, -part:], far[1][:, -part:]] + [a[:, 640:-part] for a in far])))
+    parts = [scatter_all(p).astype(F32) for p in parts]
     vecs = jnp.sum(slabs[:, :, 576 : 576 + count].astype(F32), axis=0).T
     vecs = lax.psum_scatter(vecs, "expert", scatter_dimension=1, tiled=True)
     vecs = lax.psum(vecs, "dp")
@@ -833,7 +810,6 @@
     h1, whole_o, sent_one, sent_two = mix(order, block_entries, ctx, out, vec, halved)
 
     x_one = exchange(sent_one)
-    x_one, sent_two = barrier((x_one, sent_two))
     x_two = exchange(sent_two)
     matrices = (
         specialist_widen_weights[0], specialist_widen_shift, specialist_contract_weights[0],
@@ -854,12 +830,12 @@
         (dbin_one, dbin_two), (small_one, small_two),
     )
     if place.staged:
-        grads_far, grads_across, grads = weigh(
+        grads_far, grads = weigh(
             weighed, n_dp, True, *sides
         )
         grads_far, gy, dm_two = barrier((grads_far, gy, dm_two))
         came_far = place.move(grads_far, place.core)
-        crossing = add(grads_across, came_far[0])
+        crossing = add(grads[0], came_far[0])
         crossing, h1 = barrier((crossing, h1))
         came = place.move(crossing, place.x)
     else:
@@ -883,36 +859,35 @@
         dctx, output, send = barrier((dctx, output, send))
         across, sends = reduce_y(place, add(keep, more[0]), send)
         near, keep, send, *more = back(0, dctx)
-        near, sends = barrier((near, sends))
+        near, keep, send, more, across, sends = barrier((near, keep, send, more, across, sends))
         more = [place.move(m, place.core) for m in more]
         got = reduce_z(place, sends)
         send, keep = add(send, more[1]), add(keep, more[0])
-        near, send = barrier((near, send))
+        near, send, keep = barrier((near, send, keep))
         got_y = place.move(send, place.y)
         input_grad = unproject((near, far), weights, block_entries, dh1, vec)
-        got, input_grad = barrier((got, input_grad))
-        across = (across + sum(g.astype(F32) for g in got)).astype(BF)
-        across = place.move(across, place.x)
-        got, input_grad, came = barrier((got_y, input_grad, came))
+        got_far = got
+        got, input_grad, came, got_far = barrier((got_y, input_grad, came, got_far))
+        sum_o = across + sum(g.astype(F32) for g in got_far)
+        cols = width // GROUPS
+        across = place.move(sum_o[:, :-cols].astype(BF), place.x)
         total = keep[0].astype(F32) + got[0].astype(F32)
         got = reduce_z(place, [add(keep[k], got[k]) for k in range(1, 4)])
         pick = lambda at: sum(
-            a[at : at + width].astype(F32) for a in (grads, came_far[1], came)
+            a[at : at + width].astype(F32) for a in (grads[1], came_far[1], came)
         )
         got, grads, across = barrier((got, [pick(0), pick(width), pick(2 * width)], across))
-        total += across.astype(F32)
+        total += across[:, :640].astype(F32)
+        sum_o = sum_o[:, -cols:] + across[:, 640:].astype(F32)
         total += sum(g.astype(F32) for g in got)
-        (sum_q, sum_k, sum_v, sum_o), small = columns_of(place, total, 7)
+        (sum_q, sum_k, sum_v), small = columns_of(place, total, 7)
     else:
         parts = [back(half, dctx) for half in range(2)]
-        (sum_q, sum_k, sum_v, sum_o), small = reduce_plain(
-            [
-                jnp.concatenate(p[1 + 2 * g : 3 + 2 * g]).reshape(width, SLAB)
-                for p in parts
-                for g in range(2)
-            ],
-            7,
-        )
+        slabs = [
+            [jnp.concatenate(p[1 + 2 * g : 3 + 2 * g]).reshape(width, -1) for g in range(2)]
+            for p in parts
+        ]
+        (sum_q, sum_k, sum_v, sum_o), small = reduce_plain(*slabs, 7)
         input_grad = unproject([p[0] for p in parts], weights, block_entries, dh1, vec)
         output = finish(h1, target, gy)
 

time: 346 us -> 324 us (0.936)
  Pallas kernels: 192 us -> 176 us
  waiting for transfers between devices: 35.3 us -> 31.7 us
    pallas_call x2, Pallas kernels: 48.2 us -> 35 us  [expert(): call(expert_kernel, 'expert', (ff // step,), [full((rows, width)), side,...]
    ppermute x31, waiting for transfers between devices: 32 us -> 19.9 us  [move(): return lax.ppermute(array, BOTH, way)]
    all_to_all x5, waiting for transfers between devices: 3.31 us -> 11.8 us  [exchange(): lax.all_to_all(sent, 'expert', split_axis=0, concat_axis=0, tiled=True)]
  transfers between devices with their start and end apart: 36 -> 36, of which waited for: 16 -> 17; matrix products, arithmetic and copies ran while one was open for 7% -> 7% of each run, Pallas kernels for 52% -> 51%
where the time goes in v4:
time: 324 us; the launch traced here: 320 us
  Pallas kernels  176 us (54%)
  starting transfers between devices  55.9 us (17%)
  waiting for transfers between devices  31.7 us (10%)
  blocking collectives  24.9 us (8%)
  other arithmetic  21.3 us (7%)
  local copies, waits for them, and re-layouts  9.27 us (3%)
    pallas_call x2, Pallas kernels, attend_back(): call(partial(attend_back_kernel, half), 'attend_back', (2,), [pl.BlockSpe...  46.4 us
    pallas_call x2, Pallas kernels, expert(): call(expert_kernel, 'expert', (ff // step,), [full((rows, width)), side,...  35 us
    ppermute x31, starting transfers between devices, move(): return lax.ppermute(array, BOTH, way)  34 us
    pallas_call x2, Pallas kernels, attend(): call(partial(attend_kernel, half), 'attend', (2,), [SCALARS] + ins, outs,...  27.5 us
    all_to_all x1, blocking collectives, exchange(): lax.all_to_all(sent, 'expert', split_axis=0, concat_axis=0, tiled=True)  24.9 us
    all_to_all x5, starting transfers between devices, exchange(): lax.all_to_all(sent, 'expert', split_axis=0, concat_axis=0, tiled=True)  21.9 us
    ppermute x31, waiting for transfers between devices, move(): return lax.ppermute(array, BOTH, way)  19.9 us
    pallas_call x1, Pallas kernels, weigh(): call(partial(weigh_kernel, split), 'weigh', (n,), [wide] * 4 + [full((row...  17.3 us
  transfers between devices with their start and end apart: 36, of which 17 were waited for; matrix products, arithmetic and copies ran while one was open for 7% of the time, Pallas kernels for 51%

profile of v4, /device:TPU:0, one launch (start us, length us, event | category | flops | bytes accessed | tf_op | source)
XLA Modules:
  0.0 320.3 jit_solution(5308171559732778919)
XLA Ops:
  2.5 4.1 %collective-permute-start.1 = (bf16[96,640]{1,0:T(8,128)(2,1)S(1)}, bf16[96,640]{1,0:T(8,128)(2,1)S(1)}, u32[]{:S(2)}, u32[]{:S(2)}) collective-permute-start(bf16[96,640]{1,0:T(8,128)(2,1)S(1)} %concatenate.3), channel_id=1, source_target_pairs={{0,4},{1,5},{2,6},{3,7},{4,0},{5,1},{6,2},{7,3},{8,12},{9,13},{10,... | collective-permute-start | bytes 368648 | tf_op jit(solution)/shard_map/ppermute | solution.py:651
  6.6 1.3 collective-permute-start.2
  11.6 4.4 %dispatch.1 = bf16[1024,768]{1,0:T(8,128)(2,1)} custom-call(s32[1,1024]{1,0:T(1,128)} %bitcast.93, bf16[1024,768]{1,0:T(8,128)(2,1)} %g_ref.1), custom_call_target="tpu_custom_call" | custom-call | flops 1610612736 | bytes 3000000 | tf_op jit(solution)/shard_map/dispatch/pallas_call | solution.py:295
  16.7 1.6 collective-permute-start.3
  18.4 2.0 collective-permute-start.4
  20.3 2.1 collective-permute-start.5
  24.2 1.5 collective-permute-done.5
  25.7 2.6 collective-permute-done.6
  29.8 3.0 assemble.2.refs_1_.refs_5_.refs_2_
  33.4 1.5 collective-permute-start.9
  35.9 7.0 %all-to-all-start = ((bf16[8,128,768]{2,1,0:T(8,128)(2,1)}), bf16[8,128,768]{2,1,0:T(8,128)(2,1)S(1)}, u32[]{:S(2)}, u32[]{:S(2)}) async-start(bf16[8,128,768]{2,1,0:T(8,128)(2,1)} %bitcast.17), calls=%async_computation | async-start | bytes 3145728 | tf_op jit(solution)/shard_map/all_to_all | solution.py:773
  42.9 14.3 %attend.2 = (bf16[4,1024,576]{2,1,0:T(8,128)(2,1)}, bf16[4,1024,192]{2,1,0:T(8,128)(2,1)}, f32[4,8,1024]{2,1,0:T(8,128)}, bf16[1024,768]{1,0:T(8,128)(2,1)}, f32[8,768]{1,0:T(8,128)}) custom-call(s32[4]{0:T(128)} %iota_xor_fusion.order, bf16[1024,768]{1,0:T(8,128)(2,1)} %refs_6_.1, bf16[768,640]{1,0:T(8,128)(2,1)} %assemble.2.refs_1_.refs_5_.refs_2_, ...), custom_call_target="tpu_custom_call" | custom-call | flops 12000000000 | bytes 8000000 | tf_op jit(solution)/shard_map/attend/pallas_call | solution.py:167
  57.3 2.5 assemble.3.refs_0_
  59.8 1.6 collective-permute-start.11
  63.4 13.2 %attend.3 = (bf16[4,1024,576]{2,1,0:T(8,128)(2,1)}, bf16[4,1024,192]{2,1,0:T(8,128)(2,1)}, f32[4,8,1024]{2,1,0:T(8,128)}) custom-call(s32[4]{0:T(128)} %iota_xor_fusion.order, bf16[1024,768]{1,0:T(8,128)(2,1)} %get-tuple-element.126.refs_0_.refs_4_, ...), custom_call_target="tpu_custom_call", output_to_operand_aliasing={{0}: (5, {}), {1}: (6, {}), {2}: (7, {})} | custom-call | flops 12000000000 | bytes 8000000 | tf_op jit(solution)/shard_map/attend/pallas_call | solution.py:167
  76.6 3.6 %all-to-all-done = bf16[8,128,768]{2,1,0:T(8,128)(2,1)S(1)} async-done(((bf16[8,128,768]{2,1,0:T(8,128)(2,1)}), bf16[8,128,768]{2,1,0:T(8,128)(2,1)S(1)}, u32[]{:S(2)}, u32[]{:S(2)}) %all-to-all-start) | async-done | bytes 1572896 | tf_op jit(solution)/shard_map/all_to_all | solution.py:773
  80.2 1.9 collective-permute-done.13.refs_3_
  82.9 9.9 %mix.1 = (f32[1024,768]{1,0:T(8,128)}, bf16[768,768]{1,0:T(8,128)(2,1)}, bf16[512,768]{1,0:T(8,128)(2,1)}, bf16[512,768]{1,0:T(8,128)(2,1)}) custom-call(s32[4]{0:T(128)} %iota_xor_fusion.order, bf16[1024,768]{1,0:T(8,128)(2,1)} %refs_6_.1, bf16[4,1024,192]{2,1,0:T(8,128)(2,1)} %get-tuple-element.145.ctx_ref.refs_1_, ...), custom_call_target="tpu_custom_call" | custom-call | flops 2818572288 | bytes 12000000 | tf_op jit(solution)/shard_map/mix/pallas_call | solution.py:343
  92.8 24.9 %all_to_all.30 = bf16[8,64,768]{2,1,0:T(8,128)(2,1)} all-to-all(bf16[8,64,768]{2,1,0:T(8,128)(2,1)} %bitcast.81), channel_id=1, replica_groups=mesh['dp'=4,'expert'=8] {'expert'}, dimensions={0} | all-to-all | bytes 1572864 | tf_op jit(solution)/shard_map/all_to_all | solution.py:773
  117.7 3.6 %all-to-all-start.2 = ((bf16[8,64,768]{2,1,0:T(8,128)(2,1)}), bf16[8,64,768]{2,1,0:T(8,128)(2,1)S(1)}, u32[]{:S(2)}, u32[]{:S(2)}) async-start(bf16[8,64,768]{2,1,0:T(8,128)(2,1)} %bitcast.80), calls=%async_computation.2 | async-start | bytes 1572864 | tf_op jit(solution)/shard_map/all_to_all | solution.py:773
  121.3 17.5 %expert.2 = (bf16[8,2,64,768]{3,2,1,0:T(8,128)(2,1)}, bf16[512,768]{1,0:T(8,128)(2,1)}, bf16[512,768]{1,0:T(8,128)(2,1)}, bf16[512,3072]{1,0:T(8,128)(2,1)}, bf1...) custom-call(bf16[512,768]{1,0:T(8,128)(2,1)} %bitcast.73, bf16[8,2,64,768]{3,2,1,0:T(8,128)(2,1)} %bitcast.69, ...), custom_call_target="tpu_custom_call" | custom-call | flops 9663676416 | bytes 22000000 | tf_op jit(solution)/shard_map/expert/pallas_call | solution.py:504
  138.8 2.9 all-to-all-done.2
  141.7 4.0 %all-to-all-start.3 = ((bf16[8,64,768]{2,1,0:T(8,128)(2,1)}), bf16[8,64,768]{2,1,0:T(8,128)(2,1)S(1)}, u32[]{:S(2)}, u32[]{:S(2)}) async-start(bf16[8,64,768]{2,1,0:T(8,128)(2,1)} %bitcast.79), calls=%async_computation.3 | async-start | bytes 1572864 | tf_op jit(solution)/shard_map/all_to_all | solution.py:773
  145.7 17.5 %expert.3 = (bf16[8,2,64,768]{3,2,1,0:T(8,128)(2,1)}, bf16[512,768]{1,0:T(8,128)(2,1)}, bf16[512,768]{1,0:T(8,128)(2,1)}, bf16[512,3072]{1,0:T(8,128)(2,1)}, bf1...) custom-call(bf16[512,768]{1,0:T(8,128)(2,1)} %bitcast.76, ...), custom_call_target="tpu_custom_call", output_to_operand_aliasing={{0}: (7, {})} | custom-call | flops 9663676416 | bytes 22000000 | tf_op jit(solution)/shard_map/expert/pallas_call | solution.py:504
  163.2 2.8 all-to-all-done.3
  166.0 3.6 %all-to-all-start.4 = ((bf16[8,64,768]{2,1,0:T(8,128)(2,1)}), bf16[8,64,768]{2,1,0:T(8,128)(2,1)S(1)}, u32[]{:S(2)}, u32[]{:S(2)}) async-start(bf16[8,64,768]{2,1,0:T(8,128)(2,1)} %bitcast.78), calls=%async_computation.4 | async-start | bytes 1572864 | tf_op jit(solution)/shard_map/all_to_all | solution.py:773
  170.1 17.3 %weigh.1 = (bf16[2,1552,768]{2,1,0:T(8,128)(2,1)}, bf16[2,1552,768]{2,1,0:T(8,128)(2,1)}) custom-call(s32[4]{0:T(128)} %fusion.12.which, bf16[512,3072]{1,0:T(8,128)(2,1)} %get-tuple-element.149.refs_0_, bf16[512,3072]{1,0:T(8,128)(2,1)} %get-tuple-element.157.refs_1_, bf16[512,3072]{1,0:T(8,128)(2,1)} %get-tuple-element.158.refs_2_, ...), custom_call_target="tpu_custom_call" | custom-call | flops 9663676416 | bytes 26000000 | tf_op jit(solution)/shard_map/weigh/pallas_call | solution.py:584
  187.3 2.6 all-to-all-done.4
  191.0 3.8 %all-to-all-start.5 = ((bf16[8,128,768]{2,1,0:T(8,128)(2,1)}), bf16[8,128,768]{2,1,0:T(8,128)(2,1)S(1)}, u32[]{:S(2)}, u32[]{:S(2)}) async-start(bf16[8,128,768]{2,1,0:T(8,128)(2,1)} %bitcast.33), calls=%async_computation.5 | async-start | bytes 3145728 | tf_op jit(solution)/shard_map/all_to_all | solution.py:773
  194.8 3.5 %collective-permute-done.14 = bf16[2,1552,768]{2,1,0:T(8,128)(2,1)} collective-permute-done((bf16[2,1552,768]{2,1,0:T(8,128)(2,1)}, bf16[2,1552,768]{2,1,0:T(8,128)(2,1)}, u32[]{:S(2)}, u32[]{:S(2)}) %collective-permute-start.14) | collective-permute-done | bytes 4767776 | tf_op jit(solution)/shard_map/ppermute | solution.py:651
  198.2 4.5 %fusion = bf16[1552,768]{1,0:T(8,128)(2,1)} fusion(bf16[2,1552,768]{2,1,0:T(8,128)(2,1)} %collective-permute-done.14, bf16[2,1552,768]{2,1,0:T(8,128)(2,1)} %get-tuple-element.166), kind=kLoop, calls=%fused_computation.1 | loop fusion | flops 4767744 | bytes 7151616 | tf_op jit(solution)/shard_map/convert_element_type | solution.py:620
  202.7 13.2 %unmix.1 = (f32[1024,768]{1,0:T(8,128)}, bf16[4,1024,192]{2,1,0:T(8,128)(2,1)}, bf16[4,768,192]{2,1,0:T(8,128)(2,1)}, f32[8,768]{1,0:T(8,128)}) custom-call(s32[4]{0:T(128)} %iota_xor_fusion.order, f32[1024,768]{1,0:T(8,128)} %get-tuple-element.172.h_ref, bf16[1024,768]{1,0:T(8,128)(2,1)} %g_ref.1, bf16[512,768]{1,0:T(8,128)(2,1)} %bitcast.71, ...), custom_call_target="tpu_custom_call" | custom-call | flops 4026531840 | bytes 20000000 | tf_op jit(solution)/shard_map/unmix/pallas_call | solution.py:411
  215.9 23.6 %attend_back.2 = (bf16[2,1024,576]{2,1,0:T(8,128)(2,1)}, bf16[4,96,1024]{2,1,0:T(8,128)(2,1)}, bf16[4,96,1024]{2,1,0:T(8,128)(2,1)}, bf16[4,96,1024]{2,1,0:T(8,128)(2,1)}, bf16[4,96,1024]{2,1,0:T(8,128)(2,1)}) custom-call(s32[4]{0:T(128)} %iota_xor_fusion.order, s32[8]{0:T(128)} %fusion.15.table, bf16[4,1024,576]{2,1,0:T(8,128)(2,1)} %get-tuple-element.177.refs_0_, ...), custom_call_target="tpu_custom_call" | custom-call | flops 24000000000 | bytes 14000000 | tf_op jit(solution)/shard_map/attend_back/pallas_call | solution.py:263
  241.1 1.5 collective-permute-start.21
  242.6 6.2 %finish.1 = bf16[1024,768]{1,0:T(8,128)(2,1)} custom-call(f32[1024,768]{1,0:T(8,128)} %get-tuple-element.172.h_ref, s32[1024,1]{1,0:T(8,128)} %copy.64.target_ref, bf16[1024,768]{1,0:T(8,128)(2,1)} %bitcast.66), custom_call_target="tpu_custom_call" | custom-call | flops 1610612736 | bytes 6000000 | tf_op jit(solution)/shard_map/finish/pallas_call | solution.py:435
  248.8 2.3 add_convert_fusion.2
  251.2 1.4 collective-permute-start.17
  252.5 22.8 %attend_back.3 = (bf16[2,1024,576]{2,1,0:T(8,128)(2,1)}, bf16[4,96,640]{2,1,0:T(8,128)(2,1)}, bf16[4,96,640]{2,1,0:T(8,128)(2,1)}, bf16[4,96,640]{2,1,0:T(8,128)(2,1)}, bf16[4,96,640]{2,1,0:T(8,128)(2,1)}) custom-call(s32[4]{0:T(128)} %iota_xor_fusion.order, s32[8]{0:T(128)} %fusion.15.table, bf16[4,1024,576]{2,1,0:T(8,128)(2,1)} %get-tuple-element.177.refs_0_, ...), custom_call_target="tpu_custom_call" | custom-call | flops 24000000000 | bytes 14000000 | tf_op jit(solution)/shard_map/attend_back/pallas_call | solution.py:263
  276.9 1.4 collective-permute-done.19
  280.1 1.6 collective-permute-start.23
  281.7 2.5 collective-permute-start.24
  284.2 10.7 %unproject.1 = f32[1024,768]{1,0:T(8,128)} custom-call(bf16[2,1024,576]{2,1,0:T(8,128)(2,1)} %get-tuple-element.202.refs_0_, bf16[2,1024,576]{2,1,0:T(8,128)(2,1)} %get-tuple-element.203.refs_1_, bf16[768,640]{1,0:T(8,128)(2,1)} %assemble.2.refs_1_.refs_5_.refs_2_, bf16[768,640]{1,0:T(8,128)(2,1)} %copy-done.3, bf16[768,640]{1,0:T(8,128)(2,1)} %copy-done.4, ...), custom_call_target="tpu_custom_call" | custom-call | flops 3623878656 | bytes 20000000 | tf_op jit(solution)/shard_map/unproject/pallas_call | solution.py:610
  294.9 2.3 collective-permute-done.23
  298.8 3.4 %collective-permute-start.25 = (bf16[96,640]{1,0:T(8,128)(2,1)S(1)}, bf16[96,640]{1,0:T(8,128)(2,1)S(1)}, u32[]{:S(2)}, u32[]{:S(2)}) collective-permute-start(bf16[96,640]{1,0:T(8,128)(2,1)S(1)} %get-tuple-element.241), channel_id=1, source_target_pairs={{0,2},{1,3},{2,0},{3,1},{4,6},{5,7},{6,4},{7,5},{8,10},{9,11},{10,... | collective-permute-start | bytes 368648 | tf_op jit(solution)/shard_map/ppermute | solution.py:651
  302.4 2.2 collective-permute-start.27
  304.6 6.0 %bitcast_add_fusion = (f32[768,768]{1,0:T(8,128)}, f32[768,768]{1,0:T(8,128)}) fusion(bf16[2,1552,768]{2,1,0:T(8,128)(2,1)} %collective-permute-done.14, bf16[1552,768]{1,0:T(8,128)(2,1)} %collective-permute-done.21, bf16[2,1552,768]{2,1,0:T(8,128)(2,1)} %get-tuple-element.166), kind=kLoop, calls=%fused_computation.2 | loop fusion | flops 5898240 | bytes 11796480 | tf_op jit(solution)/shard_map/add | solution.py:876
  311.4 1.3 collective-permute-done.26
  316.6 2.6 collective-permute-done.30
  (112 shorter events, 27.7 us)
Async XLA Ops:
  2.5 13.6 %collective-permute-start.1 = (bf16[96,640]{1,0:T(8,128)(2,1)S(1)}, bf16[96,640]{1,0:T(8,128)(2,1)S(1)}, u32[]{:S(2)}, u32[]{:S(2)}) collective-permute-start(bf16[96,640]{1,0:T(8,128)(2,1)S(1)} %concatenate.3), channel_id=1, source_target_pairs={{0,4},{1,5},{2,6},{3,7},{4,0},{5,1},{6,2},{7,3},{8,12},{9,13},{10,... | collective-permute-start | bytes 368648 | tf_op jit(solution)/shard_map/ppermute | solution.py:651
  6.6 9.5 %collective-permute-start.2 = (bf16[96,640]{1,0:T(8,128)(2,1)S(1)}, bf16[96,640]{1,0:T(8,128)(2,1)S(1)}, u32[]{:S(2)}, u32[]{:S(2)}) collective-permute-start(bf16[96,640]{1,0:T(8,128)(2,1)S(1)} %concatenate.3), channel_id=1, source_target_pairs={{0,6},{1,7},{2,4},{3,5},{4,2},{5,3},{6,0},{7,1},{8,14},{9,15},{10,... | collective-permute-start | bytes 368648 | tf_op jit(solution)/shard_map/ppermute | solution.py:651
  8.0 8.6 %collective-permute-start = (bf16[96,640]{1,0:T(8,128)(2,1)S(1)}, bf16[96,640]{1,0:T(8,128)(2,1)S(1)}, u32[]{:S(2)}, u32[]{:S(2)}) collective-permute-start(bf16[96,640]{1,0:T(8,128)(2,1)S(1)} %concatenate.3), channel_id=1, source_target_pairs={{0,2},{1,3},{2,0},{3,1},{4,6},{5,7},{6,4},{7,5},{8,10},{9,11},{10,... | collective-permute-start | bytes 368648 | tf_op jit(solution)/shard_map/ppermute | solution.py:651
  11.6 6.8 %copy-start.14 = (bf16[96,192]{1,0:T(8,128)(2,1)S(1)}, bf16[96,192]{1,0:T(8,128)(2,1)}, u32[]{:S(2)}) copy-start(bf16[96,192]{1,0:T(8,128)(2,1)} %param.32) | copy-start | bytes 110596
  16.7 12.3 %copy-start.1 = (bf16[4,96,640]{2,1,0:T(8,128)(2,1)}, bf16[4,96,640]{2,1,0:T(8,128)(2,1)S(1)}, u32[]{:S(2)}) copy-start(bf16[4,96,640]{2,1,0:T(8,128)(2,1)S(1)} %pad_maximum_fusion.own_ref) | copy-start | bytes 1474564
  16.7 12.3 %collective-permute-start.3 = (bf16[4,96,640]{2,1,0:T(8,128)(2,1)S(1)}, bf16[4,96,640]{2,1,0:T(8,128)(2,1)S(1)}, u32[]{:S(2)}, u32[]{:S(2)}) collective-permute-start(bf16[4,96,640]{2,1,0:T(8,128)(2,1)S(1)} %pad_maximum_fusion.own_ref), channel_id=1, source_target_pairs={{0,1},{1,0},{2,3},{3,2},{4,5},{5,4},{6,7},{7,6},{8,9},{9,8},{10,11... | collective-permute-start | bytes 1474568 | tf_op jit(solution)/shard_map/ppermute | solution.py:651
  18.4 5.9 %collective-permute-start.4 = (bf16[96,192]{1,0:T(8,128)(2,1)S(1)}, bf16[96,192]{1,0:T(8,128)(2,1)S(1)}, u32[]{:S(2)}, u32[]{:S(2)}) collective-permute-start(bf16[96,192]{1,0:T(8,128)(2,1)S(1)} %copy-done.14), channel_id=1, source_target_pairs={{0,2},{1,3},{2,0},{3,1},{4,6},{5,7},{6,4},{7,5},{8,10},{9,11},{10,... | collective-permute-start | bytes 110600 | tf_op jit(solution)/shard_map/ppermute | solution.py:651
  20.3 5.4 %collective-permute-start.5 = (bf16[96,192]{1,0:T(8,128)(2,1)S(1)}, bf16[96,192]{1,0:T(8,128)(2,1)S(1)}, u32[]{:S(2)}, u32[]{:S(2)}) collective-permute-start(bf16[96,192]{1,0:T(8,128)(2,1)S(1)} %copy-done.14), channel_id=1, source_target_pairs={{0,4},{1,5},{2,6},{3,7},{4,0},{5,1},{6,2},{7,3},{8,12},{9,13},{10,... | collective-permute-start | bytes 110600 | tf_op jit(solution)/shard_map/ppermute | solution.py:651
  22.4 5.9 %collective-permute-start.6 = (bf16[96,192]{1,0:T(8,128)(2,1)S(1)}, bf16[96,192]{1,0:T(8,128)(2,1)S(1)}, u32[]{:S(2)}, u32[]{:S(2)}) collective-permute-start(bf16[96,192]{1,0:T(8,128)(2,1)S(1)} %copy-done.14), channel_id=1, source_target_pairs={{0,6},{1,7},{2,4},{3,5},{4,2},{5,3},{6,0},{7,1},{8,14},{9,15},{10,... | collective-permute-start | bytes 110600 | tf_op jit(solution)/shard_map/ppermute | solution.py:651
  32.8 3.1 collective-permute-start.7
  33.4 26.3 %collective-permute-start.9 = (bf16[768,640]{1,0:T(8,128)(2,1)}, bf16[768,640]{1,0:T(8,128)(2,1)S(1)}, u32[]{:S(2)}, u32[]{:S(2)}) collective-permute-start(bf16[768,640]{1,0:T(8,128)(2,1)} %assemble.2.refs_1_.refs_5_.refs_2_), channel_id=1, source_target_pairs={{0,16},{1,17},{2,18},{3,19},{4,20},{5,21},{6,22},{7,23},{8,24},{9,... | collective-permute-start | bytes 2949128 | tf_op jit(solution)/shard_map/ppermute | solution.py:651
  34.9 22.3 %collective-permute-start.8 = (bf16[4,96,192]{2,1,0:T(8,128)(2,1)}, bf16[4,96,192]{2,1,0:T(8,128)(2,1)}, u32[]{:S(2)}, u32[]{:S(2)}) collective-permute-start(bf16[4,96,192]{2,1,0:T(8,128)(2,1)} %pad_maximum_fusion.1.own_ref), channel_id=1, source_target_pairs={{0,1},{1,0},{2,3},{3,2},{4,5},{5,4},{6,7},{7,6},{8,9},{9,8},{10,11... | collective-permute-start | bytes 442376 | tf_op jit(solution)/shard_map/ppermute | solution.py:651
  35.9 7.0 %copy-start.3 = (bf16[768,640]{1,0:T(8,128)(2,1)}, bf16[768,640]{1,0:T(8,128)(2,1)S(1)}, u32[]{:S(2)}) copy-start(bf16[768,640]{1,0:T(8,128)(2,1)S(1)} %collective-permute-done.7.refs_2_.refs_6_.refs_3_) | copy-start | bytes 2949124
  35.9 44.2 %all-to-all-start = ((bf16[8,128,768]{2,1,0:T(8,128)(2,1)}), bf16[8,128,768]{2,1,0:T(8,128)(2,1)S(1)}, u32[]{:S(2)}, u32[]{:S(2)}) async-start(bf16[8,128,768]{2,1,0:T(8,128)(2,1)} %bitcast.17), calls=%async_computation | async-start | bytes 3145728 | tf_op jit(solution)/shard_map/all_to_all | solution.py:773
  59.8 2.6 collective-permute-start.10
  59.8 20.3 %collective-permute-start.11 = (bf16[768,192]{1,0:T(8,128)(2,1)}, bf16[768,192]{1,0:T(8,128)(2,1)}, u32[]{:S(2)}, u32[]{:S(2)}) collective-permute-start(bf16[768,192]{1,0:T(8,128)(2,1)} %assemble.3.refs_0_), channel_id=1, source_target_pairs={{0,16},{1,17},{2,18},{3,19},{4,20},{5,21},{6,22},{7,23},{8,24},{9,... | collective-permute-start | bytes 884744 | tf_op jit(solution)/shard_map/ppermute | solution.py:651
  61.4 18.8 %collective-permute-start.12 = (bf16[768,192]{1,0:T(8,128)(2,1)}, bf16[768,192]{1,0:T(8,128)(2,1)}, u32[]{:S(2)}, u32[]{:S(2)}) collective-permute-start(bf16[768,192]{1,0:T(8,128)(2,1)} %assemble.3.refs_0_), channel_id=1, source_target_pairs={{0,8},{1,9},{2,10},{3,11},{4,12},{5,13},{6,14},{7,15},{8,0},{9,1},... | collective-permute-start | bytes 884744 | tf_op jit(solution)/shard_map/ppermute | solution.py:651
  80.2 12.6 %copy-start.2 = (bf16[8,128,768]{2,1,0:T(8,128)(2,1)}, bf16[8,128,768]{2,1,0:T(8,128)(2,1)S(1)}, u32[]{:S(2)}) copy-start(bf16[8,128,768]{2,1,0:T(8,128)(2,1)S(1)} %all-to-all-done) | copy-start | bytes 4718596
  80.2 1.9 collective-permute-start.13
  117.7 24.0 %all-to-all-start.2 = ((bf16[8,64,768]{2,1,0:T(8,128)(2,1)}), bf16[8,64,768]{2,1,0:T(8,128)(2,1)S(1)}, u32[]{:S(2)}, u32[]{:S(2)}) async-start(bf16[8,64,768]{2,1,0:T(8,128)(2,1)} %bitcast.80), calls=%async_computation.2 | async-start | bytes 1572864 | tf_op jit(solution)/shard_map/all_to_all | solution.py:773
  141.7 4.0 %copy-start.8 = (bf16[8,64,768]{2,1,0:T(8,128)(2,1)}, bf16[8,64,768]{2,1,0:T(8,128)(2,1)S(1)}, u32[]{:S(2)}) copy-start(bf16[8,64,768]{2,1,0:T(8,128)(2,1)S(1)} %all-to-all-done.2) | copy-start | bytes 2359300
  141.7 24.3 %all-to-all-start.3 = ((bf16[8,64,768]{2,1,0:T(8,128)(2,1)}), bf16[8,64,768]{2,1,0:T(8,128)(2,1)S(1)}, u32[]{:S(2)}, u32[]{:S(2)}) async-start(bf16[8,64,768]{2,1,0:T(8,128)(2,1)} %bitcast.79), calls=%async_computation.3 | async-start | bytes 1572864 | tf_op jit(solution)/shard_map/all_to_all | solution.py:773
  166.0 21.3 %copy-start.6 = (bf16[8,64,768]{2,1,0:T(8,128)(2,1)}, bf16[8,64,768]{2,1,0:T(8,128)(2,1)S(1)}, u32[]{:S(2)}) copy-start(bf16[8,64,768]{2,1,0:T(8,128)(2,1)S(1)} %all-to-all-done.3) | copy-start | bytes 2359300
  166.0 23.9 %all-to-all-start.4 = ((bf16[8,64,768]{2,1,0:T(8,128)(2,1)}), bf16[8,64,768]{2,1,0:T(8,128)(2,1)S(1)}, u32[]{:S(2)}, u32[]{:S(2)}) async-start(bf16[8,64,768]{2,1,0:T(8,128)(2,1)} %bitcast.78), calls=%async_computation.4 | async-start | bytes 1572864 | tf_op jit(solution)/shard_map/all_to_all | solution.py:773
  170.1 19.9 %copy-start.15 = (s32[1024]{0:T(1024)S(1)}, s32[1024]{0:T(1024)}, u32[]{:S(2)}) copy-start(s32[1024]{0:T(1024)} %get-tuple-element.231) | copy-start | bytes 12292
  189.9 12.8 %copy-start.7 = (bf16[8,64,768]{2,1,0:T(8,128)(2,1)}, bf16[8,64,768]{2,1,0:T(8,128)(2,1)S(1)}, u32[]{:S(2)}) copy-start(bf16[8,64,768]{2,1,0:T(8,128)(2,1)S(1)} %all-to-all-done.4) | copy-start | bytes 2359300
  189.9 8.3 %collective-permute-start.14 = (bf16[2,1552,768]{2,1,0:T(8,128)(2,1)}, bf16[2,1552,768]{2,1,0:T(8,128)(2,1)}, u32[]{:S(2)}, u32[]{:S(2)}) collective-permute-start(bf16[2,1552,768]{2,1,0:T(8,128)(2,1)} %get-tuple-element.170), channel_id=1, source_target_pairs={{0,8},{1,9},{2,10},{3,11},{4,12},{5,13},{6,14},{7,15},{8,0},{9,1},... | collective-permute-start | bytes 14303240 | tf_op jit(solution)/shard_map/ppermute | solution.py:651
  191.0 50.1 %all-to-all-start.5 = ((bf16[8,128,768]{2,1,0:T(8,128)(2,1)}), bf16[8,128,768]{2,1,0:T(8,128)(2,1)S(1)}, u32[]{:S(2)}, u32[]{:S(2)}) async-start(bf16[8,128,768]{2,1,0:T(8,128)(2,1)} %bitcast.33), calls=%async_computation.5 | async-start | bytes 3145728 | tf_op jit(solution)/shard_map/all_to_all | solution.py:773
  215.9 23.8 %copy-start.16 = (s32[1024]{0:T(1024)S(1)}, s32[1024]{0:T(1024)}, u32[]{:S(2)}) copy-start(s32[1024]{0:T(1024)} %add_select_fusion) | copy-start | bytes 12292
  239.5 9.4 %collective-permute-start.15 = (bf16[4,96,1024]{2,1,0:T(8,128)(2,1)}, bf16[4,96,1024]{2,1,0:T(8,128)(2,1)}, u32[]{:S(2)}, u32[]{:S(2)}) collective-permute-start(bf16[4,96,1024]{2,1,0:T(8,128)(2,1)} %get-tuple-element.185), channel_id=1, source_target_pairs={{0,8},{1,9},{2,10},{3,11},{4,12},{5,13},{6,14},{7,15},{8,0},{9,1},... | collective-permute-start | bytes 2359304 | tf_op jit(solution)/shard_map/ppermute | solution.py:651
  240.7 34.6 %collective-permute-start.16 = (bf16[4,96,1024]{2,1,0:T(8,128)(2,1)}, bf16[4,96,1024]{2,1,0:T(8,128)(2,1)S(1)}, u32[]{:S(2)}, u32[]{:S(2)}) collective-permute-start(bf16[4,96,1024]{2,1,0:T(8,128)(2,1)} %get-tuple-element.194), channel_id=1, source_target_pairs={{0,8},{1,9},{2,10},{3,11},{4,12},{5,13},{6,14},{7,15},{8,0},{9,1},... | collective-permute-start | bytes 2359304 | tf_op jit(solution)/shard_map/ppermute | solution.py:651
  241.1 7.7 %copy-start.10 = (bf16[4,96,1024]{2,1,0:T(8,128)(2,1)S(1)}, bf16[4,96,1024]{2,1,0:T(8,128)(2,1)}, u32[]{:S(2)}) copy-start(bf16[4,96,1024]{2,1,0:T(8,128)(2,1)} %get-tuple-element.184) | copy-start | bytes 2359300
  241.1 56.2 %collective-permute-start.21 = (bf16[1552,768]{1,0:T(8,128)(2,1)}, bf16[1552,768]{1,0:T(8,128)(2,1)}, u32[]{:S(2)}, u32[]{:S(2)}) collective-permute-start(bf16[1552,768]{1,0:T(8,128)(2,1)} %fusion), channel_id=1, source_target_pairs={{0,16},{1,17},{2,18},{3,19},{4,20},{5,21},{6,22},{7,23},{8,24},{9,... | collective-permute-start | bytes 7151624 | tf_op jit(solution)/shard_map/ppermute | solution.py:651
  251.2 24.2 %copy-start.9 = (bf16[4,96,1024]{2,1,0:T(8,128)(2,1)S(1)}, bf16[4,96,1024]{2,1,0:T(8,128)(2,1)}, u32[]{:S(2)}) copy-start(bf16[4,96,1024]{2,1,0:T(8,128)(2,1)} %get-tuple-element.193) | copy-start | bytes 2359300
  251.2 24.5 %collective-permute-start.17 = (bf16[4,96,1024]{2,1,0:T(8,128)(2,1)}, bf16[4,96,1024]{2,1,0:T(8,128)(2,1)S(1)}, u32[]{:S(2)}, u32[]{:S(2)}) collective-permute-start(bf16[4,96,1024]{2,1,0:T(8,128)(2,1)} %add_convert_fusion.2), channel_id=1, source_target_pairs={{0,1},{1,0},{2,3},{3,2},{4,5},{5,4},{6,7},{7,6},{8,9},{9,8},{10,11... | collective-permute-start | bytes 2359304 | tf_op jit(solution)/shard_map/ppermute | solution.py:651
  275.7 3.3 %copy-start.12 = (bf16[4,96,640]{2,1,0:T(8,128)(2,1)S(1)}, bf16[4,96,640]{2,1,0:T(8,128)(2,1)}, u32[]{:S(2)}) copy-start(bf16[4,96,640]{2,1,0:T(8,128)(2,1)} %get-tuple-element.197) | copy-start | bytes 1474564
  276.4 1.9 collective-permute-start.19
  276.6 2.4 collective-permute-start.18
  279.1 18.2 %collective-permute-start.20 = (bf16[4,96,640]{2,1,0:T(8,128)(2,1)S(1)}, bf16[4,96,640]{2,1,0:T(8,128)(2,1)S(1)}, u32[]{:S(2)}, u32[]{:S(2)}) collective-permute-start(bf16[4,96,640]{2,1,0:T(8,128)(2,1)S(1)} %add_convert_fusion.4), channel_id=1, source_target_pairs={{0,1},{1,0},{2,3},{3,2},{4,5},{5,4},{6,7},{7,6},{8,9},{9,8},{10,11... | collective-permute-start | bytes 1474568 | tf_op jit(solution)/shard_map/ppermute | solution.py:651
  279.8 15.1 %collective-permute-start.22 = (bf16[96,1024]{1,0:T(8,128)(2,1)S(1)}, bf16[96,1024]{1,0:T(8,128)(2,1)S(1)}, u32[]{:S(2)}, u32[]{:S(2)}) collective-permute-start(bf16[96,1024]{1,0:T(8,128)(2,1)S(1)} %get-tuple-element.206), channel_id=1, source_target_pairs={{0,2},{1,3},{2,0},{3,1},{4,6},{5,7},{6,4},{7,5},{8,10},{9,11},{10,... | collective-permute-start | bytes 589832 | tf_op jit(solution)/shard_map/ppermute | solution.py:651
  280.1 17.2 %collective-permute-start.23 = (bf16[96,1024]{1,0:T(8,128)(2,1)S(1)}, bf16[96,1024]{1,0:T(8,128)(2,1)S(1)}, u32[]{:S(2)}, u32[]{:S(2)}) collective-permute-start(bf16[96,1024]{1,0:T(8,128)(2,1)S(1)} %get-tuple-element.207), channel_id=1, source_target_pairs={{0,4},{1,5},{2,6},{3,7},{4,0},{5,1},{6,2},{7,3},{8,12},{9,13},{10,... | collective-permute-start | bytes 589832 | tf_op jit(solution)/shard_map/ppermute | solution.py:651
  281.7 15.6 %collective-permute-start.24 = (bf16[96,1024]{1,0:T(8,128)(2,1)S(1)}, bf16[96,1024]{1,0:T(8,128)(2,1)S(1)}, u32[]{:S(2)}, u32[]{:S(2)}) collective-permute-start(bf16[96,1024]{1,0:T(8,128)(2,1)S(1)} %get-tuple-element.208), channel_id=1, source_target_pairs={{0,6},{1,7},{2,4},{3,5},{4,2},{5,3},{6,0},{7,1},{8,14},{9,15},{10,... | collective-permute-start | bytes 589832 | tf_op jit(solution)/shard_map/ppermute | solution.py:651
  297.4 15.3 %collective-permute-start.28 = (bf16[96,832]{1,0:T(8,128)(2,1)S(1)}, bf16[96,832]{1,0:T(8,128)(2,1)S(1)}, u32[]{:S(2)}, u32[]{:S(2)}) collective-permute-start(bf16[96,832]{1,0:T(8,128)(2,1)S(1)} %slice.265), channel_id=1, source_target_pairs={{0,16},{1,17},{2,18},{3,19},{4,20},{5,21},{6,22},{7,23},{8,24},{9,... | collective-permute-start | bytes 479240 | tf_op jit(solution)/shard_map/ppermute | solution.py:651
  298.8 12.6 %collective-permute-start.25 = (bf16[96,640]{1,0:T(8,128)(2,1)S(1)}, bf16[96,640]{1,0:T(8,128)(2,1)S(1)}, u32[]{:S(2)}, u32[]{:S(2)}) collective-permute-start(bf16[96,640]{1,0:T(8,128)(2,1)S(1)} %get-tuple-element.241), channel_id=1, source_target_pairs={{0,2},{1,3},{2,0},{3,1},{4,6},{5,7},{6,4},{7,5},{8,10},{9,11},{10,... | collective-permute-start | bytes 368648 | tf_op jit(solution)/shard_map/ppermute | solution.py:651
  302.2 10.5 %collective-permute-start.26 = (bf16[96,640]{1,0:T(8,128)(2,1)S(1)}, bf16[96,640]{1,0:T(8,128)(2,1)S(1)}, u32[]{:S(2)}, u32[]{:S(2)}) collective-permute-start(bf16[96,640]{1,0:T(8,128)(2,1)S(1)} %get-tuple-element.240), channel_id=1, source_target_pairs={{0,4},{1,5},{2,6},{3,7},{4,0},{5,1},{6,2},{7,3},{8,12},{9,13},{10,... | collective-permute-start | bytes 368648 | tf_op jit(solution)/shard_map/ppermute | solution.py:651
  302.4 10.3 %collective-permute-start.27 = (bf16[96,640]{1,0:T(8,128)(2,1)S(1)}, bf16[96,640]{1,0:T(8,128)(2,1)S(1)}, u32[]{:S(2)}, u32[]{:S(2)}) collective-permute-start(bf16[96,640]{1,0:T(8,128)(2,1)S(1)} %get-tuple-element.239), channel_id=1, source_target_pairs={{0,6},{1,7},{2,4},{3,5},{4,2},{5,3},{6,0},{7,1},{8,14},{9,15},{10,... | collective-permute-start | bytes 368648 | tf_op jit(solution)/shard_map/ppermute | solution.py:651
  313.7 1.2 collective-permute-start.29
  315.1 4.2 %collective-permute-start.30 = (f32[8,96]{0,1:T(8,128)S(1)}, f32[8,96]{0,1:T(8,128)S(1)}, u32[]{:S(2)}, u32[]{:S(2)}) collective-permute-start(f32[8,96]{0,1:T(8,128)S(1)} %fusion.17), channel_id=1, source_target_pairs={{0,16},{1,17},{2,18},{3,19},{4,20},{5,21},{6,22},{7,23},{8,24},{9,... | collective-permute-start | bytes 9224 | tf_op jit(solution)/shard_map/ppermute | solution.py:651
  (8 other events, 11.8 us)

commit v5 on v4

--- a/solution.py
+++ b/solution.py
@@ -240,9 +240,8 @@
             copies = []
             for i in range(8):
                 src = stage.at[pl.ds(pl.multiple_of(rows * table[i], 32), rows)]
-                copies.append(
-                    pltpu.make_async_copy(src, slabs[2 * g + i // 4].at[i % 4], sems.at[i])
-                )
+                dst = slabs[2].at[i] if g else slabs[i // 4].at[i % 4]
+                copies.append(pltpu.make_async_copy(src, dst, sems.at[i]))
             for c in copies:
                 c.start()
             for c in copies:
@@ -255,7 +254,7 @@
     width = low.shape[1]
     at = lambda g, *_: (2 * half + g, 0, 0)
     cols = FAR if half else 640
-    slab = (PLACED, (4, width // 8, cols), BF)
+    slabs = [(PLACED, (n, width // 8, cols), BF) for n in (4, 4, 8)]
     o_specs = [
         pl.BlockSpec((1, width, part), lambda g, order, table, b=b: (order[b + g], 0, 0))
         for b in ((2, 0) if half else ())
@@ -272,7 +271,7 @@
         + [pl.BlockSpec((width, 640), lambda *_: (0, 0), pipeline_mode=pl.Buffered(1))] * 2
         + [full((8, width))] + o_specs,
         [(pl.BlockSpec((1, count, 3 * part), lambda g, *_: (g, 0, 0)), (2, count, 3 * part), BF)]
-        + [slab] * 4,
+        + slabs,
         [
             pltpu.VMEM((HEAD_DIM, SEQ_LEN), F32),
             pltpu.VMEM((width, cols), BF),
@@ -282,26 +281,27 @@
     )(order, table, qkv, ctx, dctx, lse, low, *weights, two, *[o_part] * len(o_specs))
 
 
-def dispatch_kernel(target_ref, rows_ref, out_ref):
+def dispatch_kernel(first, target_ref, rows_ref, out_ref):
     count = rows_ref.shape[0]
-    for at in range(0, count, 256):
-        slot = lax.broadcasted_iota(jnp.int32, (256, count), 0) + at
+    for at in range(0, out_ref.shape[0], 256):
+        slot = lax.broadcasted_iota(jnp.int32, (256, count), 0) + (first + at)
         picks = (target_ref[...] == slot).astype(F32).astype(BF)
         out_ref[at : at + 256] = dot(picks, rows_ref[...], 1, 0).astype(BF)
 
 
-def dispatch(target, rows):
+def dispatch(target, rows, first=0):
     count, width = rows.shape
+    slots = count - first
     return call(
-        dispatch_kernel, "dispatch", (1,),
+        partial(dispatch_kernel, first), "dispatch", (1,),
         [full((1, count)), full((count, width))],
-        [(full((count, width)), (count, width), BF)],
+        [(full((slots, width)), (slots, width), BF)],
         cost=(2 * count * count * width, 3_000_000, 0),
     )(target.reshape(1, count), rows)[0]
 
 
 def mix_kernel(order, x_ref, ctx_ref, vec_ref, target_ref, *refs):
-    wo_refs, (h_ref, whole_ref, *sent, low_ref) = refs[:GROUPS], refs[GROUPS:]
+    wo_refs, (h_ref, whole_ref, low_ref, sent_ref) = refs[:GROUPS], refs[GROUPS:]
     rows, width = x_ref.shape
     count = low_ref.shape[0]
     part = width // GROUPS
@@ -329,11 +329,10 @@
 
     @pl.when(step == pl.num_programs(0) - 1)
     def _():
-        for half in range(2):
-            for at in range(0, count // 2, 256):
-                index = lax.broadcasted_iota(jnp.int32, (256, count), 0) + (half * count // 2 + at)
-                picks = (target_ref[...] == index).astype(F32).astype(BF)
-                sent[half][at : at + 256] = dot(picks, low_ref[...], 1, 0).astype(BF)
+        for at in range(0, count // 2, 256):
+            index = lax.broadcasted_iota(jnp.int32, (256, count), 0) + at
+            picks = (target_ref[...] == index).astype(F32).astype(BF)
+            sent_ref[at : at + 256] = dot(picks, low_ref[...], 1, 0).astype(BF)
 
 
 def mix(order, x, ctx, weights, vec, target):
@@ -347,10 +346,9 @@
         [
             (chunk((rows, width)), (count, width), F32),
             (full((width, width)), (width, width), BF),
-            (full((count // 2, width)), (count // 2, width), BF),
+            (full((count, width)), (count, width), BF),
             (full((count // 2, width)), (count // 2, width), BF),
         ],
-        [pltpu.VMEM((count, width), BF)],
         cost=(2 * count * width * (width + count), 12_000_000, 0),
     )(order, x, ctx, vec, target.reshape(1, count), *weights)
 
@@ -634,6 +632,7 @@
         to = lambda move: [(dev(*p), dev(*move(*p))) for p in every]
         self.core = to(lambda x, c, z, y: (x, 1 - c, z, y))
         self.x = to(lambda x, c, z, y: (1 - x, c, z, y))
+        self.across = to(lambda x, c, z, y: (1 - x, 1 - c, z, y))
         self.y = to(lambda x, c, z, y: (x, c, z, 1 - y))
         self.z = [to(lambda x, c, z, y, k=k: (x, c, z ^ k, y)) for k in range(1, 4)]
 
@@ -710,8 +709,7 @@
     cols = (FAR - 640) // 2
     parts = [total[:, i * cols : (i + 1) * cols] for i in range(3)]
     vecs = total[:, 576 : 576 + 8].T
-    vecs = vecs + place.move(vecs, place.core)
-    vecs = vecs + place.move(vecs, place.x)
+    vecs = vecs + sum(place.move(vecs, way) for way in (place.core, place.x, place.across))
     return parts, [vecs[i] for i in range(count)]
 
 
@@ -807,9 +805,10 @@
     if place.staged:
         ctx, out_across = barrier((ctx, out_across))
         out += (out_across, place.move(out_across, place.core))
-    h1, whole_o, sent_one, sent_two = mix(order, block_entries, ctx, out, vec, halved)
-
-    x_one = exchange(sent_one)
+    h1, whole_o, low_mid, sent_one = mix(order, block_entries, ctx, out, vec, halved)
+
+    sent_two = dispatch(halved, low_mid, count // 2)
+    x_one, sent_two = barrier((exchange(sent_one), sent_two))
     x_two = exchange(sent_two)
     matrices = (
         specialist_widen_weights[0], specialist_widen_shift, specialist_contract_weights[0],
@@ -836,8 +835,6 @@
         grads_far, gy, dm_two = barrier((grads_far, gy, dm_two))
         came_far = place.move(grads_far, place.core)
         crossing = add(grads[0], came_far[0])
-        crossing, h1 = barrier((crossing, h1))
-        came = place.move(crossing, place.x)
     else:
         grads = weigh(jnp.arange(n_dp, dtype=jnp.int32), n_dp, False, *sides)
         grads = lax.psum_scatter(grads, "dp", scatter_dimension=0, tiled=False)
@@ -851,28 +848,31 @@
         two,
     )
     if place.staged:
-        far, keep, send, *more = back(1, dctx)
-        more = [place.move(m, place.core) for m in more]
+        dctx, crossing = barrier((dctx, crossing))
+        came = place.move(crossing, place.x)
+        far, keep, send, more = back(1, dctx)
+        more = place.move(more, place.core)
         far, gy = barrier((far, gy))
         output = finish(h1, target, gy)
-        send = add(send, more[1])
+        send = add(send, more[4:])
         dctx, output, send = barrier((dctx, output, send))
-        across, sends = reduce_y(place, add(keep, more[0]), send)
-        near, keep, send, *more = back(0, dctx)
+        across, sends = reduce_y(place, add(keep, more[:4]), send)
+        near, keep, send, more = back(0, dctx)
         near, keep, send, more, across, sends = barrier((near, keep, send, more, across, sends))
-        more = [place.move(m, place.core) for m in more]
+        more = place.move(more, place.core)
         got = reduce_z(place, sends)
-        send, keep = add(send, more[1]), add(keep, more[0])
+        send, keep = add(send, more[4:]), add(keep, more[:4])
         near, send, keep = barrier((near, send, keep))
         got_y = place.move(send, place.y)
         input_grad = unproject((near, far), weights, block_entries, dh1, vec)
         got_far = got
-        got, input_grad, came, got_far = barrier((got_y, input_grad, came, got_far))
+        got, input_grad, came = barrier((got_y, input_grad, came))
+        total = keep[0].astype(F32) + got[0].astype(F32)
+        got = reduce_z(place, [add(keep[k], got[k]) for k in range(1, 4)])
+        got_far, came, input_grad = barrier((got_far, came, input_grad))
         sum_o = across + sum(g.astype(F32) for g in got_far)
         cols = width // GROUPS
         across = place.move(sum_o[:, :-cols].astype(BF), place.x)
-        total = keep[0].astype(F32) + got[0].astype(F32)
-        got = reduce_z(place, [add(keep[k], got[k]) for k in range(1, 4)])
         pick = lambda at: sum(
             a[at : at + width].astype(F32) for a in (grads[1], came_far[1], came)
         )
@@ -884,7 +884,7 @@
     else:
         parts = [back(half, dctx) for half in range(2)]
         slabs = [
-            [jnp.concatenate(p[1 + 2 * g : 3 + 2 * g]).reshape(width, -1) for g in range(2)]
+            [jnp.concatenate(p[1:3]).reshape(width, -1), p[3].reshape(width, -1)]
             for p in parts
         ]
         (sum_q, sum_k, sum_v, sum_o), small = reduce_plain(*slabs, 7)

time: 324 us -> 322 us (level)
  blocking collectives: 24.9 us -> 0 us
  waiting for transfers between devices: 31.7 us -> 47.1 us
  starting transfers between devices: 55.9 us -> 60.1 us
    all_to_all x1 -> x0, blocking collectives: 24.9 us -> none  [exchange(): lax.all_to_all(sent, 'expert', split_axis=0, concat_axis=0, tiled=True)]
    all_to_all x5 -> x6, waiting for transfers between devices: 11.8 us -> 29.7 us  [exchange(): lax.all_to_all(sent, 'expert', split_axis=0, concat_axis=0, tiled=True)]
    all_to_all x5 -> x6, starting transfers between devices: 21.9 us -> 25.5 us  [exchange(): lax.all_to_all(sent, 'expert', split_axis=0, concat_axis=0, tiled=True)]
    pallas_call x1 -> x2, Pallas kernels: 4.36 us -> 7.62 us  [dispatch(): call(partial(dispatch_kernel, first), 'dispatch', (1,), [full((1, count))...]
    ppermute x31 -> x30, waiting for transfers between devices: 19.9 us -> 17.4 us  [move(): return lax.ppermute(array, BOTH, way)]
    convert_element_type x7 -> x5, other arithmetic: 7.71 us -> 7.07 us  [add(): return (a.astype(F32) + b.astype(F32)).astype(BF)]
    ppermute x31 -> x30, starting transfers between devices: 34 us -> 34.6 us  [move(): return lax.ppermute(array, BOTH, way)]
  transfers between devices with their start and end apart: 36 -> 36, of which waited for: 17 -> 17; matrix products, arithmetic and copies ran while one was open for 7% -> 7% of each run, Pallas kernels for 51% -> 52%
where the time goes in v5:
time: 322 us; the launch traced here: 318 us
  Pallas kernels  179 us (56%)
  starting transfers between devices  60.1 us (19%)
  waiting for transfers between devices  47.1 us (15%)
  other arithmetic  20.1 us (6%)
  local copies, waits for them, and re-layouts  10.4 us (3%)
    pallas_call x2, Pallas kernels, attend_back(): call(partial(attend_back_kernel, half), 'attend_back', (2,), [pl.BlockSpe...  46.6 us
    pallas_call x2, Pallas kernels, expert(): call(expert_kernel, 'expert', (ff // step,), [full((rows, width)), side,...  35.1 us
    ppermute x30, starting transfers between devices, move(): return lax.ppermute(array, BOTH, way)  34.6 us
    all_to_all x6, waiting for transfers between devices, exchange(): lax.all_to_all(sent, 'expert', split_axis=0, concat_axis=0, tiled=True)  29.7 us
    pallas_call x2, Pallas kernels, attend(): call(partial(attend_kernel, half), 'attend', (2,), [SCALARS] + ins, outs,...  27.5 us
    all_to_all x6, starting transfers between devices, exchange(): lax.all_to_all(sent, 'expert', split_axis=0, concat_axis=0, tiled=True)  25.5 us
    ppermute x30, waiting for transfers between devices, move(): return lax.ppermute(array, BOTH, way)  17.4 us
    pallas_call x1, Pallas kernels, weigh(): call(partial(weigh_kernel, split), 'weigh', (n,), [wide] * 4 + [full((row...  17.2 us
  transfers between devices with their start and end apart: 36, of which 17 were waited for; matrix products, arithmetic and copies ran while one was open for 7% of the time, Pallas kernels for 52%

profile of v5, /device:TPU:0, one launch (start us, length us, event | category | flops | bytes accessed | tf_op | source)
XLA Modules:
  0.0 318.0 jit_solution(389354868838568253)
XLA Ops:
  2.5 4.1 %collective-permute-start.1 = (bf16[96,640]{1,0:T(8,128)(2,1)S(1)}, bf16[96,640]{1,0:T(8,128)(2,1)S(1)}, u32[]{:S(2)}, u32[]{:S(2)}) collective-permute-start(bf16[96,640]{1,0:T(8,128)(2,1)S(1)} %concatenate.3), channel_id=1, source_target_pairs={{0,4},{1,5},{2,6},{3,7},{4,0},{5,1},{6,2},{7,3},{8,12},{9,13},{10,... | collective-permute-start | bytes 368648 | tf_op jit(solution)/shard_map/ppermute | solution.py:650
  6.6 1.3 collective-permute-start.2
  11.6 4.4 %dispatch.2 = bf16[1024,768]{1,0:T(8,128)(2,1)} custom-call(s32[1,1024]{1,0:T(1,128)} %bitcast.94, bf16[1024,768]{1,0:T(8,128)(2,1)} %g_ref.1), custom_call_target="tpu_custom_call" | custom-call | flops 1610612736 | bytes 3000000 | tf_op jit(solution)/shard_map/dispatch/pallas_call | solution.py:295
  16.7 1.6 collective-permute-start.3
  18.4 2.0 collective-permute-start.4
  20.3 2.1 collective-permute-start.5
  24.2 1.5 collective-permute-done.5
  25.7 2.6 collective-permute-done.6
  29.8 3.0 assemble.2.refs_1_.refs_5_.refs_2_
  33.4 1.5 collective-permute-start.9
  35.9 7.0 %all-to-all-start = ((bf16[8,128,768]{2,1,0:T(8,128)(2,1)}), bf16[8,128,768]{2,1,0:T(8,128)(2,1)S(1)}, u32[]{:S(2)}, u32[]{:S(2)}) async-start(bf16[8,128,768]{2,1,0:T(8,128)(2,1)} %bitcast.17), calls=%async_computation | async-start | bytes 3145728 | tf_op jit(solution)/shard_map/all_to_all | solution.py:771
  42.9 14.3 %attend.2 = (bf16[4,1024,576]{2,1,0:T(8,128)(2,1)}, bf16[4,1024,192]{2,1,0:T(8,128)(2,1)}, f32[4,8,1024]{2,1,0:T(8,128)}, bf16[1024,768]{1,0:T(8,128)(2,1)}, f32[8,768]{1,0:T(8,128)}) custom-call(s32[4]{0:T(128)} %get-tuple-element.255.order, bf16[1024,768]{1,0:T(8,128)(2,1)} %refs_6_.1, bf16[768,640]{1,0:T(8,128)(2,1)} %assemble.2.refs_1_.refs_5_.refs_2_, ...), custom_call_target="tpu_custom_call" | custom-call | flops 12000000000 | bytes 8000000 | tf_op jit(solution)/shard_map/attend/pallas_call | solution.py:167
  57.3 2.5 assemble.3.refs_0_
  59.8 1.6 collective-permute-start.11
  63.4 13.2 %attend.3 = (bf16[4,1024,576]{2,1,0:T(8,128)(2,1)}, bf16[4,1024,192]{2,1,0:T(8,128)(2,1)}, f32[4,8,1024]{2,1,0:T(8,128)}) custom-call(s32[4]{0:T(128)} %get-tuple-element.255.order, bf16[1024,768]{1,0:T(8,128)(2,1)} %get-tuple-element.127.refs_0_.refs_4_, ...), custom_call_target="tpu_custom_call", output_to_operand_aliasing={{0}: (5, {}), {1}: (6, {}), {2}: (7, {})} | custom-call | flops 12000000000 | bytes 8000000 | tf_op jit(solution)/shard_map/attend/pallas_call | solution.py:167
  76.6 3.6 %all-to-all-done = bf16[8,128,768]{2,1,0:T(8,128)(2,1)S(1)} async-done(((bf16[8,128,768]{2,1,0:T(8,128)(2,1)}), bf16[8,128,768]{2,1,0:T(8,128)(2,1)S(1)}, u32[]{:S(2)}, u32[]{:S(2)}) %all-to-all-start) | async-done | bytes 1572896 | tf_op jit(solution)/shard_map/all_to_all | solution.py:771
  80.2 1.9 collective-permute-done.13.refs_3_
  82.9 9.4 %mix.1 = (f32[1024,768]{1,0:T(8,128)}, bf16[768,768]{1,0:T(8,128)(2,1)}, bf16[1024,768]{1,0:T(8,128)(2,1)}, bf16[512,768]{1,0:T(8,128)(2,1)}) custom-call(s32[4]{0:T(128)} %get-tuple-element.255.order, bf16[1024,768]{1,0:T(8,128)(2,1)} %refs_6_.1, bf16[4,1024,192]{2,1,0:T(8,128)(2,1)} %get-tuple-element.146.ctx_ref.refs_1_, ...), custom_call_target="tpu_custom_call" | custom-call | flops 2818572288 | bytes 12000000 | tf_op jit(solution)/shard_map/mix/pallas_call | solution.py:342
  92.3 3.7 %all-to-all-start.1 = ((bf16[8,64,768]{2,1,0:T(8,128)(2,1)}), bf16[8,64,768]{2,1,0:T(8,128)(2,1)S(1)}, u32[]{:S(2)}, u32[]{:S(2)}) async-start(bf16[8,64,768]{2,1,0:T(8,128)(2,1)} %bitcast.81), calls=%async_computation.1 | async-start | bytes 1572864 | tf_op jit(solution)/shard_map/all_to_all | solution.py:771
  95.9 3.3 %dispatch.3 = bf16[512,768]{1,0:T(8,128)(2,1)} custom-call(s32[1,1024]{1,0:T(1,128)} %bitcast.92, bf16[1024,768]{1,0:T(8,128)(2,1)} %get-tuple-element.150.rows_ref), custom_call_target="tpu_custom_call" | custom-call | flops 1610612736 | bytes 3000000 | tf_op jit(solution)/shard_map/dispatch/pallas_call | solution.py:295
  99.2 17.3 %all-to-all-done.1 = bf16[8,64,768]{2,1,0:T(8,128)(2,1)S(1)} async-done(((bf16[8,64,768]{2,1,0:T(8,128)(2,1)}), bf16[8,64,768]{2,1,0:T(8,128)(2,1)S(1)}, u32[]{:S(2)}, u32[]{:S(2)}) %all-to-all-start.1) | async-done | bytes 786464 | tf_op jit(solution)/shard_map/all_to_all | solution.py:771
  116.5 3.6 %all-to-all-start.2 = ((bf16[8,64,768]{2,1,0:T(8,128)(2,1)}), bf16[8,64,768]{2,1,0:T(8,128)(2,1)S(1)}, u32[]{:S(2)}, u32[]{:S(2)}) async-start(bf16[8,64,768]{2,1,0:T(8,128)(2,1)} %bitcast.80), calls=%async_computation.2 | async-start | bytes 1572864 | tf_op jit(solution)/shard_map/all_to_all | solution.py:771
  120.1 17.6 %expert.2 = (bf16[8,2,64,768]{3,2,1,0:T(8,128)(2,1)}, bf16[512,768]{1,0:T(8,128)(2,1)}, bf16[512,768]{1,0:T(8,128)(2,1)}, bf16[512,3072]{1,0:T(8,128)(2,1)}, bf1...) custom-call(bf16[512,768]{1,0:T(8,128)(2,1)} %bitcast.72, bf16[8,2,64,768]{3,2,1,0:T(8,128)(2,1)} %bitcast.69, ...), custom_call_target="tpu_custom_call" | custom-call | flops 9663676416 | bytes 22000000 | tf_op jit(solution)/shard_map/expert/pallas_call | solution.py:502
  137.7 2.8 all-to-all-done.2
  140.5 4.0 %all-to-all-start.3 = ((bf16[8,64,768]{2,1,0:T(8,128)(2,1)}), bf16[8,64,768]{2,1,0:T(8,128)(2,1)S(1)}, u32[]{:S(2)}, u32[]{:S(2)}) async-start(bf16[8,64,768]{2,1,0:T(8,128)(2,1)} %bitcast.79), calls=%async_computation.3 | async-start | bytes 1572864 | tf_op jit(solution)/shard_map/all_to_all | solution.py:771
  144.5 17.6 %expert.3 = (bf16[8,2,64,768]{3,2,1,0:T(8,128)(2,1)}, bf16[512,768]{1,0:T(8,128)(2,1)}, bf16[512,768]{1,0:T(8,128)(2,1)}, bf16[512,3072]{1,0:T(8,128)(2,1)}, bf1...) custom-call(bf16[512,768]{1,0:T(8,128)(2,1)} %bitcast.75, ...), custom_call_target="tpu_custom_call", output_to_operand_aliasing={{0}: (7, {})} | custom-call | flops 9663676416 | bytes 22000000 | tf_op jit(solution)/shard_map/expert/pallas_call | solution.py:502
  162.1 2.8 all-to-all-done.3
  164.8 3.6 %all-to-all-start.4 = ((bf16[8,64,768]{2,1,0:T(8,128)(2,1)}), bf16[8,64,768]{2,1,0:T(8,128)(2,1)S(1)}, u32[]{:S(2)}, u32[]{:S(2)}) async-start(bf16[8,64,768]{2,1,0:T(8,128)(2,1)} %bitcast.78), calls=%async_computation.4 | async-start | bytes 1572864 | tf_op jit(solution)/shard_map/all_to_all | solution.py:771
  168.4 17.2 %weigh.1 = (bf16[2,1552,768]{2,1,0:T(8,128)(2,1)}, bf16[2,1552,768]{2,1,0:T(8,128)(2,1)}) custom-call(s32[4]{0:T(128)} %get-tuple-element.254.which, bf16[512,3072]{1,0:T(8,128)(2,1)} %get-tuple-element.161.refs_0_, bf16[512,3072]{1,0:T(8,128)(2,1)} %get-tuple-element.162.refs_1_, bf16[512,3072]{1,0:T(8,128)(2,1)} %get-tuple-element.163.refs_2_, ...), custom_call_target="tpu_custom_call" | custom-call | flops 9663676416 | bytes 26000000 | tf_op jit(solution)/shard_map/weigh/pallas_call | solution.py:582
  185.5 3.2 %all-to-all-done.4 = bf16[8,64,768]{2,1,0:T(8,128)(2,1)S(1)} async-done(((bf16[8,64,768]{2,1,0:T(8,128)(2,1)}), bf16[8,64,768]{2,1,0:T(8,128)(2,1)S(1)}, u32[]{:S(2)}, u32[]{:S(2)}) %all-to-all-start.4) | async-done | bytes 786464 | tf_op jit(solution)/shard_map/all_to_all | solution.py:771
  189.8 3.8 %all-to-all-start.5 = ((bf16[8,128,768]{2,1,0:T(8,128)(2,1)}), bf16[8,128,768]{2,1,0:T(8,128)(2,1)S(1)}, u32[]{:S(2)}, u32[]{:S(2)}) async-start(bf16[8,128,768]{2,1,0:T(8,128)(2,1)} %bitcast.33), calls=%async_computation.5 | async-start | bytes 3145728 | tf_op jit(solution)/shard_map/all_to_all | solution.py:771
  193.6 13.3 %unmix.1 = (f32[1024,768]{1,0:T(8,128)}, bf16[4,1024,192]{2,1,0:T(8,128)(2,1)}, bf16[4,768,192]{2,1,0:T(8,128)(2,1)}, f32[8,768]{1,0:T(8,128)}) custom-call(s32[4]{0:T(128)} %get-tuple-element.255.order, f32[1024,768]{1,0:T(8,128)} %get-tuple-element.148.h_ref, bf16[1024,768]{1,0:T(8,128)(2,1)} %g_ref.1, bf16[512,768]{1,0:T(8,128)(2,1)} %bitcast.71, ...), custom_call_target="tpu_custom_call" | custom-call | flops 4026531840 | bytes 20000000 | tf_op jit(solution)/shard_map/unmix/pallas_call | solution.py:409
  206.9 4.4 %fusion = bf16[1552,768]{1,0:T(8,128)(2,1)} fusion(bf16[2,1552,768]{2,1,0:T(8,128)(2,1)} %collective-permute-done.14, bf16[2,1552,768]{2,1,0:T(8,128)(2,1)} %get-tuple-element.177), kind=kLoop, calls=%fused_computation.1 | loop fusion | flops 4767744 | bytes 7151616 | tf_op jit(solution)/shard_map/convert_element_type | solution.py:618
  211.3 23.8 %attend_back.2 = (bf16[2,1024,576]{2,1,0:T(8,128)(2,1)}, bf16[4,96,1024]{2,1,0:T(8,128)(2,1)}, bf16[4,96,1024]{2,1,0:T(8,128)(2,1)}, bf16[8,96,1024]{2,1,0:T(8,128)(2,1)}) custom-call(s32[4]{0:T(128)} %get-tuple-element.255.order, s32[8]{0:T(128)} %fusion.15.table, bf16[4,1024,576]{2,1,0:T(8,128)(2,1)} %get-tuple-element.180.refs_0_, ...), custom_call_target="tpu_custom_call" | custom-call | flops 24000000000 | bytes 14000000 | tf_op jit(solution)/shard_map/attend_back/pallas_call | solution.py:262
  236.6 1.5 collective-permute-start.22
  238.1 6.2 %finish.1 = bf16[1024,768]{1,0:T(8,128)(2,1)} custom-call(f32[1024,768]{1,0:T(8,128)} %get-tuple-element.148.h_ref, s32[1024,1]{1,0:T(8,128)} %copy.64.target_ref, bf16[1024,768]{1,0:T(8,128)(2,1)} %bitcast.66), custom_call_target="tpu_custom_call" | custom-call | flops 1610612736 | bytes 6000000 | tf_op jit(solution)/shard_map/finish/pallas_call | solution.py:433
  244.4 2.0 add_convert_fusion.1
  246.4 1.7 collective-permute-start.16
  248.2 22.9 %attend_back.3 = (bf16[2,1024,576]{2,1,0:T(8,128)(2,1)}, bf16[4,96,640]{2,1,0:T(8,128)(2,1)}, bf16[4,96,640]{2,1,0:T(8,128)(2,1)}, bf16[8,96,640]{2,1,0:T(8,128)(2,1)}) custom-call(s32[4]{0:T(128)} %get-tuple-element.255.order, s32[8]{0:T(128)} %fusion.15.table, bf16[4,1024,576]{2,1,0:T(8,128)(2,1)} %get-tuple-element.180.refs_0_, ...), custom_call_target="tpu_custom_call" | custom-call | flops 24000000000 | bytes 14000000 | tf_op jit(solution)/shard_map/attend_back/pallas_call | solution.py:262
  272.3 2.6 collective-permute-done.20
  275.5 1.7 collective-permute-start.17
  277.2 2.4 collective-permute-start.18
  279.9 10.7 %unproject.1 = f32[1024,768]{1,0:T(8,128)} custom-call(bf16[2,1024,576]{2,1,0:T(8,128)(2,1)} %get-tuple-element.205.refs_0_, bf16[2,1024,576]{2,1,0:T(8,128)(2,1)} %get-tuple-element.206.refs_1_, bf16[768,640]{1,0:T(8,128)(2,1)} %assemble.2.refs_1_.refs_5_.refs_2_, bf16[768,640]{1,0:T(8,128)(2,1)} %copy-done.3, bf16[768,640]{1,0:T(8,128)(2,1)} %copy-done.4, ...), custom_call_target="tpu_custom_call" | custom-call | flops 3623878656 | bytes 20000000 | tf_op jit(solution)/shard_map/unproject/pallas_call | solution.py:608
  290.7 3.7 %collective-permute-done.18 = bf16[96,1024]{1,0:T(8,128)(2,1)S(1)} collective-permute-done((bf16[96,1024]{1,0:T(8,128)(2,1)S(1)}, bf16[96,1024]{1,0:T(8,128)(2,1)S(1)}, u32[]{:S(2)}, u32[]{:S(2)}) %collective-permute-start.18) | collective-permute-done | bytes 196640 | tf_op jit(solution)/shard_map/ppermute | solution.py:650
  295.8 3.4 %collective-permute-start.23 = (bf16[96,640]{1,0:T(8,128)(2,1)S(1)}, bf16[96,640]{1,0:T(8,128)(2,1)S(1)}, u32[]{:S(2)}, u32[]{:S(2)}) collective-permute-start(bf16[96,640]{1,0:T(8,128)(2,1)S(1)} %get-tuple-element.245), channel_id=1, source_target_pairs={{0,2},{1,3},{2,0},{3,1},{4,6},{5,7},{6,4},{7,5},{8,10},{9,11},{10,... | collective-permute-start | bytes 368648 | tf_op jit(solution)/shard_map/ppermute | solution.py:650
  300.2 1.5 collective-permute-start.25
  301.7 6.0 %bitcast_add_fusion = (f32[768,768]{1,0:T(8,128)}, f32[768,768]{1,0:T(8,128)}) fusion(bf16[2,1552,768]{2,1,0:T(8,128)(2,1)} %collective-permute-done.14, bf16[1552,768]{1,0:T(8,128)(2,1)} %collective-permute-done.22, bf16[2,1552,768]{2,1,0:T(8,128)(2,1)} %get-tuple-element.177), kind=kLoop, calls=%fused_computation.2 | loop fusion | flops 5898240 | bytes 11796480 | tf_op jit(solution)/shard_map/add | solution.py:876
  308.4 1.7 collective-permute-done.24
  (105 shorter events, 29.7 us)
Async XLA Ops:
  2.5 13.6 %collective-permute-start.1 = (bf16[96,640]{1,0:T(8,128)(2,1)S(1)}, bf16[96,640]{1,0:T(8,128)(2,1)S(1)}, u32[]{:S(2)}, u32[]{:S(2)}) collective-permute-start(bf16[96,640]{1,0:T(8,128)(2,1)S(1)} %concatenate.3), channel_id=1, source_target_pairs={{0,4},{1,5},{2,6},{3,7},{4,0},{5,1},{6,2},{7,3},{8,12},{9,13},{10,... | collective-permute-start | bytes 368648 | tf_op jit(solution)/shard_map/ppermute | solution.py:650
  6.6 9.5 %collective-permute-start.2 = (bf16[96,640]{1,0:T(8,128)(2,1)S(1)}, bf16[96,640]{1,0:T(8,128)(2,1)S(1)}, u32[]{:S(2)}, u32[]{:S(2)}) collective-permute-start(bf16[96,640]{1,0:T(8,128)(2,1)S(1)} %concatenate.3), channel_id=1, source_target_pairs={{0,6},{1,7},{2,4},{3,5},{4,2},{5,3},{6,0},{7,1},{8,14},{9,15},{10,... | collective-permute-start | bytes 368648 | tf_op jit(solution)/shard_map/ppermute | solution.py:650
  8.0 8.6 %collective-permute-start = (bf16[96,640]{1,0:T(8,128)(2,1)S(1)}, bf16[96,640]{1,0:T(8,128)(2,1)S(1)}, u32[]{:S(2)}, u32[]{:S(2)}) collective-permute-start(bf16[96,640]{1,0:T(8,128)(2,1)S(1)} %concatenate.3), channel_id=1, source_target_pairs={{0,2},{1,3},{2,0},{3,1},{4,6},{5,7},{6,4},{7,5},{8,10},{9,11},{10,... | collective-permute-start | bytes 368648 | tf_op jit(solution)/shard_map/ppermute | solution.py:650
  11.6 6.8 %copy-start.13 = (bf16[96,192]{1,0:T(8,128)(2,1)S(1)}, bf16[96,192]{1,0:T(8,128)(2,1)}, u32[]{:S(2)}) copy-start(bf16[96,192]{1,0:T(8,128)(2,1)} %param.32) | copy-start | bytes 110596
  16.7 12.3 %copy-start.1 = (bf16[4,96,640]{2,1,0:T(8,128)(2,1)}, bf16[4,96,640]{2,1,0:T(8,128)(2,1)S(1)}, u32[]{:S(2)}) copy-start(bf16[4,96,640]{2,1,0:T(8,128)(2,1)S(1)} %pad_maximum_fusion.own_ref) | copy-start | bytes 1474564
  16.7 12.3 %collective-permute-start.3 = (bf16[4,96,640]{2,1,0:T(8,128)(2,1)S(1)}, bf16[4,96,640]{2,1,0:T(8,128)(2,1)S(1)}, u32[]{:S(2)}, u32[]{:S(2)}) collective-permute-start(bf16[4,96,640]{2,1,0:T(8,128)(2,1)S(1)} %pad_maximum_fusion.own_ref), channel_id=1, source_target_pairs={{0,1},{1,0},{2,3},{3,2},{4,5},{5,4},{6,7},{7,6},{8,9},{9,8},{10,11... | collective-permute-start | bytes 1474568 | tf_op jit(solution)/shard_map/ppermute | solution.py:650
  18.4 5.9 %collective-permute-start.4 = (bf16[96,192]{1,0:T(8,128)(2,1)S(1)}, bf16[96,192]{1,0:T(8,128)(2,1)S(1)}, u32[]{:S(2)}, u32[]{:S(2)}) collective-permute-start(bf16[96,192]{1,0:T(8,128)(2,1)S(1)} %copy-done.13), channel_id=1, source_target_pairs={{0,2},{1,3},{2,0},{3,1},{4,6},{5,7},{6,4},{7,5},{8,10},{9,11},{10,... | collective-permute-start | bytes 110600 | tf_op jit(solution)/shard_map/ppermute | solution.py:650
  20.3 5.4 %collective-permute-start.5 = (bf16[96,192]{1,0:T(8,128)(2,1)S(1)}, bf16[96,192]{1,0:T(8,128)(2,1)S(1)}, u32[]{:S(2)}, u32[]{:S(2)}) collective-permute-start(bf16[96,192]{1,0:T(8,128)(2,1)S(1)} %copy-done.13), channel_id=1, source_target_pairs={{0,4},{1,5},{2,6},{3,7},{4,0},{5,1},{6,2},{7,3},{8,12},{9,13},{10,... | collective-permute-start | bytes 110600 | tf_op jit(solution)/shard_map/ppermute | solution.py:650
  22.4 5.9 %collective-permute-start.6 = (bf16[96,192]{1,0:T(8,128)(2,1)S(1)}, bf16[96,192]{1,0:T(8,128)(2,1)S(1)}, u32[]{:S(2)}, u32[]{:S(2)}) collective-permute-start(bf16[96,192]{1,0:T(8,128)(2,1)S(1)} %copy-done.13), channel_id=1, source_target_pairs={{0,6},{1,7},{2,4},{3,5},{4,2},{5,3},{6,0},{7,1},{8,14},{9,15},{10,... | collective-permute-start | bytes 110600 | tf_op jit(solution)/shard_map/ppermute | solution.py:650
  32.8 3.1 collective-permute-start.7
  33.4 26.3 %collective-permute-start.9 = (bf16[768,640]{1,0:T(8,128)(2,1)}, bf16[768,640]{1,0:T(8,128)(2,1)S(1)}, u32[]{:S(2)}, u32[]{:S(2)}) collective-permute-start(bf16[768,640]{1,0:T(8,128)(2,1)} %assemble.2.refs_1_.refs_5_.refs_2_), channel_id=1, source_target_pairs={{0,16},{1,17},{2,18},{3,19},{4,20},{5,21},{6,22},{7,23},{8,24},{9,... | collective-permute-start | bytes 2949128 | tf_op jit(solution)/shard_map/ppermute | solution.py:650
  34.9 22.3 %collective-permute-start.8 = (bf16[4,96,192]{2,1,0:T(8,128)(2,1)}, bf16[4,96,192]{2,1,0:T(8,128)(2,1)}, u32[]{:S(2)}, u32[]{:S(2)}) collective-permute-start(bf16[4,96,192]{2,1,0:T(8,128)(2,1)} %pad_maximum_fusion.1.own_ref), channel_id=1, source_target_pairs={{0,1},{1,0},{2,3},{3,2},{4,5},{5,4},{6,7},{7,6},{8,9},{9,8},{10,11... | collective-permute-start | bytes 442376 | tf_op jit(solution)/shard_map/ppermute | solution.py:650
  35.9 7.0 %copy-start.3 = (bf16[768,640]{1,0:T(8,128)(2,1)}, bf16[768,640]{1,0:T(8,128)(2,1)S(1)}, u32[]{:S(2)}) copy-start(bf16[768,640]{1,0:T(8,128)(2,1)S(1)} %collective-permute-done.7.refs_2_.refs_6_.refs_3_) | copy-start | bytes 2949124
  35.9 44.2 %all-to-all-start = ((bf16[8,128,768]{2,1,0:T(8,128)(2,1)}), bf16[8,128,768]{2,1,0:T(8,128)(2,1)S(1)}, u32[]{:S(2)}, u32[]{:S(2)}) async-start(bf16[8,128,768]{2,1,0:T(8,128)(2,1)} %bitcast.17), calls=%async_computation | async-start | bytes 3145728 | tf_op jit(solution)/shard_map/all_to_all | solution.py:771
  59.7 2.6 collective-permute-start.10
  59.8 20.3 %collective-permute-start.11 = (bf16[768,192]{1,0:T(8,128)(2,1)}, bf16[768,192]{1,0:T(8,128)(2,1)}, u32[]{:S(2)}, u32[]{:S(2)}) collective-permute-start(bf16[768,192]{1,0:T(8,128)(2,1)} %assemble.3.refs_0_), channel_id=1, source_target_pairs={{0,16},{1,17},{2,18},{3,19},{4,20},{5,21},{6,22},{7,23},{8,24},{9,... | collective-permute-start | bytes 884744 | tf_op jit(solution)/shard_map/ppermute | solution.py:650
  61.4 18.8 %collective-permute-start.12 = (bf16[768,192]{1,0:T(8,128)(2,1)}, bf16[768,192]{1,0:T(8,128)(2,1)}, u32[]{:S(2)}, u32[]{:S(2)}) collective-permute-start(bf16[768,192]{1,0:T(8,128)(2,1)} %assemble.3.refs_0_), channel_id=1, source_target_pairs={{0,8},{1,9},{2,10},{3,11},{4,12},{5,13},{6,14},{7,15},{8,0},{9,1},... | collective-permute-start | bytes 884744 | tf_op jit(solution)/shard_map/ppermute | solution.py:650
  80.2 12.1 %copy-start.2 = (bf16[8,128,768]{2,1,0:T(8,128)(2,1)}, bf16[8,128,768]{2,1,0:T(8,128)(2,1)S(1)}, u32[]{:S(2)}) copy-start(bf16[8,128,768]{2,1,0:T(8,128)(2,1)S(1)} %all-to-all-done) | copy-start | bytes 4718596
  80.2 1.9 collective-permute-start.13
  92.3 24.2 %all-to-all-start.1 = ((bf16[8,64,768]{2,1,0:T(8,128)(2,1)}), bf16[8,64,768]{2,1,0:T(8,128)(2,1)S(1)}, u32[]{:S(2)}, u32[]{:S(2)}) async-start(bf16[8,64,768]{2,1,0:T(8,128)(2,1)} %bitcast.81), calls=%async_computation.1 | async-start | bytes 1572864 | tf_op jit(solution)/shard_map/all_to_all | solution.py:771
  116.5 3.6 %copy-start.7 = (bf16[8,64,768]{2,1,0:T(8,128)(2,1)}, bf16[8,64,768]{2,1,0:T(8,128)(2,1)S(1)}, u32[]{:S(2)}) copy-start(bf16[8,64,768]{2,1,0:T(8,128)(2,1)S(1)} %all-to-all-done.1) | copy-start | bytes 2359300
  116.5 24.0 %all-to-all-start.2 = ((bf16[8,64,768]{2,1,0:T(8,128)(2,1)}), bf16[8,64,768]{2,1,0:T(8,128)(2,1)S(1)}, u32[]{:S(2)}, u32[]{:S(2)}) async-start(bf16[8,64,768]{2,1,0:T(8,128)(2,1)} %bitcast.80), calls=%async_computation.2 | async-start | bytes 1572864 | tf_op jit(solution)/shard_map/all_to_all | solution.py:771
  140.5 4.0 %copy-start.8 = (bf16[8,64,768]{2,1,0:T(8,128)(2,1)}, bf16[8,64,768]{2,1,0:T(8,128)(2,1)S(1)}, u32[]{:S(2)}) copy-start(bf16[8,64,768]{2,1,0:T(8,128)(2,1)S(1)} %all-to-all-done.2) | copy-start | bytes 2359300
  140.5 24.3 %all-to-all-start.3 = ((bf16[8,64,768]{2,1,0:T(8,128)(2,1)}), bf16[8,64,768]{2,1,0:T(8,128)(2,1)S(1)}, u32[]{:S(2)}, u32[]{:S(2)}) async-start(bf16[8,64,768]{2,1,0:T(8,128)(2,1)} %bitcast.79), calls=%async_computation.3 | async-start | bytes 1572864 | tf_op jit(solution)/shard_map/all_to_all | solution.py:771
  164.8 20.7 %copy-start.6 = (bf16[8,64,768]{2,1,0:T(8,128)(2,1)}, bf16[8,64,768]{2,1,0:T(8,128)(2,1)S(1)}, u32[]{:S(2)}) copy-start(bf16[8,64,768]{2,1,0:T(8,128)(2,1)S(1)} %all-to-all-done.3) | copy-start | bytes 2359300
  164.8 23.9 %all-to-all-start.4 = ((bf16[8,64,768]{2,1,0:T(8,128)(2,1)}), bf16[8,64,768]{2,1,0:T(8,128)(2,1)S(1)}, u32[]{:S(2)}, u32[]{:S(2)}) async-start(bf16[8,64,768]{2,1,0:T(8,128)(2,1)} %bitcast.78), calls=%async_computation.4 | async-start | bytes 1572864 | tf_op jit(solution)/shard_map/all_to_all | solution.py:771
  168.4 20.4 %copy-start.14 = (s32[1024]{0:T(1024)S(1)}, s32[1024]{0:T(1024)}, u32[]{:S(2)}) copy-start(s32[1024]{0:T(1024)} %get-tuple-element.233) | copy-start | bytes 12292
  188.8 4.8 %copy-start.9 = (bf16[8,64,768]{2,1,0:T(8,128)(2,1)}, bf16[8,64,768]{2,1,0:T(8,128)(2,1)S(1)}, u32[]{:S(2)}) copy-start(bf16[8,64,768]{2,1,0:T(8,128)(2,1)S(1)} %all-to-all-done.4) | copy-start | bytes 2359300
  188.8 18.1 %collective-permute-start.14 = (bf16[2,1552,768]{2,1,0:T(8,128)(2,1)}, bf16[2,1552,768]{2,1,0:T(8,128)(2,1)}, u32[]{:S(2)}, u32[]{:S(2)}) collective-permute-start(bf16[2,1552,768]{2,1,0:T(8,128)(2,1)} %get-tuple-element.178), channel_id=1, source_target_pairs={{0,8},{1,9},{2,10},{3,11},{4,12},{5,13},{6,14},{7,15},{8,0},{9,1},... | collective-permute-start | bytes 14303240 | tf_op jit(solution)/shard_map/ppermute | solution.py:650
  189.8 46.8 %all-to-all-start.5 = ((bf16[8,128,768]{2,1,0:T(8,128)(2,1)}), bf16[8,128,768]{2,1,0:T(8,128)(2,1)S(1)}, u32[]{:S(2)}, u32[]{:S(2)}) async-start(bf16[8,128,768]{2,1,0:T(8,128)(2,1)} %bitcast.33), calls=%async_computation.5 | async-start | bytes 3145728 | tf_op jit(solution)/shard_map/all_to_all | solution.py:771
  211.3 24.3 %copy-start.15 = (s32[1024]{0:T(1024)S(1)}, s32[1024]{0:T(1024)}, u32[]{:S(2)}) copy-start(s32[1024]{0:T(1024)} %add_select_fusion) | copy-start | bytes 12292
  235.1 9.3 %collective-permute-start.15 = (bf16[8,96,1024]{2,1,0:T(8,128)(2,1)}, bf16[8,96,1024]{2,1,0:T(8,128)(2,1)S(1)}, u32[]{:S(2)}, u32[]{:S(2)}) collective-permute-start(bf16[8,96,1024]{2,1,0:T(8,128)(2,1)} %get-tuple-element.188), channel_id=1, source_target_pairs={{0,8},{1,9},{2,10},{3,11},{4,12},{5,13},{6,14},{7,15},{8,0},{9,1},... | collective-permute-start | bytes 4718600 | tf_op jit(solution)/shard_map/ppermute | solution.py:650
  236.6 54.0 %collective-permute-start.22 = (bf16[1552,768]{1,0:T(8,128)(2,1)}, bf16[1552,768]{1,0:T(8,128)(2,1)}, u32[]{:S(2)}, u32[]{:S(2)}) collective-permute-start(bf16[1552,768]{1,0:T(8,128)(2,1)} %fusion), channel_id=1, source_target_pairs={{0,16},{1,17},{2,18},{3,19},{4,20},{5,21},{6,22},{7,23},{8,24},{9,... | collective-permute-start | bytes 7151624 | tf_op jit(solution)/shard_map/ppermute | solution.py:650
  246.4 24.7 %collective-permute-start.16 = (bf16[4,96,1024]{2,1,0:T(8,128)(2,1)S(1)}, bf16[4,96,1024]{2,1,0:T(8,128)(2,1)S(1)}, u32[]{:S(2)}, u32[]{:S(2)}) collective-permute-start(bf16[4,96,1024]{2,1,0:T(8,128)(2,1)S(1)} %get-tuple-element.196), channel_id=1, source_target_pairs={{0,1},{1,0},{2,3},{3,2},{4,5},{5,4},{6,7},{7,6},{8,9},{9,8},{10,11... | collective-permute-start | bytes 2359304 | tf_op jit(solution)/shard_map/ppermute | solution.py:650
  271.1 3.8 %copy-start.11 = (bf16[4,96,640]{2,1,0:T(8,128)(2,1)S(1)}, bf16[4,96,640]{2,1,0:T(8,128)(2,1)}, u32[]{:S(2)}) copy-start(bf16[4,96,640]{2,1,0:T(8,128)(2,1)} %get-tuple-element.203) | copy-start | bytes 1474564
  271.1 3.8 %copy-start.12 = (bf16[4,96,640]{2,1,0:T(8,128)(2,1)S(1)}, bf16[4,96,640]{2,1,0:T(8,128)(2,1)}, u32[]{:S(2)}) copy-start(bf16[4,96,640]{2,1,0:T(8,128)(2,1)} %get-tuple-element.201) | copy-start | bytes 1474564
  272.3 2.6 collective-permute-start.20
  275.1 15.6 %collective-permute-start.21 = (bf16[4,96,640]{2,1,0:T(8,128)(2,1)S(1)}, bf16[4,96,640]{2,1,0:T(8,128)(2,1)S(1)}, u32[]{:S(2)}, u32[]{:S(2)}) collective-permute-start(bf16[4,96,640]{2,1,0:T(8,128)(2,1)S(1)} %get-tuple-element.204), channel_id=1, source_target_pairs={{0,1},{1,0},{2,3},{3,2},{4,5},{5,4},{6,7},{7,6},{8,9},{9,8},{10,11... | collective-permute-start | bytes 1474568 | tf_op jit(solution)/shard_map/ppermute | solution.py:650
  275.5 15.2 %collective-permute-start.17 = (bf16[96,1024]{1,0:T(8,128)(2,1)S(1)}, bf16[96,1024]{1,0:T(8,128)(2,1)S(1)}, u32[]{:S(2)}, u32[]{:S(2)}) collective-permute-start(bf16[96,1024]{1,0:T(8,128)(2,1)S(1)} %get-tuple-element.197), channel_id=1, source_target_pairs={{0,2},{1,3},{2,0},{3,1},{4,6},{5,7},{6,4},{7,5},{8,10},{9,11},{10,... | collective-permute-start | bytes 589832 | tf_op jit(solution)/shard_map/ppermute | solution.py:650
  277.2 17.2 %collective-permute-start.18 = (bf16[96,1024]{1,0:T(8,128)(2,1)S(1)}, bf16[96,1024]{1,0:T(8,128)(2,1)S(1)}, u32[]{:S(2)}, u32[]{:S(2)}) collective-permute-start(bf16[96,1024]{1,0:T(8,128)(2,1)S(1)} %get-tuple-element.198), channel_id=1, source_target_pairs={{0,4},{1,5},{2,6},{3,7},{4,0},{5,1},{6,2},{7,3},{8,12},{9,13},{10,... | collective-permute-start | bytes 589832 | tf_op jit(solution)/shard_map/ppermute | solution.py:650
  279.6 14.8 %collective-permute-start.19 = (bf16[96,1024]{1,0:T(8,128)(2,1)S(1)}, bf16[96,1024]{1,0:T(8,128)(2,1)S(1)}, u32[]{:S(2)}, u32[]{:S(2)}) collective-permute-start(bf16[96,1024]{1,0:T(8,128)(2,1)S(1)} %get-tuple-element.199), channel_id=1, source_target_pairs={{0,6},{1,7},{2,4},{3,5},{4,2},{5,3},{6,0},{7,1},{8,14},{9,15},{10,... | collective-permute-start | bytes 589832 | tf_op jit(solution)/shard_map/ppermute | solution.py:650
  294.5 15.7 %collective-permute-start.26 = (bf16[96,832]{1,0:T(8,128)(2,1)S(1)}, bf16[96,832]{1,0:T(8,128)(2,1)S(1)}, u32[]{:S(2)}, u32[]{:S(2)}) collective-permute-start(bf16[96,832]{1,0:T(8,128)(2,1)S(1)} %slice.289), channel_id=1, source_target_pairs={{0,16},{1,17},{2,18},{3,19},{4,20},{5,21},{6,22},{7,23},{8,24},{9,... | collective-permute-start | bytes 479240 | tf_op jit(solution)/shard_map/ppermute | solution.py:650
  295.8 12.7 %collective-permute-start.23 = (bf16[96,640]{1,0:T(8,128)(2,1)S(1)}, bf16[96,640]{1,0:T(8,128)(2,1)S(1)}, u32[]{:S(2)}, u32[]{:S(2)}) collective-permute-start(bf16[96,640]{1,0:T(8,128)(2,1)S(1)} %get-tuple-element.245), channel_id=1, source_target_pairs={{0,2},{1,3},{2,0},{3,1},{4,6},{5,7},{6,4},{7,5},{8,10},{9,11},{10,... | collective-permute-start | bytes 368648 | tf_op jit(solution)/shard_map/ppermute | solution.py:650
  299.2 10.9 %collective-permute-start.24 = (bf16[96,640]{1,0:T(8,128)(2,1)S(1)}, bf16[96,640]{1,0:T(8,128)(2,1)S(1)}, u32[]{:S(2)}, u32[]{:S(2)}) collective-permute-start(bf16[96,640]{1,0:T(8,128)(2,1)S(1)} %get-tuple-element.244), channel_id=1, source_target_pairs={{0,4},{1,5},{2,6},{3,7},{4,0},{5,1},{6,2},{7,3},{8,12},{9,13},{10,... | collective-permute-start | bytes 368648 | tf_op jit(solution)/shard_map/ppermute | solution.py:650
  300.2 9.9 %collective-permute-start.25 = (bf16[96,640]{1,0:T(8,128)(2,1)S(1)}, bf16[96,640]{1,0:T(8,128)(2,1)S(1)}, u32[]{:S(2)}, u32[]{:S(2)}) collective-permute-start(bf16[96,640]{1,0:T(8,128)(2,1)S(1)} %get-tuple-element.243), channel_id=1, source_target_pairs={{0,6},{1,7},{2,4},{3,5},{4,2},{5,3},{6,0},{7,1},{8,14},{9,15},{10,... | collective-permute-start | bytes 368648 | tf_op jit(solution)/shard_map/ppermute | solution.py:650
  311.8 3.1 collective-permute-start.27
  311.8 4.4 %collective-permute-start.28 = (f32[8,96]{0,1:T(8,128)S(1)}, f32[8,96]{0,1:T(8,128)S(1)}, u32[]{:S(2)}, u32[]{:S(2)}) collective-permute-start(f32[8,96]{0,1:T(8,128)S(1)} %slice_bitcast_fusion), channel_id=1, source_target_pairs={{0,16},{1,17},{2,18},{3,19},{4,20},{5,21},{6,22},{7,23},{8,24},{9,... | collective-permute-start | bytes 9224 | tf_op jit(solution)/shard_map/ppermute | solution.py:650
  312.8 4.0 %collective-permute-start.29 = (f32[8,96]{0,1:T(8,128)S(1)}, f32[8,96]{0,1:T(8,128)S(1)}, u32[]{:S(2)}, u32[]{:S(2)}) collective-permute-start(f32[8,96]{0,1:T(8,128)S(1)} %slice_bitcast_fusion), channel_id=1, source_target_pairs={{0,24},{1,25},{2,26},{3,27},{4,28},{5,29},{6,30},{7,31},{8,16},{9,... | collective-permute-start | bytes 9224 | tf_op jit(solution)/shard_map/ppermute | solution.py:650
  (6 other events, 7.9 us)

commit v6 on v5

--- a/solution.py
+++ b/solution.py
@@ -300,7 +300,12 @@
     )(target.reshape(1, count), rows)[0]
 
 
-def mix_kernel(order, x_ref, ctx_ref, vec_ref, target_ref, *refs):
+def column(row_ref):
+    row = row_ref[...].astype(F32)
+    return jnp.broadcast_to(row, (8, row.shape[1])).T[:, :1].astype(jnp.int32)
+
+
+def mix_kernel(order, slab, x_ref, ctx_ref, vec_ref, target_ref, *refs):
     wo_refs, (h_ref, whole_ref, low_ref, sent_ref) = refs[:GROUPS], refs[GROUPS:]
     rows, width = x_ref.shape
     count = low_ref.shape[0]
@@ -310,8 +315,8 @@
     @pl.when(step == 0)
     def _():
         for q in range(GROUPS):
-            at = pl.ds(pl.multiple_of(order[q] * part, 64), part)
-            pieces = [wo[at, :] for wo in wo_refs]
+            first, second = slab[2 * order[q]], slab[2 * order[q] + 1]
+            pieces = [jnp.concatenate([wo[first], wo[second]]) for wo in wo_refs]
             for n in range(GROUPS):
                 piece = pieces[0]
                 for r in range(1, GROUPS):
@@ -335,14 +340,14 @@
             sent_ref[at : at + 256] = dot(picks, low_ref[...], 1, 0).astype(BF)
 
 
-def mix(order, x, ctx, weights, vec, target):
+def mix(order, slab, x, ctx, weights, vec, target):
     count, width = x.shape
     part = width // GROUPS
     rows = min(256, count)
     return call(
         mix_kernel, "mix", (count // rows,),
-        [SCALARS, chunk((rows, width)), chunk((GROUPS, rows, part), 1), full((8, width)),
-         full((1, count))] + [full((width, part))] * GROUPS,
+        [SCALARS, SCALARS, chunk((rows, width)), chunk((GROUPS, rows, part), 1), full((8, width)),
+         full((1, count))] + [full((8, width // 8, part))] * GROUPS,
         [
             (chunk((rows, width)), (count, width), F32),
             (full((width, width)), (width, width), BF),
@@ -350,7 +355,7 @@
             (full((count // 2, width)), (count // 2, width), BF),
         ],
         cost=(2 * count * width * (width + count), 12_000_000, 0),
-    )(order, x, ctx, vec, target.reshape(1, count), *weights)
+    )(order, slab, x, ctx, vec, target.reshape(1, count), *weights)
 
 
 def unmix_kernel(
@@ -361,9 +366,10 @@
     part = width // GROUPS
     step = pl.program_id(0)
     dm = None
+    target = column(target_ref)
     for half, sent in enumerate((dm_one, dm_two)):
         index = lax.broadcasted_iota(jnp.int32, (rows, sent.shape[0]), 1) + half * sent.shape[0]
-        picks = (target_ref[...] == index).astype(F32).astype(BF)
+        picks = (target == index).astype(F32).astype(BF)
         got = dot(picks, sent[...], 1, 0)
         dm = got if dm is None else dm + got
     unit, inverse = normalize(h_ref[...])
@@ -408,7 +414,7 @@
     by_rows, by_ctx = chunk((rows, width)), chunk((GROUPS, rows, part), 1)
     return call(
         unmix_kernel, "unmix", (count // rows,),
-        [SCALARS, by_rows, by_rows, half, half, chunk((rows, 1)), by_ctx, full((width, width)),
+        [SCALARS, by_rows, by_rows, half, half, chunk((1, rows), 1), by_ctx, full((width, width)),
          full((8, width))],
         [
             (by_rows, (count, width), F32),
@@ -418,12 +424,12 @@
         ],
         [pltpu.VMEM((GROUPS, part, width), F32)],
         cost=(2 * count * width * (2 * width + count), 20_000_000, 0),
-    )(order, h, g, dm_one, dm_two, target.reshape(count, 1), ctx, whole, vec)
+    )(order, h, g, dm_one, dm_two, target.reshape(1, count), ctx, whole, vec)
 
 
 def finish_kernel(h_ref, target_ref, gy_ref, out_ref):
     slot = lax.broadcasted_iota(jnp.int32, (h_ref.shape[0], gy_ref.shape[0]), 1)
-    picks = (target_ref[...] == slot).astype(F32).astype(BF)
+    picks = (column(target_ref) == slot).astype(F32).astype(BF)
     out_ref[...] = (h_ref[...] + dot(picks, gy_ref[...], 1, 0)).astype(BF)
 
 
@@ -432,10 +438,10 @@
     rows = min(256, count)
     return call(
         finish_kernel, "finish", (count // rows,),
-        [chunk((rows, width)), chunk((rows, 1)), full((count, width))],
+        [chunk((rows, width)), chunk((1, rows), 1), full((count, width))],
         [(chunk((rows, width)), (count, width), BF)],
         cost=(2 * count * count * width, 6_000_000, 0),
-    )(h, target.reshape(count, 1), gy)[0]
+    )(h, target.reshape(1, count), gy)[0]
 
 
 def gelu_pair(v):
@@ -640,11 +646,11 @@
         r = jnp.arange(4, dtype=jnp.int32)
         i = jnp.arange(8, dtype=jnp.int32)
         if not self.staged:
-            return r, i, r
+            return r, i, r, i
         d, e = lax.axis_index("dp"), lax.axis_index("expert")
         z, y = e // 2, e % 2
         weighed = d ^ jnp.where(r < 2, 3 - 2 * r, 6 - 2 * r)
-        return d ^ r, (z ^ i % 4) * 2 + (y ^ i // 4), weighed
+        return d ^ r, (z ^ i % 4) * 2 + (y ^ i // 4), weighed, (y ^ i % 2) * 4 + (z ^ i // 2)
 
     def move(self, array, way):
         return lax.ppermute(array, BOTH, way)
@@ -693,6 +699,7 @@
     by_group = lambda w: gather_all(w).reshape(width, GROUPS, -1).transpose(1, 0, 2)
     grouped = jnp.concatenate([*(by_group(w) for w in weights), extra], axis=2)
     out = by_group(out_weights)
+    out = out.reshape(GROUPS, 8, width // 8, -1)
     return [grouped[i] for i in range(GROUPS)], [out[i] for i in range(GROUPS)], filler
 
 
@@ -755,7 +762,7 @@
     experts = specialist_quotas.shape[0]
     cap = count // experts
     n_dp = place.n_dp
-    order, table, weighed = place.tables()
+    order, table, weighed, place_of = place.tables()
     barrier = lax.optimization_barrier
 
     chosen = assignments[:, None] == lax.broadcasted_iota(jnp.int32, (count, experts), 1)
@@ -795,7 +802,7 @@
     *before, low_in, vec = attend(0, order, weights[:2], x=block_entries)
     if place.staged:
         before, out = barrier((before, out))
-        out_near = assemble(table, *out)
+        out_near = jnp.concatenate(out)
         before, across, out_near = barrier((before, weights[2], out_near))
         weights = (*weights[:2], across, place.move(across, place.core))
         out_across = place.move(out_near, place.x)
@@ -805,7 +812,7 @@
     if place.staged:
         ctx, out_across = barrier((ctx, out_across))
         out += (out_across, place.move(out_across, place.core))
-    h1, whole_o, low_mid, sent_one = mix(order, block_entries, ctx, out, vec, halved)
+    h1, whole_o, low_mid, sent_one = mix(order, place_of, block_entries, ctx, out, vec, halved)
 
     sent_two = dispatch(halved, low_mid, count // 2)
     x_one, sent_two = barrier((exchange(sent_one), sent_two))

time: 322 us -> 317 us (0.984)
  starting transfers between devices: 60.1 us -> 56.6 us
  transfers between devices with their start and end apart: 36 -> 36, of which waited for: 17 -> 17; matrix products, arithmetic and copies ran while one was open for 7% -> 7% of each run, Pallas kernels for 52% -> 53%
where the time goes in v6:
time: 317 us; the launch traced here: 314 us
  Pallas kernels  177 us (56%)
  starting transfers between devices  56.6 us (18%)
  waiting for transfers between devices  46.9 us (15%)
  other arithmetic  22.5 us (7%)
  local copies, waits for them, and re-layouts  9.46 us (3%)
    pallas_call x2, Pallas kernels, attend_back(): call(partial(attend_back_kernel, half), 'attend_back', (2,), [pl.BlockSpe...  46.5 us
    pallas_call x2, Pallas kernels, expert(): call(expert_kernel, 'expert', (ff // step,), [full((rows, width)), side,...  35.1 us
    ppermute x30, starting transfers between devices, move(): return lax.ppermute(array, BOTH, way)  34.1 us
    all_to_all x6, waiting for transfers between devices, exchange(): lax.all_to_all(sent, 'expert', split_axis=0, concat_axis=0, tiled=True)  28.7 us
    pallas_call x2, Pallas kernels, attend(): call(partial(attend_kernel, half), 'attend', (2,), [SCALARS] + ins, outs,...  27.5 us
    all_to_all x6, starting transfers between devices, exchange(): lax.all_to_all(sent, 'expert', split_axis=0, concat_axis=0, tiled=True)  22.5 us
    ppermute x30, waiting for transfers between devices, move(): return lax.ppermute(array, BOTH, way)  18.2 us
    pallas_call x1, Pallas kernels, weigh(): call(partial(weigh_kernel, split), 'weigh', (n,), [wide] * 4 + [full((row...  17.1 us
  transfers between devices with their start and end apart: 36, of which 17 were waited for; matrix products, arithmetic and copies ran while one was open for 7% of the time, Pallas kernels for 53%

profile of v6, /device:TPU:0, one launch (start us, length us, event | category | flops | bytes accessed | tf_op | source)
XLA Modules:
  0.0 313.6 jit_solution(7327102349957344888)
XLA Ops:
  2.5 5.1 %collective-permute-start.2 = (bf16[96,640]{1,0:T(8,128)(2,1)S(1)}, bf16[96,640]{1,0:T(8,128)(2,1)S(1)}, u32[]{:S(2)}, u32[]{:S(2)}) collective-permute-start(bf16[96,640]{1,0:T(8,128)(2,1)S(1)} %concatenate.6), channel_id=1, source_target_pairs={{0,6},{1,7},{2,4},{3,5},{4,2},{5,3},{6,0},{7,1},{8,14},{9,15},{10,... | collective-permute-start | bytes 368648 | tf_op jit(solution)/shard_map/ppermute | solution.py:656
  11.7 4.4 %dispatch.2 = bf16[1024,768]{1,0:T(8,128)(2,1)} custom-call(s32[1,1024]{1,0:T(1,128)} %bitcast.89, bf16[1024,768]{1,0:T(8,128)(2,1)} %g_ref.1), custom_call_target="tpu_custom_call" | custom-call | flops 1610612736 | bytes 3000000 | tf_op jit(solution)/shard_map/dispatch/pallas_call | solution.py:295
  16.0 2.0 collective-permute-done.1
  18.1 1.6 collective-permute-start.3
  19.7 2.5 collective-permute-start.6
  22.2 1.9 collective-permute-start.4
  27.9 2.6 collective-permute-done.3.got_ref
  31.2 3.0 assemble.1.refs_1_.refs_5_.refs_2_
  34.8 1.5 collective-permute-start.9
  36.3 1.5 collective-permute-start.8
  37.9 3.9 %all-to-all-start = ((bf16[8,128,768]{2,1,0:T(8,128)(2,1)}), bf16[8,128,768]{2,1,0:T(8,128)(2,1)S(1)}, u32[]{:S(2)}, u32[]{:S(2)}) async-start(bf16[8,128,768]{2,1,0:T(8,128)(2,1)} %bitcast.17), calls=%async_computation | async-start | bytes 3145728 | tf_op jit(solution)/shard_map/all_to_all | solution.py:778
  41.8 14.3 %attend.2 = (bf16[4,1024,576]{2,1,0:T(8,128)(2,1)}, bf16[4,1024,192]{2,1,0:T(8,128)(2,1)}, f32[4,8,1024]{2,1,0:T(8,128)}, bf16[1024,768]{1,0:T(8,128)(2,1)}, f32[8,768]{1,0:T(8,128)}) custom-call(s32[4]{0:T(128)} %get-tuple-element.255.order, bf16[1024,768]{1,0:T(8,128)(2,1)} %refs_6_.1, bf16[768,640]{1,0:T(8,128)(2,1)} %assemble.1.refs_1_.refs_5_.refs_2_, ...), custom_call_target="tpu_custom_call" | custom-call | flops 12000000000 | bytes 8000000 | tf_op jit(solution)/shard_map/attend/pallas_call | solution.py:167
  56.2 1.8 pad_maximum_fusion.1.refs_0_
  59.7 1.5 collective-permute-start.11
  63.3 13.2 %attend.3 = (bf16[4,1024,576]{2,1,0:T(8,128)(2,1)}, bf16[4,1024,192]{2,1,0:T(8,128)(2,1)}, f32[4,8,1024]{2,1,0:T(8,128)}) custom-call(s32[4]{0:T(128)} %get-tuple-element.255.order, bf16[1024,768]{1,0:T(8,128)(2,1)} %get-tuple-element.127.refs_0_.refs_4_, ...), custom_call_target="tpu_custom_call", output_to_operand_aliasing={{0}: (5, {}), {1}: (6, {}), {2}: (7, {})} | custom-call | flops 12000000000 | bytes 8000000 | tf_op jit(solution)/shard_map/attend/pallas_call | solution.py:167
  76.5 2.5 all-to-all-done
  79.6 1.4 collective-permute-done.13.refs_3_
  81.8 9.3 %mix.1 = (f32[1024,768]{1,0:T(8,128)}, bf16[768,768]{1,0:T(8,128)(2,1)}, bf16[1024,768]{1,0:T(8,128)(2,1)}, bf16[512,768]{1,0:T(8,128)(2,1)}) custom-call(s32[4]{0:T(128)} %get-tuple-element.255.order, s32[8]{0:T(128)} %fusion.15.slab, bf16[1024,768]{1,0:T(8,128)(2,1)} %refs_6_.1, bf16[4,1024,192]{2,1,0:T(8,128)(2,1)} %get-tuple-element.146.ctx_ref.refs_1_, ...), custom_call_target="tpu_custom_call" | custom-call | flops 2818572288 | bytes 12000000 | tf_op jit(solution)/shard_map/mix/pallas_call | solution.py:347
  91.1 3.7 %all-to-all-start.1 = ((bf16[8,64,768]{2,1,0:T(8,128)(2,1)}), bf16[8,64,768]{2,1,0:T(8,128)(2,1)S(1)}, u32[]{:S(2)}, u32[]{:S(2)}) async-start(bf16[8,64,768]{2,1,0:T(8,128)(2,1)} %bitcast.79), calls=%async_computation.1 | async-start | bytes 1572864 | tf_op jit(solution)/shard_map/all_to_all | solution.py:778
  94.8 3.3 %dispatch.3 = bf16[512,768]{1,0:T(8,128)(2,1)} custom-call(s32[1,1024]{1,0:T(1,128)} %bitcast.92, bf16[1024,768]{1,0:T(8,128)(2,1)} %get-tuple-element.150.rows_ref), custom_call_target="tpu_custom_call" | custom-call | flops 1610612736 | bytes 3000000 | tf_op jit(solution)/shard_map/dispatch/pallas_call | solution.py:295
  98.0 17.3 %all-to-all-done.1 = bf16[8,64,768]{2,1,0:T(8,128)(2,1)S(1)} async-done(((bf16[8,64,768]{2,1,0:T(8,128)(2,1)}), bf16[8,64,768]{2,1,0:T(8,128)(2,1)S(1)}, u32[]{:S(2)}, u32[]{:S(2)}) %all-to-all-start.1) | async-done | bytes 786464 | tf_op jit(solution)/shard_map/all_to_all | solution.py:778
  115.3 3.6 %all-to-all-start.2 = ((bf16[8,64,768]{2,1,0:T(8,128)(2,1)}), bf16[8,64,768]{2,1,0:T(8,128)(2,1)S(1)}, u32[]{:S(2)}, u32[]{:S(2)}) async-start(bf16[8,64,768]{2,1,0:T(8,128)(2,1)} %bitcast.78), calls=%async_computation.2 | async-start | bytes 1572864 | tf_op jit(solution)/shard_map/all_to_all | solution.py:778
  118.9 17.6 %expert.2 = (bf16[8,2,64,768]{3,2,1,0:T(8,128)(2,1)}, bf16[512,768]{1,0:T(8,128)(2,1)}, bf16[512,768]{1,0:T(8,128)(2,1)}, bf16[512,3072]{1,0:T(8,128)(2,1)}, bf1...) custom-call(bf16[512,768]{1,0:T(8,128)(2,1)} %bitcast.70, bf16[8,2,64,768]{3,2,1,0:T(8,128)(2,1)} %bitcast.67, ...), custom_call_target="tpu_custom_call" | custom-call | flops 9663676416 | bytes 22000000 | tf_op jit(solution)/shard_map/expert/pallas_call | solution.py:508
  136.5 2.8 all-to-all-done.2
  139.3 4.0 %all-to-all-start.3 = ((bf16[8,64,768]{2,1,0:T(8,128)(2,1)}), bf16[8,64,768]{2,1,0:T(8,128)(2,1)S(1)}, u32[]{:S(2)}, u32[]{:S(2)}) async-start(bf16[8,64,768]{2,1,0:T(8,128)(2,1)} %bitcast.77), calls=%async_computation.3 | async-start | bytes 1572864 | tf_op jit(solution)/shard_map/all_to_all | solution.py:778
  143.3 17.5 %expert.3 = (bf16[8,2,64,768]{3,2,1,0:T(8,128)(2,1)}, bf16[512,768]{1,0:T(8,128)(2,1)}, bf16[512,768]{1,0:T(8,128)(2,1)}, bf16[512,3072]{1,0:T(8,128)(2,1)}, bf1...) custom-call(bf16[512,768]{1,0:T(8,128)(2,1)} %bitcast.73, ...), custom_call_target="tpu_custom_call", output_to_operand_aliasing={{0}: (7, {})} | custom-call | flops 9663676416 | bytes 22000000 | tf_op jit(solution)/shard_map/expert/pallas_call | solution.py:508
  160.8 2.8 all-to-all-done.3
  163.6 3.6 %all-to-all-start.4 = ((bf16[8,64,768]{2,1,0:T(8,128)(2,1)}), bf16[8,64,768]{2,1,0:T(8,128)(2,1)S(1)}, u32[]{:S(2)}, u32[]{:S(2)}) async-start(bf16[8,64,768]{2,1,0:T(8,128)(2,1)} %bitcast.76), calls=%async_computation.4 | async-start | bytes 1572864 | tf_op jit(solution)/shard_map/all_to_all | solution.py:778
  167.2 17.1 %weigh.1 = (bf16[2,1552,768]{2,1,0:T(8,128)(2,1)}, bf16[2,1552,768]{2,1,0:T(8,128)(2,1)}) custom-call(s32[4]{0:T(128)} %get-tuple-element.254.which, bf16[512,3072]{1,0:T(8,128)(2,1)} %get-tuple-element.161.refs_0_, bf16[512,3072]{1,0:T(8,128)(2,1)} %get-tuple-element.162.refs_1_, bf16[512,3072]{1,0:T(8,128)(2,1)} %get-tuple-element.163.refs_2_, ...), custom_call_target="tpu_custom_call" | custom-call | flops 9663676416 | bytes 26000000 | tf_op jit(solution)/shard_map/weigh/pallas_call | solution.py:588
  184.3 3.2 %all-to-all-done.4 = bf16[8,64,768]{2,1,0:T(8,128)(2,1)S(1)} async-done(((bf16[8,64,768]{2,1,0:T(8,128)(2,1)}), bf16[8,64,768]{2,1,0:T(8,128)(2,1)S(1)}, u32[]{:S(2)}, u32[]{:S(2)}) %all-to-all-start.4) | async-done | bytes 786464 | tf_op jit(solution)/shard_map/all_to_all | solution.py:778
  187.6 3.8 %all-to-all-start.5 = ((bf16[8,128,768]{2,1,0:T(8,128)(2,1)}), bf16[8,128,768]{2,1,0:T(8,128)(2,1)S(1)}, u32[]{:S(2)}, u32[]{:S(2)}) async-start(bf16[8,128,768]{2,1,0:T(8,128)(2,1)} %bitcast.31), calls=%async_computation.5 | async-start | bytes 3145728 | tf_op jit(solution)/shard_map/all_to_all | solution.py:778
  191.3 13.8 %unmix.1 = (f32[1024,768]{1,0:T(8,128)}, bf16[4,1024,192]{2,1,0:T(8,128)(2,1)}, bf16[4,768,192]{2,1,0:T(8,128)(2,1)}, f32[8,768]{1,0:T(8,128)}) custom-call(s32[4]{0:T(128)} %get-tuple-element.255.order, f32[1024,768]{1,0:T(8,128)} %get-tuple-element.148.h_ref, bf16[1024,768]{1,0:T(8,128)(2,1)} %g_ref.1, bf16[512,768]{1,0:T(8,128)(2,1)} %bitcast.69, ...), custom_call_target="tpu_custom_call" | custom-call | flops 4026531840 | bytes 20000000 | tf_op jit(solution)/shard_map/unmix/pallas_call | solution.py:415
  205.2 4.4 %fusion = bf16[1552,768]{1,0:T(8,128)(2,1)} fusion(bf16[2,1552,768]{2,1,0:T(8,128)(2,1)} %collective-permute-done.14, bf16[2,1552,768]{2,1,0:T(8,128)(2,1)} %get-tuple-element.177), kind=kLoop, calls=%fused_computation.1 | loop fusion | flops 4767744 | bytes 7151616 | tf_op jit(solution)/shard_map/convert_element_type | solution.py:624
  209.6 23.6 %attend_back.2 = (bf16[2,1024,576]{2,1,0:T(8,128)(2,1)}, bf16[4,96,1024]{2,1,0:T(8,128)(2,1)}, bf16[4,96,1024]{2,1,0:T(8,128)(2,1)}, bf16[8,96,1024]{2,1,0:T(8,128)(2,1)}) custom-call(s32[4]{0:T(128)} %get-tuple-element.255.order, s32[8]{0:T(128)} %fusion.19.table, bf16[4,1024,576]{2,1,0:T(8,128)(2,1)} %get-tuple-element.180.refs_0_, ...), custom_call_target="tpu_custom_call" | custom-call | flops 24000000000 | bytes 14000000 | tf_op jit(solution)/shard_map/attend_back/pallas_call | solution.py:262
  233.8 1.5 collective-permute-start.22
  236.5 6.2 %finish.1 = bf16[1024,768]{1,0:T(8,128)(2,1)} custom-call(f32[1024,768]{1,0:T(8,128)} %get-tuple-element.148.h_ref, s32[1,1024]{1,0:T(1,128)} %bitcast.90, bf16[1024,768]{1,0:T(8,128)(2,1)} %bitcast.64), custom_call_target="tpu_custom_call" | custom-call | flops 1610612736 | bytes 6000000 | tf_op jit(solution)/shard_map/finish/pallas_call | solution.py:439
  242.7 2.0 add_convert_fusion.1
  244.8 1.7 collective-permute-start.16
  246.5 22.9 %attend_back.3 = (bf16[2,1024,576]{2,1,0:T(8,128)(2,1)}, bf16[4,96,640]{2,1,0:T(8,128)(2,1)}, bf16[4,96,640]{2,1,0:T(8,128)(2,1)}, bf16[8,96,640]{2,1,0:T(8,128)(2,1)}) custom-call(s32[4]{0:T(128)} %get-tuple-element.255.order, s32[8]{0:T(128)} %fusion.19.table, bf16[4,1024,576]{2,1,0:T(8,128)(2,1)} %get-tuple-element.180.refs_0_, ...), custom_call_target="tpu_custom_call" | custom-call | flops 24000000000 | bytes 14000000 | tf_op jit(solution)/shard_map/attend_back/pallas_call | solution.py:262
  270.6 2.6 collective-permute-done.20
  273.8 1.6 collective-permute-start.17
  275.5 2.4 collective-permute-start.18
  278.2 10.7 %unproject.1 = f32[1024,768]{1,0:T(8,128)} custom-call(bf16[2,1024,576]{2,1,0:T(8,128)(2,1)} %get-tuple-element.205.refs_0_, bf16[2,1024,576]{2,1,0:T(8,128)(2,1)} %get-tuple-element.206.refs_1_, bf16[768,640]{1,0:T(8,128)(2,1)} %assemble.1.refs_1_.refs_5_.refs_2_, bf16[768,640]{1,0:T(8,128)(2,1)} %copy-done.3, bf16[768,640]{1,0:T(8,128)(2,1)} %copy-done.4, ...), custom_call_target="tpu_custom_call" | custom-call | flops 3623878656 | bytes 20000000 | tf_op jit(solution)/shard_map/unproject/pallas_call | solution.py:614
  289.0 3.6 %collective-permute-done.18 = bf16[96,1024]{1,0:T(8,128)(2,1)S(1)} collective-permute-done((bf16[96,1024]{1,0:T(8,128)(2,1)S(1)}, bf16[96,1024]{1,0:T(8,128)(2,1)S(1)}, u32[]{:S(2)}, u32[]{:S(2)}) %collective-permute-start.18) | collective-permute-done | bytes 196640 | tf_op jit(solution)/shard_map/ppermute | solution.py:656
  293.4 2.4 collective-permute-start.25
  295.9 3.3 %collective-permute-start.24 = (bf16[96,640]{1,0:T(8,128)(2,1)S(1)}, bf16[96,640]{1,0:T(8,128)(2,1)S(1)}, u32[]{:S(2)}, u32[]{:S(2)}) collective-permute-start(bf16[96,640]{1,0:T(8,128)(2,1)S(1)} %get-tuple-element.244), channel_id=1, source_target_pairs={{0,4},{1,5},{2,6},{3,7},{4,0},{5,1},{6,2},{7,3},{8,12},{9,13},{10,... | collective-permute-start | bytes 368648 | tf_op jit(solution)/shard_map/ppermute | solution.py:656
  299.7 6.0 %bitcast_add_fusion = (f32[768,768]{1,0:T(8,128)}, f32[768,768]{1,0:T(8,128)}) fusion(bf16[2,1552,768]{2,1,0:T(8,128)(2,1)} %collective-permute-done.14, bf16[1552,768]{1,0:T(8,128)(2,1)} %collective-permute-done.22, bf16[2,1552,768]{2,1,0:T(8,128)(2,1)} %get-tuple-element.177), kind=kLoop, calls=%fused_computation.2 | loop fusion | flops 5898240 | bytes 11796480 | tf_op jit(solution)/shard_map/add | solution.py:883
  307.5 1.6 collective-permute-start.28
  (100 shorter events, 27.8 us)
Async XLA Ops:
  2.5 13.5 %collective-permute-start.2 = (bf16[96,640]{1,0:T(8,128)(2,1)S(1)}, bf16[96,640]{1,0:T(8,128)(2,1)S(1)}, u32[]{:S(2)}, u32[]{:S(2)}) collective-permute-start(bf16[96,640]{1,0:T(8,128)(2,1)S(1)} %concatenate.6), channel_id=1, source_target_pairs={{0,6},{1,7},{2,4},{3,5},{4,2},{5,3},{6,0},{7,1},{8,14},{9,15},{10,... | collective-permute-start | bytes 368648 | tf_op jit(solution)/shard_map/ppermute | solution.py:656
  7.7 10.4 %collective-permute-start.1 = (bf16[96,640]{1,0:T(8,128)(2,1)S(1)}, bf16[96,640]{1,0:T(8,128)(2,1)S(1)}, u32[]{:S(2)}, u32[]{:S(2)}) collective-permute-start(bf16[96,640]{1,0:T(8,128)(2,1)S(1)} %concatenate.6), channel_id=1, source_target_pairs={{0,4},{1,5},{2,6},{3,7},{4,0},{5,1},{6,2},{7,3},{8,12},{9,13},{10,... | collective-permute-start | bytes 368648 | tf_op jit(solution)/shard_map/ppermute | solution.py:656
  7.7 10.4 %collective-permute-start = (bf16[96,640]{1,0:T(8,128)(2,1)S(1)}, bf16[96,640]{1,0:T(8,128)(2,1)S(1)}, u32[]{:S(2)}, u32[]{:S(2)}) collective-permute-start(bf16[96,640]{1,0:T(8,128)(2,1)S(1)} %concatenate.6), channel_id=1, source_target_pairs={{0,2},{1,3},{2,0},{3,1},{4,6},{5,7},{6,4},{7,5},{8,10},{9,11},{10,... | collective-permute-start | bytes 368648 | tf_op jit(solution)/shard_map/ppermute | solution.py:656
  11.7 8.0 %copy-start.13 = (bf16[96,192]{1,0:T(8,128)(2,1)S(1)}, bf16[96,192]{1,0:T(8,128)(2,1)}, u32[]{:S(2)}) copy-start(bf16[96,192]{1,0:T(8,128)(2,1)} %param.32) | copy-start | bytes 110596
  18.1 12.4 %copy-start.1 = (bf16[4,96,640]{2,1,0:T(8,128)(2,1)}, bf16[4,96,640]{2,1,0:T(8,128)(2,1)S(1)}, u32[]{:S(2)}) copy-start(bf16[4,96,640]{2,1,0:T(8,128)(2,1)S(1)} %pad_maximum_fusion.own_ref) | copy-start | bytes 1474564
  18.1 12.3 %collective-permute-start.3 = (bf16[4,96,640]{2,1,0:T(8,128)(2,1)S(1)}, bf16[4,96,640]{2,1,0:T(8,128)(2,1)S(1)}, u32[]{:S(2)}, u32[]{:S(2)}) collective-permute-start(bf16[4,96,640]{2,1,0:T(8,128)(2,1)S(1)} %pad_maximum_fusion.own_ref), channel_id=1, source_target_pairs={{0,1},{1,0},{2,3},{3,2},{4,5},{5,4},{6,7},{7,6},{8,9},{9,8},{10,11... | collective-permute-start | bytes 1474568 | tf_op jit(solution)/shard_map/ppermute | solution.py:656
  19.7 6.2 %collective-permute-start.6 = (bf16[96,192]{1,0:T(8,128)(2,1)S(1)}, bf16[96,192]{1,0:T(8,128)(2,1)S(1)}, u32[]{:S(2)}, u32[]{:S(2)}) collective-permute-start(bf16[96,192]{1,0:T(8,128)(2,1)S(1)} %copy-done.13), channel_id=1, source_target_pairs={{0,6},{1,7},{2,4},{3,5},{4,2},{5,3},{6,0},{7,1},{8,14},{9,15},{10,... | collective-permute-start | bytes 110600 | tf_op jit(solution)/shard_map/ppermute | solution.py:656
  22.2 5.0 %collective-permute-start.5 = (bf16[96,192]{1,0:T(8,128)(2,1)S(1)}, bf16[96,192]{1,0:T(8,128)(2,1)S(1)}, u32[]{:S(2)}, u32[]{:S(2)}) collective-permute-start(bf16[96,192]{1,0:T(8,128)(2,1)S(1)} %copy-done.13), channel_id=1, source_target_pairs={{0,4},{1,5},{2,6},{3,7},{4,0},{5,1},{6,2},{7,3},{8,12},{9,13},{10,... | collective-permute-start | bytes 110600 | tf_op jit(solution)/shard_map/ppermute | solution.py:656
  22.2 5.0 %collective-permute-start.4 = (bf16[96,192]{1,0:T(8,128)(2,1)S(1)}, bf16[96,192]{1,0:T(8,128)(2,1)S(1)}, u32[]{:S(2)}, u32[]{:S(2)}) collective-permute-start(bf16[96,192]{1,0:T(8,128)(2,1)S(1)} %copy-done.13), channel_id=1, source_target_pairs={{0,2},{1,3},{2,0},{3,1},{4,6},{5,7},{6,4},{7,5},{8,10},{9,11},{10,... | collective-permute-start | bytes 110600 | tf_op jit(solution)/shard_map/ppermute | solution.py:656
  34.2 3.6 %collective-permute-start.7 = (bf16[768,640]{1,0:T(8,128)(2,1)}, bf16[768,640]{1,0:T(8,128)(2,1)S(1)}, u32[]{:S(2)}, u32[]{:S(2)}) collective-permute-start(bf16[768,640]{1,0:T(8,128)(2,1)} %assemble.1.refs_1_.refs_5_.refs_2_), channel_id=1, source_target_pairs={{0,8},{1,9},{2,10},{3,11},{4,12},{5,13},{6,14},{7,15},{8,0},{9,1},... | collective-permute-start | bytes 2949128 | tf_op jit(solution)/shard_map/ppermute | solution.py:656
  34.8 24.4 %collective-permute-start.9 = (bf16[768,640]{1,0:T(8,128)(2,1)}, bf16[768,640]{1,0:T(8,128)(2,1)S(1)}, u32[]{:S(2)}, u32[]{:S(2)}) collective-permute-start(bf16[768,640]{1,0:T(8,128)(2,1)} %assemble.1.refs_1_.refs_5_.refs_2_), channel_id=1, source_target_pairs={{0,16},{1,17},{2,18},{3,19},{4,20},{5,21},{6,22},{7,23},{8,24},{9,... | collective-permute-start | bytes 2949128 | tf_op jit(solution)/shard_map/ppermute | solution.py:656
  36.3 19.8 %collective-permute-start.8 = (bf16[4,96,192]{2,1,0:T(8,128)(2,1)}, bf16[4,96,192]{2,1,0:T(8,128)(2,1)}, u32[]{:S(2)}, u32[]{:S(2)}) collective-permute-start(bf16[4,96,192]{2,1,0:T(8,128)(2,1)} %pad_maximum_fusion.2), channel_id=1, source_target_pairs={{0,1},{1,0},{2,3},{3,2},{4,5},{5,4},{6,7},{7,6},{8,9},{9,8},{10,11... | collective-permute-start | bytes 442376 | tf_op jit(solution)/shard_map/ppermute | solution.py:656
  37.8 4.0 %copy-start.3 = (bf16[768,640]{1,0:T(8,128)(2,1)}, bf16[768,640]{1,0:T(8,128)(2,1)S(1)}, u32[]{:S(2)}) copy-start(bf16[768,640]{1,0:T(8,128)(2,1)S(1)} %collective-permute-done.7.refs_2_.refs_6_.refs_3_) | copy-start | bytes 2949124
  37.9 41.2 %all-to-all-start = ((bf16[8,128,768]{2,1,0:T(8,128)(2,1)}), bf16[8,128,768]{2,1,0:T(8,128)(2,1)S(1)}, u32[]{:S(2)}, u32[]{:S(2)}) async-start(bf16[8,128,768]{2,1,0:T(8,128)(2,1)} %bitcast.17), calls=%async_computation | async-start | bytes 3145728 | tf_op jit(solution)/shard_map/all_to_all | solution.py:778
  59.2 3.1 %copy-start.4 = (bf16[768,640]{1,0:T(8,128)(2,1)}, bf16[768,640]{1,0:T(8,128)(2,1)S(1)}, u32[]{:S(2)}) copy-start(bf16[768,640]{1,0:T(8,128)(2,1)S(1)} %collective-permute-done.9.refs_2_.refs_5_.refs_4_) | copy-start | bytes 2949124
  59.2 3.1 collective-permute-start.10
  59.2 20.4 %collective-permute-start.12 = (bf16[8,96,192]{2,1,0:T(8,128)(2,1)}, bf16[8,96,192]{2,1,0:T(8,128)(2,1)}, u32[]{:S(2)}, u32[]{:S(2)}) collective-permute-start(bf16[8,96,192]{2,1,0:T(8,128)(2,1)} %pad_maximum_fusion.1.refs_0_), channel_id=1, source_target_pairs={{0,8},{1,9},{2,10},{3,11},{4,12},{5,13},{6,14},{7,15},{8,0},{9,1},... | collective-permute-start | bytes 884744 | tf_op jit(solution)/shard_map/ppermute | solution.py:656
  59.7 19.4 %collective-permute-start.11 = (bf16[8,96,192]{2,1,0:T(8,128)(2,1)}, bf16[8,96,192]{2,1,0:T(8,128)(2,1)}, u32[]{:S(2)}, u32[]{:S(2)}) collective-permute-start(bf16[8,96,192]{2,1,0:T(8,128)(2,1)} %pad_maximum_fusion.1.refs_0_), channel_id=1, source_target_pairs={{0,16},{1,17},{2,18},{3,19},{4,20},{5,21},{6,22},{7,23},{8,24},{9,... | collective-permute-start | bytes 884744 | tf_op jit(solution)/shard_map/ppermute | solution.py:656
  79.1 12.0 %copy-start.2 = (bf16[8,128,768]{2,1,0:T(8,128)(2,1)}, bf16[8,128,768]{2,1,0:T(8,128)(2,1)S(1)}, u32[]{:S(2)}) copy-start(bf16[8,128,768]{2,1,0:T(8,128)(2,1)S(1)} %all-to-all-done) | copy-start | bytes 4718596
  79.1 1.9 collective-permute-start.13
  91.1 24.2 %all-to-all-start.1 = ((bf16[8,64,768]{2,1,0:T(8,128)(2,1)}), bf16[8,64,768]{2,1,0:T(8,128)(2,1)S(1)}, u32[]{:S(2)}, u32[]{:S(2)}) async-start(bf16[8,64,768]{2,1,0:T(8,128)(2,1)} %bitcast.79), calls=%async_computation.1 | async-start | bytes 1572864 | tf_op jit(solution)/shard_map/all_to_all | solution.py:778
  115.3 3.6 %copy-start.7 = (bf16[8,64,768]{2,1,0:T(8,128)(2,1)}, bf16[8,64,768]{2,1,0:T(8,128)(2,1)S(1)}, u32[]{:S(2)}) copy-start(bf16[8,64,768]{2,1,0:T(8,128)(2,1)S(1)} %all-to-all-done.1) | copy-start | bytes 2359300
  115.3 24.0 %all-to-all-start.2 = ((bf16[8,64,768]{2,1,0:T(8,128)(2,1)}), bf16[8,64,768]{2,1,0:T(8,128)(2,1)S(1)}, u32[]{:S(2)}, u32[]{:S(2)}) async-start(bf16[8,64,768]{2,1,0:T(8,128)(2,1)} %bitcast.78), calls=%async_computation.2 | async-start | bytes 1572864 | tf_op jit(solution)/shard_map/all_to_all | solution.py:778
  139.3 4.0 %copy-start.8 = (bf16[8,64,768]{2,1,0:T(8,128)(2,1)}, bf16[8,64,768]{2,1,0:T(8,128)(2,1)S(1)}, u32[]{:S(2)}) copy-start(bf16[8,64,768]{2,1,0:T(8,128)(2,1)S(1)} %all-to-all-done.2) | copy-start | bytes 2359300
  139.3 24.3 %all-to-all-start.3 = ((bf16[8,64,768]{2,1,0:T(8,128)(2,1)}), bf16[8,64,768]{2,1,0:T(8,128)(2,1)S(1)}, u32[]{:S(2)}, u32[]{:S(2)}) async-start(bf16[8,64,768]{2,1,0:T(8,128)(2,1)} %bitcast.77), calls=%async_computation.3 | async-start | bytes 1572864 | tf_op jit(solution)/shard_map/all_to_all | solution.py:778
  163.6 20.7 %copy-start.6 = (bf16[8,64,768]{2,1,0:T(8,128)(2,1)}, bf16[8,64,768]{2,1,0:T(8,128)(2,1)S(1)}, u32[]{:S(2)}) copy-start(bf16[8,64,768]{2,1,0:T(8,128)(2,1)S(1)} %all-to-all-done.3) | copy-start | bytes 2359300
  163.6 23.9 %all-to-all-start.4 = ((bf16[8,64,768]{2,1,0:T(8,128)(2,1)}), bf16[8,64,768]{2,1,0:T(8,128)(2,1)S(1)}, u32[]{:S(2)}, u32[]{:S(2)}) async-start(bf16[8,64,768]{2,1,0:T(8,128)(2,1)} %bitcast.76), calls=%async_computation.4 | async-start | bytes 1572864 | tf_op jit(solution)/shard_map/all_to_all | solution.py:778
  187.6 3.8 %copy-start.9 = (bf16[8,64,768]{2,1,0:T(8,128)(2,1)}, bf16[8,64,768]{2,1,0:T(8,128)(2,1)S(1)}, u32[]{:S(2)}) copy-start(bf16[8,64,768]{2,1,0:T(8,128)(2,1)S(1)} %all-to-all-done.4) | copy-start | bytes 2359300
  187.6 17.6 %collective-permute-start.14 = (bf16[2,1552,768]{2,1,0:T(8,128)(2,1)}, bf16[2,1552,768]{2,1,0:T(8,128)(2,1)}, u32[]{:S(2)}, u32[]{:S(2)}) collective-permute-start(bf16[2,1552,768]{2,1,0:T(8,128)(2,1)} %get-tuple-element.178), channel_id=1, source_target_pairs={{0,8},{1,9},{2,10},{3,11},{4,12},{5,13},{6,14},{7,15},{8,0},{9,1},... | collective-permute-start | bytes 14303240 | tf_op jit(solution)/shard_map/ppermute | solution.py:656
  187.6 47.7 %all-to-all-start.5 = ((bf16[8,128,768]{2,1,0:T(8,128)(2,1)}), bf16[8,128,768]{2,1,0:T(8,128)(2,1)S(1)}, u32[]{:S(2)}, u32[]{:S(2)}) async-start(bf16[8,128,768]{2,1,0:T(8,128)(2,1)} %bitcast.31), calls=%async_computation.5 | async-start | bytes 3145728 | tf_op jit(solution)/shard_map/all_to_all | solution.py:778
  233.2 9.5 %collective-permute-start.15 = (bf16[8,96,1024]{2,1,0:T(8,128)(2,1)}, bf16[8,96,1024]{2,1,0:T(8,128)(2,1)S(1)}, u32[]{:S(2)}, u32[]{:S(2)}) collective-permute-start(bf16[8,96,1024]{2,1,0:T(8,128)(2,1)} %get-tuple-element.188), channel_id=1, source_target_pairs={{0,8},{1,9},{2,10},{3,11},{4,12},{5,13},{6,14},{7,15},{8,0},{9,1},... | collective-permute-start | bytes 4718600 | tf_op jit(solution)/shard_map/ppermute | solution.py:656
  233.8 55.2 %collective-permute-start.22 = (bf16[1552,768]{1,0:T(8,128)(2,1)}, bf16[1552,768]{1,0:T(8,128)(2,1)}, u32[]{:S(2)}, u32[]{:S(2)}) collective-permute-start(bf16[1552,768]{1,0:T(8,128)(2,1)} %fusion), channel_id=1, source_target_pairs={{0,16},{1,17},{2,18},{3,19},{4,20},{5,21},{6,22},{7,23},{8,24},{9,... | collective-permute-start | bytes 7151624 | tf_op jit(solution)/shard_map/ppermute | solution.py:656
  244.8 24.6 %collective-permute-start.16 = (bf16[4,96,1024]{2,1,0:T(8,128)(2,1)S(1)}, bf16[4,96,1024]{2,1,0:T(8,128)(2,1)S(1)}, u32[]{:S(2)}, u32[]{:S(2)}) collective-permute-start(bf16[4,96,1024]{2,1,0:T(8,128)(2,1)S(1)} %get-tuple-element.196), channel_id=1, source_target_pairs={{0,1},{1,0},{2,3},{3,2},{4,5},{5,4},{6,7},{7,6},{8,9},{9,8},{10,11... | collective-permute-start | bytes 2359304 | tf_op jit(solution)/shard_map/ppermute | solution.py:656
  269.4 1.2 copy-start.14
  269.4 3.8 %copy-start.11 = (bf16[4,96,640]{2,1,0:T(8,128)(2,1)S(1)}, bf16[4,96,640]{2,1,0:T(8,128)(2,1)}, u32[]{:S(2)}) copy-start(bf16[4,96,640]{2,1,0:T(8,128)(2,1)} %get-tuple-element.203) | copy-start | bytes 1474564
  269.4 3.8 %copy-start.12 = (bf16[4,96,640]{2,1,0:T(8,128)(2,1)S(1)}, bf16[4,96,640]{2,1,0:T(8,128)(2,1)}, u32[]{:S(2)}) copy-start(bf16[4,96,640]{2,1,0:T(8,128)(2,1)} %get-tuple-element.201) | copy-start | bytes 1474564
  270.6 2.6 collective-permute-start.20
  273.4 15.5 %collective-permute-start.21 = (bf16[4,96,640]{2,1,0:T(8,128)(2,1)S(1)}, bf16[4,96,640]{2,1,0:T(8,128)(2,1)S(1)}, u32[]{:S(2)}, u32[]{:S(2)}) collective-permute-start(bf16[4,96,640]{2,1,0:T(8,128)(2,1)S(1)} %get-tuple-element.204), channel_id=1, source_target_pairs={{0,1},{1,0},{2,3},{3,2},{4,5},{5,4},{6,7},{7,6},{8,9},{9,8},{10,11... | collective-permute-start | bytes 1474568 | tf_op jit(solution)/shard_map/ppermute | solution.py:656
  273.8 15.1 %collective-permute-start.17 = (bf16[96,1024]{1,0:T(8,128)(2,1)S(1)}, bf16[96,1024]{1,0:T(8,128)(2,1)S(1)}, u32[]{:S(2)}, u32[]{:S(2)}) collective-permute-start(bf16[96,1024]{1,0:T(8,128)(2,1)S(1)} %get-tuple-element.197), channel_id=1, source_target_pairs={{0,2},{1,3},{2,0},{3,1},{4,6},{5,7},{6,4},{7,5},{8,10},{9,11},{10,... | collective-permute-start | bytes 589832 | tf_op jit(solution)/shard_map/ppermute | solution.py:656
  275.5 17.2 %collective-permute-start.18 = (bf16[96,1024]{1,0:T(8,128)(2,1)S(1)}, bf16[96,1024]{1,0:T(8,128)(2,1)S(1)}, u32[]{:S(2)}, u32[]{:S(2)}) collective-permute-start(bf16[96,1024]{1,0:T(8,128)(2,1)S(1)} %get-tuple-element.198), channel_id=1, source_target_pairs={{0,4},{1,5},{2,6},{3,7},{4,0},{5,1},{6,2},{7,3},{8,12},{9,13},{10,... | collective-permute-start | bytes 589832 | tf_op jit(solution)/shard_map/ppermute | solution.py:656
  277.8 14.8 %collective-permute-start.19 = (bf16[96,1024]{1,0:T(8,128)(2,1)S(1)}, bf16[96,1024]{1,0:T(8,128)(2,1)S(1)}, u32[]{:S(2)}, u32[]{:S(2)}) collective-permute-start(bf16[96,1024]{1,0:T(8,128)(2,1)S(1)} %get-tuple-element.199), channel_id=1, source_target_pairs={{0,6},{1,7},{2,4},{3,5},{4,2},{5,3},{6,0},{7,1},{8,14},{9,15},{10,... | collective-permute-start | bytes 589832 | tf_op jit(solution)/shard_map/ppermute | solution.py:656
  292.7 13.8 %collective-permute-start.26 = (bf16[96,832]{1,0:T(8,128)(2,1)S(1)}, bf16[96,832]{1,0:T(8,128)(2,1)S(1)}, u32[]{:S(2)}, u32[]{:S(2)}) collective-permute-start(bf16[96,832]{1,0:T(8,128)(2,1)S(1)} %slice.289), channel_id=1, source_target_pairs={{0,16},{1,17},{2,18},{3,19},{4,20},{5,21},{6,22},{7,23},{8,24},{9,... | collective-permute-start | bytes 479240 | tf_op jit(solution)/shard_map/ppermute | solution.py:656
  293.4 13.0 %collective-permute-start.25 = (bf16[96,640]{1,0:T(8,128)(2,1)S(1)}, bf16[96,640]{1,0:T(8,128)(2,1)S(1)}, u32[]{:S(2)}, u32[]{:S(2)}) collective-permute-start(bf16[96,640]{1,0:T(8,128)(2,1)S(1)} %get-tuple-element.243), channel_id=1, source_target_pairs={{0,6},{1,7},{2,4},{3,5},{4,2},{5,3},{6,0},{7,1},{8,14},{9,15},{10,... | collective-permute-start | bytes 368648 | tf_op jit(solution)/shard_map/ppermute | solution.py:656
  295.9 10.7 %collective-permute-start.24 = (bf16[96,640]{1,0:T(8,128)(2,1)S(1)}, bf16[96,640]{1,0:T(8,128)(2,1)S(1)}, u32[]{:S(2)}, u32[]{:S(2)}) collective-permute-start(bf16[96,640]{1,0:T(8,128)(2,1)S(1)} %get-tuple-element.244), channel_id=1, source_target_pairs={{0,4},{1,5},{2,6},{3,7},{4,0},{5,1},{6,2},{7,3},{8,12},{9,13},{10,... | collective-permute-start | bytes 368648 | tf_op jit(solution)/shard_map/ppermute | solution.py:656
  299.2 7.4 %collective-permute-start.23 = (bf16[96,640]{1,0:T(8,128)(2,1)S(1)}, bf16[96,640]{1,0:T(8,128)(2,1)S(1)}, u32[]{:S(2)}, u32[]{:S(2)}) collective-permute-start(bf16[96,640]{1,0:T(8,128)(2,1)S(1)} %get-tuple-element.245), channel_id=1, source_target_pairs={{0,2},{1,3},{2,0},{3,1},{4,6},{5,7},{6,4},{7,5},{8,10},{9,11},{10,... | collective-permute-start | bytes 368648 | tf_op jit(solution)/shard_map/ppermute | solution.py:656
  307.5 4.0 %collective-permute-start.29 = (f32[8,96]{0,1:T(8,128)S(1)}, f32[8,96]{0,1:T(8,128)S(1)}, u32[]{:S(2)}, u32[]{:S(2)}) collective-permute-start(f32[8,96]{0,1:T(8,128)S(1)} %slice_bitcast_fusion), channel_id=1, source_target_pairs={{0,24},{1,25},{2,26},{3,27},{4,28},{5,29},{6,30},{7,31},{8,16},{9,... | collective-permute-start | bytes 9224 | tf_op jit(solution)/shard_map/ppermute | solution.py:656
  307.5 4.9 %collective-permute-start.28 = (f32[8,96]{0,1:T(8,128)S(1)}, f32[8,96]{0,1:T(8,128)S(1)}, u32[]{:S(2)}, u32[]{:S(2)}) collective-permute-start(f32[8,96]{0,1:T(8,128)S(1)} %slice_bitcast_fusion), channel_id=1, source_target_pairs={{0,16},{1,17},{2,18},{3,19},{4,20},{5,21},{6,22},{7,23},{8,24},{9,... | collective-permute-start | bytes 9224 | tf_op jit(solution)/shard_map/ppermute | solution.py:656
  309.1 3.3 %collective-permute-start.27 = (f32[8,96]{0,1:T(8,128)S(1)}, f32[8,96]{0,1:T(8,128)S(1)}, u32[]{:S(2)}, u32[]{:S(2)}) collective-permute-start(f32[8,96]{0,1:T(8,128)S(1)} %slice_bitcast_fusion), channel_id=1, source_target_pairs={{0,8},{1,9},{2,10},{3,11},{4,12},{5,13},{6,14},{7,15},{8,0},{9,1},... | collective-permute-start | bytes 9224 | tf_op jit(solution)/shard_map/ppermute | solution.py:656
  (4 other events, 3.7 us)

commit v7 on v6

--- a/solution.py
+++ b/solution.py
@@ -130,7 +130,7 @@
     for at in range(0, count, 512):
         qkv_ref[0, at : at + 512] = (dot(low_ref[at : at + 512], w, 1, 0) + bias).astype(BF)
     for base in range(0, count, SEQ_LEN):
-        block = min(512, SEQ_LEN)
+        block = min(1024, SEQ_LEN)
         for h in range(part // HEAD_DIM):
             at = h * HEAD_DIM
             v = qkv_ref[0, base : base + SEQ_LEN, 2 * part + at : 2 * part + at + HEAD_DIM].T
@@ -374,8 +374,8 @@
         dm = got if dm is None else dm + got
     unit, inverse = normalize(h_ref[...])
     dh = g_ref[...].astype(F32) + normalize_back(dm, unit, inverse, vec_ref[5:6])
-    dh_ref[...] = dh
     low = dh.astype(BF)
+    dh_ref[...] = low
     sums = [
         jnp.sum(term, axis=0, keepdims=True) for term in (low.astype(F32), dm * unit, dm)
     ]
@@ -417,7 +417,7 @@
         [SCALARS, by_rows, by_rows, half, half, chunk((1, rows), 1), by_ctx, full((width, width)),
          full((8, width))],
         [
-            (by_rows, (count, width), F32),
+            (by_rows, (count, width), BF),
             (by_ctx, (GROUPS, count, part), BF),
             (full((GROUPS, width, part)), (GROUPS, width, part), BF),
             (full((8, width)), (8, width), F32),
@@ -603,7 +603,7 @@
         got = dot((one_ref, two_ref)[r // 2][r % 2], w[:, : 3 * part], 1, 1)
         da = got if da is None else da + got
     unit, inverse = normalize(x_ref[...].astype(F32))
-    out_ref[...] = dh_ref[...] + normalize_back(da, unit, inverse, vec_ref[0:1])
+    out_ref[...] = dh_ref[...].astype(F32) + normalize_back(da, unit, inverse, vec_ref[0:1])
 
 
 def unproject(grads, weights, x, dh, vec):
@@ -703,9 +703,11 @@
     return [grouped[i] for i in range(GROUPS)], [out[i] for i in range(GROUPS)], filler
 
 
-def reduce_y(place, keep, send):
+def reduce_y(place, keep, send, cols):
     got = place.move(send, place.y)
-    return keep[0].astype(F32) + got[0].astype(F32), [add(keep[k], got[k]) for k in range(1, 4)]
+    total = keep[0, :, :cols].astype(F32) + got[0, :, :cols].astype(F32)
+    sends = [add(keep[k, :, :cols], got[k, :, :cols]) for k in range(1, 4)]
+    return total, sends, add(keep[:, :, cols:], got[:, :, cols:])
 
 
 def reduce_z(place, sends):
@@ -863,9 +865,12 @@
         output = finish(h1, target, gy)
         send = add(send, more[4:])
         dctx, output, send = barrier((dctx, output, send))
-        across, sends = reduce_y(place, add(keep, more[:4]), send)
+        cols = width // GROUPS
+        across, sends, own_o = reduce_y(place, add(keep, more[:4]), send, FAR - cols)
         near, keep, send, more = back(0, dctx)
-        near, keep, send, more, across, sends = barrier((near, keep, send, more, across, sends))
+        near, keep, send, more, across, sends, own_o = barrier(
+            (near, keep, send, more, across, sends, own_o)
+        )
         more = place.move(more, place.core)
         got = reduce_z(place, sends)
         send, keep = add(send, more[4:]), add(keep, more[:4])
@@ -874,20 +879,20 @@
         input_grad = unproject((near, far), weights, block_entries, dh1, vec)
         got_far = got
         got, input_grad, came = barrier((got_y, input_grad, came))
-        total = keep[0].astype(F32) + got[0].astype(F32)
-        got = reduce_z(place, [add(keep[k], got[k]) for k in range(1, 4)])
+        wide = lambda k, a: jnp.concatenate([a, own_o[k].astype(a.dtype)], axis=1)
+        total = wide(0, keep[0].astype(F32) + got[0].astype(F32))
+        got = reduce_z(place, [wide(k, add(keep[k], got[k])) for k in range(1, 4)])
         got_far, came, input_grad = barrier((got_far, came, input_grad))
-        sum_o = across + sum(g.astype(F32) for g in got_far)
-        cols = width // GROUPS
-        across = place.move(sum_o[:, :-cols].astype(BF), place.x)
+        across = across + sum(g.astype(F32) for g in got_far)
+        across = place.move(across.astype(BF), place.x)
         pick = lambda at: sum(
             a[at : at + width].astype(F32) for a in (grads[1], came_far[1], came)
         )
         got, grads, across = barrier((got, [pick(0), pick(width), pick(2 * width)], across))
-        total += across[:, :640].astype(F32)
-        sum_o = sum_o[:, -cols:] + across[:, 640:].astype(F32)
+        total += across.astype(F32)
         total += sum(g.astype(F32) for g in got)
         (sum_q, sum_k, sum_v), small = columns_of(place, total, 7)
+        sum_o = total[:, 640:]
     else:
         parts = [back(half, dctx) for half in range(2)]
         slabs = [

time: 317 us -> 317 us (level)
    convert_element_type x5 -> x6, other arithmetic: 7.06 us -> 7.94 us  [add(): return (a.astype(F32) + b.astype(F32)).astype(BF)]
  transfers between devices with their start and end apart: 36 -> 36, of which waited for: 17 -> 15; matrix products, arithmetic and copies ran while one was open for 7% -> 8% of each run, Pallas kernels for 53% -> 53%
where the time goes in v7:
time: 317 us; the launch traced here: 313 us
  Pallas kernels  177 us (56%)
  starting transfers between devices  56.3 us (18%)
  waiting for transfers between devices  46 us (15%)
  other arithmetic  23.6 us (7%)
  local copies, waits for them, and re-layouts  8.49 us (3%)
    pallas_call x2, Pallas kernels, attend_back(): call(partial(attend_back_kernel, half), 'attend_back', (2,), [pl.BlockSpe...  46.3 us
    pallas_call x2, Pallas kernels, expert(): call(expert_kernel, 'expert', (ff // step,), [full((rows, width)), side,...  35.1 us
    ppermute x30, starting transfers between devices, move(): return lax.ppermute(array, BOTH, way)  33.8 us
    pallas_call x2, Pallas kernels, attend(): call(partial(attend_kernel, half), 'attend', (2,), [SCALARS] + ins, outs,...  28.4 us
    all_to_all x6, waiting for transfers between devices, exchange(): lax.all_to_all(sent, 'expert', split_axis=0, concat_axis=0, tiled=True)  28.3 us
    all_to_all x6, starting transfers between devices, exchange(): lax.all_to_all(sent, 'expert', split_axis=0, concat_axis=0, tiled=True)  22.5 us
    ppermute x30, waiting for transfers between devices, move(): return lax.ppermute(array, BOTH, way)  17.7 us
    pallas_call x1, Pallas kernels, weigh(): call(partial(weigh_kernel, split), 'weigh', (n,), [wide] * 4 + [full((row...  17.2 us
  transfers between devices with their start and end apart: 36, of which 15 were waited for; matrix products, arithmetic and copies ran while one was open for 8% of the time, Pallas kernels for 53%

profile of v7, /device:TPU:0, one launch (start us, length us, event | category | flops | bytes accessed | tf_op | source)
XLA Modules:
  0.0 312.7 jit_solution(15205545667320158662)
XLA Ops:
  2.5 5.1 %collective-permute-start.2 = (bf16[96,640]{1,0:T(8,128)(2,1)S(1)}, bf16[96,640]{1,0:T(8,128)(2,1)S(1)}, u32[]{:S(2)}, u32[]{:S(2)}) collective-permute-start(bf16[96,640]{1,0:T(8,128)(2,1)S(1)} %concatenate.18), channel_id=1, source_target_pairs={{0,6},{1,7},{2,4},{3,5},{4,2},{5,3},{6,0},{7,1},{8,14},{9,15},{10,... | collective-permute-start | bytes 368648 | tf_op jit(solution)/shard_map/ppermute | solution.py:656
  11.7 4.4 %dispatch.2 = bf16[1024,768]{1,0:T(8,128)(2,1)} custom-call(s32[1,1024]{1,0:T(1,128)} %bitcast.96, bf16[1024,768]{1,0:T(8,128)(2,1)} %g_ref.1), custom_call_target="tpu_custom_call" | custom-call | flops 1610612736 | bytes 3000000 | tf_op jit(solution)/shard_map/dispatch/pallas_call | solution.py:295
  16.0 2.0 collective-permute-done.1
  18.1 1.6 collective-permute-start.3
  19.7 2.5 collective-permute-start.6
  22.2 1.9 collective-permute-start.4
  24.6 1.3 collective-permute-done.6
  27.9 2.6 collective-permute-done.3.got_ref
  31.2 3.0 assemble.1.refs_1_.refs_5_.refs_2_
  34.9 1.5 collective-permute-start.9
  36.4 1.5 collective-permute-start.8
  37.9 3.9 %all-to-all-start = ((bf16[8,128,768]{2,1,0:T(8,128)(2,1)}), bf16[8,128,768]{2,1,0:T(8,128)(2,1)S(1)}, u32[]{:S(2)}, u32[]{:S(2)}) async-start(bf16[8,128,768]{2,1,0:T(8,128)(2,1)} %bitcast.17), calls=%async_computation | async-start | bytes 3145728 | tf_op jit(solution)/shard_map/all_to_all | solution.py:780
  41.8 14.8 %attend.2 = (bf16[4,1024,576]{2,1,0:T(8,128)(2,1)}, bf16[4,1024,192]{2,1,0:T(8,128)(2,1)}, f32[4,8,1024]{2,1,0:T(8,128)}, bf16[1024,768]{1,0:T(8,128)(2,1)}, f32[8,768]{1,0:T(8,128)}) custom-call(s32[4]{0:T(128)} %get-tuple-element.263.order, bf16[1024,768]{1,0:T(8,128)(2,1)} %refs_6_.1, bf16[768,640]{1,0:T(8,128)(2,1)} %assemble.1.refs_1_.refs_5_.refs_2_, ...), custom_call_target="tpu_custom_call" | custom-call | flops 12000000000 | bytes 8000000 | tf_op jit(solution)/shard_map/attend/pallas_call | solution.py:167
  56.6 1.8 pad_maximum_fusion.1.refs_0_
  59.7 1.5 collective-permute-start.11
  63.3 13.6 %attend.3 = (bf16[4,1024,576]{2,1,0:T(8,128)(2,1)}, bf16[4,1024,192]{2,1,0:T(8,128)(2,1)}, f32[4,8,1024]{2,1,0:T(8,128)}) custom-call(s32[4]{0:T(128)} %get-tuple-element.263.order, bf16[1024,768]{1,0:T(8,128)(2,1)} %get-tuple-element.128.refs_0_.refs_4_, ...), custom_call_target="tpu_custom_call", output_to_operand_aliasing={{0}: (5, {}), {1}: (6, {}), {2}: (7, {})} | custom-call | flops 12000000000 | bytes 8000000 | tf_op jit(solution)/shard_map/attend/pallas_call | solution.py:167
  76.9 2.2 all-to-all-done
  79.7 1.4 collective-permute-done.13.refs_3_
  81.8 9.3 %mix.1 = (f32[1024,768]{1,0:T(8,128)}, bf16[768,768]{1,0:T(8,128)(2,1)}, bf16[1024,768]{1,0:T(8,128)(2,1)}, bf16[512,768]{1,0:T(8,128)(2,1)}) custom-call(s32[4]{0:T(128)} %get-tuple-element.263.order, s32[8]{0:T(128)} %fusion.15.slab, bf16[1024,768]{1,0:T(8,128)(2,1)} %refs_6_.1, bf16[4,1024,192]{2,1,0:T(8,128)(2,1)} %get-tuple-element.147.ctx_ref.refs_1_, ...), custom_call_target="tpu_custom_call" | custom-call | flops 2818572288 | bytes 12000000 | tf_op jit(solution)/shard_map/mix/pallas_call | solution.py:347
  91.1 3.7 %all-to-all-start.1 = ((bf16[8,64,768]{2,1,0:T(8,128)(2,1)}), bf16[8,64,768]{2,1,0:T(8,128)(2,1)S(1)}, u32[]{:S(2)}, u32[]{:S(2)}) async-start(bf16[8,64,768]{2,1,0:T(8,128)(2,1)} %bitcast.86), calls=%async_computation.1 | async-start | bytes 1572864 | tf_op jit(solution)/shard_map/all_to_all | solution.py:780
  94.8 3.3 %dispatch.3 = bf16[512,768]{1,0:T(8,128)(2,1)} custom-call(s32[1,1024]{1,0:T(1,128)} %bitcast.99, bf16[1024,768]{1,0:T(8,128)(2,1)} %get-tuple-element.151.rows_ref), custom_call_target="tpu_custom_call" | custom-call | flops 1610612736 | bytes 3000000 | tf_op jit(solution)/shard_map/dispatch/pallas_call | solution.py:295
  98.1 17.3 %all-to-all-done.1 = bf16[8,64,768]{2,1,0:T(8,128)(2,1)S(1)} async-done(((bf16[8,64,768]{2,1,0:T(8,128)(2,1)}), bf16[8,64,768]{2,1,0:T(8,128)(2,1)S(1)}, u32[]{:S(2)}, u32[]{:S(2)}) %all-to-all-start.1) | async-done | bytes 786464 | tf_op jit(solution)/shard_map/all_to_all | solution.py:780
  115.3 3.6 %all-to-all-start.2 = ((bf16[8,64,768]{2,1,0:T(8,128)(2,1)}), bf16[8,64,768]{2,1,0:T(8,128)(2,1)S(1)}, u32[]{:S(2)}, u32[]{:S(2)}) async-start(bf16[8,64,768]{2,1,0:T(8,128)(2,1)} %bitcast.85), calls=%async_computation.2 | async-start | bytes 1572864 | tf_op jit(solution)/shard_map/all_to_all | solution.py:780
  119.0 17.6 %expert.2 = (bf16[8,2,64,768]{3,2,1,0:T(8,128)(2,1)}, bf16[512,768]{1,0:T(8,128)(2,1)}, bf16[512,768]{1,0:T(8,128)(2,1)}, bf16[512,3072]{1,0:T(8,128)(2,1)}, bf1...) custom-call(bf16[512,768]{1,0:T(8,128)(2,1)} %bitcast.77, bf16[8,2,64,768]{3,2,1,0:T(8,128)(2,1)} %bitcast.74, ...), custom_call_target="tpu_custom_call" | custom-call | flops 9663676416 | bytes 22000000 | tf_op jit(solution)/shard_map/expert/pallas_call | solution.py:508
  136.5 2.8 all-to-all-done.2
  139.3 4.0 %all-to-all-start.3 = ((bf16[8,64,768]{2,1,0:T(8,128)(2,1)}), bf16[8,64,768]{2,1,0:T(8,128)(2,1)S(1)}, u32[]{:S(2)}, u32[]{:S(2)}) async-start(bf16[8,64,768]{2,1,0:T(8,128)(2,1)} %bitcast.84), calls=%async_computation.3 | async-start | bytes 1572864 | tf_op jit(solution)/shard_map/all_to_all | solution.py:780
  143.3 17.5 %expert.3 = (bf16[8,2,64,768]{3,2,1,0:T(8,128)(2,1)}, bf16[512,768]{1,0:T(8,128)(2,1)}, bf16[512,768]{1,0:T(8,128)(2,1)}, bf16[512,3072]{1,0:T(8,128)(2,1)}, bf1...) custom-call(bf16[512,768]{1,0:T(8,128)(2,1)} %bitcast.80, ...), custom_call_target="tpu_custom_call", output_to_operand_aliasing={{0}: (7, {})} | custom-call | flops 9663676416 | bytes 22000000 | tf_op jit(solution)/shard_map/expert/pallas_call | solution.py:508
  160.9 2.8 all-to-all-done.3
  163.6 3.6 %all-to-all-start.4 = ((bf16[8,64,768]{2,1,0:T(8,128)(2,1)}), bf16[8,64,768]{2,1,0:T(8,128)(2,1)S(1)}, u32[]{:S(2)}, u32[]{:S(2)}) async-start(bf16[8,64,768]{2,1,0:T(8,128)(2,1)} %bitcast.83), calls=%async_computation.4 | async-start | bytes 1572864 | tf_op jit(solution)/shard_map/all_to_all | solution.py:780
  167.2 17.2 %weigh.1 = (bf16[2,1552,768]{2,1,0:T(8,128)(2,1)}, bf16[2,1552,768]{2,1,0:T(8,128)(2,1)}) custom-call(s32[4]{0:T(128)} %get-tuple-element.262.which, bf16[512,3072]{1,0:T(8,128)(2,1)} %get-tuple-element.162.refs_0_, bf16[512,3072]{1,0:T(8,128)(2,1)} %get-tuple-element.163.refs_1_, bf16[512,3072]{1,0:T(8,128)(2,1)} %get-tuple-element.164.refs_2_, ...), custom_call_target="tpu_custom_call" | custom-call | flops 9663676416 | bytes 26000000 | tf_op jit(solution)/shard_map/weigh/pallas_call | solution.py:588
  184.4 3.2 %all-to-all-done.4 = bf16[8,64,768]{2,1,0:T(8,128)(2,1)S(1)} async-done(((bf16[8,64,768]{2,1,0:T(8,128)(2,1)}), bf16[8,64,768]{2,1,0:T(8,128)(2,1)S(1)}, u32[]{:S(2)}, u32[]{:S(2)}) %all-to-all-start.4) | async-done | bytes 786464 | tf_op jit(solution)/shard_map/all_to_all | solution.py:780
  187.6 3.8 %all-to-all-start.5 = ((bf16[8,128,768]{2,1,0:T(8,128)(2,1)}), bf16[8,128,768]{2,1,0:T(8,128)(2,1)S(1)}, u32[]{:S(2)}, u32[]{:S(2)}) async-start(bf16[8,128,768]{2,1,0:T(8,128)(2,1)} %bitcast.31), calls=%async_computation.5 | async-start | bytes 3145728 | tf_op jit(solution)/shard_map/all_to_all | solution.py:780
  191.4 13.6 %unmix.1 = (bf16[1024,768]{1,0:T(8,128)(2,1)}, bf16[4,1024,192]{2,1,0:T(8,128)(2,1)}, bf16[4,768,192]{2,1,0:T(8,128)(2,1)}, f32[8,768]{1,0:T(8,128)}) custom-call(s32[4]{0:T(128)} %get-tuple-element.263.order, f32[1024,768]{1,0:T(8,128)} %get-tuple-element.149.h_ref, bf16[1024,768]{1,0:T(8,128)(2,1)} %g_ref.1, bf16[512,768]{1,0:T(8,128)(2,1)} %bitcast.76, ...), custom_call_target="tpu_custom_call" | custom-call | flops 4026531840 | bytes 20000000 | tf_op jit(solution)/shard_map/unmix/pallas_call | solution.py:415
  204.9 4.4 %fusion = bf16[1552,768]{1,0:T(8,128)(2,1)} fusion(bf16[2,1552,768]{2,1,0:T(8,128)(2,1)} %collective-permute-done.14, bf16[2,1552,768]{2,1,0:T(8,128)(2,1)} %get-tuple-element.178), kind=kLoop, calls=%fused_computation.1 | loop fusion | flops 4767744 | bytes 7151616 | tf_op jit(solution)/shard_map/convert_element_type | solution.py:624
  209.4 23.6 %attend_back.2 = (bf16[2,1024,576]{2,1,0:T(8,128)(2,1)}, bf16[4,96,1024]{2,1,0:T(8,128)(2,1)}, bf16[4,96,1024]{2,1,0:T(8,128)(2,1)}, bf16[8,96,1024]{2,1,0:T(8,128)(2,1)}) custom-call(s32[4]{0:T(128)} %get-tuple-element.263.order, s32[8]{0:T(128)} %fusion.19.table, bf16[4,1024,576]{2,1,0:T(8,128)(2,1)} %get-tuple-element.181.refs_0_, ...), custom_call_target="tpu_custom_call" | custom-call | flops 24000000000 | bytes 14000000 | tf_op jit(solution)/shard_map/attend_back/pallas_call | solution.py:262
  233.5 1.5 collective-permute-start.22
  236.2 6.2 %finish.1 = bf16[1024,768]{1,0:T(8,128)(2,1)} custom-call(f32[1024,768]{1,0:T(8,128)} %get-tuple-element.149.h_ref, s32[1,1024]{1,0:T(1,128)} %bitcast.97, bf16[1024,768]{1,0:T(8,128)(2,1)} %bitcast.71), custom_call_target="tpu_custom_call" | custom-call | flops 1610612736 | bytes 6000000 | tf_op jit(solution)/shard_map/finish/pallas_call | solution.py:439
  242.4 2.0 add_convert_fusion.1
  244.5 1.7 collective-permute-start.16
  246.2 22.7 %attend_back.3 = (bf16[2,1024,576]{2,1,0:T(8,128)(2,1)}, bf16[4,96,640]{2,1,0:T(8,128)(2,1)}, bf16[4,96,640]{2,1,0:T(8,128)(2,1)}, bf16[8,96,640]{2,1,0:T(8,128)(2,1)}) custom-call(s32[4]{0:T(128)} %get-tuple-element.263.order, s32[8]{0:T(128)} %fusion.19.table, bf16[4,1024,576]{2,1,0:T(8,128)(2,1)} %get-tuple-element.181.refs_0_, ...), custom_call_target="tpu_custom_call" | custom-call | flops 24000000000 | bytes 14000000 | tf_op jit(solution)/shard_map/attend_back/pallas_call | solution.py:262
  270.1 1.5 collective-permute-start.17
  271.6 2.4 collective-permute-start.18
  275.2 10.5 %unproject.1 = f32[1024,768]{1,0:T(8,128)} custom-call(bf16[2,1024,576]{2,1,0:T(8,128)(2,1)} %get-tuple-element.206.refs_0_, bf16[2,1024,576]{2,1,0:T(8,128)(2,1)} %get-tuple-element.207.refs_1_, bf16[768,640]{1,0:T(8,128)(2,1)} %assemble.1.refs_1_.refs_5_.refs_2_, bf16[768,640]{1,0:T(8,128)(2,1)} %copy-done.3, bf16[768,640]{1,0:T(8,128)(2,1)} %copy-done.4, ...), custom_call_target="tpu_custom_call" | custom-call | flops 3623878656 | bytes 20000000 | tf_op jit(solution)/shard_map/unproject/pallas_call | solution.py:614
  285.7 1.9 collective-permute-done.22
  287.8 3.4 %collective-permute-start.23 = (bf16[96,832]{1,0:T(8,128)(2,1)S(1)}, bf16[96,832]{1,0:T(8,128)(2,1)S(1)}, u32[]{:S(2)}, u32[]{:S(2)}) collective-permute-start(bf16[96,832]{1,0:T(8,128)(2,1)S(1)} %pad_maximum_fusion.3), channel_id=1, source_target_pairs={{0,2},{1,3},{2,0},{3,1},{4,6},{5,7},{6,4},{7,5},{8,10},{9,11},{10,... | collective-permute-start | bytes 479240 | tf_op jit(solution)/shard_map/ppermute | solution.py:656
  292.2 1.5 collective-permute-start.25
  295.4 6.0 %bitcast_add_fusion = (f32[768,768]{1,0:T(8,128)}, f32[768,768]{1,0:T(8,128)}) fusion(bf16[2,1552,768]{2,1,0:T(8,128)(2,1)} %collective-permute-done.14, bf16[1552,768]{1,0:T(8,128)(2,1)} %collective-permute-done.22, bf16[2,1552,768]{2,1,0:T(8,128)(2,1)} %get-tuple-element.178), kind=kLoop, calls=%fused_computation.2 | loop fusion | flops 5898240 | bytes 11796480 | tf_op jit(solution)/shard_map/add | solution.py:888
  302.1 4.7 %collective-permute-done.24 = bf16[96,832]{1,0:T(8,128)(2,1)S(1)} collective-permute-done((bf16[96,832]{1,0:T(8,128)(2,1)S(1)}, bf16[96,832]{1,0:T(8,128)(2,1)S(1)}, u32[]{:S(2)}, u32[]{:S(2)}) %collective-permute-start.24) | collective-permute-done | bytes 159776 | tf_op jit(solution)/shard_map/ppermute | solution.py:656
  (101 shorter events, 28.0 us)
Async XLA Ops:
  2.5 13.5 %collective-permute-start.2 = (bf16[96,640]{1,0:T(8,128)(2,1)S(1)}, bf16[96,640]{1,0:T(8,128)(2,1)S(1)}, u32[]{:S(2)}, u32[]{:S(2)}) collective-permute-start(bf16[96,640]{1,0:T(8,128)(2,1)S(1)} %concatenate.18), channel_id=1, source_target_pairs={{0,6},{1,7},{2,4},{3,5},{4,2},{5,3},{6,0},{7,1},{8,14},{9,15},{10,... | collective-permute-start | bytes 368648 | tf_op jit(solution)/shard_map/ppermute | solution.py:656
  7.7 10.4 %collective-permute-start.1 = (bf16[96,640]{1,0:T(8,128)(2,1)S(1)}, bf16[96,640]{1,0:T(8,128)(2,1)S(1)}, u32[]{:S(2)}, u32[]{:S(2)}) collective-permute-start(bf16[96,640]{1,0:T(8,128)(2,1)S(1)} %concatenate.18), channel_id=1, source_target_pairs={{0,4},{1,5},{2,6},{3,7},{4,0},{5,1},{6,2},{7,3},{8,12},{9,13},{10,... | collective-permute-start | bytes 368648 | tf_op jit(solution)/shard_map/ppermute | solution.py:656
  7.7 10.4 %collective-permute-start = (bf16[96,640]{1,0:T(8,128)(2,1)S(1)}, bf16[96,640]{1,0:T(8,128)(2,1)S(1)}, u32[]{:S(2)}, u32[]{:S(2)}) collective-permute-start(bf16[96,640]{1,0:T(8,128)(2,1)S(1)} %concatenate.18), channel_id=1, source_target_pairs={{0,2},{1,3},{2,0},{3,1},{4,6},{5,7},{6,4},{7,5},{8,10},{9,11},{10,... | collective-permute-start | bytes 368648 | tf_op jit(solution)/shard_map/ppermute | solution.py:656
  11.7 8.0 %copy-start.13 = (bf16[96,192]{1,0:T(8,128)(2,1)S(1)}, bf16[96,192]{1,0:T(8,128)(2,1)}, u32[]{:S(2)}) copy-start(bf16[96,192]{1,0:T(8,128)(2,1)} %param.32) | copy-start | bytes 110596
  18.1 12.4 %copy-start.1 = (bf16[4,96,640]{2,1,0:T(8,128)(2,1)}, bf16[4,96,640]{2,1,0:T(8,128)(2,1)S(1)}, u32[]{:S(2)}) copy-start(bf16[4,96,640]{2,1,0:T(8,128)(2,1)S(1)} %pad_maximum_fusion.own_ref) | copy-start | bytes 1474564
  18.1 12.3 %collective-permute-start.3 = (bf16[4,96,640]{2,1,0:T(8,128)(2,1)S(1)}, bf16[4,96,640]{2,1,0:T(8,128)(2,1)S(1)}, u32[]{:S(2)}, u32[]{:S(2)}) collective-permute-start(bf16[4,96,640]{2,1,0:T(8,128)(2,1)S(1)} %pad_maximum_fusion.own_ref), channel_id=1, source_target_pairs={{0,1},{1,0},{2,3},{3,2},{4,5},{5,4},{6,7},{7,6},{8,9},{9,8},{10,11... | collective-permute-start | bytes 1474568 | tf_op jit(solution)/shard_map/ppermute | solution.py:656
  19.7 6.2 %collective-permute-start.6 = (bf16[96,192]{1,0:T(8,128)(2,1)S(1)}, bf16[96,192]{1,0:T(8,128)(2,1)S(1)}, u32[]{:S(2)}, u32[]{:S(2)}) collective-permute-start(bf16[96,192]{1,0:T(8,128)(2,1)S(1)} %copy-done.13), channel_id=1, source_target_pairs={{0,6},{1,7},{2,4},{3,5},{4,2},{5,3},{6,0},{7,1},{8,14},{9,15},{10,... | collective-permute-start | bytes 110600 | tf_op jit(solution)/shard_map/ppermute | solution.py:656
  22.2 5.0 %collective-permute-start.5 = (bf16[96,192]{1,0:T(8,128)(2,1)S(1)}, bf16[96,192]{1,0:T(8,128)(2,1)S(1)}, u32[]{:S(2)}, u32[]{:S(2)}) collective-permute-start(bf16[96,192]{1,0:T(8,128)(2,1)S(1)} %copy-done.13), channel_id=1, source_target_pairs={{0,4},{1,5},{2,6},{3,7},{4,0},{5,1},{6,2},{7,3},{8,12},{9,13},{10,... | collective-permute-start | bytes 110600 | tf_op jit(solution)/shard_map/ppermute | solution.py:656
  22.2 5.0 %collective-permute-start.4 = (bf16[96,192]{1,0:T(8,128)(2,1)S(1)}, bf16[96,192]{1,0:T(8,128)(2,1)S(1)}, u32[]{:S(2)}, u32[]{:S(2)}) collective-permute-start(bf16[96,192]{1,0:T(8,128)(2,1)S(1)} %copy-done.13), channel_id=1, source_target_pairs={{0,2},{1,3},{2,0},{3,1},{4,6},{5,7},{6,4},{7,5},{8,10},{9,11},{10,... | collective-permute-start | bytes 110600 | tf_op jit(solution)/shard_map/ppermute | solution.py:656
  34.3 3.6 %collective-permute-start.7 = (bf16[768,640]{1,0:T(8,128)(2,1)}, bf16[768,640]{1,0:T(8,128)(2,1)S(1)}, u32[]{:S(2)}, u32[]{:S(2)}) collective-permute-start(bf16[768,640]{1,0:T(8,128)(2,1)} %assemble.1.refs_1_.refs_5_.refs_2_), channel_id=1, source_target_pairs={{0,8},{1,9},{2,10},{3,11},{4,12},{5,13},{6,14},{7,15},{8,0},{9,1},... | collective-permute-start | bytes 2949128 | tf_op jit(solution)/shard_map/ppermute | solution.py:656
  34.9 24.4 %collective-permute-start.9 = (bf16[768,640]{1,0:T(8,128)(2,1)}, bf16[768,640]{1,0:T(8,128)(2,1)S(1)}, u32[]{:S(2)}, u32[]{:S(2)}) collective-permute-start(bf16[768,640]{1,0:T(8,128)(2,1)} %assemble.1.refs_1_.refs_5_.refs_2_), channel_id=1, source_target_pairs={{0,16},{1,17},{2,18},{3,19},{4,20},{5,21},{6,22},{7,23},{8,24},{9,... | collective-permute-start | bytes 2949128 | tf_op jit(solution)/shard_map/ppermute | solution.py:656
  36.4 20.3 %collective-permute-start.8 = (bf16[4,96,192]{2,1,0:T(8,128)(2,1)}, bf16[4,96,192]{2,1,0:T(8,128)(2,1)}, u32[]{:S(2)}, u32[]{:S(2)}) collective-permute-start(bf16[4,96,192]{2,1,0:T(8,128)(2,1)} %pad_maximum_fusion.2), channel_id=1, source_target_pairs={{0,1},{1,0},{2,3},{3,2},{4,5},{5,4},{6,7},{7,6},{8,9},{9,8},{10,11... | collective-permute-start | bytes 442376 | tf_op jit(solution)/shard_map/ppermute | solution.py:656
  37.9 4.0 %copy-start.3 = (bf16[768,640]{1,0:T(8,128)(2,1)}, bf16[768,640]{1,0:T(8,128)(2,1)S(1)}, u32[]{:S(2)}) copy-start(bf16[768,640]{1,0:T(8,128)(2,1)S(1)} %collective-permute-done.7.refs_2_.refs_6_.refs_3_) | copy-start | bytes 2949124
  37.9 41.2 %all-to-all-start = ((bf16[8,128,768]{2,1,0:T(8,128)(2,1)}), bf16[8,128,768]{2,1,0:T(8,128)(2,1)S(1)}, u32[]{:S(2)}, u32[]{:S(2)}) async-start(bf16[8,128,768]{2,1,0:T(8,128)(2,1)} %bitcast.17), calls=%async_computation | async-start | bytes 3145728 | tf_op jit(solution)/shard_map/all_to_all | solution.py:780
  59.2 3.1 %copy-start.4 = (bf16[768,640]{1,0:T(8,128)(2,1)}, bf16[768,640]{1,0:T(8,128)(2,1)S(1)}, u32[]{:S(2)}) copy-start(bf16[768,640]{1,0:T(8,128)(2,1)S(1)} %collective-permute-done.9.refs_2_.refs_5_.refs_4_) | copy-start | bytes 2949124
  59.2 3.1 %collective-permute-start.10 = (bf16[768,640]{1,0:T(8,128)(2,1)S(1)}, bf16[768,640]{1,0:T(8,128)(2,1)S(1)}, u32[]{:S(2)}, u32[]{:S(2)}) collective-permute-start(bf16[768,640]{1,0:T(8,128)(2,1)S(1)} %collective-permute-done.9.refs_2_.refs_5_.refs_4_), channel_id=1, source_target_pairs={{0,8},{1,9},{2,10},{3,11},{4,12},{5,13},{6,14},{7,15},{8,0},{9,1},... | collective-permute-start | bytes 2949128 | tf_op jit(solution)/shard_map/ppermute | solution.py:656
  59.2 20.4 %collective-permute-start.12 = (bf16[8,96,192]{2,1,0:T(8,128)(2,1)}, bf16[8,96,192]{2,1,0:T(8,128)(2,1)}, u32[]{:S(2)}, u32[]{:S(2)}) collective-permute-start(bf16[8,96,192]{2,1,0:T(8,128)(2,1)} %pad_maximum_fusion.1.refs_0_), channel_id=1, source_target_pairs={{0,8},{1,9},{2,10},{3,11},{4,12},{5,13},{6,14},{7,15},{8,0},{9,1},... | collective-permute-start | bytes 884744 | tf_op jit(solution)/shard_map/ppermute | solution.py:656
  59.7 19.4 %collective-permute-start.11 = (bf16[8,96,192]{2,1,0:T(8,128)(2,1)}, bf16[8,96,192]{2,1,0:T(8,128)(2,1)}, u32[]{:S(2)}, u32[]{:S(2)}) collective-permute-start(bf16[8,96,192]{2,1,0:T(8,128)(2,1)} %pad_maximum_fusion.1.refs_0_), channel_id=1, source_target_pairs={{0,16},{1,17},{2,18},{3,19},{4,20},{5,21},{6,22},{7,23},{8,24},{9,... | collective-permute-start | bytes 884744 | tf_op jit(solution)/shard_map/ppermute | solution.py:656
  79.1 12.0 %copy-start.2 = (bf16[8,128,768]{2,1,0:T(8,128)(2,1)}, bf16[8,128,768]{2,1,0:T(8,128)(2,1)S(1)}, u32[]{:S(2)}) copy-start(bf16[8,128,768]{2,1,0:T(8,128)(2,1)S(1)} %all-to-all-done) | copy-start | bytes 4718596
  79.1 1.9 collective-permute-start.13
  91.1 24.2 %all-to-all-start.1 = ((bf16[8,64,768]{2,1,0:T(8,128)(2,1)}), bf16[8,64,768]{2,1,0:T(8,128)(2,1)S(1)}, u32[]{:S(2)}, u32[]{:S(2)}) async-start(bf16[8,64,768]{2,1,0:T(8,128)(2,1)} %bitcast.86), calls=%async_computation.1 | async-start | bytes 1572864 | tf_op jit(solution)/shard_map/all_to_all | solution.py:780
  115.3 3.6 %copy-start.7 = (bf16[8,64,768]{2,1,0:T(8,128)(2,1)}, bf16[8,64,768]{2,1,0:T(8,128)(2,1)S(1)}, u32[]{:S(2)}) copy-start(bf16[8,64,768]{2,1,0:T(8,128)(2,1)S(1)} %all-to-all-done.1) | copy-start | bytes 2359300
  115.3 24.0 %all-to-all-start.2 = ((bf16[8,64,768]{2,1,0:T(8,128)(2,1)}), bf16[8,64,768]{2,1,0:T(8,128)(2,1)S(1)}, u32[]{:S(2)}, u32[]{:S(2)}) async-start(bf16[8,64,768]{2,1,0:T(8,128)(2,1)} %bitcast.85), calls=%async_computation.2 | async-start | bytes 1572864 | tf_op jit(solution)/shard_map/all_to_all | solution.py:780
  139.3 4.0 %copy-start.8 = (bf16[8,64,768]{2,1,0:T(8,128)(2,1)}, bf16[8,64,768]{2,1,0:T(8,128)(2,1)S(1)}, u32[]{:S(2)}) copy-start(bf16[8,64,768]{2,1,0:T(8,128)(2,1)S(1)} %all-to-all-done.2) | copy-start | bytes 2359300
  139.3 24.3 %all-to-all-start.3 = ((bf16[8,64,768]{2,1,0:T(8,128)(2,1)}), bf16[8,64,768]{2,1,0:T(8,128)(2,1)S(1)}, u32[]{:S(2)}, u32[]{:S(2)}) async-start(bf16[8,64,768]{2,1,0:T(8,128)(2,1)} %bitcast.84), calls=%async_computation.3 | async-start | bytes 1572864 | tf_op jit(solution)/shard_map/all_to_all | solution.py:780
  163.6 20.7 %copy-start.6 = (bf16[8,64,768]{2,1,0:T(8,128)(2,1)}, bf16[8,64,768]{2,1,0:T(8,128)(2,1)S(1)}, u32[]{:S(2)}) copy-start(bf16[8,64,768]{2,1,0:T(8,128)(2,1)S(1)} %all-to-all-done.3) | copy-start | bytes 2359300
  163.6 23.9 %all-to-all-start.4 = ((bf16[8,64,768]{2,1,0:T(8,128)(2,1)}), bf16[8,64,768]{2,1,0:T(8,128)(2,1)S(1)}, u32[]{:S(2)}, u32[]{:S(2)}) async-start(bf16[8,64,768]{2,1,0:T(8,128)(2,1)} %bitcast.83), calls=%async_computation.4 | async-start | bytes 1572864 | tf_op jit(solution)/shard_map/all_to_all | solution.py:780
  187.6 3.8 %copy-start.9 = (bf16[8,64,768]{2,1,0:T(8,128)(2,1)}, bf16[8,64,768]{2,1,0:T(8,128)(2,1)S(1)}, u32[]{:S(2)}) copy-start(bf16[8,64,768]{2,1,0:T(8,128)(2,1)S(1)} %all-to-all-done.4) | copy-start | bytes 2359300
  187.6 17.4 %collective-permute-start.14 = (bf16[2,1552,768]{2,1,0:T(8,128)(2,1)}, bf16[2,1552,768]{2,1,0:T(8,128)(2,1)}, u32[]{:S(2)}, u32[]{:S(2)}) collective-permute-start(bf16[2,1552,768]{2,1,0:T(8,128)(2,1)} %get-tuple-element.179), channel_id=1, source_target_pairs={{0,8},{1,9},{2,10},{3,11},{4,12},{5,13},{6,14},{7,15},{8,0},{9,1},... | collective-permute-start | bytes 14303240 | tf_op jit(solution)/shard_map/ppermute | solution.py:656
  187.6 47.4 %all-to-all-start.5 = ((bf16[8,128,768]{2,1,0:T(8,128)(2,1)}), bf16[8,128,768]{2,1,0:T(8,128)(2,1)S(1)}, u32[]{:S(2)}, u32[]{:S(2)}) async-start(bf16[8,128,768]{2,1,0:T(8,128)(2,1)} %bitcast.31), calls=%async_computation.5 | async-start | bytes 3145728 | tf_op jit(solution)/shard_map/all_to_all | solution.py:780
  232.9 9.5 %collective-permute-start.15 = (bf16[8,96,1024]{2,1,0:T(8,128)(2,1)}, bf16[8,96,1024]{2,1,0:T(8,128)(2,1)S(1)}, u32[]{:S(2)}, u32[]{:S(2)}) collective-permute-start(bf16[8,96,1024]{2,1,0:T(8,128)(2,1)} %get-tuple-element.189), channel_id=1, source_target_pairs={{0,8},{1,9},{2,10},{3,11},{4,12},{5,13},{6,14},{7,15},{8,0},{9,1},... | collective-permute-start | bytes 4718600 | tf_op jit(solution)/shard_map/ppermute | solution.py:656
  233.5 54.1 %collective-permute-start.22 = (bf16[1552,768]{1,0:T(8,128)(2,1)}, bf16[1552,768]{1,0:T(8,128)(2,1)}, u32[]{:S(2)}, u32[]{:S(2)}) collective-permute-start(bf16[1552,768]{1,0:T(8,128)(2,1)} %fusion), channel_id=1, source_target_pairs={{0,16},{1,17},{2,18},{3,19},{4,20},{5,21},{6,22},{7,23},{8,24},{9,... | collective-permute-start | bytes 7151624 | tf_op jit(solution)/shard_map/ppermute | solution.py:656
  235.0 1.1 copy-start
  244.5 24.5 %collective-permute-start.16 = (bf16[4,96,1024]{2,1,0:T(8,128)(2,1)S(1)}, bf16[4,96,1024]{2,1,0:T(8,128)(2,1)S(1)}, u32[]{:S(2)}, u32[]{:S(2)}) collective-permute-start(bf16[4,96,1024]{2,1,0:T(8,128)(2,1)S(1)} %get-tuple-element.197), channel_id=1, source_target_pairs={{0,1},{1,0},{2,3},{3,2},{4,5},{5,4},{6,7},{7,6},{8,9},{9,8},{10,11... | collective-permute-start | bytes 2359304 | tf_op jit(solution)/shard_map/ppermute | solution.py:656
  268.9 5.6 %copy-start.11 = (bf16[4,96,640]{2,1,0:T(8,128)(2,1)S(1)}, bf16[4,96,640]{2,1,0:T(8,128)(2,1)}, u32[]{:S(2)}) copy-start(bf16[4,96,640]{2,1,0:T(8,128)(2,1)} %get-tuple-element.204) | copy-start | bytes 1474564
  269.0 5.6 %copy-start.12 = (bf16[4,96,640]{2,1,0:T(8,128)(2,1)S(1)}, bf16[4,96,640]{2,1,0:T(8,128)(2,1)}, u32[]{:S(2)}) copy-start(bf16[4,96,640]{2,1,0:T(8,128)(2,1)} %get-tuple-element.202) | copy-start | bytes 1474564
  270.1 4.4 %collective-permute-start.20 = (bf16[8,96,640]{2,1,0:T(8,128)(2,1)}, bf16[8,96,640]{2,1,0:T(8,128)(2,1)S(1)}, u32[]{:S(2)}, u32[]{:S(2)}) collective-permute-start(bf16[8,96,640]{2,1,0:T(8,128)(2,1)} %get-tuple-element.203), channel_id=1, source_target_pairs={{0,8},{1,9},{2,10},{3,11},{4,12},{5,13},{6,14},{7,15},{8,0},{9,1},... | collective-permute-start | bytes 2949128 | tf_op jit(solution)/shard_map/ppermute | solution.py:656
  270.1 17.5 %collective-permute-start.17 = (bf16[96,832]{1,0:T(8,128)(2,1)}, bf16[96,832]{1,0:T(8,128)(2,1)S(1)}, u32[]{:S(2)}, u32[]{:S(2)}) collective-permute-start(bf16[96,832]{1,0:T(8,128)(2,1)} %get-tuple-element.198), channel_id=1, source_target_pairs={{0,2},{1,3},{2,0},{3,1},{4,6},{5,7},{6,4},{7,5},{8,10},{9,11},{10,... | collective-permute-start | bytes 479240 | tf_op jit(solution)/shard_map/ppermute | solution.py:656
  271.6 16.0 %collective-permute-start.18 = (bf16[96,832]{1,0:T(8,128)(2,1)}, bf16[96,832]{1,0:T(8,128)(2,1)S(1)}, u32[]{:S(2)}, u32[]{:S(2)}) collective-permute-start(bf16[96,832]{1,0:T(8,128)(2,1)} %get-tuple-element.199), channel_id=1, source_target_pairs={{0,4},{1,5},{2,6},{3,7},{4,0},{5,1},{6,2},{7,3},{8,12},{9,13},{10,... | collective-permute-start | bytes 479240 | tf_op jit(solution)/shard_map/ppermute | solution.py:656
  274.0 13.7 %collective-permute-start.19 = (bf16[96,832]{1,0:T(8,128)(2,1)}, bf16[96,832]{1,0:T(8,128)(2,1)}, u32[]{:S(2)}, u32[]{:S(2)}) collective-permute-start(bf16[96,832]{1,0:T(8,128)(2,1)} %get-tuple-element.200), channel_id=1, source_target_pairs={{0,6},{1,7},{2,4},{3,5},{4,2},{5,3},{6,0},{7,1},{8,14},{9,15},{10,... | collective-permute-start | bytes 479240 | tf_op jit(solution)/shard_map/ppermute | solution.py:656
  274.8 12.9 %collective-permute-start.21 = (bf16[4,96,640]{2,1,0:T(8,128)(2,1)S(1)}, bf16[4,96,640]{2,1,0:T(8,128)(2,1)S(1)}, u32[]{:S(2)}, u32[]{:S(2)}) collective-permute-start(bf16[4,96,640]{2,1,0:T(8,128)(2,1)S(1)} %get-tuple-element.205), channel_id=1, source_target_pairs={{0,1},{1,0},{2,3},{3,2},{4,5},{5,4},{6,7},{7,6},{8,9},{9,8},{10,11... | collective-permute-start | bytes 1474568 | tf_op jit(solution)/shard_map/ppermute | solution.py:656
  287.8 14.3 %collective-permute-start.23 = (bf16[96,832]{1,0:T(8,128)(2,1)S(1)}, bf16[96,832]{1,0:T(8,128)(2,1)S(1)}, u32[]{:S(2)}, u32[]{:S(2)}) collective-permute-start(bf16[96,832]{1,0:T(8,128)(2,1)S(1)} %pad_maximum_fusion.3), channel_id=1, source_target_pairs={{0,2},{1,3},{2,0},{3,1},{4,6},{5,7},{6,4},{7,5},{8,10},{9,11},{10,... | collective-permute-start | bytes 479240 | tf_op jit(solution)/shard_map/ppermute | solution.py:656
  291.2 15.6 %collective-permute-start.24 = (bf16[96,832]{1,0:T(8,128)(2,1)S(1)}, bf16[96,832]{1,0:T(8,128)(2,1)S(1)}, u32[]{:S(2)}, u32[]{:S(2)}) collective-permute-start(bf16[96,832]{1,0:T(8,128)(2,1)S(1)} %pad_maximum_fusion.4), channel_id=1, source_target_pairs={{0,4},{1,5},{2,6},{3,7},{4,0},{5,1},{6,2},{7,3},{8,12},{9,13},{10,... | collective-permute-start | bytes 479240 | tf_op jit(solution)/shard_map/ppermute | solution.py:656
  292.2 14.6 %collective-permute-start.25 = (bf16[96,832]{1,0:T(8,128)(2,1)S(1)}, bf16[96,832]{1,0:T(8,128)(2,1)S(1)}, u32[]{:S(2)}, u32[]{:S(2)}) collective-permute-start(bf16[96,832]{1,0:T(8,128)(2,1)S(1)} %pad_maximum_fusion.5), channel_id=1, source_target_pairs={{0,6},{1,7},{2,4},{3,5},{4,2},{5,3},{6,0},{7,1},{8,14},{9,15},{10,... | collective-permute-start | bytes 479240 | tf_op jit(solution)/shard_map/ppermute | solution.py:656
  294.8 12.0 %collective-permute-start.26 = (bf16[96,832]{1,0:T(8,128)(2,1)S(1)}, bf16[96,832]{1,0:T(8,128)(2,1)S(1)}, u32[]{:S(2)}, u32[]{:S(2)}) collective-permute-start(bf16[96,832]{1,0:T(8,128)(2,1)S(1)} %add_convert_fusion.6), channel_id=1, source_target_pairs={{0,16},{1,17},{2,18},{3,19},{4,20},{5,21},{6,22},{7,23},{8,24},{9,... | collective-permute-start | bytes 479240 | tf_op jit(solution)/shard_map/ppermute | solution.py:656
  307.0 3.9 %collective-permute-start.29 = (f32[8,96]{0,1:T(8,128)S(1)}, f32[8,96]{0,1:T(8,128)S(1)}, u32[]{:S(2)}, u32[]{:S(2)}) collective-permute-start(f32[8,96]{0,1:T(8,128)S(1)} %slice_bitcast_fusion), channel_id=1, source_target_pairs={{0,24},{1,25},{2,26},{3,27},{4,28},{5,29},{6,30},{7,31},{8,16},{9,... | collective-permute-start | bytes 9224 | tf_op jit(solution)/shard_map/ppermute | solution.py:656
  307.0 4.6 %collective-permute-start.28 = (f32[8,96]{0,1:T(8,128)S(1)}, f32[8,96]{0,1:T(8,128)S(1)}, u32[]{:S(2)}, u32[]{:S(2)}) collective-permute-start(f32[8,96]{0,1:T(8,128)S(1)} %slice_bitcast_fusion), channel_id=1, source_target_pairs={{0,16},{1,17},{2,18},{3,19},{4,20},{5,21},{6,22},{7,23},{8,24},{9,... | collective-permute-start | bytes 9224 | tf_op jit(solution)/shard_map/ppermute | solution.py:656
  307.6 4.0 %collective-permute-start.27 = (f32[8,96]{0,1:T(8,128)S(1)}, f32[8,96]{0,1:T(8,128)S(1)}, u32[]{:S(2)}, u32[]{:S(2)}) collective-permute-start(f32[8,96]{0,1:T(8,128)S(1)} %slice_bitcast_fusion), channel_id=1, source_target_pairs={{0,8},{1,9},{2,10},{3,11},{4,12},{5,13},{6,14},{7,15},{8,0},{9,1},... | collective-permute-start | bytes 9224 | tf_op jit(solution)/shard_map/ppermute | solution.py:656
  (3 other events, 2.5 us)

commit v8 on v7

--- a/solution.py
+++ b/solution.py
@@ -409,7 +409,7 @@
 def unmix(order, h, g, dm_one, dm_two, target, ctx, whole, vec):
     count, width = h.shape
     part = width // GROUPS
-    rows = min(256, count)
+    rows = min(512, count)
     half = full((count // 2, width))
     by_rows, by_ctx = chunk((rows, width)), chunk((GROUPS, rows, part), 1)
     return call(

time: 317 us -> 316 us (level)
  transfers between devices with their start and end apart: 36 -> 36, of which waited for: 15 -> 16; matrix products, arithmetic and copies ran while one was open for 8% -> 8% of each run, Pallas kernels for 53% -> 53%
where the time goes in v8:
time: 316 us; the launch traced here: 312 us
  Pallas kernels  177 us (56%)
  starting transfers between devices  56.3 us (18%)
  waiting for transfers between devices  46 us (15%)
  other arithmetic  23.6 us (7%)
  local copies, waits for them, and re-layouts  8.49 us (3%)
    pallas_call x2, Pallas kernels, attend_back(): call(partial(attend_back_kernel, half), 'attend_back', (2,), [pl.BlockSpe...  46.5 us
    pallas_call x2, Pallas kernels, expert(): call(expert_kernel, 'expert', (ff // step,), [full((rows, width)), side,...  35.1 us
    ppermute x30, starting transfers between devices, move(): return lax.ppermute(array, BOTH, way)  33.8 us
    pallas_call x2, Pallas kernels, attend(): call(partial(attend_kernel, half), 'attend', (2,), [SCALARS] + ins, outs,...  28.4 us
    all_to_all x6, waiting for transfers between devices, exchange(): lax.all_to_all(sent, 'expert', split_axis=0, concat_axis=0, tiled=True)  28.3 us
    all_to_all x6, starting transfers between devices, exchange(): lax.all_to_all(sent, 'expert', split_axis=0, concat_axis=0, tiled=True)  22.5 us
    ppermute x30, waiting for transfers between devices, move(): return lax.ppermute(array, BOTH, way)  17.7 us
    pallas_call x1, Pallas kernels, weigh(): call(partial(weigh_kernel, split), 'weigh', (n,), [wide] * 4 + [full((row...  17.1 us
  transfers between devices with their start and end apart: 36, of which 16 were waited for; matrix products, arithmetic and copies ran while one was open for 8% of the time, Pallas kernels for 53%

profile of v8, /device:TPU:0, one launch (start us, length us, event | category | flops | bytes accessed | tf_op | source)
XLA Modules:
  0.0 312.3 jit_solution(6834298513822403735)
XLA Ops:
  2.5 5.1 %collective-permute-start.2 = (bf16[96,640]{1,0:T(8,128)(2,1)S(1)}, bf16[96,640]{1,0:T(8,128)(2,1)S(1)}, u32[]{:S(2)}, u32[]{:S(2)}) collective-permute-start(bf16[96,640]{1,0:T(8,128)(2,1)S(1)} %concatenate.18), channel_id=1, source_target_pairs={{0,6},{1,7},{2,4},{3,5},{4,2},{5,3},{6,0},{7,1},{8,14},{9,15},{10,... | collective-permute-start | bytes 368648 | tf_op jit(solution)/shard_map/ppermute | solution.py:656
  11.7 4.4 %dispatch.2 = bf16[1024,768]{1,0:T(8,128)(2,1)} custom-call(s32[1,1024]{1,0:T(1,128)} %bitcast.96, bf16[1024,768]{1,0:T(8,128)(2,1)} %g_ref.1), custom_call_target="tpu_custom_call" | custom-call | flops 1610612736 | bytes 3000000 | tf_op jit(solution)/shard_map/dispatch/pallas_call | solution.py:295
  16.0 2.0 collective-permute-done.1
  18.1 1.6 collective-permute-start.3
  19.7 2.5 collective-permute-start.6
  22.2 1.9 collective-permute-start.4
  24.6 1.3 collective-permute-done.6
  27.9 2.6 collective-permute-done.3.got_ref
  31.2 3.0 assemble.1.refs_1_.refs_5_.refs_2_
  34.9 1.5 collective-permute-start.9
  36.4 1.5 collective-permute-start.8
  37.9 3.9 %all-to-all-start = ((bf16[8,128,768]{2,1,0:T(8,128)(2,1)}), bf16[8,128,768]{2,1,0:T(8,128)(2,1)S(1)}, u32[]{:S(2)}, u32[]{:S(2)}) async-start(bf16[8,128,768]{2,1,0:T(8,128)(2,1)} %bitcast.17), calls=%async_computation | async-start | bytes 3145728 | tf_op jit(solution)/shard_map/all_to_all | solution.py:780
  41.8 14.8 %attend.2 = (bf16[4,1024,576]{2,1,0:T(8,128)(2,1)}, bf16[4,1024,192]{2,1,0:T(8,128)(2,1)}, f32[4,8,1024]{2,1,0:T(8,128)}, bf16[1024,768]{1,0:T(8,128)(2,1)}, f32[8,768]{1,0:T(8,128)}) custom-call(s32[4]{0:T(128)} %get-tuple-element.263.order, bf16[1024,768]{1,0:T(8,128)(2,1)} %refs_6_.1, bf16[768,640]{1,0:T(8,128)(2,1)} %assemble.1.refs_1_.refs_5_.refs_2_, ...), custom_call_target="tpu_custom_call" | custom-call | flops 12000000000 | bytes 8000000 | tf_op jit(solution)/shard_map/attend/pallas_call | solution.py:167
  56.6 1.8 pad_maximum_fusion.1.refs_0_
  59.7 1.5 collective-permute-start.11
  63.3 13.6 %attend.3 = (bf16[4,1024,576]{2,1,0:T(8,128)(2,1)}, bf16[4,1024,192]{2,1,0:T(8,128)(2,1)}, f32[4,8,1024]{2,1,0:T(8,128)}) custom-call(s32[4]{0:T(128)} %get-tuple-element.263.order, bf16[1024,768]{1,0:T(8,128)(2,1)} %get-tuple-element.128.refs_0_.refs_4_, ...), custom_call_target="tpu_custom_call", output_to_operand_aliasing={{0}: (5, {}), {1}: (6, {}), {2}: (7, {})} | custom-call | flops 12000000000 | bytes 8000000 | tf_op jit(solution)/shard_map/attend/pallas_call | solution.py:167
  76.9 2.2 all-to-all-done
  79.7 1.4 collective-permute-done.13.refs_3_
  81.8 9.3 %mix.1 = (f32[1024,768]{1,0:T(8,128)}, bf16[768,768]{1,0:T(8,128)(2,1)}, bf16[1024,768]{1,0:T(8,128)(2,1)}, bf16[512,768]{1,0:T(8,128)(2,1)}) custom-call(s32[4]{0:T(128)} %get-tuple-element.263.order, s32[8]{0:T(128)} %fusion.15.slab, bf16[1024,768]{1,0:T(8,128)(2,1)} %refs_6_.1, bf16[4,1024,192]{2,1,0:T(8,128)(2,1)} %get-tuple-element.147.ctx_ref.refs_1_, ...), custom_call_target="tpu_custom_call" | custom-call | flops 2818572288 | bytes 12000000 | tf_op jit(solution)/shard_map/mix/pallas_call | solution.py:347
  91.1 3.7 %all-to-all-start.1 = ((bf16[8,64,768]{2,1,0:T(8,128)(2,1)}), bf16[8,64,768]{2,1,0:T(8,128)(2,1)S(1)}, u32[]{:S(2)}, u32[]{:S(2)}) async-start(bf16[8,64,768]{2,1,0:T(8,128)(2,1)} %bitcast.86), calls=%async_computation.1 | async-start | bytes 1572864 | tf_op jit(solution)/shard_map/all_to_all | solution.py:780
  94.8 3.3 %dispatch.3 = bf16[512,768]{1,0:T(8,128)(2,1)} custom-call(s32[1,1024]{1,0:T(1,128)} %bitcast.99, bf16[1024,768]{1,0:T(8,128)(2,1)} %get-tuple-element.151.rows_ref), custom_call_target="tpu_custom_call" | custom-call | flops 1610612736 | bytes 3000000 | tf_op jit(solution)/shard_map/dispatch/pallas_call | solution.py:295
  98.1 17.3 %all-to-all-done.1 = bf16[8,64,768]{2,1,0:T(8,128)(2,1)S(1)} async-done(((bf16[8,64,768]{2,1,0:T(8,128)(2,1)}), bf16[8,64,768]{2,1,0:T(8,128)(2,1)S(1)}, u32[]{:S(2)}, u32[]{:S(2)}) %all-to-all-start.1) | async-done | bytes 786464 | tf_op jit(solution)/shard_map/all_to_all | solution.py:780
  115.3 3.6 %all-to-all-start.2 = ((bf16[8,64,768]{2,1,0:T(8,128)(2,1)}), bf16[8,64,768]{2,1,0:T(8,128)(2,1)S(1)}, u32[]{:S(2)}, u32[]{:S(2)}) async-start(bf16[8,64,768]{2,1,0:T(8,128)(2,1)} %bitcast.85), calls=%async_computation.2 | async-start | bytes 1572864 | tf_op jit(solution)/shard_map/all_to_all | solution.py:780
  119.0 17.6 %expert.2 = (bf16[8,2,64,768]{3,2,1,0:T(8,128)(2,1)}, bf16[512,768]{1,0:T(8,128)(2,1)}, bf16[512,768]{1,0:T(8,128)(2,1)}, bf16[512,3072]{1,0:T(8,128)(2,1)}, bf1...) custom-call(bf16[512,768]{1,0:T(8,128)(2,1)} %bitcast.77, bf16[8,2,64,768]{3,2,1,0:T(8,128)(2,1)} %bitcast.74, ...), custom_call_target="tpu_custom_call" | custom-call | flops 9663676416 | bytes 22000000 | tf_op jit(solution)/shard_map/expert/pallas_call | solution.py:508
  136.5 2.8 all-to-all-done.2
  139.3 4.0 %all-to-all-start.3 = ((bf16[8,64,768]{2,1,0:T(8,128)(2,1)}), bf16[8,64,768]{2,1,0:T(8,128)(2,1)S(1)}, u32[]{:S(2)}, u32[]{:S(2)}) async-start(bf16[8,64,768]{2,1,0:T(8,128)(2,1)} %bitcast.84), calls=%async_computation.3 | async-start | bytes 1572864 | tf_op jit(solution)/shard_map/all_to_all | solution.py:780
  143.3 17.5 %expert.3 = (bf16[8,2,64,768]{3,2,1,0:T(8,128)(2,1)}, bf16[512,768]{1,0:T(8,128)(2,1)}, bf16[512,768]{1,0:T(8,128)(2,1)}, bf16[512,3072]{1,0:T(8,128)(2,1)}, bf1...) custom-call(bf16[512,768]{1,0:T(8,128)(2,1)} %bitcast.80, ...), custom_call_target="tpu_custom_call", output_to_operand_aliasing={{0}: (7, {})} | custom-call | flops 9663676416 | bytes 22000000 | tf_op jit(solution)/shard_map/expert/pallas_call | solution.py:508
  160.8 2.8 all-to-all-done.3
  163.6 3.6 %all-to-all-start.4 = ((bf16[8,64,768]{2,1,0:T(8,128)(2,1)}), bf16[8,64,768]{2,1,0:T(8,128)(2,1)S(1)}, u32[]{:S(2)}, u32[]{:S(2)}) async-start(bf16[8,64,768]{2,1,0:T(8,128)(2,1)} %bitcast.83), calls=%async_computation.4 | async-start | bytes 1572864 | tf_op jit(solution)/shard_map/all_to_all | solution.py:780
  167.2 17.1 %weigh.1 = (bf16[2,1552,768]{2,1,0:T(8,128)(2,1)}, bf16[2,1552,768]{2,1,0:T(8,128)(2,1)}) custom-call(s32[4]{0:T(128)} %get-tuple-element.262.which, bf16[512,3072]{1,0:T(8,128)(2,1)} %get-tuple-element.162.refs_0_, bf16[512,3072]{1,0:T(8,128)(2,1)} %get-tuple-element.163.refs_1_, bf16[512,3072]{1,0:T(8,128)(2,1)} %get-tuple-element.164.refs_2_, ...), custom_call_target="tpu_custom_call" | custom-call | flops 9663676416 | bytes 26000000 | tf_op jit(solution)/shard_map/weigh/pallas_call | solution.py:588
  184.4 3.2 %all-to-all-done.4 = bf16[8,64,768]{2,1,0:T(8,128)(2,1)S(1)} async-done(((bf16[8,64,768]{2,1,0:T(8,128)(2,1)}), bf16[8,64,768]{2,1,0:T(8,128)(2,1)S(1)}, u32[]{:S(2)}, u32[]{:S(2)}) %all-to-all-start.4) | async-done | bytes 786464 | tf_op jit(solution)/shard_map/all_to_all | solution.py:780
  187.6 3.8 %all-to-all-start.5 = ((bf16[8,128,768]{2,1,0:T(8,128)(2,1)}), bf16[8,128,768]{2,1,0:T(8,128)(2,1)S(1)}, u32[]{:S(2)}, u32[]{:S(2)}) async-start(bf16[8,128,768]{2,1,0:T(8,128)(2,1)} %bitcast.31), calls=%async_computation.5 | async-start | bytes 3145728 | tf_op jit(solution)/shard_map/all_to_all | solution.py:780
  191.4 13.2 %unmix.1 = (bf16[1024,768]{1,0:T(8,128)(2,1)}, bf16[4,1024,192]{2,1,0:T(8,128)(2,1)}, bf16[4,768,192]{2,1,0:T(8,128)(2,1)}, f32[8,768]{1,0:T(8,128)}) custom-call(s32[4]{0:T(128)} %get-tuple-element.263.order, f32[1024,768]{1,0:T(8,128)} %get-tuple-element.149.h_ref, bf16[1024,768]{1,0:T(8,128)(2,1)} %g_ref.1, bf16[512,768]{1,0:T(8,128)(2,1)} %bitcast.76, ...), custom_call_target="tpu_custom_call" | custom-call | flops 4026531840 | bytes 20000000 | tf_op jit(solution)/shard_map/unmix/pallas_call | solution.py:415
  204.5 4.4 %fusion = bf16[1552,768]{1,0:T(8,128)(2,1)} fusion(bf16[2,1552,768]{2,1,0:T(8,128)(2,1)} %collective-permute-done.14, bf16[2,1552,768]{2,1,0:T(8,128)(2,1)} %get-tuple-element.178), kind=kLoop, calls=%fused_computation.1 | loop fusion | flops 4767744 | bytes 7151616 | tf_op jit(solution)/shard_map/convert_element_type | solution.py:624
  208.9 23.6 %attend_back.2 = (bf16[2,1024,576]{2,1,0:T(8,128)(2,1)}, bf16[4,96,1024]{2,1,0:T(8,128)(2,1)}, bf16[4,96,1024]{2,1,0:T(8,128)(2,1)}, bf16[8,96,1024]{2,1,0:T(8,128)(2,1)}) custom-call(s32[4]{0:T(128)} %get-tuple-element.263.order, s32[8]{0:T(128)} %fusion.19.table, bf16[4,1024,576]{2,1,0:T(8,128)(2,1)} %get-tuple-element.181.refs_0_, ...), custom_call_target="tpu_custom_call" | custom-call | flops 24000000000 | bytes 14000000 | tf_op jit(solution)/shard_map/attend_back/pallas_call | solution.py:262
  233.1 1.5 collective-permute-start.22
  235.7 6.1 %finish.1 = bf16[1024,768]{1,0:T(8,128)(2,1)} custom-call(f32[1024,768]{1,0:T(8,128)} %get-tuple-element.149.h_ref, s32[1,1024]{1,0:T(1,128)} %bitcast.97, bf16[1024,768]{1,0:T(8,128)(2,1)} %bitcast.71), custom_call_target="tpu_custom_call" | custom-call | flops 1610612736 | bytes 6000000 | tf_op jit(solution)/shard_map/finish/pallas_call | solution.py:439
  241.8 2.0 add_convert_fusion.1
  243.8 1.7 collective-permute-start.16
  245.6 22.9 %attend_back.3 = (bf16[2,1024,576]{2,1,0:T(8,128)(2,1)}, bf16[4,96,640]{2,1,0:T(8,128)(2,1)}, bf16[4,96,640]{2,1,0:T(8,128)(2,1)}, bf16[8,96,640]{2,1,0:T(8,128)(2,1)}) custom-call(s32[4]{0:T(128)} %get-tuple-element.263.order, s32[8]{0:T(128)} %fusion.19.table, bf16[4,1024,576]{2,1,0:T(8,128)(2,1)} %get-tuple-element.181.refs_0_, ...), custom_call_target="tpu_custom_call" | custom-call | flops 24000000000 | bytes 14000000 | tf_op jit(solution)/shard_map/attend_back/pallas_call | solution.py:262
  269.7 1.5 collective-permute-start.17
  271.2 2.4 collective-permute-start.18
  274.8 10.5 %unproject.1 = f32[1024,768]{1,0:T(8,128)} custom-call(bf16[2,1024,576]{2,1,0:T(8,128)(2,1)} %get-tuple-element.206.refs_0_, bf16[2,1024,576]{2,1,0:T(8,128)(2,1)} %get-tuple-element.207.refs_1_, bf16[768,640]{1,0:T(8,128)(2,1)} %assemble.1.refs_1_.refs_5_.refs_2_, bf16[768,640]{1,0:T(8,128)(2,1)} %copy-done.3, bf16[768,640]{1,0:T(8,128)(2,1)} %copy-done.4, ...), custom_call_target="tpu_custom_call" | custom-call | flops 3623878656 | bytes 20000000 | tf_op jit(solution)/shard_map/unproject/pallas_call | solution.py:614
  285.3 1.9 collective-permute-done.22
  287.4 3.4 %collective-permute-start.23 = (bf16[96,832]{1,0:T(8,128)(2,1)S(1)}, bf16[96,832]{1,0:T(8,128)(2,1)S(1)}, u32[]{:S(2)}, u32[]{:S(2)}) collective-permute-start(bf16[96,832]{1,0:T(8,128)(2,1)S(1)} %pad_maximum_fusion.3), channel_id=1, source_target_pairs={{0,2},{1,3},{2,0},{3,1},{4,6},{5,7},{6,4},{7,5},{8,10},{9,11},{10,... | collective-permute-start | bytes 479240 | tf_op jit(solution)/shard_map/ppermute | solution.py:656
  291.8 1.5 collective-permute-start.25
  295.0 6.0 %bitcast_add_fusion = (f32[768,768]{1,0:T(8,128)}, f32[768,768]{1,0:T(8,128)}) fusion(bf16[2,1552,768]{2,1,0:T(8,128)(2,1)} %collective-permute-done.14, bf16[1552,768]{1,0:T(8,128)(2,1)} %collective-permute-done.22, bf16[2,1552,768]{2,1,0:T(8,128)(2,1)} %get-tuple-element.178), kind=kLoop, calls=%fused_computation.2 | loop fusion | flops 5898240 | bytes 11796480 | tf_op jit(solution)/shard_map/add | solution.py:888
  301.7 4.6 %collective-permute-done.24 = bf16[96,832]{1,0:T(8,128)(2,1)S(1)} collective-permute-done((bf16[96,832]{1,0:T(8,128)(2,1)S(1)}, bf16[96,832]{1,0:T(8,128)(2,1)S(1)}, u32[]{:S(2)}, u32[]{:S(2)}) %collective-permute-start.24) | collective-permute-done | bytes 159776 | tf_op jit(solution)/shard_map/ppermute | solution.py:656
  (101 shorter events, 28.0 us)
Async XLA Ops:
  2.5 13.5 %collective-permute-start.2 = (bf16[96,640]{1,0:T(8,128)(2,1)S(1)}, bf16[96,640]{1,0:T(8,128)(2,1)S(1)}, u32[]{:S(2)}, u32[]{:S(2)}) collective-permute-start(bf16[96,640]{1,0:T(8,128)(2,1)S(1)} %concatenate.18), channel_id=1, source_target_pairs={{0,6},{1,7},{2,4},{3,5},{4,2},{5,3},{6,0},{7,1},{8,14},{9,15},{10,... | collective-permute-start | bytes 368648 | tf_op jit(solution)/shard_map/ppermute | solution.py:656
  7.7 10.4 %collective-permute-start.1 = (bf16[96,640]{1,0:T(8,128)(2,1)S(1)}, bf16[96,640]{1,0:T(8,128)(2,1)S(1)}, u32[]{:S(2)}, u32[]{:S(2)}) collective-permute-start(bf16[96,640]{1,0:T(8,128)(2,1)S(1)} %concatenate.18), channel_id=1, source_target_pairs={{0,4},{1,5},{2,6},{3,7},{4,0},{5,1},{6,2},{7,3},{8,12},{9,13},{10,... | collective-permute-start | bytes 368648 | tf_op jit(solution)/shard_map/ppermute | solution.py:656
  7.7 10.4 %collective-permute-start = (bf16[96,640]{1,0:T(8,128)(2,1)S(1)}, bf16[96,640]{1,0:T(8,128)(2,1)S(1)}, u32[]{:S(2)}, u32[]{:S(2)}) collective-permute-start(bf16[96,640]{1,0:T(8,128)(2,1)S(1)} %concatenate.18), channel_id=1, source_target_pairs={{0,2},{1,3},{2,0},{3,1},{4,6},{5,7},{6,4},{7,5},{8,10},{9,11},{10,... | collective-permute-start | bytes 368648 | tf_op jit(solution)/shard_map/ppermute | solution.py:656
  11.7 8.0 %copy-start.13 = (bf16[96,192]{1,0:T(8,128)(2,1)S(1)}, bf16[96,192]{1,0:T(8,128)(2,1)}, u32[]{:S(2)}) copy-start(bf16[96,192]{1,0:T(8,128)(2,1)} %param.32) | copy-start | bytes 110596
  18.1 12.4 %copy-start.1 = (bf16[4,96,640]{2,1,0:T(8,128)(2,1)}, bf16[4,96,640]{2,1,0:T(8,128)(2,1)S(1)}, u32[]{:S(2)}) copy-start(bf16[4,96,640]{2,1,0:T(8,128)(2,1)S(1)} %pad_maximum_fusion.own_ref) | copy-start | bytes 1474564
  18.1 12.3 %collective-permute-start.3 = (bf16[4,96,640]{2,1,0:T(8,128)(2,1)S(1)}, bf16[4,96,640]{2,1,0:T(8,128)(2,1)S(1)}, u32[]{:S(2)}, u32[]{:S(2)}) collective-permute-start(bf16[4,96,640]{2,1,0:T(8,128)(2,1)S(1)} %pad_maximum_fusion.own_ref), channel_id=1, source_target_pairs={{0,1},{1,0},{2,3},{3,2},{4,5},{5,4},{6,7},{7,6},{8,9},{9,8},{10,11... | collective-permute-start | bytes 1474568 | tf_op jit(solution)/shard_map/ppermute | solution.py:656
  19.7 6.2 %collective-permute-start.6 = (bf16[96,192]{1,0:T(8,128)(2,1)S(1)}, bf16[96,192]{1,0:T(8,128)(2,1)S(1)}, u32[]{:S(2)}, u32[]{:S(2)}) collective-permute-start(bf16[96,192]{1,0:T(8,128)(2,1)S(1)} %copy-done.13), channel_id=1, source_target_pairs={{0,6},{1,7},{2,4},{3,5},{4,2},{5,3},{6,0},{7,1},{8,14},{9,15},{10,... | collective-permute-start | bytes 110600 | tf_op jit(solution)/shard_map/ppermute | solution.py:656
  22.2 5.0 %collective-permute-start.5 = (bf16[96,192]{1,0:T(8,128)(2,1)S(1)}, bf16[96,192]{1,0:T(8,128)(2,1)S(1)}, u32[]{:S(2)}, u32[]{:S(2)}) collective-permute-start(bf16[96,192]{1,0:T(8,128)(2,1)S(1)} %copy-done.13), channel_id=1, source_target_pairs={{0,4},{1,5},{2,6},{3,7},{4,0},{5,1},{6,2},{7,3},{8,12},{9,13},{10,... | collective-permute-start | bytes 110600 | tf_op jit(solution)/shard_map/ppermute | solution.py:656
  22.2 5.0 %collective-permute-start.4 = (bf16[96,192]{1,0:T(8,128)(2,1)S(1)}, bf16[96,192]{1,0:T(8,128)(2,1)S(1)}, u32[]{:S(2)}, u32[]{:S(2)}) collective-permute-start(bf16[96,192]{1,0:T(8,128)(2,1)S(1)} %copy-done.13), channel_id=1, source_target_pairs={{0,2},{1,3},{2,0},{3,1},{4,6},{5,7},{6,4},{7,5},{8,10},{9,11},{10,... | collective-permute-start | bytes 110600 | tf_op jit(solution)/shard_map/ppermute | solution.py:656
  34.3 3.6 %collective-permute-start.7 = (bf16[768,640]{1,0:T(8,128)(2,1)}, bf16[768,640]{1,0:T(8,128)(2,1)S(1)}, u32[]{:S(2)}, u32[]{:S(2)}) collective-permute-start(bf16[768,640]{1,0:T(8,128)(2,1)} %assemble.1.refs_1_.refs_5_.refs_2_), channel_id=1, source_target_pairs={{0,8},{1,9},{2,10},{3,11},{4,12},{5,13},{6,14},{7,15},{8,0},{9,1},... | collective-permute-start | bytes 2949128 | tf_op jit(solution)/shard_map/ppermute | solution.py:656
  34.9 24.4 %collective-permute-start.9 = (bf16[768,640]{1,0:T(8,128)(2,1)}, bf16[768,640]{1,0:T(8,128)(2,1)S(1)}, u32[]{:S(2)}, u32[]{:S(2)}) collective-permute-start(bf16[768,640]{1,0:T(8,128)(2,1)} %assemble.1.refs_1_.refs_5_.refs_2_), channel_id=1, source_target_pairs={{0,16},{1,17},{2,18},{3,19},{4,20},{5,21},{6,22},{7,23},{8,24},{9,... | collective-permute-start | bytes 2949128 | tf_op jit(solution)/shard_map/ppermute | solution.py:656
  36.4 20.3 %collective-permute-start.8 = (bf16[4,96,192]{2,1,0:T(8,128)(2,1)}, bf16[4,96,192]{2,1,0:T(8,128)(2,1)}, u32[]{:S(2)}, u32[]{:S(2)}) collective-permute-start(bf16[4,96,192]{2,1,0:T(8,128)(2,1)} %pad_maximum_fusion.2), channel_id=1, source_target_pairs={{0,1},{1,0},{2,3},{3,2},{4,5},{5,4},{6,7},{7,6},{8,9},{9,8},{10,11... | collective-permute-start | bytes 442376 | tf_op jit(solution)/shard_map/ppermute | solution.py:656
  37.9 4.0 %copy-start.3 = (bf16[768,640]{1,0:T(8,128)(2,1)}, bf16[768,640]{1,0:T(8,128)(2,1)S(1)}, u32[]{:S(2)}) copy-start(bf16[768,640]{1,0:T(8,128)(2,1)S(1)} %collective-permute-done.7.refs_2_.refs_6_.refs_3_) | copy-start | bytes 2949124
  37.9 41.2 %all-to-all-start = ((bf16[8,128,768]{2,1,0:T(8,128)(2,1)}), bf16[8,128,768]{2,1,0:T(8,128)(2,1)S(1)}, u32[]{:S(2)}, u32[]{:S(2)}) async-start(bf16[8,128,768]{2,1,0:T(8,128)(2,1)} %bitcast.17), calls=%async_computation | async-start | bytes 3145728 | tf_op jit(solution)/shard_map/all_to_all | solution.py:780
  59.2 3.1 %copy-start.4 = (bf16[768,640]{1,0:T(8,128)(2,1)}, bf16[768,640]{1,0:T(8,128)(2,1)S(1)}, u32[]{:S(2)}) copy-start(bf16[768,640]{1,0:T(8,128)(2,1)S(1)} %collective-permute-done.9.refs_2_.refs_5_.refs_4_) | copy-start | bytes 2949124
  59.2 3.1 %collective-permute-start.10 = (bf16[768,640]{1,0:T(8,128)(2,1)S(1)}, bf16[768,640]{1,0:T(8,128)(2,1)S(1)}, u32[]{:S(2)}, u32[]{:S(2)}) collective-permute-start(bf16[768,640]{1,0:T(8,128)(2,1)S(1)} %collective-permute-done.9.refs_2_.refs_5_.refs_4_), channel_id=1, source_target_pairs={{0,8},{1,9},{2,10},{3,11},{4,12},{5,13},{6,14},{7,15},{8,0},{9,1},... | collective-permute-start | bytes 2949128 | tf_op jit(solution)/shard_map/ppermute | solution.py:656
  59.2 20.4 %collective-permute-start.12 = (bf16[8,96,192]{2,1,0:T(8,128)(2,1)}, bf16[8,96,192]{2,1,0:T(8,128)(2,1)}, u32[]{:S(2)}, u32[]{:S(2)}) collective-permute-start(bf16[8,96,192]{2,1,0:T(8,128)(2,1)} %pad_maximum_fusion.1.refs_0_), channel_id=1, source_target_pairs={{0,8},{1,9},{2,10},{3,11},{4,12},{5,13},{6,14},{7,15},{8,0},{9,1},... | collective-permute-start | bytes 884744 | tf_op jit(solution)/shard_map/ppermute | solution.py:656
  59.7 19.4 %collective-permute-start.11 = (bf16[8,96,192]{2,1,0:T(8,128)(2,1)}, bf16[8,96,192]{2,1,0:T(8,128)(2,1)}, u32[]{:S(2)}, u32[]{:S(2)}) collective-permute-start(bf16[8,96,192]{2,1,0:T(8,128)(2,1)} %pad_maximum_fusion.1.refs_0_), channel_id=1, source_target_pairs={{0,16},{1,17},{2,18},{3,19},{4,20},{5,21},{6,22},{7,23},{8,24},{9,... | collective-permute-start | bytes 884744 | tf_op jit(solution)/shard_map/ppermute | solution.py:656
  79.1 12.0 %copy-start.2 = (bf16[8,128,768]{2,1,0:T(8,128)(2,1)}, bf16[8,128,768]{2,1,0:T(8,128)(2,1)S(1)}, u32[]{:S(2)}) copy-start(bf16[8,128,768]{2,1,0:T(8,128)(2,1)S(1)} %all-to-all-done) | copy-start | bytes 4718596
  79.1 1.9 collective-permute-start.13
  91.1 24.2 %all-to-all-start.1 = ((bf16[8,64,768]{2,1,0:T(8,128)(2,1)}), bf16[8,64,768]{2,1,0:T(8,128)(2,1)S(1)}, u32[]{:S(2)}, u32[]{:S(2)}) async-start(bf16[8,64,768]{2,1,0:T(8,128)(2,1)} %bitcast.86), calls=%async_computation.1 | async-start | bytes 1572864 | tf_op jit(solution)/shard_map/all_to_all | solution.py:780
  115.3 3.6 %copy-start.7 = (bf16[8,64,768]{2,1,0:T(8,128)(2,1)}, bf16[8,64,768]{2,1,0:T(8,128)(2,1)S(1)}, u32[]{:S(2)}) copy-start(bf16[8,64,768]{2,1,0:T(8,128)(2,1)S(1)} %all-to-all-done.1) | copy-start | bytes 2359300
  115.3 24.0 %all-to-all-start.2 = ((bf16[8,64,768]{2,1,0:T(8,128)(2,1)}), bf16[8,64,768]{2,1,0:T(8,128)(2,1)S(1)}, u32[]{:S(2)}, u32[]{:S(2)}) async-start(bf16[8,64,768]{2,1,0:T(8,128)(2,1)} %bitcast.85), calls=%async_computation.2 | async-start | bytes 1572864 | tf_op jit(solution)/shard_map/all_to_all | solution.py:780
  139.3 4.0 %copy-start.8 = (bf16[8,64,768]{2,1,0:T(8,128)(2,1)}, bf16[8,64,768]{2,1,0:T(8,128)(2,1)S(1)}, u32[]{:S(2)}) copy-start(bf16[8,64,768]{2,1,0:T(8,128)(2,1)S(1)} %all-to-all-done.2) | copy-start | bytes 2359300
  139.3 24.3 %all-to-all-start.3 = ((bf16[8,64,768]{2,1,0:T(8,128)(2,1)}), bf16[8,64,768]{2,1,0:T(8,128)(2,1)S(1)}, u32[]{:S(2)}, u32[]{:S(2)}) async-start(bf16[8,64,768]{2,1,0:T(8,128)(2,1)} %bitcast.84), calls=%async_computation.3 | async-start | bytes 1572864 | tf_op jit(solution)/shard_map/all_to_all | solution.py:780
  163.6 20.7 %copy-start.6 = (bf16[8,64,768]{2,1,0:T(8,128)(2,1)}, bf16[8,64,768]{2,1,0:T(8,128)(2,1)S(1)}, u32[]{:S(2)}) copy-start(bf16[8,64,768]{2,1,0:T(8,128)(2,1)S(1)} %all-to-all-done.3) | copy-start | bytes 2359300
  163.6 23.9 %all-to-all-start.4 = ((bf16[8,64,768]{2,1,0:T(8,128)(2,1)}), bf16[8,64,768]{2,1,0:T(8,128)(2,1)S(1)}, u32[]{:S(2)}, u32[]{:S(2)}) async-start(bf16[8,64,768]{2,1,0:T(8,128)(2,1)} %bitcast.83), calls=%async_computation.4 | async-start | bytes 1572864 | tf_op jit(solution)/shard_map/all_to_all | solution.py:780
  187.6 3.8 %copy-start.9 = (bf16[8,64,768]{2,1,0:T(8,128)(2,1)}, bf16[8,64,768]{2,1,0:T(8,128)(2,1)S(1)}, u32[]{:S(2)}) copy-start(bf16[8,64,768]{2,1,0:T(8,128)(2,1)S(1)} %all-to-all-done.4) | copy-start | bytes 2359300
  187.6 16.9 %collective-permute-start.14 = (bf16[2,1552,768]{2,1,0:T(8,128)(2,1)}, bf16[2,1552,768]{2,1,0:T(8,128)(2,1)}, u32[]{:S(2)}, u32[]{:S(2)}) collective-permute-start(bf16[2,1552,768]{2,1,0:T(8,128)(2,1)} %get-tuple-element.179), channel_id=1, source_target_pairs={{0,8},{1,9},{2,10},{3,11},{4,12},{5,13},{6,14},{7,15},{8,0},{9,1},... | collective-permute-start | bytes 14303240 | tf_op jit(solution)/shard_map/ppermute | solution.py:656
  187.6 47.0 %all-to-all-start.5 = ((bf16[8,128,768]{2,1,0:T(8,128)(2,1)}), bf16[8,128,768]{2,1,0:T(8,128)(2,1)S(1)}, u32[]{:S(2)}, u32[]{:S(2)}) async-start(bf16[8,128,768]{2,1,0:T(8,128)(2,1)} %bitcast.31), calls=%async_computation.5 | async-start | bytes 3145728 | tf_op jit(solution)/shard_map/all_to_all | solution.py:780
  232.5 9.3 %collective-permute-start.15 = (bf16[8,96,1024]{2,1,0:T(8,128)(2,1)}, bf16[8,96,1024]{2,1,0:T(8,128)(2,1)S(1)}, u32[]{:S(2)}, u32[]{:S(2)}) collective-permute-start(bf16[8,96,1024]{2,1,0:T(8,128)(2,1)} %get-tuple-element.189), channel_id=1, source_target_pairs={{0,8},{1,9},{2,10},{3,11},{4,12},{5,13},{6,14},{7,15},{8,0},{9,1},... | collective-permute-start | bytes 4718600 | tf_op jit(solution)/shard_map/ppermute | solution.py:656
  233.1 54.1 %collective-permute-start.22 = (bf16[1552,768]{1,0:T(8,128)(2,1)}, bf16[1552,768]{1,0:T(8,128)(2,1)}, u32[]{:S(2)}, u32[]{:S(2)}) collective-permute-start(bf16[1552,768]{1,0:T(8,128)(2,1)} %fusion), channel_id=1, source_target_pairs={{0,16},{1,17},{2,18},{3,19},{4,20},{5,21},{6,22},{7,23},{8,24},{9,... | collective-permute-start | bytes 7151624 | tf_op jit(solution)/shard_map/ppermute | solution.py:656
  234.6 1.1 copy-start
  243.8 24.7 %collective-permute-start.16 = (bf16[4,96,1024]{2,1,0:T(8,128)(2,1)S(1)}, bf16[4,96,1024]{2,1,0:T(8,128)(2,1)S(1)}, u32[]{:S(2)}, u32[]{:S(2)}) collective-permute-start(bf16[4,96,1024]{2,1,0:T(8,128)(2,1)S(1)} %get-tuple-element.197), channel_id=1, source_target_pairs={{0,1},{1,0},{2,3},{3,2},{4,5},{5,4},{6,7},{7,6},{8,9},{9,8},{10,11... | collective-permute-start | bytes 2359304 | tf_op jit(solution)/shard_map/ppermute | solution.py:656
  268.5 5.6 %copy-start.11 = (bf16[4,96,640]{2,1,0:T(8,128)(2,1)S(1)}, bf16[4,96,640]{2,1,0:T(8,128)(2,1)}, u32[]{:S(2)}) copy-start(bf16[4,96,640]{2,1,0:T(8,128)(2,1)} %get-tuple-element.204) | copy-start | bytes 1474564
  268.5 5.6 %copy-start.12 = (bf16[4,96,640]{2,1,0:T(8,128)(2,1)S(1)}, bf16[4,96,640]{2,1,0:T(8,128)(2,1)}, u32[]{:S(2)}) copy-start(bf16[4,96,640]{2,1,0:T(8,128)(2,1)} %get-tuple-element.202) | copy-start | bytes 1474564
  269.7 4.4 %collective-permute-start.20 = (bf16[8,96,640]{2,1,0:T(8,128)(2,1)}, bf16[8,96,640]{2,1,0:T(8,128)(2,1)S(1)}, u32[]{:S(2)}, u32[]{:S(2)}) collective-permute-start(bf16[8,96,640]{2,1,0:T(8,128)(2,1)} %get-tuple-element.203), channel_id=1, source_target_pairs={{0,8},{1,9},{2,10},{3,11},{4,12},{5,13},{6,14},{7,15},{8,0},{9,1},... | collective-permute-start | bytes 2949128 | tf_op jit(solution)/shard_map/ppermute | solution.py:656
  269.7 17.5 %collective-permute-start.17 = (bf16[96,832]{1,0:T(8,128)(2,1)}, bf16[96,832]{1,0:T(8,128)(2,1)S(1)}, u32[]{:S(2)}, u32[]{:S(2)}) collective-permute-start(bf16[96,832]{1,0:T(8,128)(2,1)} %get-tuple-element.198), channel_id=1, source_target_pairs={{0,2},{1,3},{2,0},{3,1},{4,6},{5,7},{6,4},{7,5},{8,10},{9,11},{10,... | collective-permute-start | bytes 479240 | tf_op jit(solution)/shard_map/ppermute | solution.py:656
  271.2 16.0 %collective-permute-start.18 = (bf16[96,832]{1,0:T(8,128)(2,1)}, bf16[96,832]{1,0:T(8,128)(2,1)S(1)}, u32[]{:S(2)}, u32[]{:S(2)}) collective-permute-start(bf16[96,832]{1,0:T(8,128)(2,1)} %get-tuple-element.199), channel_id=1, source_target_pairs={{0,4},{1,5},{2,6},{3,7},{4,0},{5,1},{6,2},{7,3},{8,12},{9,13},{10,... | collective-permute-start | bytes 479240 | tf_op jit(solution)/shard_map/ppermute | solution.py:656
  273.6 13.7 %collective-permute-start.19 = (bf16[96,832]{1,0:T(8,128)(2,1)}, bf16[96,832]{1,0:T(8,128)(2,1)}, u32[]{:S(2)}, u32[]{:S(2)}) collective-permute-start(bf16[96,832]{1,0:T(8,128)(2,1)} %get-tuple-element.200), channel_id=1, source_target_pairs={{0,6},{1,7},{2,4},{3,5},{4,2},{5,3},{6,0},{7,1},{8,14},{9,15},{10,... | collective-permute-start | bytes 479240 | tf_op jit(solution)/shard_map/ppermute | solution.py:656
  274.4 12.9 %collective-permute-start.21 = (bf16[4,96,640]{2,1,0:T(8,128)(2,1)S(1)}, bf16[4,96,640]{2,1,0:T(8,128)(2,1)S(1)}, u32[]{:S(2)}, u32[]{:S(2)}) collective-permute-start(bf16[4,96,640]{2,1,0:T(8,128)(2,1)S(1)} %get-tuple-element.205), channel_id=1, source_target_pairs={{0,1},{1,0},{2,3},{3,2},{4,5},{5,4},{6,7},{7,6},{8,9},{9,8},{10,11... | collective-permute-start | bytes 1474568 | tf_op jit(solution)/shard_map/ppermute | solution.py:656
  287.4 14.4 %collective-permute-start.23 = (bf16[96,832]{1,0:T(8,128)(2,1)S(1)}, bf16[96,832]{1,0:T(8,128)(2,1)S(1)}, u32[]{:S(2)}, u32[]{:S(2)}) collective-permute-start(bf16[96,832]{1,0:T(8,128)(2,1)S(1)} %pad_maximum_fusion.3), channel_id=1, source_target_pairs={{0,2},{1,3},{2,0},{3,1},{4,6},{5,7},{6,4},{7,5},{8,10},{9,11},{10,... | collective-permute-start | bytes 479240 | tf_op jit(solution)/shard_map/ppermute | solution.py:656
  290.8 15.6 %collective-permute-start.24 = (bf16[96,832]{1,0:T(8,128)(2,1)S(1)}, bf16[96,832]{1,0:T(8,128)(2,1)S(1)}, u32[]{:S(2)}, u32[]{:S(2)}) collective-permute-start(bf16[96,832]{1,0:T(8,128)(2,1)S(1)} %pad_maximum_fusion.4), channel_id=1, source_target_pairs={{0,4},{1,5},{2,6},{3,7},{4,0},{5,1},{6,2},{7,3},{8,12},{9,13},{10,... | collective-permute-start | bytes 479240 | tf_op jit(solution)/shard_map/ppermute | solution.py:656
  291.8 14.6 %collective-permute-start.25 = (bf16[96,832]{1,0:T(8,128)(2,1)S(1)}, bf16[96,832]{1,0:T(8,128)(2,1)S(1)}, u32[]{:S(2)}, u32[]{:S(2)}) collective-permute-start(bf16[96,832]{1,0:T(8,128)(2,1)S(1)} %pad_maximum_fusion.5), channel_id=1, source_target_pairs={{0,6},{1,7},{2,4},{3,5},{4,2},{5,3},{6,0},{7,1},{8,14},{9,15},{10,... | collective-permute-start | bytes 479240 | tf_op jit(solution)/shard_map/ppermute | solution.py:656
  294.4 12.0 %collective-permute-start.26 = (bf16[96,832]{1,0:T(8,128)(2,1)S(1)}, bf16[96,832]{1,0:T(8,128)(2,1)S(1)}, u32[]{:S(2)}, u32[]{:S(2)}) collective-permute-start(bf16[96,832]{1,0:T(8,128)(2,1)S(1)} %add_convert_fusion.6), channel_id=1, source_target_pairs={{0,16},{1,17},{2,18},{3,19},{4,20},{5,21},{6,22},{7,23},{8,24},{9,... | collective-permute-start | bytes 479240 | tf_op jit(solution)/shard_map/ppermute | solution.py:656
  306.6 3.9 %collective-permute-start.29 = (f32[8,96]{0,1:T(8,128)S(1)}, f32[8,96]{0,1:T(8,128)S(1)}, u32[]{:S(2)}, u32[]{:S(2)}) collective-permute-start(f32[8,96]{0,1:T(8,128)S(1)} %slice_bitcast_fusion), channel_id=1, source_target_pairs={{0,24},{1,25},{2,26},{3,27},{4,28},{5,29},{6,30},{7,31},{8,16},{9,... | collective-permute-start | bytes 9224 | tf_op jit(solution)/shard_map/ppermute | solution.py:656
  306.6 4.6 %collective-permute-start.28 = (f32[8,96]{0,1:T(8,128)S(1)}, f32[8,96]{0,1:T(8,128)S(1)}, u32[]{:S(2)}, u32[]{:S(2)}) collective-permute-start(f32[8,96]{0,1:T(8,128)S(1)} %slice_bitcast_fusion), channel_id=1, source_target_pairs={{0,16},{1,17},{2,18},{3,19},{4,20},{5,21},{6,22},{7,23},{8,24},{9,... | collective-permute-start | bytes 9224 | tf_op jit(solution)/shard_map/ppermute | solution.py:656
  307.2 4.0 %collective-permute-start.27 = (f32[8,96]{0,1:T(8,128)S(1)}, f32[8,96]{0,1:T(8,128)S(1)}, u32[]{:S(2)}, u32[]{:S(2)}) collective-permute-start(f32[8,96]{0,1:T(8,128)S(1)} %slice_bitcast_fusion), channel_id=1, source_target_pairs={{0,8},{1,9},{2,10},{3,11},{4,12},{5,13},{6,14},{7,15},{8,0},{9,1},... | collective-permute-start | bytes 9224 | tf_op jit(solution)/shard_map/ppermute | solution.py:656
  (3 other events, 2.5 us)
